TPU v7x, 32 devices: a whole 2x2x4 slice. The times are simulated.
32 devices in a mesh: cp: 2 (over core), sp: 4 (over y, x), fsdp: 4 (over z).
Axes of the slice: x: 2, y: 2, z: 4, core: 2. Of those that a mesh axis runs over, the one named last changes fastest.
Arguments:
- tokens: bfloat16 [4, 2048, 1536], P('fsdp', ('cp', 'sp')), may hold values from -6 to 6
- out_cotangent: bfloat16 [4, 2048, 1536], P('fsdp', ('cp', 'sp')), may hold values from -6 to 6
- seq_lengths: int32 [4, 8], P('fsdp'), may hold values from 1 to 1024, 2048 in all within a row
- slab_place: int32 [4, 4], P('fsdp'), may hold values from 0 to 3, as said below
- attn_gain: float32 [1536], replicated, may hold values from 0.25 to 1.75
- query_weight: bfloat16 [1536, 1536], P('fsdp'), may hold values from -0.15625 to 0.15625
- key_weight: bfloat16 [1536, 1536], P('fsdp'), may hold values from -0.15625 to 0.15625
- value_weight: bfloat16 [1536, 1536], P('fsdp'), may hold values from -0.15625 to 0.15625
- outgate_weight: bfloat16 [1536, 1536], P('fsdp'), may hold values from -0.15625 to 0.15625
- forget_weight: bfloat16 [1536, 24], P('fsdp'), may hold values from -0.15625 to 0.15625
- forget_bias: float32 [24], replicated, may hold values from 3 to 9
- output_weight: bfloat16 [1536, 1536], P('fsdp'), may hold values from -1.25 to 1.25
- mlp_gain: float32 [1536], replicated, may hold values from 0.25 to 1.75
- gate_weight: bfloat16 [1536, 4096], P('fsdp'), may hold values from -0.15625 to 0.15625
- up_weight: bfloat16 [1536, 4096], P('fsdp'), may hold values from -0.15625 to 0.15625
- down_weight: bfloat16 [1536, 4096], P('fsdp'), may hold values from -0.09375 to 0.09375
Outputs:
- block_out: bfloat16 [4, 2048, 1536], P('fsdp', ('cp', 'sp'))
- tokens_grad: float32 [4, 2048, 1536], P('fsdp', ('cp', 'sp'))
- attn_gain_grad: float32 [1536], replicated
- query_grad: float32 [1536, 1536], P(('cp', 'sp', 'fsdp'))
- key_grad: float32 [1536, 1536], P(('cp', 'sp', 'fsdp'))
- value_grad: float32 [1536, 1536], P(('cp', 'sp', 'fsdp'))
- outgate_grad: float32 [1536, 1536], P(('cp', 'sp', 'fsdp'))
- forget_grad: float32 [1536, 24], P(('cp', 'sp', 'fsdp'))
- forget_bias_grad: float32 [24], replicated
- output_weight_grad: float32 [1536, 1536], P(('cp', 'sp', 'fsdp'))
- mlp_gain_grad: float32 [1536], replicated
- gate_grad: float32 [1536, 4096], P(('cp', 'sp', 'fsdp'))
- up_grad: float32 [1536, 4096], P(('cp', 'sp', 'fsdp'))
- down_grad: float32 [1536, 4096], P(('cp', 'sp', 'fsdp'))
Inputs may be any that keep to these rules, and one draw needn't show every extreme that they name: `seq_lengths`: each row sums to 2048, and its largest entry is exactly 1024. `slab_place`: each row is a permutation of 0 to 3 in which entries 2 * c and 2 * c + 1 sum to 3.
All inputs are finite; a program needn't handle non-finite values.
Results may differ from a plain program's by a relative error of at most 0.017.
Values may be sent and summed in bfloat16 or wider, within the bound.
A program may use at most 320 MiB of HBM per device.

v0:
```python
import jax
import jax.numpy as jnp
from jax import lax
from jax.sharding import PartitionSpec as P

epsilon = 1e-06
very_low = -1e30


def matmul(left, right):
    return jnp.dot(left, right, preferred_element_type=jnp.float32)


def matmul_right_t(left, right):
    return lax.dot_general(
        left, right, (((1,), (1,)), ((), ())), preferred_element_type=jnp.float32
    )


def matmul_left_t(left, right):
    return lax.dot_general(
        left, right, (((0,), (0,)), ((), ())), preferred_element_type=jnp.float32
    )


def rms_inverse(values):
    return lax.rsqrt(jnp.mean(values * values, axis=1, keepdims=True) + epsilon)


def norm_back(upstream, values, inverse, gain):
    weighted = upstream * gain
    return inverse * weighted - values * inverse**3 * jnp.mean(
        weighted * values, axis=1, keepdims=True
    )


def row_layout(place_row, lens_row, count, slab_rows):
    rows = jnp.arange(count, dtype=jnp.int32)
    slab_index = rows // slab_rows
    table = (
        slab_index[:, None] == jnp.arange(place_row.shape[0], dtype=jnp.int32)[None, :]
    ).astype(jnp.int32)
    position = jnp.sum(table * place_row[None, :], axis=1) * slab_rows + rows % slab_rows
    ends = jnp.cumsum(lens_row)
    segment = jnp.sum((position[:, None] >= ends[None, :]).astype(jnp.int32), axis=1)
    return (position, segment)


def forget_prefix(log_all, place_row, slab_rows):
    slabs = place_row.shape[0]
    steps = log_all.astype(jnp.float32).reshape(slabs, slab_rows, -1)
    inside = jnp.cumsum(steps, axis=1)
    totals = inside[:, -1, :]
    earlier = (place_row[None, :] < place_row[:, None]).astype(jnp.float32)
    offsets = jnp.dot(earlier, totals, precision=lax.Precision.HIGHEST)
    return (inside + offsets[:, None, :]).reshape(slabs * slab_rows, -1)


def prefix_back(grad_prefix, place_row, slab_rows):
    slabs = place_row.shape[0]
    steps = grad_prefix.reshape(slabs, slab_rows, -1)
    inside = jnp.flip(jnp.cumsum(jnp.flip(steps, 1), axis=1), 1)
    totals = inside[:, 0, :]
    later = (place_row[None, :] > place_row[:, None]).astype(jnp.float32)
    offsets = jnp.dot(later, totals, precision=lax.Precision.HIGHEST)
    return (inside + offsets[:, None, :]).reshape(slabs * slab_rows, -1)


def local(
    tokens,
    out_cotangent,
    seq_lengths,
    slab_place,
    attn_gain,
    query_weight,
    key_weight,
    value_weight,
    outgate_weight,
    forget_weight,
    forget_bias,
    output_weight,
    mlp_gain,
    gate_weight,
    up_weight,
    down_weight,
):
    seq_devices = lax.axis_size("sp")
    ctx_devices = lax.axis_size("cp")
    ctx_index = lax.axis_index("cp")
    tok_rows = tokens.shape[1]
    model_width = tokens.shape[2]
    head_count = forget_weight.shape[1]
    local_heads = head_count // seq_devices
    head_size = model_width // head_count
    ctx_rows = tok_rows * seq_devices
    group_rows = ctx_rows * ctx_devices
    slab_rows = ctx_rows // 2
    key_block = min(512, group_rows)
    key_blocks = group_rows // key_block
    score_scale = head_size ** (-0.5)
    place_row = slab_place[0]
    lens_row = seq_lengths[0]
    ctx_start = ctx_index * ctx_rows
    inputs = tokens[0]
    input_f = inputs.astype(jnp.float32)
    weights_attn = (
        lax.all_gather(query_weight, "fsdp", axis=0, tiled=True),
        lax.all_gather(key_weight, "fsdp", axis=0, tiled=True),
        lax.all_gather(value_weight, "fsdp", axis=0, tiled=True),
        lax.all_gather(outgate_weight, "fsdp", axis=0, tiled=True),
        lax.all_gather(forget_weight, "fsdp", axis=0, tiled=True),
        lax.all_gather(output_weight, "fsdp", axis=0, tiled=True),
    )
    full_query, full_key, full_value, full_outgate, full_forget, full_output = weights_attn
    inv_first = rms_inverse(input_f)
    normed = (input_f * inv_first * attn_gain).astype(jnp.bfloat16)
    queries = matmul(normed, full_query).astype(jnp.bfloat16)
    keys = matmul(normed, full_key).astype(jnp.bfloat16)
    values = matmul(normed, full_value).astype(jnp.bfloat16)
    out_gate = jax.nn.sigmoid(matmul(normed, full_outgate))
    forget_pre = matmul(normed, full_forget) + forget_bias
    log_forget = jax.nn.log_sigmoid(forget_pre).astype(jnp.bfloat16)
    head_query, head_key, head_value, head_forget = (
        lax.all_to_all(queries, "sp", split_axis=1, concat_axis=0, tiled=True),
        lax.all_to_all(keys, "sp", split_axis=1, concat_axis=0, tiled=True),
        lax.all_to_all(values, "sp", split_axis=1, concat_axis=0, tiled=True),
        lax.all_to_all(log_forget, "sp", split_axis=1, concat_axis=0, tiled=True),
    )
    keys_all, values_all, forget_all = (
        lax.all_gather(head_key, "cp", axis=0, tiled=True),
        lax.all_gather(head_value, "cp", axis=0, tiled=True),
        lax.all_gather(head_forget, "cp", axis=0, tiled=True),
    )
    prefix_all = forget_prefix(forget_all, place_row, slab_rows)
    pos_all, seg_all = row_layout(place_row, lens_row, group_rows, slab_rows)
    query_pos = lax.dynamic_slice_in_dim(pos_all, ctx_start, ctx_rows, 0)
    query_seg = lax.dynamic_slice_in_dim(seg_all, ctx_start, ctx_rows, 0)
    query_prefix = lax.dynamic_slice_in_dim(prefix_all, ctx_start, ctx_rows, 0)
    query_three = head_query.reshape(ctx_rows, local_heads, head_size)
    query_pos_top = jnp.max(query_pos)
    query_seg_low = jnp.min(query_seg)
    query_seg_top = jnp.max(query_seg)
    key_pieces = (
        keys_all.reshape(key_blocks, key_block, local_heads, head_size),
        values_all.reshape(key_blocks, key_block, local_heads, head_size),
        prefix_all.reshape(key_blocks, key_block, local_heads),
        pos_all.reshape(key_blocks, key_block),
        seg_all.reshape(key_blocks, key_block),
    )

    def block_live(key_pos, key_seg):
        return (
            (query_pos_top >= jnp.min(key_pos))
            & (query_seg_top >= jnp.min(key_seg))
            & (jnp.max(key_seg) >= query_seg_low)
        )

    def block_scores(key_piece, key_prefix, key_pos, key_seg):
        raw = (
            jnp.einsum("qhd,khd->hqk", query_three, key_piece, preferred_element_type=jnp.float32)
            * score_scale
        )
        raw = raw + query_prefix.T[:, :, None] - key_prefix.T[:, None, :]
        allowed = (query_pos[:, None] >= key_pos[None, :]) & (
            query_seg[:, None] == key_seg[None, :]
        )
        return (raw, allowed[None, :, :])

    def total_work(carry, piece):
        running_max, running_sum = carry
        key_piece, value_piece, key_prefix, key_pos, key_seg = piece
        raw, allowed = block_scores(key_piece, key_prefix, key_pos, key_seg)
        new_max = jnp.maximum(running_max, jnp.max(jnp.where(allowed, raw, very_low), axis=2))
        terms = jnp.where(allowed, jnp.exp(raw - new_max[:, :, None]), 0.0)
        new_sum = running_sum * jnp.exp(running_max - new_max) + jnp.sum(terms, axis=2)
        return (new_max, new_sum)

    def total_step(carry, piece):
        live = block_live(piece[3], piece[4])
        return (lax.cond(live, total_work, lambda held, unused: held, carry, piece), None)

    start_max = jnp.full((local_heads, ctx_rows), very_low, jnp.float32)
    start_sum = jnp.zeros((local_heads, ctx_rows), jnp.float32)
    (final_max, final_sum), _ = lax.scan(total_step, (start_max, start_sum), key_pieces)
    log_total = final_max + jnp.log(final_sum)

    def output_work(carry, piece):
        coarse, fine = carry
        key_piece, value_piece, key_prefix, key_pos, key_seg = piece
        raw, allowed = block_scores(key_piece, key_prefix, key_pos, key_seg)
        probs = jnp.where(allowed, jnp.exp(raw - log_total[:, :, None]), 0.0)
        rounded = probs.astype(jnp.bfloat16)
        rest = (probs - rounded.astype(jnp.float32)).astype(jnp.bfloat16)
        coarse = coarse + jnp.einsum(
            "hqk,khd->qhd", rounded, value_piece, preferred_element_type=jnp.float32
        )
        fine = fine + jnp.einsum(
            "hqk,khd->qhd", rest, value_piece, preferred_element_type=jnp.float32
        )
        return (coarse, fine)

    def output_step(carry, piece):
        live = block_live(piece[3], piece[4])
        return (lax.cond(live, output_work, lambda held, unused: held, carry, piece), None)

    zero_out = jnp.zeros((ctx_rows, local_heads, head_size), jnp.float32)
    (coarse_out, fine_out), _ = lax.scan(output_step, (zero_out, zero_out), key_pieces)
    exact_out = coarse_out + fine_out
    head_out = coarse_out.reshape(ctx_rows, local_heads * head_size).astype(jnp.bfloat16)
    token_out = lax.all_to_all(head_out, "sp", split_axis=0, concat_axis=1, tiled=True)
    token_out_f = token_out.astype(jnp.float32)
    gated = (token_out_f * out_gate).astype(jnp.bfloat16)
    mid = input_f + matmul(gated, full_output)
    weights_mlp = (
        lax.all_gather(gate_weight, "fsdp", axis=0, tiled=True),
        lax.all_gather(up_weight, "fsdp", axis=0, tiled=True),
        lax.all_gather(down_weight, "fsdp", axis=0, tiled=True),
    )
    full_gate, full_up, full_down = weights_mlp
    inv_second = rms_inverse(mid)
    normed_mlp = (mid * inv_second * mlp_gain).astype(jnp.bfloat16)
    gate_lin = matmul(normed_mlp, full_gate)
    up_lin = matmul(normed_mlp, full_up)
    gate_sig = jax.nn.sigmoid(gate_lin)
    activated = gate_lin * gate_sig
    hidden = (activated * up_lin).astype(jnp.bfloat16)
    block_out = (mid + matmul_right_t(hidden, full_down)).astype(jnp.bfloat16)
    cotangent = out_cotangent[0]
    grad_hidden = matmul(cotangent, full_down)
    grad_gate_lin = (grad_hidden * up_lin * gate_sig * (1.0 + gate_lin * (1.0 - gate_sig))).astype(
        jnp.bfloat16
    )
    grad_up_lin = (grad_hidden * activated).astype(jnp.bfloat16)
    grad_normed_mlp = matmul_right_t(grad_gate_lin, full_gate) + matmul_right_t(
        grad_up_lin, full_up
    )
    mlp_gain_term = jnp.sum(grad_normed_mlp * mid * inv_second, axis=0)
    grad_mid = cotangent.astype(jnp.float32) + norm_back(grad_normed_mlp, mid, inv_second, mlp_gain)
    gate_term = matmul_left_t(normed_mlp, grad_gate_lin)
    up_term = matmul_left_t(normed_mlp, grad_up_lin)
    down_term = matmul_left_t(cotangent, hidden)
    grad_branch = grad_mid.astype(jnp.bfloat16)
    grad_gated = matmul_right_t(grad_branch, full_output)
    grad_attended = (grad_gated * out_gate).astype(jnp.bfloat16)
    grad_gate_pre = (grad_gated * token_out_f * out_gate * (1.0 - out_gate)).astype(jnp.bfloat16)
    head_grad = lax.all_to_all(grad_attended, "sp", split_axis=1, concat_axis=0, tiled=True)
    grad_three = head_grad.reshape(ctx_rows, local_heads, head_size)
    delta = jnp.sum(grad_three.astype(jnp.float32) * exact_out, axis=2).T

    def back_work(carry, piece):
        grad_query_acc, grad_prefix_acc = carry
        key_piece, value_piece, key_prefix, key_pos, key_seg = piece
        raw, allowed = block_scores(key_piece, key_prefix, key_pos, key_seg)
        probs = jnp.where(allowed, jnp.exp(raw - log_total[:, :, None]), 0.0)
        rounded = probs.astype(jnp.bfloat16)
        grad_probs = jnp.einsum(
            "qhd,khd->hqk", grad_three, value_piece, preferred_element_type=jnp.float32
        )
        grad_scores = (probs * (grad_probs - delta[:, :, None])).astype(jnp.bfloat16)
        grad_query_acc = (
            grad_query_acc
            + jnp.einsum("hqk,khd->qhd", grad_scores, key_piece, preferred_element_type=jnp.float32)
            * score_scale
        )
        key_term = (
            jnp.einsum("hqk,qhd->khd", grad_scores, query_three, preferred_element_type=jnp.float32)
            * score_scale
        )
        value_term = jnp.einsum(
            "hqk,qhd->khd", rounded, grad_three, preferred_element_type=jnp.float32
        )
        score_f = grad_scores.astype(jnp.float32)
        grad_prefix_acc = grad_prefix_acc + jnp.sum(score_f, axis=2)
        prefix_term = -jnp.sum(score_f, axis=1)
        return ((grad_query_acc, grad_prefix_acc), (key_term, value_term, prefix_term))

    def back_skip(carry, piece):
        empty_kv = jnp.zeros((key_block, local_heads, head_size), jnp.float32)
        empty_prefix = jnp.zeros((local_heads, key_block), jnp.float32)
        return (carry, (empty_kv, empty_kv, empty_prefix))

    def back_step(carry, piece):
        live = block_live(piece[3], piece[4])
        return lax.cond(live, back_work, back_skip, carry, piece)

    start_prefix = jnp.zeros((local_heads, ctx_rows), jnp.float32)
    (grad_query_acc, grad_prefix_q), (key_terms, value_terms, prefix_terms) = lax.scan(
        back_step, (zero_out, start_prefix), key_pieces
    )
    keys_grad_all = key_terms.reshape(group_rows, local_heads * head_size)
    values_grad_all = value_terms.reshape(group_rows, local_heads * head_size)
    prefix_grad_all = jnp.transpose(prefix_terms, (0, 2, 1)).reshape(group_rows, local_heads)
    own_prefix = lax.dynamic_slice_in_dim(prefix_grad_all, ctx_start, ctx_rows, 0)
    prefix_grad_all = lax.dynamic_update_slice_in_dim(
        prefix_grad_all, own_prefix + grad_prefix_q.T, ctx_start, 0
    )
    forget_grad_term = prefix_back(prefix_grad_all, place_row, slab_rows)
    key_sum, value_sum, forget_sum = (
        lax.psum_scatter(keys_grad_all, "cp", scatter_dimension=0, tiled=True),
        lax.psum_scatter(values_grad_all, "cp", scatter_dimension=0, tiled=True),
        lax.psum_scatter(forget_grad_term, "cp", scatter_dimension=0, tiled=True),
    )
    grad_query_head = grad_query_acc.reshape(ctx_rows, local_heads * head_size).astype(jnp.bfloat16)
    grad_query_tok, grad_key_tok, grad_value_tok, grad_forget_tok = (
        lax.all_to_all(grad_query_head, "sp", split_axis=0, concat_axis=1, tiled=True),
        lax.all_to_all(key_sum.astype(jnp.bfloat16), "sp", split_axis=0, concat_axis=1, tiled=True),
        lax.all_to_all(
            value_sum.astype(jnp.bfloat16), "sp", split_axis=0, concat_axis=1, tiled=True
        ),
        lax.all_to_all(
            forget_sum.astype(jnp.bfloat16), "sp", split_axis=0, concat_axis=1, tiled=True
        ),
    )
    grad_forget_pre = (grad_forget_tok.astype(jnp.float32) * jax.nn.sigmoid(-forget_pre)).astype(
        jnp.bfloat16
    )
    grad_normed = (
        matmul_right_t(grad_query_tok, full_query)
        + matmul_right_t(grad_key_tok, full_key)
        + matmul_right_t(grad_value_tok, full_value)
        + matmul_right_t(grad_gate_pre, full_outgate)
        + matmul_right_t(grad_forget_pre, full_forget)
    )
    attn_gain_term = jnp.sum(grad_normed * input_f * inv_first, axis=0)
    bias_term = jnp.sum(grad_forget_pre.astype(jnp.float32), axis=0)
    tokens_grad = grad_mid + norm_back(grad_normed, input_f, inv_first, attn_gain)
    query_term = matmul_left_t(normed, grad_query_tok)
    key_term_w = matmul_left_t(normed, grad_key_tok)
    value_term_w = matmul_left_t(normed, grad_value_tok)
    outgate_term = matmul_left_t(normed, grad_gate_pre)
    forget_term = matmul_left_t(normed, grad_forget_pre)
    output_term = matmul_left_t(gated, grad_branch)
    (
        query_grad,
        key_grad,
        value_grad,
        outgate_grad,
        forget_grad,
        output_weight_grad,
        gate_grad,
        up_grad,
        down_grad,
    ) = (
        lax.psum_scatter(query_term, ("cp", "sp", "fsdp"), scatter_dimension=0, tiled=True),
        lax.psum_scatter(key_term_w, ("cp", "sp", "fsdp"), scatter_dimension=0, tiled=True),
        lax.psum_scatter(value_term_w, ("cp", "sp", "fsdp"), scatter_dimension=0, tiled=True),
        lax.psum_scatter(outgate_term, ("cp", "sp", "fsdp"), scatter_dimension=0, tiled=True),
        lax.psum_scatter(forget_term, ("cp", "sp", "fsdp"), scatter_dimension=0, tiled=True),
        lax.psum_scatter(output_term, ("cp", "sp", "fsdp"), scatter_dimension=0, tiled=True),
        lax.psum_scatter(gate_term, ("cp", "sp", "fsdp"), scatter_dimension=0, tiled=True),
        lax.psum_scatter(up_term, ("cp", "sp", "fsdp"), scatter_dimension=0, tiled=True),
        lax.psum_scatter(down_term, ("cp", "sp", "fsdp"), scatter_dimension=0, tiled=True),
    )
    attn_gain_grad, mlp_gain_grad, forget_bias_grad = lax.psum(
        (attn_gain_term, mlp_gain_term, bias_term), ("cp", "sp", "fsdp")
    )
    return (
        block_out[None],
        tokens_grad[None],
        attn_gain_grad,
        query_grad,
        key_grad,
        value_grad,
        outgate_grad,
        forget_grad,
        forget_bias_grad,
        output_weight_grad,
        mlp_gain_grad,
        gate_grad,
        up_grad,
        down_grad,
    )


def solution(mesh):
    return jax.shard_map(
        local,
        mesh=mesh,
        in_specs=(
            P("fsdp", ("cp", "sp"), None),
            P("fsdp", ("cp", "sp"), None),
            P("fsdp", None),
            P("fsdp", None),
            P(),
            P("fsdp", None),
            P("fsdp", None),
            P("fsdp", None),
            P("fsdp", None),
            P("fsdp", None),
            P(),
            P("fsdp", None),
            P(),
            P("fsdp", None),
            P("fsdp", None),
            P("fsdp", None),
        ),
        out_specs=(
            P("fsdp", ("cp", "sp"), None),
            P("fsdp", ("cp", "sp"), None),
            P(),
            P(("cp", "sp", "fsdp"), None),
            P(("cp", "sp", "fsdp"), None),
            P(("cp", "sp", "fsdp"), None),
            P(("cp", "sp", "fsdp"), None),
            P(("cp", "sp", "fsdp"), None),
            P(),
            P(("cp", "sp", "fsdp"), None),
            P(),
            P(("cp", "sp", "fsdp"), None),
            P(("cp", "sp", "fsdp"), None),
            P(("cp", "sp", "fsdp"), None),
        ),
        check_vma=False,
    )
```

profile of v0, /device:TPU:0, one launch (start us, length us, event | category | flops | bytes accessed | tf_op | source)
XLA Modules:
  0.0 3057.0 jit_solution(643972691816850880)
XLA Ops:
  10.3 91.5 %all-gather.11.cloned.1.call-done = bf16[1536,1536]{1,0:T(8,128)(2,1)} async-done(((bf16[384,1536]{1,0:T(8,128)(2,1)}), bf16[1536,1536]{1,0:T(8,128)(2,1)}) %all-gather.11.cloned.1.call-update) | async-done | bytes 4718608 | tf_op jit(solution)/shard_map/all_gather | solution.py:108
  120.7 70.6 %all-gather.17.cloned.1.call-done = bf16[1536,1536]{1,0:T(8,128)(2,1)} async-done(((bf16[384,1536]{1,0:T(8,128)(2,1)}), bf16[1536,1536]{1,0:T(8,128)(2,1)}) %all-gather.17.cloned.1.call-update) | async-done | bytes 4718608 | tf_op jit(solution)/shard_map/all_gather | solution.py:109
  246.8 34.9 %all-gather.15.cloned.1.call-done = bf16[1536,1536]{1,0:T(8,128)(2,1)} async-done(((bf16[384,1536]{1,0:T(8,128)(2,1)}), bf16[1536,1536]{1,0:T(8,128)(2,1)}) %all-gather.15.cloned.1.call-update) | async-done | bytes 4718608 | tf_op jit(solution)/shard_map/all_gather | solution.py:107
  318.0 53.0 %while.42 = (s32[]{:T(128)}, f32[6,1024]{1,0:T(8,128)S(1)}, f32[6,1024]{1,0:T(8,128)S(1)}, s32[4,512]{1,0:T(4,128)S(1)}, s32[]{:T(128)}, /*index=5*/s32[4,512]{1...) while((s32[]{:T(128)}, f32[6,1024]{1,0:T(8,128)S(1)}, ...), condition=%wide.region_17.18_spmd, body=%wide.region_9.17_spmd.sunk | while | flops 438842880 | bytes 28369236 | solution.py:184
  373.8 67.4 %while.43 = (s32[]{:T(128)}, f32[1024,6,64]{0,2,1:T(8,128)}, f32[1024,6,64]{0,2,1:T(8,128)}, s32[4,512]{1,0:T(4,128)S(1)}, s32[]{:T(128)}, /*index=5*/s32[4,512]...) while((s32[]{:T(128)}, f32[1024,6,64]{0,2,1:T(8,128)}, ...), condition=%wide.region_24.25_spmd, body=%wide.region_18.24_spmd.sunk | while | flops 1257506304 | bytes 79245824 | solution.py:207
  466.3 19.2 all-gather.23.cloned.1.call-done
  489.7 213.9 %all-gather.25.cloned.1.call-done = bf16[1536,4096]{1,0:T(8,128)(2,1)} async-done(((bf16[384,4096]{1,0:T(8,128)(2,1)}), bf16[1536,4096]{1,0:T(8,128)(2,1)}) %all-gather.25.cloned.1.call-update) | async-done | bytes 12582928 | tf_op jit(solution)/shard_map/all_gather | solution.py:215
  713.2 208.5 %all-gather.27.cloned.1.call-done = bf16[1536,4096]{1,0:T(8,128)(2,1)} async-done(((bf16[384,4096]{1,0:T(8,128)(2,1)}), bf16[1536,4096]{1,0:T(8,128)(2,1)}) %all-gather.27.cloned.1.call-update) | async-done | bytes 12582928 | tf_op jit(solution)/shard_map/all_gather | solution.py:216
  931.2 208.3 %all-gather.29.cloned.1.call-done = bf16[1536,4096]{1,0:T(8,128)(2,1)} async-done(((bf16[384,4096]{1,0:T(8,128)(2,1)}), bf16[1536,4096]{1,0:T(8,128)(2,1)}) %all-gather.29.cloned.1.call-update) | async-done | bytes 12582928 | tf_op jit(solution)/shard_map/all_gather | solution.py:217
  1196.7 242.5 %while.44 = (s32[]{:T(128)}, f32[1024,6,64]{0,2,1:T(8,128)S(1)}, f32[6,1024]{1,0:T(8,128)S(1)}, f32[4,512,6,64]{1,0,3,2:T(4,128)}, f32[4,512,6,64]{1,0,3,2:T(4,1...) while((s32[]{:T(128)}, f32[1024,6,64]{0,2,1:T(8,128)S(1)}, ...), condition=%wide.region_36.37_spmd, body=%wide.region_28.36_spmd.sunk | while | flops 2069300736 | bytes 73893824 | solution.py:287
  1201.7 21.0 conditional.8
  1262.2 21.0 conditional.8
  1322.7 21.0 conditional.8
  1383.2 21.0 conditional.8
  1575.0 24.9 copy.260
  1626.1 40.5 %all-reduce = (f32[1536]{0:T(1024)}, f32[24]{0:T(128)}, f32[1536]{0:T(1024)}) all-reduce(f32[1536]{0:T(1024)S(1)} %get-tuple-element.989, f32[24]{0:T(128)S(1)} %get-tuple-element.1107, f32[1536]{0:T(1024)S(1)} %copy-done.43), channel_id=1, replica_groups=mesh['cp'=2,'sp'=4,'fsdp'=4] {'cp','sp','fsdp'}, use_global_device_ids=true, to_apply=%region_44.45 | all-reduce | flops 3096 | bytes 24768 | tf_op jit(solution)/shard_map/psum | solution.py:354
  1669.7 56.7 %reduce-scatter.29.cloned.1.call-done = f32[48,1536]{1,0:T(8,128)} async-done(((f32[1536,1536]{1,0:T(8,128)}), f32[48,1536]{1,0:T(8,128)}) %reduce-scatter.29.cloned.1.call-update) | async-done | bytes 294928 | tf_op jit(solution)/shard_map/reduce_scatter | solution.py:347
  1726.4 141.9 %reduce-scatter.31.cloned.1.call-done = f32[48,1536]{1,0:T(8,128)} async-done(((f32[1536,1536]{1,0:T(8,128)}), f32[48,1536]{1,0:T(8,128)}) %reduce-scatter.31.cloned.1.call-update) | async-done | bytes 294928 | tf_op jit(solution)/shard_map/reduce_scatter | solution.py:349
  1868.2 141.0 %reduce-scatter.23.cloned.1.call-done = f32[48,1536]{1,0:T(8,128)} async-done(((f32[1536,1536]{1,0:T(8,128)}), f32[48,1536]{1,0:T(8,128)}) %reduce-scatter.23.cloned.1.call-update) | async-done | bytes 294928 | tf_op jit(solution)/shard_map/reduce_scatter | solution.py:344
  2009.2 141.9 %reduce-scatter.25.cloned.1.call-done = f32[48,1536]{1,0:T(8,128)} async-done(((f32[1536,1536]{1,0:T(8,128)}), f32[48,1536]{1,0:T(8,128)}) %reduce-scatter.25.cloned.1.call-update) | async-done | bytes 294928 | tf_op jit(solution)/shard_map/reduce_scatter | solution.py:345
  2151.1 141.1 %reduce-scatter.27.cloned.1.call-done = f32[48,1536]{1,0:T(8,128)} async-done(((f32[1536,1536]{1,0:T(8,128)}), f32[48,1536]{1,0:T(8,128)}) %reduce-scatter.27.cloned.1.call-update) | async-done | bytes 294928 | tf_op jit(solution)/shard_map/reduce_scatter | solution.py:346
  2292.2 252.4 %reduce-scatter.33.cloned.1.call-done = f32[48,4096]{1,0:T(8,128)} async-done(((f32[1536,4096]{1,0:T(8,128)}), f32[48,4096]{1,0:T(8,128)}) %reduce-scatter.33.cloned.1.call-update) | async-done | bytes 786448 | tf_op jit(solution)/shard_map/reduce_scatter | solution.py:350
  2544.6 252.0 %reduce-scatter.35.cloned.1.call-done = f32[48,4096]{1,0:T(8,128)} async-done(((f32[1536,4096]{1,0:T(8,128)}), f32[48,4096]{1,0:T(8,128)}) %reduce-scatter.35.cloned.1.call-update) | async-done | bytes 786448 | tf_op jit(solution)/shard_map/reduce_scatter | solution.py:351
  2796.7 253.2 %reduce-scatter.39.cloned.1.call-done = f32[48,4096]{1,0:T(8,128)} async-done(((f32[1536,4096]{1,0:T(8,128)}), f32[48,4096]{1,0:T(8,128)}) %reduce-scatter.39.cloned.1.call-update) | async-done | bytes 786448
  (462 shorter events, 783.4 us)
Async XLA Ops:
  7.2 94.5 %all-gather.11.cloned.1.call-start = ((), (), s32[]{:S(2)}) async-start(), calls=%async_computation.22 | async-start | bytes 5898240 | tf_op jit(solution)/shard_map/all_gather | solution.py:108
  7.9 183.3 %all-gather.17.cloned.1.call-start = ((), (), s32[]{:S(2)}) async-start(), calls=%async_computation.25 | async-start | bytes 5898240 | tf_op jit(solution)/shard_map/all_gather | solution.py:109
  8.7 273.1 %all-gather.15.cloned.1.call-start = ((), (), s32[]{:S(2)}) async-start(), calls=%async_computation.24 | async-start | bytes 5898240 | tf_op jit(solution)/shard_map/all_gather | solution.py:107
  9.4 293.3 %all-gather.13.cloned.1.call-start = ((), (), s32[]{:S(2)}) async-start(), calls=%async_computation.23 | async-start | bytes 2359296 | tf_op jit(solution)/shard_map/all_gather | solution.py:130
  120.6 188.0 %all-gather.19.cloned.1.call-start = ((), (), s32[]{:S(2)}) async-start(), calls=%async_computation.26 | async-start | bytes 2359296 | tf_op jit(solution)/shard_map/all_gather | solution.py:131
  210.1 250.0 %all-gather.21.cloned.1.call-start = ((), (), s32[]{:S(2)}) async-start(), calls=%async_computation.27 | async-start | bytes 5898240 | tf_op jit(solution)/shard_map/all_gather | solution.py:110
  210.6 274.8 %all-gather.23.cloned.1.call-start = ((), (), s32[]{:S(2)}) async-start(), calls=%async_computation.28 | async-start | bytes 5898240 | tf_op jit(solution)/shard_map/all_gather | solution.py:112
  211.4 492.3 %all-gather.25.cloned.1.call-start = ((), (), s32[]{:S(2)}) async-start(), calls=%async_computation.29 | async-start | bytes 15728640 | tf_op jit(solution)/shard_map/all_gather | solution.py:215
  212.1 709.5 %all-gather.27.cloned.1.call-start = ((), (), s32[]{:S(2)}) async-start(), calls=%async_computation.30 | async-start | bytes 15728640 | tf_op jit(solution)/shard_map/all_gather | solution.py:216
  212.9 926.6 %all-gather.29.cloned.1.call-start = ((), (), s32[]{:S(2)}) async-start(), calls=%async_computation.31 | async-start | bytes 15728640 | tf_op jit(solution)/shard_map/all_gather | solution.py:217
  286.5 14.8 all-to-all-start.1
  1175.8 14.9 all-to-all-start.5
  1179.5 279.9 %reduce-scatter.21.cloned.1.call-start = ((), (), s32[]{:S(2)}) async-start(), calls=%async_computation.34 | async-start | bytes 98304 | tf_op jit(solution)/shard_map/reduce_scatter | solution.py:301
  1449.2 50.6 %reduce-scatter.17.cloned.1.call-start = ((), (), s32[]{:S(2)}) async-start(), calls=%async_computation.32 | async-start | bytes 4718592 | tf_op jit(solution)/shard_map/reduce_scatter | solution.py:299
  1454.3 64.2 %reduce-scatter.19.cloned.1.call-start = ((), (), s32[]{:S(2)}) async-start(), calls=%async_computation.33 | async-start | bytes 4718592 | tf_op jit(solution)/shard_map/reduce_scatter | solution.py:300
  1459.3 152.3 %reduce-scatter.37.cloned.1.call-start = ((), (), s32[]{:S(2)}) async-start(), calls=%async_computation.42 | async-start | bytes 811008
  1469.2 257.2 %reduce-scatter.29.cloned.1.call-start = ((), (), s32[]{:S(2)}) async-start(), calls=%async_computation.38 | async-start | bytes 9732096 | tf_op jit(solution)/shard_map/reduce_scatter | solution.py:347
  1474.4 393.8 %reduce-scatter.31.cloned.1.call-start = ((), (), s32[]{:S(2)}) async-start(), calls=%async_computation.39 | async-start | bytes 9732096 | tf_op jit(solution)/shard_map/reduce_scatter | solution.py:349
  1482.0 527.2 %reduce-scatter.23.cloned.1.call-start = ((), (), s32[]{:S(2)}) async-start(), calls=%async_computation.35 | async-start | bytes 9732096 | tf_op jit(solution)/shard_map/reduce_scatter | solution.py:344
  1499.8 651.3 %reduce-scatter.25.cloned.1.call-start = ((), (), s32[]{:S(2)}) async-start(), calls=%async_computation.36 | async-start | bytes 9732096 | tf_op jit(solution)/shard_map/reduce_scatter | solution.py:345
  1518.4 773.8 %reduce-scatter.27.cloned.1.call-start = ((), (), s32[]{:S(2)}) async-start(), calls=%async_computation.37 | async-start | bytes 9732096 | tf_op jit(solution)/shard_map/reduce_scatter | solution.py:346
  1537.1 1007.5 %reduce-scatter.33.cloned.1.call-start = ((), (), s32[]{:S(2)}) async-start(), calls=%async_computation.40 | async-start | bytes 25952256 | tf_op jit(solution)/shard_map/reduce_scatter | solution.py:350
  1550.1 1246.6 %reduce-scatter.35.cloned.1.call-start = ((), (), s32[]{:S(2)}) async-start(), calls=%async_computation.41 | async-start | bytes 25952256 | tf_op jit(solution)/shard_map/reduce_scatter | solution.py:351
  1561.9 1488.0 %reduce-scatter.39.cloned.1.call-start = ((), (), s32[]{:S(2)}) async-start(), calls=%async_computation.43 | async-start | bytes 25952256
  (71 other events, 2166.4 us)
Sparse Core Ops, SparseCore 0:
  9.6 92.0 all-gather.10
  103.3 87.8 all-gather.16
  192.8 88.9 all-gather.14
  283.1 8.3 all-gather.12
  292.9 10.9 all-gather.18
  305.3 90.5 all-gather.20
  397.5 87.8 all-gather.22
  487.0 216.6 all-gather.24
  705.3 216.3 all-gather.26
  923.1 216.3 all-gather.28
  1449.4 4.6 reduce-scatter.20
  1456.2 12.0 reduce-scatter.16
  1470.6 12.0 reduce-scatter.18
  1487.7 96.6 reduce-scatter.36
  1590.7 135.6 reduce-scatter.28
  1733.7 134.4 reduce-scatter.30
  1874.5 134.6 reduce-scatter.22
  2016.5 134.5 reduce-scatter.24
  2157.6 134.6 reduce-scatter.26
  2300.2 244.3 reduce-scatter.32
  2551.6 244.9 reduce-scatter.34
  2804.8 245.0 reduce-scatter.38
where the time goes:
time: 3070 us; the launch traced here: 3060 us
  waiting for transfers between devices  2260 us (74%)
  matrix products  298 us (10%)
  local copies, waits for them, and re-layouts  223 us (7%)
  blocking collectives  138 us (4%)
  other arithmetic  63.5 us (2%)
  loops' own time  48.8 us (2%)
    unnamed x24, waiting for transfers between devices  259 us
    reduce_scatter x1, waiting for transfers between devices, local(): lax.psum_scatter(gate_term, ('cp', 'sp', 'fsdp'), scatter_dimension=0, ti...  252 us
    reduce_scatter x1, waiting for transfers between devices, local(): lax.psum_scatter(up_term, ('cp', 'sp', 'fsdp'), scatter_dimension=0, tile...  252 us
    all_gather x1, waiting for transfers between devices, local(): lax.all_gather(gate_weight, 'fsdp', axis=0, tiled=True)  214 us
    all_gather x1, waiting for transfers between devices, local(): lax.all_gather(up_weight, 'fsdp', axis=0, tiled=True)  208 us
    all_gather x1, waiting for transfers between devices, local(): lax.all_gather(down_weight, 'fsdp', axis=0, tiled=True)  208 us
    reduce_scatter x1, waiting for transfers between devices, local(): lax.psum_scatter(key_term_w, ('cp', 'sp', 'fsdp'), scatter_dimension=0, t...  142 us
    reduce_scatter x1, waiting for transfers between devices, local(): lax.psum_scatter(output_term, ('cp', 'sp', 'fsdp'), scatter_dimension=0,...  142 us
  transfers between devices with their start and end apart: 25, of which 18 were waited for; matrix products, arithmetic and copies ran while one was open for 10% of the time, Pallas kernels for 0%

commit v1 on v0

--- a/solution.py
+++ b/solution.py
@@ -1,10 +1,19 @@
+import functools
+
 import jax
 import jax.numpy as jnp
 from jax import lax
+from jax.experimental import pallas as pl
+from jax.experimental.pallas import tpu as pltpu
 from jax.sharding import PartitionSpec as P
 
 epsilon = 1e-06
 very_low = -1e30
+MESH = pl.DeviceIdType.MESH
+BF = jnp.bfloat16
+F32 = jnp.float32
+REMOTE = pltpu.make_async_remote_copy
+VMEM_BYTES = 60 * 1024 * 1024
 
 
 def matmul(left, right):
@@ -372,9 +381,891 @@
     )
 
 
-def solution(mesh):
+def here():
+    return (lax.axis_index("cp"), lax.axis_index("sp"), lax.axis_index("fsdp"))
+
+
+def flip(s, k):
+    if k == 1:
+        return s + 1 - 2 * lax.rem(s, 2)
+    if k == 2:
+        return lax.rem(s + 2, 4)
+    return 3 - s
+
+
+def greet(devices):
+    sem = pltpu.get_barrier_semaphore()
+    for device in devices:
+        pl.semaphore_signal(sem, inc=1, device_id=device, device_id_type=MESH)
+    pl.semaphore_wait(sem, len(devices))
+
+
+def rows_of(index, count):
+    return pl.ds(pl.multiple_of(index * count, count), count)
+
+
+def row_loop(total, step, body):
+    def one(i, carry):
+        return body(rows_of(i, step), carry)
+
+    return one, total // step
+
+
+class Gather:
+    sems = 13
+
+    def __init__(self, src, out, send, recv):
+        c, s, f = here()
+        self.src, self.out, self.send, self.recv = src, out, send, recv
+        self.c, self.s, self.rows = c, s, src.shape[0]
+        self.x, self.y, self.sib = (c, flip(s, 1), f), (c, flip(s, 2), f), (1 - c, s, f)
+        self.made = []
+
+    def block(self, k, half=None):
+        index = self.c * 4 + (self.s if k == 0 else flip(self.s, k))
+        n = self.rows
+        if half is None:
+            return self.out.at[pl.ds(pl.multiple_of(index * n, n), n)]
+        return self.out.at[pl.ds(pl.multiple_of(index * n + half * (n // 2), n // 2), n // 2)]
+
+    def copy(self, src, dst, k, device):
+        made = REMOTE(src, dst, self.send.at[k], self.recv.at[k], device, MESH)
+        made.start()
+        self.made.append(made)
+        return made
+
+    def start(self):
+        half = self.rows // 2
+        low, high = self.src.at[pl.ds(0, half)], self.src.at[pl.ds(half, half)]
+        self.a = [
+            self.copy(low, self.block(0, 0), 0, self.x),
+            self.copy(high, self.block(0, 1), 1, self.y),
+            self.copy(high, self.block(0, 1), 2, self.x),
+            self.copy(low, self.block(0, 0), 3, self.y),
+        ]
+        self.g = [self.copy(self.src, self.block(0), 4, self.sib)]
+
+    def pass_on(self, ref, k):
+        self.g.append(self.copy(ref, ref, k, self.sib))
+
+    def relay(self):
+        self.a[0].wait_recv()
+        self.b0 = self.copy(self.block(1, 0), self.block(1, 0), 5, self.y)
+        self.a[1].wait_recv()
+        self.b1 = self.copy(self.block(2, 1), self.block(2, 1), 6, self.x)
+        self.pass_on(self.block(1, 0), 7)
+        self.pass_on(self.block(2, 1), 8)
+        self.a[2].wait_recv()
+        self.pass_on(self.block(1, 1), 9)
+        self.a[3].wait_recv()
+        self.pass_on(self.block(2, 0), 10)
+
+    def finish(self):
+        self.b0.wait_recv()
+        self.pass_on(self.block(3, 0), 11)
+        self.b1.wait_recv()
+        self.pass_on(self.block(3, 1), 12)
+        for made in self.g:
+            made.wait_recv()
+        for made in self.made:
+            made.wait_send()
+
+
+class Reduce:
+    sems = 10
+
+    @staticmethod
+    def scratch(n, w):
+        return [
+            pltpu.VMEM((4, n, w), BF),
+            pltpu.VMEM((4, n, w), BF),
+            pltpu.VMEM((4, n, w // 2), BF),
+            pltpu.VMEM((2, n, w // 2), BF),
+        ]
+
+    def __init__(self, part, refs, send, recv):
+        c, s, f = here()
+        self.part, self.send, self.recv = part, send, recv
+        self.near, self.sums, self.far, self.last = refs
+        self.c, self.s = c, s
+        self.n, self.w = self.sums.shape[1], self.sums.shape[2]
+        self.x, self.y, self.sib = (c, flip(s, 1), f), (c, flip(s, 2), f), (1 - c, s, f)
+        self.made = []
+
+    def copy(self, src, dst, k, device):
+        made = REMOTE(src, dst, self.send.at[k], self.recv.at[k], device, MESH)
+        made.start()
+        self.made.append(made)
+        return made
+
+    def own(self, k, core):
+        index = core * 4 + (self.s if k == 0 else flip(self.s, k))
+        return index * self.n
+
+    def start(self):
+        self.a = {}
+        for sem, k in enumerate((3, 1, 2, 0)):
+            src = self.part.at[pl.ds(pl.multiple_of(self.own(k, 1 - self.c), self.n), self.n)]
+            self.a[k] = self.copy(src, self.near.at[k], sem, self.sib)
+
+    def chip_sum(self, k):
+        self.a[k].wait_recv()
+        base = self.own(k, self.c)
+
+        def body(i, carry):
+            r = rows_of(i, 32)
+            p = self.part[pl.ds(pl.multiple_of(base + i * 32, 32), 32), :].astype(F32)
+            self.sums[k, r, :] = (p + self.near[k, r, :].astype(F32)).astype(BF)
+            return carry
+
+        lax.fori_loop(0, self.n // 32, body, 0)
+
+    def add(self, k, cols, slot):
+        def body(i, carry):
+            r = rows_of(i, 32)
+            total = self.sums[k, r, cols].astype(F32) + self.far[slot, r, :].astype(F32)
+            self.sums[k, r, cols] = total.astype(BF)
+            return carry
+
+        lax.fori_loop(0, self.n // 32, body, 0)
+
+    def run(self):
+        left, right = pl.ds(0, self.w // 2), pl.ds(self.w // 2, self.w // 2)
+        self.chip_sum(3)
+        fx = self.copy(self.sums.at[3, :, left], self.far.at[1], 4, self.x)
+        fy = self.copy(self.sums.at[3, :, right], self.far.at[3], 5, self.y)
+        self.chip_sum(1)
+        self.nx = self.copy(self.sums.at[1, :, left], self.far.at[0], 6, self.x)
+        self.chip_sum(2)
+        self.ny = self.copy(self.sums.at[2, :, right], self.far.at[2], 7, self.y)
+        fx.wait_recv()
+        self.add(2, left, 1)
+        self.by = self.copy(self.sums.at[2, :, left], self.last.at[0], 8, self.y)
+        fy.wait_recv()
+        self.add(1, right, 3)
+        self.bx = self.copy(self.sums.at[1, :, right], self.last.at[1], 9, self.x)
+        self.a[0].wait_recv()
+
+    def arrive(self):
+        for made in (self.nx, self.ny, self.by, self.bx):
+            made.wait_recv()
+
+    def total(self, i, step):
+        r = rows_of(i, step)
+        base = self.own(0, self.c)
+        p = self.part[pl.ds(pl.multiple_of(base + i * step, step), step), :].astype(F32)
+        p = p + self.near[0, r, :].astype(F32)
+        far = jnp.concatenate([self.far[0, r, :], self.far[2, r, :]], axis=1).astype(F32)
+        last = jnp.concatenate([self.last[0, r, :], self.last[1, r, :]], axis=1).astype(F32)
+        return p + far + last
+
+    def finish(self):
+        for made in self.made:
+            made.wait_send()
+
+
+def partners():
+    c, s, f = here()
+    return [(c, flip(s, 1), f), (c, flip(s, 2), f), (1 - c, s, f)]
+
+
+STEP = 32
+
+
+def mean_square_inverse(values):
+    return lax.rsqrt(jnp.mean(values * values, axis=1, keepdims=True) + epsilon)
+
+
+def enter_kernel(tok_ref, dy_ref, gain_ref, normed_ref, dy_all_ref, mine, s0, r0, s1, r1, l0):
+    greet(partners())
+    c, s, f = here()
+    n = tok_ref.shape[0]
+
+    def body(i, carry):
+        r = rows_of(i, STEP)
+        v = tok_ref[r, :].astype(F32)
+        mine[r, :] = (v * mean_square_inverse(v) * gain_ref[...]).astype(BF)
+        return carry
+
+    lax.fori_loop(0, n // STEP, body, 0)
+    first = Gather(mine, normed_ref, s0, r0)
+    second = Gather(dy_ref, dy_all_ref, s1, r1)
+    first.start()
+    second.start()
+    keep = [
+        pltpu.make_async_copy(mine, first.block(0), l0.at[0]),
+        pltpu.make_async_copy(dy_ref, second.block(0), l0.at[1]),
+    ]
+    for made in keep:
+        made.start()
+    first.relay()
+    first.finish()
+    second.relay()
+    second.finish()
+    for made in keep:
+        made.wait()
+
+
+def enter(tokens, cotangent, gain):
+    n, w = tokens.shape
+    whole = jax.ShapeDtypeStruct((8 * n, w), BF)
+    dma = pltpu.SemaphoreType.DMA((Gather.sems,))
+    return pl.pallas_call(
+        enter_kernel,
+        name="enter",
+        out_shape=(whole, whole),
+        in_specs=[pl.BlockSpec(memory_space=pltpu.VMEM)] * 3,
+        out_specs=[pl.BlockSpec(memory_space=pl.ANY)] * 2,
+        scratch_shapes=[pltpu.VMEM((n, w), BF), dma, dma, dma, dma, pltpu.SemaphoreType.DMA((2,))],
+        compiler_params=pltpu.CompilerParams(
+            collective_id=1, has_side_effects=True, vmem_limit_bytes=VMEM_BYTES
+        ),
+        cost_estimate=pl.CostEstimate(
+            flops=50_000_000, bytes_accessed=4 * 8 * n * w * 2, transcendentals=0
+        ),
+    )(tokens, cotangent, gain[None])
+
+
+def middle_kernel(
+    part_ref, tok_ref, gain_ref, mid_ref, normed_ref,
+    near, sums, far, last, mine, s0, r0, s1, r1, l0,
+):
+    greet(partners())
+    reduce = Reduce(part_ref, (near, sums, far, last), s0, r0)
+    reduce.start()
+    reduce.run()
+    reduce.arrive()
+
+    def body(i, carry):
+        r = rows_of(i, STEP)
+        mid = tok_ref[r, :].astype(F32) + reduce.total(i, STEP)
+        mid_ref[r, :] = mid
+        mine[r, :] = (mid * mean_square_inverse(mid) * gain_ref[...]).astype(BF)
+        return carry
+
+    lax.fori_loop(0, mine.shape[0] // STEP, body, 0)
+    gather = Gather(mine, normed_ref, s1, r1)
+    gather.start()
+    keep = pltpu.make_async_copy(mine, gather.block(0), l0.at[0])
+    keep.start()
+    reduce.finish()
+    gather.relay()
+    gather.finish()
+    keep.wait()
+
+
+def middle(part, tokens, gain):
+    n, w = tokens.shape
+    dma = pltpu.SemaphoreType.DMA((16,))
+    vmem = pl.BlockSpec(memory_space=pltpu.VMEM)
+    return pl.pallas_call(
+        middle_kernel,
+        name="middle",
+        out_shape=(jax.ShapeDtypeStruct((n, w), F32), jax.ShapeDtypeStruct((8 * n, w), BF)),
+        in_specs=[vmem] * 3,
+        out_specs=[vmem, pl.BlockSpec(memory_space=pl.ANY)],
+        scratch_shapes=Reduce.scratch(n, w)
+        + [pltpu.VMEM((n, w), BF), dma, dma, dma, dma, pltpu.SemaphoreType.DMA((2,))],
+        compiler_params=pltpu.CompilerParams(
+            collective_id=2, has_side_effects=True, vmem_limit_bytes=VMEM_BYTES
+        ),
+        cost_estimate=pl.CostEstimate(
+            flops=50_000_000, bytes_accessed=4 * 8 * n * w * 2, transcendentals=0
+        ),
+    )(part, tokens, gain[None])
+
+
+def turn_kernel(
+    part_ref, dy_ref, mid_ref, gain_ref, grad_mid_ref, gain_term_ref, branch_ref,
+    near, sums, far, last, mine, s0, r0, s1, r1, l0,
+):
+    greet(partners())
+    reduce = Reduce(part_ref, (near, sums, far, last), s0, r0)
+    reduce.start()
+    reduce.run()
+    reduce.arrive()
+
+    def body(i, carry):
+        r = rows_of(i, STEP)
+        grad = reduce.total(i, STEP)
+        mid = mid_ref[r, :]
+        inverse = mean_square_inverse(mid)
+        weighted = grad * gain_ref[...]
+        back = inverse * weighted - mid * inverse**3 * jnp.mean(
+            weighted * mid, axis=1, keepdims=True
+        )
+        grad_mid = dy_ref[r, :].astype(F32) + back
+        grad_mid_ref[r, :] = grad_mid
+        mine[r, :] = grad_mid.astype(BF)
+        return carry + jnp.sum(grad * mid * inverse, axis=0, keepdims=True)
+
+    n, w = mine.shape
+    gain_term_ref[...] = lax.fori_loop(0, n // STEP, body, jnp.zeros((1, w), F32))
+    gather = Gather(mine, branch_ref, s1, r1)
+    gather.start()
+    keep = pltpu.make_async_copy(mine, gather.block(0), l0.at[0])
+    keep.start()
+    reduce.finish()
+    gather.relay()
+    gather.finish()
+    keep.wait()
+
+
+def turn(part, cotangent, mid, gain):
+    n, w = mid.shape
+    dma = pltpu.SemaphoreType.DMA((16,))
+    vmem = pl.BlockSpec(memory_space=pltpu.VMEM)
+    return pl.pallas_call(
+        turn_kernel,
+        name="turn",
+        out_shape=(
+            jax.ShapeDtypeStruct((n, w), F32),
+            jax.ShapeDtypeStruct((1, w), F32),
+            jax.ShapeDtypeStruct((8 * n, w), BF),
+        ),
+        in_specs=[vmem] * 4,
+        out_specs=[vmem, vmem, pl.BlockSpec(memory_space=pl.ANY)],
+        scratch_shapes=Reduce.scratch(n, w)
+        + [pltpu.VMEM((n, w), BF), dma, dma, dma, dma, pltpu.SemaphoreType.DMA((2,))],
+        compiler_params=pltpu.CompilerParams(
+            collective_id=3, has_side_effects=True, vmem_limit_bytes=VMEM_BYTES
+        ),
+        cost_estimate=pl.CostEstimate(
+            flops=50_000_000, bytes_accessed=4 * 8 * n * w * 2, transcendentals=0
+        ),
+    )(part, cotangent, mid, gain[None])
+
+
+def leave_kernel(
+    part_ref, down_ref, tok_ref, grad_mid_ref, mid_ref, gain_ref,
+    grad_ref, gain_term_ref, out_ref,
+    near, sums, far, last, near2, sums2, far2, last2, s0, r0, s1, r1,
+):
+    greet(partners())
+    reduce = Reduce(part_ref, (near, sums, far, last), s0, r0)
+    other = Reduce(down_ref, (near2, sums2, far2, last2), s1, r1)
+    reduce.start()
+    other.start()
+    reduce.run()
+    other.run()
+    reduce.arrive()
+
+    def body(i, carry):
+        r = rows_of(i, STEP)
+        grad = reduce.total(i, STEP)
+        tok = tok_ref[r, :].astype(F32)
+        inverse = mean_square_inverse(tok)
+        weighted = grad * gain_ref[...]
+        back = inverse * weighted - tok * inverse**3 * jnp.mean(
+            weighted * tok, axis=1, keepdims=True
+        )
+        grad_ref[r, :] = grad_mid_ref[r, :] + back
+        return carry + jnp.sum(grad * tok * inverse, axis=0, keepdims=True)
+
+    n, w = tok_ref.shape
+    gain_term_ref[...] = lax.fori_loop(0, n // STEP, body, jnp.zeros((1, w), F32))
+    other.arrive()
+
+    def body2(i, carry):
+        r = rows_of(i, STEP)
+        out_ref[r, :] = (mid_ref[r, :] + other.total(i, STEP)).astype(BF)
+        return carry
+
+    lax.fori_loop(0, n // STEP, body2, 0)
+    reduce.finish()
+    other.finish()
+
+
+def leave(part, down_part, tokens, grad_mid, mid, gain):
+    n, w = mid.shape
+    dma = pltpu.SemaphoreType.DMA((16,))
+    vmem = pl.BlockSpec(memory_space=pltpu.VMEM)
+    return pl.pallas_call(
+        leave_kernel,
+        name="leave",
+        out_shape=(
+            jax.ShapeDtypeStruct((n, w), F32),
+            jax.ShapeDtypeStruct((1, w), F32),
+            jax.ShapeDtypeStruct((n, w), BF),
+        ),
+        in_specs=[vmem] * 6,
+        out_specs=[vmem] * 3,
+        scratch_shapes=Reduce.scratch(n, w) + Reduce.scratch(n, w) + [dma, dma, dma, dma],
+        compiler_params=pltpu.CompilerParams(
+            collective_id=4, has_side_effects=True, vmem_limit_bytes=VMEM_BYTES
+        ),
+        cost_estimate=pl.CostEstimate(
+            flops=50_000_000, bytes_accessed=4 * 8 * n * w * 2, transcendentals=0
+        ),
+    )(part, down_part, tokens, grad_mid, mid, gain[None])
+
+
+BQ = 256
+BK = 256
+AUG = 128
+
+
+def dot(a, b, ca, cb):
+    return lax.dot_general(a, b, (((ca,), (cb,)), ((), ())), preferred_element_type=F32)
+
+
+def three_parts(v):
+    hi = v.astype(BF).astype(F32)
+    mid = (v - hi).astype(BF).astype(F32)
+    low = (v - hi - mid).astype(BF).astype(F32)
+    return hi, mid, low
+
+
+def triangle(n, suffix):
+    a = lax.broadcasted_iota(jnp.int32, (n, n), 0)
+    b = lax.broadcasted_iota(jnp.int32, (n, n), 1)
+    return jnp.where(a >= b if suffix else a <= b, 1.0, 0.0).astype(BF)
+
+
+def log_sigmoid(v):
+    return jnp.minimum(v, 0.0) - jnp.log1p(jnp.exp(-jnp.abs(v)))
+
+
+def doc_starts(ends_ref, pos):
+    start = jnp.zeros_like(pos)
+    for n in range(ends_ref.shape[0]):
+        end = ends_ref[n]
+        start = jnp.where(pos >= end, jnp.maximum(start, end), start)
+    return start
+
+
+def first_block(ends_ref, pos):
+    start = jnp.int32(0)
+    for n in range(ends_ref.shape[0]):
+        end = ends_ref[n]
+        start = jnp.where(pos >= end, jnp.maximum(start, end), start)
+    return start // BK
+
+
+def extend(prefix_row, sign_first):
+    hi, mid, low = three_parts(prefix_row)
+    r = lax.broadcasted_iota(jnp.int32, (16, prefix_row.shape[1]), 0)
+    base = 0 if sign_first else 3
+    sign = 1.0 if sign_first else -1.0
+    ones = (r >= 3) & (r < 6) if sign_first else r < 3
+    out = jnp.where(ones, 1.0, 0.0)
+    out = jnp.where(r == base, sign * hi, out)
+    out = jnp.where(r == base + 1, sign * mid, out)
+    return jnp.where(r == base + 2, sign * low, out)
+
+
+def lay_out(place_ref, cat_ref, prefix_ref, heads, hd, slab, qa, ka, kta):
+    hw = heads * hd
+    slabs = cat_ref.shape[1] // slab
+    for p in range(slabs):
+        src = pl.ds(pl.multiple_of(place_ref[p] * slab, slab), slab)
+        dst = pl.ds(p * slab, slab)
+        for h in range(heads):
+            q = cat_ref[h * hd : (h + 1) * hd, src].astype(BF).astype(F32)
+            row = prefix_ref[h : h + 1, dst]
+            rest = jnp.zeros((AUG - hd - 16, slab), F32)
+            qe = jnp.concatenate([q * hd**-0.5, extend(row, True), rest], axis=0)
+            qa[h, :, dst] = qe.astype(BF)
+            k = cat_ref[hw + h * hd : hw + (h + 1) * hd, src].astype(BF).astype(F32)
+            ke = jnp.concatenate([k, extend(row, False), rest], axis=0)
+            if kta is not None:
+                kta[h, :, dst] = ke.astype(BF)
+            ka[h, dst, :] = ke.T.astype(BF)
+
+
+def attention_kernel(
+    place_ref, ends_ref, cat_ref, bias_ref,
+    gated_ref, att_ref, exact_ref, lse_ref, prefix_ref,
+    qa, ka, va, *, heads, hd, slab,
+):
+    hw = heads * hd
+    tokens = cat_ref.shape[1]
+    slabs = tokens // slab
+    tri = triangle(slab, False)
+    carry = jnp.zeros((16, 1), F32)
+    for p in range(slabs):
+        src = pl.ds(pl.multiple_of(place_ref[p] * slab, slab), slab)
+        pre = cat_ref[4 * hw : 4 * hw + 16, src] + bias_ref[:, 0:1]
+        steps = log_sigmoid(pre).astype(BF)
+        part = dot(steps, tri, 1, 0) + carry
+        prefix_ref[:, p * slab : (p + 1) * slab] = part
+        carry = part[:, slab - 1 : slab]
+        for h in range(heads):
+            va[h, :, p * slab : (p + 1) * slab] = cat_ref[
+                2 * hw + h * hd : 2 * hw + (h + 1) * hd, src
+            ].astype(BF)
+    lay_out(place_ref, cat_ref, prefix_ref, heads, hd, slab, qa, ka, None)
+    per = slab // BQ
+
+    def one_query_block(qb, unused):
+        q0 = pl.multiple_of(qb * BQ, BQ)
+        pos = q0 + lax.broadcasted_iota(jnp.int32, (1, BQ), 1)
+        start = doc_starts(ends_ref, pos)
+        low = first_block(ends_ref, q0)
+        inside = lax.broadcasted_iota(jnp.int32, (BK, BQ), 0)
+
+        def one_key_block(kb, held):
+            k0 = pl.multiple_of(kb * BK, BK)
+            allowed = (inside <= pos - k0) & (inside >= start - k0)
+            out = []
+            for h in range(heads):
+                m, l, acc = held[h]
+                st = dot(ka[h, pl.ds(k0, BK), :], qa[h, :, pl.ds(q0, BQ)], 1, 0)
+                st = jnp.where(allowed, st, very_low)
+                new = jnp.maximum(m, jnp.max(st, axis=0, keepdims=True))
+                p = jnp.exp(st - new)
+                scale = jnp.exp(m - new)
+                l = l * scale + jnp.sum(p, axis=0, keepdims=True)
+                acc = acc * scale + dot(va[h, :, pl.ds(k0, BK)], p.astype(BF), 1, 0)
+                out.append((new, l, acc))
+            return tuple(out)
+
+        begin = tuple(
+            (jnp.full((1, BQ), very_low, F32), jnp.zeros((1, BQ), F32), jnp.zeros((hd, BQ), F32))
+            for _ in range(heads)
+        )
+        done = lax.fori_loop(low, qb + 1, one_key_block, begin)
+        dst = pl.ds(pl.multiple_of(place_ref[qb // per] * slab + lax.rem(qb, per) * BQ, BQ), BQ)
+        for h in range(heads):
+            m, l, acc = done[h]
+            lse_ref[h : h + 1, pl.ds(q0, BQ)] = m + jnp.log(l)
+            exact = acc / l
+            rounded = exact.astype(BF)
+            exact_ref[h * hd : (h + 1) * hd, dst] = exact
+            att_ref[h * hd : (h + 1) * hd, dst] = rounded
+            gate = jax.nn.sigmoid(cat_ref[3 * hw + h * hd : 3 * hw + (h + 1) * hd, dst])
+            gated_ref[h * hd : (h + 1) * hd, dst] = (rounded.astype(F32) * gate).astype(BF)
+        return unused
+
+    lse_ref[...] = jnp.zeros_like(lse_ref)
+    lax.fori_loop(0, tokens // BQ, one_query_block, 0)
+
+
+def attention(place, ends, cat, bias, heads, hd, slab):
+    tokens = cat.shape[1]
+    hw = heads * hd
+    vmem = pl.BlockSpec(memory_space=pltpu.VMEM)
+    smem = pl.BlockSpec(memory_space=pltpu.SMEM)
+    return pl.pallas_call(
+        functools.partial(attention_kernel, heads=heads, hd=hd, slab=slab),
+        name="attention",
+        out_shape=(
+            jax.ShapeDtypeStruct((hw, tokens), BF),
+            jax.ShapeDtypeStruct((hw, tokens), BF),
+            jax.ShapeDtypeStruct((hw, tokens), F32),
+            jax.ShapeDtypeStruct((8, tokens), F32),
+            jax.ShapeDtypeStruct((16, tokens), F32),
+        ),
+        in_specs=[smem, smem, vmem, vmem],
+        out_specs=[vmem] * 5,
+        scratch_shapes=[
+            pltpu.VMEM((heads, AUG, tokens), BF),
+            pltpu.VMEM((heads, tokens, AUG), BF),
+            pltpu.VMEM((heads, hd, tokens), BF),
+        ],
+        compiler_params=pltpu.CompilerParams(vmem_limit_bytes=VMEM_BYTES),
+        cost_estimate=pl.CostEstimate(
+            flops=8 * heads * tokens * tokens * hd, bytes_accessed=cat.size * 4,
+            transcendentals=heads * tokens * tokens // 2,
+        ),
+    )(place, ends, cat, bias)
+
+
+def attention_back_kernel(
+    place_ref, ends_ref, cat_ref, bias_ref, gg_ref, att_ref, exact_ref, lse_ref, prefix_ref,
+    out_ref, bias_grad_ref,
+    qa, ka, kta, va, do, delta_ref, dk, dv, gp, *, heads, hd, slab,
+):
+    hw = heads * hd
+    tokens = cat_ref.shape[1]
+    slabs = tokens // slab
+    per = slab // BQ
+    lay_out(place_ref, cat_ref, prefix_ref, heads, hd, slab, qa, ka, kta)
+    delta_ref[...] = jnp.zeros_like(delta_ref)
+    gp[...] = jnp.zeros_like(gp)
+    dk[...] = jnp.zeros_like(dk)
+    dv[...] = jnp.zeros_like(dv)
+    out_ref[4 * hw :, :] = jnp.zeros((out_ref.shape[0] - 4 * hw, tokens), BF)
+    for p in range(slabs):
+        src = pl.ds(pl.multiple_of(place_ref[p] * slab, slab), slab)
+        dst = pl.ds(p * slab, slab)
+        for h in range(heads):
+            rows = slice(h * hd, (h + 1) * hd)
+            gate = jax.nn.sigmoid(cat_ref[3 * hw + h * hd : 3 * hw + (h + 1) * hd, src])
+            gg = gg_ref[rows, src]
+            low = (gg * gate).astype(BF)
+            do[h, :, dst] = low
+            delta_ref[h : h + 1, dst] = jnp.sum(
+                low.astype(F32) * exact_ref[rows, src], axis=0, keepdims=True
+            )
+            gate_grad = gg * att_ref[rows, src].astype(F32) * gate * (1.0 - gate)
+            out_ref[3 * hw + h * hd : 3 * hw + (h + 1) * hd, src] = gate_grad.astype(BF)
+            v = cat_ref[2 * hw + h * hd : 2 * hw + (h + 1) * hd, src]
+            va[h, dst, :] = v.T.astype(BF)
+
+    def one_query_block(qb, unused):
+        q0 = pl.multiple_of(qb * BQ, BQ)
+        pos = q0 + lax.broadcasted_iota(jnp.int32, (1, BQ), 1)
+        start = doc_starts(ends_ref, pos)
+        low = first_block(ends_ref, q0)
+        inside = lax.broadcasted_iota(jnp.int32, (BK, BQ), 0)
+
+        def one_key_block(kb, held):
+            k0 = pl.multiple_of(kb * BK, BK)
+            keys = pl.ds(k0, BK)
+            allowed = (inside <= pos - k0) & (inside >= start - k0)
+            out = []
+            for h in range(heads):
+                queries = qa[h, :, pl.ds(q0, BQ)]
+                grads = do[h, :, pl.ds(q0, BQ)]
+                st = dot(ka[h, keys, :], queries, 1, 0) - lse_ref[h : h + 1, pl.ds(q0, BQ)]
+                p = jnp.exp(jnp.where(allowed, st, very_low))
+                dp = dot(va[h, keys, :], grads, 1, 0) - delta_ref[h : h + 1, pl.ds(q0, BQ)]
+                ds = (p * dp).astype(BF)
+                out.append(held[h] + dot(kta[h, :, keys], ds, 1, 0))
+                dk[h, :, keys] += dot(queries, ds, 1, 1)
+                dv[h, :, keys] += dot(grads, p.astype(BF), 1, 1)
+            return tuple(out)
+
+        begin = tuple(jnp.zeros((AUG, BQ), F32) for _ in range(heads))
+        done = lax.fori_loop(low, qb + 1, one_key_block, begin)
+        dst = pl.ds(pl.multiple_of(place_ref[qb // per] * slab + lax.rem(qb, per) * BQ, BQ), BQ)
+        for h in range(heads):
+            out_ref[h * hd : (h + 1) * hd, dst] = (done[h][0:hd, :] * hd**-0.5).astype(BF)
+            gp[h : h + 1, pl.ds(q0, BQ)] = done[h][hd : hd + 1, :]
+        return unused
+
+    lax.fori_loop(0, tokens // BQ, one_query_block, 0)
+    tri = triangle(slab, True)
+    carry = jnp.zeros((16, 1), F32)
+    bias_grad = jnp.zeros((16, 1), F32)
+    for p in reversed(range(slabs)):
+        src = pl.ds(pl.multiple_of(place_ref[p] * slab, slab), slab)
+        dst = pl.ds(p * slab, slab)
+        for h in range(heads):
+            out_ref[hw + h * hd : hw + (h + 1) * hd, src] = dk[h, 0:hd, dst].astype(BF)
+            out_ref[2 * hw + h * hd : 2 * hw + (h + 1) * hd, src] = dv[h, :, dst].astype(BF)
+            gp[h : h + 1, dst] = gp[h : h + 1, dst] - dk[h, hd + 3 : hd + 4, dst]
+        grad = gp[:, dst]
+        total = carry
+        for piece in three_parts(grad):
+            total = total + dot(piece.astype(BF), tri, 1, 0)
+        carry = total[:, 0:1]
+        pre = cat_ref[4 * hw : 4 * hw + 16, src] + bias_ref[:, 0:1]
+        low = (total.astype(BF).astype(F32) * jax.nn.sigmoid(-pre)).astype(BF)
+        out_ref[4 * hw : 4 * hw + 16, src] = low
+        bias_grad = bias_grad + jnp.sum(low.astype(F32), axis=1, keepdims=True)
+    bias_grad_ref[...] = jnp.broadcast_to(bias_grad, bias_grad_ref.shape)
+
+
+def attention_back(place, ends, cat, bias, gg, att, exact, lse, prefix, heads, hd, slab):
+    tokens = cat.shape[1]
+    vmem = pl.BlockSpec(memory_space=pltpu.VMEM)
+    smem = pl.BlockSpec(memory_space=pltpu.SMEM)
+    return pl.pallas_call(
+        functools.partial(attention_back_kernel, heads=heads, hd=hd, slab=slab),
+        name="attention_back",
+        out_shape=(
+            jax.ShapeDtypeStruct(cat.shape, BF),
+            jax.ShapeDtypeStruct((16, 128), F32),
+        ),
+        in_specs=[smem, smem] + [vmem] * 7,
+        out_specs=[vmem] * 2,
+        scratch_shapes=[
+            pltpu.VMEM((heads, AUG, tokens), BF),
+            pltpu.VMEM((heads, tokens, AUG), BF),
+            pltpu.VMEM((heads, AUG, tokens), BF),
+            pltpu.VMEM((heads, tokens, hd), BF),
+            pltpu.VMEM((heads, hd, tokens), BF),
+            pltpu.VMEM((8, tokens), F32),
+            pltpu.VMEM((heads, AUG, tokens), F32),
+            pltpu.VMEM((heads, hd, tokens), F32),
+            pltpu.VMEM((16, tokens), F32),
+        ],
+        compiler_params=pltpu.CompilerParams(vmem_limit_bytes=VMEM_BYTES),
+        cost_estimate=pl.CostEstimate(
+            flops=20 * heads * tokens * tokens * hd, bytes_accessed=cat.size * 8,
+            transcendentals=heads * tokens * tokens // 2,
+        ),
+    )(place, ends, cat, bias, gg, att, exact, lse, prefix)
+
+
+def spread_rows(grad, plane, depth):
+    rows, cols = grad.shape
+    part = rows // (plane * depth)
+    return grad.reshape(plane, depth, part, cols).transpose(1, 0, 2, 3).reshape(rows, cols)
+
+
+def local_plane(
+    tokens, out_cotangent, seq_lengths, slab_place, attn_gain, query_weight, key_weight,
+    value_weight, outgate_weight, forget_weight, forget_bias, output_weight, mlp_gain,
+    gate_weight, up_weight, down_weight,
+):
+    plane_axes = ("cp", "sp")
+    plane = lax.axis_size("cp") * lax.axis_size("sp")
+    depth = lax.axis_size("fsdp")
+    place = lax.axis_index("cp") * lax.axis_size("sp") + lax.axis_index("sp")
+    head_count = forget_weight.shape[1]
+    width = tokens.shape[2]
+    hd = width // head_count
+    heads = head_count // plane
+    hw = heads * hd
+    fw = gate_weight.shape[1] // plane
+    shard = query_weight.shape[0]
+    group_rows = tokens.shape[1] * plane
+    slab = group_rows // slab_place.shape[1]
+
+    def columns(weight, count):
+        return lax.dynamic_slice_in_dim(weight, place * count, count, 1)
+
+    inputs, cotangent = tokens[0], out_cotangent[0]
+    slabs = slab_place.shape[1]
+    order = jnp.arange(slabs, dtype=jnp.int32)
+    storage = jnp.sum(
+        jnp.where(slab_place[0][None, :] == order[:, None], order[None, :], 0), axis=1
+    )
+    ends = jnp.cumsum(seq_lengths[0])
+
+    forget_part = jnp.pad(columns(forget_weight, heads), ((0, 0), (0, 128 - heads)))
+    own_attn = jnp.concatenate(
+        [
+            columns(query_weight, hw),
+            columns(key_weight, hw),
+            columns(value_weight, hw),
+            columns(outgate_weight, hw),
+            forget_part,
+        ],
+        axis=1,
+    )
+    own_out = columns(output_weight, hw)
+    own_mlp = jnp.concatenate(
+        [columns(gate_weight, fw), columns(up_weight, fw), columns(down_weight, fw)], axis=1
+    )
+    w_attn = lax.all_gather(own_attn, "fsdp", axis=0, tiled=True)
+    w_out_cols = lax.all_gather(own_out, "fsdp", axis=0, tiled=True)
+    w_mlp = lax.all_gather(own_mlp, "fsdp", axis=0, tiled=True)
+    w_out = lax.all_to_all(w_out_cols, plane_axes, split_axis=0, concat_axis=1, tiled=True)
+
+    normed, cotangent_all = enter(inputs, cotangent, attn_gain)
+    cat = dot(w_attn, normed, 0, 1)
+    bias_own = lax.dynamic_slice_in_dim(forget_bias, place * heads, heads, 0)
+    bias = jnp.broadcast_to(jnp.pad(bias_own, (0, 16 - heads))[:, None], (16, 128))
+    gated, att, exact, lse, prefix = attention(storage, ends, cat, bias, heads, hd, slab)
+    mid_part = dot(gated, w_out, 0, 0).astype(BF)
+    mid, normed_mlp = middle(mid_part, inputs, mlp_gain)
+
+    w_gate, w_up, w_down = w_mlp[:, :fw], w_mlp[:, fw : 2 * fw], w_mlp[:, 2 * fw :]
+    gate_lin = matmul(normed_mlp, w_gate)
+    up_lin = matmul(normed_mlp, w_up)
+    gate_sig = jax.nn.sigmoid(gate_lin)
+    activated = gate_lin * gate_sig
+    hidden = (activated * up_lin).astype(BF)
+    grad_hidden = matmul(cotangent_all, w_down)
+    grad_gate_lin = (grad_hidden * up_lin * gate_sig * (1.0 + gate_lin * (1.0 - gate_sig))).astype(
+        BF
+    )
+    grad_up_lin = (grad_hidden * activated).astype(BF)
+    mlp_part = (
+        matmul_right_t(grad_gate_lin, w_gate) + matmul_right_t(grad_up_lin, w_up)
+    ).astype(BF)
+    down_part = matmul_right_t(hidden, w_down).astype(BF)
+    mlp_terms = jnp.concatenate(
+        [
+            matmul_left_t(normed_mlp, grad_gate_lin).astype(BF),
+            matmul_left_t(normed_mlp, grad_up_lin).astype(BF),
+            matmul_left_t(cotangent_all, hidden).astype(BF),
+        ],
+        axis=1,
+    )
+    mlp_grad = lax.psum_scatter(
+        spread_rows(mlp_terms, plane, depth), "fsdp", scatter_dimension=0, tiled=True
+    )
+    grad_mid, mlp_gain_term, branch = turn(mlp_part, cotangent, mid, mlp_gain)
+
+    grad_gated = dot(w_out, branch, 1, 1)
+    grad_cat, bias_grad = attention_back(
+        storage, ends, cat, bias, grad_gated, att, exact, lse, prefix, heads, hd, slab
+    )
+    out_term = dot(gated, branch, 1, 0).astype(BF)
+    attn_term = dot(normed, grad_cat, 0, 1).astype(BF)
+    attn_part = dot(grad_cat, w_attn, 0, 1).astype(BF)
+    attn_grad = lax.psum_scatter(
+        spread_rows(attn_term, plane, depth), "fsdp", scatter_dimension=0, tiled=True
+    )
+    output_weight_grad = lax.psum_scatter(out_term, "fsdp", scatter_dimension=0, tiled=True)
+    tokens_grad, attn_gain_term, block_out = leave(
+        attn_part, down_part, inputs, grad_mid, mid, attn_gain
+    )
+
+    def to_rows(grad):
+        part = grad.shape[0] // plane
+        got = lax.all_to_all(
+            grad.reshape(plane, part, -1), plane_axes, split_axis=0, concat_axis=0, tiled=True
+        )
+        return got.astype(F32)
+
+    mlp_rows = to_rows(mlp_grad)
+    attn_rows = to_rows(attn_grad)
+
+    def pick(rows, begin, count):
+        part = rows[:, :, begin : begin + count].transpose(1, 0, 2)
+        return part.reshape(part.shape[0], -1)
+
+    gate_grad, up_grad, down_grad = (pick(mlp_rows, i * fw, fw) for i in range(3))
+    query_grad, key_grad, value_grad, outgate_grad = (
+        pick(attn_rows, i * hw, hw) for i in range(4)
+    )
+    forget_grad = pick(attn_rows, 4 * hw, heads)
+    bias_term = lax.dynamic_update_slice_in_dim(
+        jnp.zeros((head_count,), F32), bias_grad[:heads, 0], place * heads, 0
+    )
+    attn_gain_grad, mlp_gain_grad, forget_bias_grad = lax.psum(
+        (attn_gain_term[0], mlp_gain_term[0], bias_term), ("cp", "sp", "fsdp")
+    )
+    return (
+        block_out[None],
+        tokens_grad[None],
+        attn_gain_grad,
+        query_grad,
+        key_grad,
+        value_grad,
+        outgate_grad,
+        forget_grad,
+        forget_bias_grad,
+        output_weight_grad.astype(F32),
+        mlp_gain_grad,
+        gate_grad,
+        up_grad,
+        down_grad,
+    )
+
+
+def fits_plane(mesh, tokens, slab_place, forget_weight, gate_weight):
+    sizes = dict(mesh.shape)
+    if (sizes["cp"], sizes["sp"]) != (2, 4):
+        return False
+    plane = sizes["cp"] * sizes["sp"]
+    width = tokens.shape[2]
+    head_count = forget_weight.shape[1]
+    group_rows = tokens.shape[1]
+    slab = group_rows // slab_place.shape[1]
+    heads = head_count // plane
+    return (
+        head_count % plane == 0
+        and heads <= 8
+        and width // head_count == 64
+        and slab % 256 == 0
+        and group_rows <= 2048
+        and width % 256 == 0
+        and gate_weight.shape[1] % (128 * plane) == 0
+        and width % (16 * plane * sizes["fsdp"]) == 0
+        and (group_rows // plane) % 64 == 0
+    )
+
+
+def shard(mesh, fn):
     return jax.shard_map(
-        local,
+        fn,
         mesh=mesh,
         in_specs=(
             P("fsdp", ("cp", "sp"), None),
@@ -412,3 +1303,11 @@
         ),
         check_vma=False,
     )
+
+
+def solution(mesh):
+    def run(*args):
+        fast = fits_plane(mesh, args[0], args[3], args[9], args[13])
+        return shard(mesh, local_plane if fast else local)(*args)
+
+    return run

time: 3070 us -> 683 us (0.22)
  waiting for transfers between devices: 2260 us -> 91.9 us
  Pallas kernels: 0 us -> 325 us
  matrix products: 298 us -> 110 us
  local copies, waits for them, and re-layouts: 223 us -> 40 us
  blocking collectives: 138 us -> 70.3 us
  other arithmetic: 63.5 us -> 8.84 us
  loops' own time: 48.8 us -> 0 us
    reduce_scatter x10 -> x3, waiting for transfers between devices: 1130 us -> 91.8 us  [the longest x1 72.2 us: local_plane(): lax.psum_scatter(spread_rows(mlp_terms, plane, depth), 'fsdp', scatter_di...]
    all_gather x10 -> x2, waiting for transfers between devices: 847 us -> 0.04 us  [the longest x1 0.02 us: local_plane(): w_attn = lax.all_gather(own_attn, 'fsdp', axis=0, tiled=True)]
    pallas_call x0 -> x6, Pallas kernels: none -> 325 us  [the longest x1 68.1 us: enter(): pl.pallas_call(enter_kernel, name='enter', out_shape=(whole, whole), in_s...]
    unnamed x24 -> x5, waiting for transfers between devices: 259 us -> 0.08 us
    dynamic_update_slice x20 -> x1, local copies, waits for them, and re-layouts: 140 us -> 0.24 us  [local_plane(): lax.dynamic_update_slice_in_dim(jnp.zeros((head_count,), F32), bias_grad[...]
    dot_general x38 -> x6, matrix products: 138 us -> 48.6 us  [dot(): lax.dot_general(a, b, (((ca,), (cb,)), ((), ())), preferred_element_type=...]
    all_to_all x7 -> x0, blocking collectives: 82.2 us -> none  [the longest x1 15 us: local(): lax.all_to_all(keys, 'sp', split_axis=1, concat_axis=0, tiled=True)]
    another operation x15 -> x0, loops' own time: 48.8 us -> none  [the longest x1 16.2 us: local(): lax.scan(back_step, (zero_out, start_prefix), key_pieces)]
  transfers between devices with their start and end apart: 25 -> 8, of which waited for: 18 -> 2; matrix products, arithmetic and copies ran while one was open for 10% -> 13% of each run, Pallas kernels for 0% -> 34%
where the time goes in v1:
time: 683 us; the launch traced here: 673 us
  Pallas kernels  325 us (48%)
  matrix products  110 us (16%)
  waiting for transfers between devices  91.9 us (13%)
  blocking collectives  70.3 us (10%)
  local copies, waits for them, and re-layouts  40 us (6%)
  between operations  14.5 us (2%)
  starting transfers between devices  12.1 us (2%)
  other arithmetic  8.84 us (1%)
    reduce_scatter x1, waiting for transfers between devices, local_plane(): lax.psum_scatter(spread_rows(mlp_terms, plane, depth), 'fsdp', scatter_di...  72.2 us
    pallas_call x1, Pallas kernels, enter(): pl.pallas_call(enter_kernel, name='enter', out_shape=(whole, whole), in_s...  68.1 us
    pallas_call x1, Pallas kernels, middle(): pl.pallas_call(middle_kernel, name='middle', out_shape=(jax.ShapeDtypeStr...  66.7 us
    pallas_call x1, Pallas kernels, turn(): pl.pallas_call(turn_kernel, name='turn', out_shape=(jax.ShapeDtypeStruct(...  66.3 us
    pallas_call x1, Pallas kernels, leave(): pl.pallas_call(leave_kernel, name='leave', out_shape=(jax.ShapeDtypeStruc...  65.5 us
    dot_general x6, matrix products, dot(): lax.dot_general(a, b, (((ca,), (cb,)), ((), ())), preferred_element_type=...  48.6 us
    psum x1, blocking collectives, local_plane(): lax.psum((attn_gain_term[0], mlp_gain_term[0], bias_term), ('cp', 'sp', '...  40.3 us
    pallas_call x1, Pallas kernels, attention_back(): pl.pallas_call(functools.partial(attention_back_kernel, heads=heads, hd=h...  32.3 us
  transfers between devices with their start and end apart: 8, of which 2 were waited for; matrix products, arithmetic and copies ran while one was open for 13% of the time, Pallas kernels for 34%

profile of v1, /device:TPU:0, one launch (start us, length us, event | category | flops | bytes accessed | tf_op | source)
XLA Modules:
  0.0 672.8 jit_solution(4259859673923510689)
XLA Ops:
  19.3 30.0 %all_gather.10 = bf16[1536,192]{1,0:T(8,128)(2,1)} all-gather(bf16[384,192]{1,0:T(8,128)(2,1)S(1)} %constant_dynamic-slice_fusion.3), channel_id=1, replica_groups=mesh['cp'=2,'sp'=4,'fsdp'=4] {'fsdp'}, dimensions={0}, use_global_device_ids=true | all-gather | bytes 737280 | tf_op jit(solution)/shard_map/all_gather | solution.py:1145
  54.9 68.1 %enter.1 = (bf16[2048,1536]{1,0:T(8,128)(2,1)}, bf16[2048,1536]{1,0:T(8,128)(2,1)}) custom-call(bf16[256,1536]{1,0:T(8,128)(2,1)} %bitcast.70, bf16[256,1536]{1,0:T(8,128)(2,1)} %bitcast.73, f32[1,1536]{1,0:T(1,128)} %broadcast_in_dim.36.gain_ref), custom_call_target="tpu_custom_call" | custom-call | flops 50000000 | bytes 25165824 | tf_op jit(solution)/shard_map/enter/pallas_call | solution.py:613
  124.8 10.8 %fusion.11.cat_ref = f32[896,2048]{1,0:T(8,128)} fusion(bf16[1536,896]{1,0:T(8,128)(2,1)} %all-gather.3.cloned.1.call-done, bf16[2048,1536]{1,0:T(8,128)(2,1)} %get-tuple-element.31), kind=kOutput, calls=%fused_computation.46 | convolution fusion | flops 5637144576 | bytes 16384000 | tf_op jit(solution)/shard_map/dot_general | solution.py:809
  136.3 26.5 %attention.1 = (bf16[192,2048]{1,0:T(8,128)(2,1)}, bf16[192,2048]{1,0:T(8,128)(2,1)}, f32[192,2048]{1,0:T(8,128)}, f32[8,2048]{1,0:T(8,128)}, f32[16,2048]{1,0:T(8,128)}) custom-call(s32[4]{0:T(128)} %select_reduce_fusion.place_ref, s32[8]{0:T(128)} %bitcast.90, f32[896,2048]{1,0:T(8,128)} %fusion.11.cat_ref, f32[16,128]{1,0:T(8,128)} %broadcast_in_dim.37.bias_ref), custom_call_target="tpu_custom_call" | custom-call | flops 6442450944 | bytes 7340032 | tf_op jit(solution)/shard_map/attention/pallas_call | solution.py:949
  162.8 5.6 convolution_convert_fusion.1.part_ref
  168.4 66.7 %middle.1 = (f32[256,1536]{1,0:T(8,128)}, bf16[2048,1536]{1,0:T(8,128)(2,1)}) custom-call(bf16[2048,1536]{1,0:T(8,128)(2,1)} %convolution_convert_fusion.1.part_ref, bf16[256,1536]{1,0:T(8,128)(2,1)} %bitcast.71, f32[1,1536]{1,0:T(1,128)} %broadcast_in_dim.38.gain_ref), custom_call_target="tpu_custom_call" | custom-call | flops 50000000 | bytes 25165824 | tf_op jit(solution)/shard_map/middle/pallas_call | solution.py:661
  235.2 6.1 fusion.3
  241.3 8.0 %fusion.9 = f32[2048,512]{1,0:T(8,128)} fusion(bf16[2048,1536]{1,0:T(8,128)(2,1)} %get-tuple-element.32, bf16[1536,1536]{1,0:T(8,128)(2,1)S(1)} %copy-done.8), kind=kOutput, calls=%fused_computation.23 | convolution fusion | flops 3221225472 | bytes 12058624 | tf_op jit(solution)/shard_map/dot_general | solution.py:20
  249.3 8.1 %multiply_convert_fusion = (bf16[2048,512]{1,0:T(8,128)(2,1)}, bf16[2048,512]{1,0:T(8,128)(2,1)S(1)}, bf16[2048,512]{1,0:T(8,128)(2,1)S(1)}) fusion(f32[2048,512]{1,0:T(8,128)S(1)} %fusion.3, f32[2048,512]{1,0:T(8,128)} %fusion.9, bf16[2048,1536]{1,0:T(8,128)(2,1)S(1)} %bitcast.87, bf16[1536,1536]{1,0:T(8,128)(2,1)S(1)} %copy-done.8), kind=kOutput, calls=%fused_computation.5 | convolution fusion | flops 3236954112 | bytes 22544384 | tf_op jit(solution)/shard_map/dot_general | solution.py:20
  257.4 6.5 fusion.1
  263.8 8.5 %add_convert_fusion.part_ref = bf16[2048,1536]{1,0:T(8,128)(2,1)} fusion(f32[2048,1536]{1,0:T(8,128)} %fusion.1, bf16[2048,512]{1,0:T(8,128)(2,1)S(1)} %get-tuple-element.53, bf16[1536,1536]{1,0:T(8,128)(2,1)S(1)} %copy-done.8), kind=kOutput, calls=%fused_computation | convolution fusion | flops 3227516928 | bytes 22544384 | tf_op jit(solution)/shard_map/dot_general | solution.py:24
  272.3 66.3 %turn.1 = (f32[256,1536]{1,0:T(8,128)}, f32[1,1536]{1,0:T(1,128)}, bf16[2048,1536]{1,0:T(8,128)(2,1)}) custom-call(bf16[2048,1536]{1,0:T(8,128)(2,1)} %add_convert_fusion.part_ref, bf16[256,1536]{1,0:T(8,128)(2,1)} %bitcast.74, f32[256,1536]{1,0:T(8,128)} %get-tuple-element.35.mid_ref, f32[1,1536]{1,0:T(1,128)} %broadcast_in_dim.38.gain_ref), custom_call_target="tpu_custom_call" | custom-call | flops 50000000 | bytes 25165824 | tf_op jit(solution)/shard_map/turn/pallas_call | solution.py:718
  338.6 6.2 fusion.12.gg_ref
  344.8 32.3 %attention_back.1 = (bf16[896,2048]{1,0:T(8,128)(2,1)}, f32[16,128]{1,0:T(8,128)}) custom-call(s32[4]{0:T(128)} %select_reduce_fusion.place_ref, s32[8]{0:T(128)} %bitcast.91, f32[896,2048]{1,0:T(8,128)} %fusion.11.cat_ref, f32[16,128]{1,0:T(8,128)} %broadcast_in_dim.37.bias_ref, f32[192,2048]{1,0:T(8,128)} %fusion.12.gg_ref, ...), custom_call_target="tpu_custom_call" | custom-call | flops 16106127360 | bytes 14680064 | tf_op jit(solution)/shard_map/attention_back/pallas_call | solution.py:1065
  377.1 9.9 %convolution_convert_fusion.3 = bf16[1536,896]{1,0:T(8,128)(2,1)S(1)} fusion(bf16[2048,1536]{1,0:T(8,128)(2,1)} %get-tuple-element.31, bf16[896,2048]{1,0:T(8,128)(2,1)} %get-tuple-element.41), kind=kOutput, calls=%fused_computation.10 | convolution fusion | flops 5638520832 | bytes 12713984 | tf_op jit(solution)/shard_map/dot_general | solution.py:809
  389.1 7.0 %convolution_convert_fusion.5 = bf16[1536,512]{0,1:T(8,128)(2,1)S(1)} fusion(bf16[2048,1536]{1,0:T(8,128)(2,1)} %get-tuple-element.34, bf16[2048,512]{1,0:T(8,128)(2,1)} %copy-done.14), kind=kOutput, calls=%fused_computation.12 | convolution fusion | flops 3222011904 | bytes 9961472 | tf_op jit(solution)/shard_map/dot_general | solution.py:30
  396.2 6.9 %convolution_convert_fusion.6 = bf16[1536,512]{0,1:T(8,128)(2,1)S(1)} fusion(bf16[2048,1536]{1,0:T(8,128)(2,1)} %get-tuple-element.34, bf16[2048,512]{1,0:T(8,128)(2,1)S(1)} %copy-done.13), kind=kOutput, calls=%fused_computation.13 | convolution fusion | flops 3222011904 | bytes 9961472 | tf_op jit(solution)/shard_map/dot_general | solution.py:30
  409.0 6.7 copy.75
  426.8 19.6 %reduce-scatter.4.cloned.1.call-done = bf16[384,896]{1,0:T(8,128)(2,1)} async-done(((bf16[1536,896]{1,0:T(8,128)(2,1)}), bf16[384,896]{1,0:T(8,128)(2,1)}) %reduce-scatter.4.cloned.1.call-update) | async-done | bytes 688144 | tf_op jit(solution)/shard_map/reduce_scatter | solution.py:1192
  450.3 11.1 %convolution_convert_fusion.part_ref = bf16[2048,1536]{1,0:T(8,128)(2,1)} fusion(bf16[896,2048]{1,0:T(8,128)(2,1)} %get-tuple-element.41, bf16[1536,896]{1,0:T(8,128)(2,1)} %all-gather.3.cloned.1.call-done), kind=kOutput, calls=%fused_computation.1 | convolution fusion | flops 5640290304 | bytes 12713984 | tf_op jit(solution)/shard_map/dot_general | solution.py:809
  461.4 72.2 %reduce-scatter.8.cloned.1.call-done = bf16[384,1536]{1,0:T(8,128)(2,1)} async-done(((bf16[1536,1536]{1,0:T(8,128)(2,1)}), bf16[384,1536]{1,0:T(8,128)(2,1)}) %reduce-scatter.8.cloned.1.call-update) | async-done | bytes 1179664 | tf_op jit(solution)/shard_map/reduce_scatter | solution.py:1180
  537.9 6.8 %convolution_convert_fusion.2.down_ref = bf16[2048,1536]{1,0:T(8,128)(2,1)} fusion(bf16[2048,512]{1,0:T(8,128)(2,1)S(1)} %copy-done.16, bf16[1536,1536]{1,0:T(8,128)(2,1)} %all-gather.5.cloned.1.call-done), kind=kOutput, calls=%fused_computation.3 | convolution fusion | flops 3224371200 | bytes 9961472 | tf_op jit(solution)/shard_map/dot_general | solution.py:24
  544.7 65.5 %leave.1 = (f32[256,1536]{1,0:T(8,128)}, f32[1,1536]{1,0:T(1,128)}, bf16[256,1536]{1,0:T(8,128)(2,1)}) custom-call(bf16[2048,1536]{1,0:T(8,128)(2,1)} %convolution_convert_fusion.part_ref, bf16[2048,1536]{1,0:T(8,128)(2,1)} %convolution_convert_fusion.2.down_ref, bf16[256,1536]{1,0:T(8,128)(2,1)} %bitcast.72, f32[256,1536]{1,0:T(8,128)} %get-tuple-element.42.grad_mid_ref, ...), custom_call_target="tpu_custom_call" | custom-call | flops 50000000 | bytes 25165824 | tf_op jit(solution)/shard_map/leave/pallas_call | solution.py:783
  612.0 40.3 %all-reduce.2 = (f32[1536]{0:T(1024)}, f32[24]{0:T(128)}, f32[1536]{0:T(1024)}) all-reduce(f32[1536]{0:T(1024)S(1)} %reduce, f32[24]{0:T(128)S(1)} %dynamic_update_slice.3, f32[1536]{0:T(1024)S(1)} %reduce.2), channel_id=1, replica_groups=mesh['cp'=2,'sp'=4,'fsdp'=4] {'cp','sp','fsdp'}, use_global_device_ids=true, to_apply=%region_2.3 | all-reduce | flops 3096 | bytes 24768 | tf_op jit(solution)/shard_map/psum | solution.py:1222
  (113 shorter events, 62.8 us)
Async XLA Ops:
  7.2 8.6 %copy-start = (bf16[384,4096]{1,0:T(8,128)(2,1)S(1)}, bf16[384,4096]{1,0:T(8,128)(2,1)}, u32[]{:S(2)}) copy-start(bf16[384,4096]{1,0:T(8,128)(2,1)} %param.29) | copy-start | bytes 9437188
  7.2 117.6 %all-gather.3.cloned.1.call-start = ((), (), s32[]{:S(2)}) async-start(), calls=%async_computation.6 | async-start | bytes 3440640 | tf_op jit(solution)/shard_map/all_gather | solution.py:1144
  15.8 219.4 %all-gather.5.cloned.1.call-start = ((), (), s32[]{:S(2)}) async-start(), calls=%async_computation.7 | async-start | bytes 5898240 | tf_op jit(solution)/shard_map/all_gather | solution.py:1146
  15.9 37.1 %copy-start.5 = (f32[1536]{0:T(1024)S(1)}, f32[1536]{0:T(1024)}, u32[]{:S(2)}) copy-start(f32[1536]{0:T(1024)} %param.20) | copy-start | bytes 18436
  15.9 37.7 %copy-start.9 = (f32[24]{0:T(128)S(1)}, f32[24]{0:T(128)}, u32[]{:S(2)}) copy-start(f32[24]{0:T(128)} %param.26) | copy-start | bytes 292
  15.9 37.8 %copy-start.10 = (s32[1,8]{1,0:T(1,128)S(1)}, s32[1,8]{1,0:T(1,128)}, u32[]{:S(2)}) copy-start(s32[1,8]{1,0:T(1,128)} %param.18) | copy-start | bytes 100
  15.9 38.5 %copy-start.6 = (f32[1536]{0:T(1024)S(1)}, f32[1536]{0:T(1024)}, u32[]{:S(2)}) copy-start(f32[1536]{0:T(1024)} %param.28) | copy-start | bytes 18436
  17.1 105.9 %copy-start.11 = (s32[1,4]{1,0:T(1,128)S(1)}, s32[1,4]{1,0:T(1,128)}, u32[]{:S(2)}) copy-start(s32[1,4]{1,0:T(1,128)} %param.19) | copy-start | bytes 52
  49.4 74.3 %all-to-all-start = ((bf16[8,192,192]{2,1,0:T(8,128)(2,1)}), bf16[8,192,192]{2,1,0:T(8,128)(2,1)S(1)}, u32[]{:S(2)}, u32[]{:S(2)}) async-start(bf16[8,192,192]{2,1,0:T(8,128)(2,1)} %bitcast.5), calls=%async_computation | async-start | bytes 1572864 | tf_op jit(solution)/shard_map/all_to_all | solution.py:1147
  52.9 393.5 %reduce-scatter.4.cloned.1.call-start = ((), (), s32[]{:S(2)}) async-start(), calls=%async_computation.8 | async-start | bytes 3440640 | tf_op jit(solution)/shard_map/reduce_scatter | solution.py:1192
  235.2 14.1 %slice-start.2 = ((s8[6291456]{0:T(1024)(128)(4,1)}), s8[4194304]{0:T(1024)(128)(4,1)S(1)}, s32[]{:S(2)}) async-start(s8[6291456]{0:T(1024)(128)(4,1)} %bitcast.86), calls=%async_computation.13 | async-start | bytes 8388608
  241.3 8.0 %slice-start.3 = ((s8[6291456]{0:T(1024)(128)(4,1)}), s8[2097152]{0:T(1024)(128)(4,1)S(1)}, s32[]{:S(2)}) async-start(s8[6291456]{0:T(1024)(128)(4,1)} %bitcast.86), calls=%async_computation.14 | async-start | bytes 4194304
  257.3 6.5 copy-start.12
  257.3 6.5 copy-start.14
  388.9 144.7 %reduce-scatter.8.cloned.1.call-start = ((), (), s32[]{:S(2)}) async-start(), calls=%async_computation.10 | async-start | bytes 5898240 | tf_op jit(solution)/shard_map/reduce_scatter | solution.py:1180
  389.1 7.0 %copy-start.13 = (bf16[2048,512]{1,0:T(8,128)(2,1)S(1)}, bf16[2048,512]{1,0:T(8,128)(2,1)}, u32[]{:S(2)}) copy-start(bf16[2048,512]{1,0:T(8,128)(2,1)} %copy-done.12) | copy-start | bytes 6291460
  389.1 13.9 %slice-start = ((s8[6291456]{0:T(1024)(128)(4,1)}), s8[4194304]{0:T(1024)(128)(4,1)S(1)}, s32[]{:S(2)}) async-start(s8[6291456]{0:T(1024)(128)(4,1)} %bitcast.84), calls=%async_computation.11 | async-start | bytes 8388608
  396.1 6.9 %slice-start.1 = ((s8[6291456]{0:T(1024)(128)(4,1)}), s8[2097152]{0:T(1024)(128)(4,1)S(1)}, s32[]{:S(2)}) async-start(s8[6291456]{0:T(1024)(128)(4,1)} %bitcast.84), calls=%async_computation.12 | async-start | bytes 4194304
  396.2 6.9 %copy-start.15 = (bf16[2048,512]{1,0:T(8,128)(2,1)S(1)}, bf16[2048,512]{1,0:T(8,128)(2,1)}, u32[]{:S(2)}) copy-start(bf16[2048,512]{1,0:T(8,128)(2,1)} %get-tuple-element.51) | copy-start | bytes 6291460
  420.7 231.6 %reduce-scatter.6.cloned.1.call-start = ((), (), s32[]{:S(2)}) async-start(), calls=%async_computation.9 | async-start | bytes 737280 | tf_op jit(solution)/shard_map/reduce_scatter | solution.py:1195
  446.4 15.0 %all-to-all-start.1 = ((bf16[8,48,896]{2,1,0:T(8,128)(2,1)}), bf16[8,48,896]{2,1,0:T(8,128)(2,1)S(1)}, u32[]{:S(2)}, u32[]{:S(2)}) async-start(bf16[8,48,896]{2,1,0:T(8,128)(2,1)} %bitcast.83), calls=%async_computation.2 | async-start | bytes 1376256 | tf_op jit(solution)/shard_map/all_to_all | solution.py:1202
  450.3 87.6 %copy-start.16 = (bf16[2048,512]{1,0:T(8,128)(2,1)S(1)}, bf16[2048,512]{1,0:T(8,128)(2,1)}, u32[]{:S(2)}) copy-start(bf16[2048,512]{1,0:T(8,128)(2,1)} %get-tuple-element.51) | copy-start | bytes 6291460
  533.6 125.8 %all-to-all-start.2 = ((bf16[8,48,1536]{2,1,0:T(8,128)(2,1)}), bf16[8,48,1536]{2,1,0:T(8,128)(2,1)}, u32[]{:S(2)}, u32[]{:S(2)}) async-start(bf16[8,48,1536]{2,1,0:T(8,128)(2,1)} %bitcast.78), calls=%async_computation.5 | async-start | bytes 2359296 | tf_op jit(solution)/shard_map/all_to_all | solution.py:1202
  544.7 66.2 %copy-start.7 = (f32[1,1536]{1,0:T(1,128)S(1)}, f32[1,1536]{1,0:T(1,128)}, u32[]{:S(2)}) copy-start(f32[1,1536]{1,0:T(1,128)} %get-tuple-element.47) | copy-start | bytes 18436
  (5 other events, 18.0 us)
Sparse Core Ops, SparseCore 0:
  15.9 67.5 all-gather.2
  85.0 89.3 all-gather.4
  389.0 57.3 reduce-scatter.3
  448.6 85.0 reduce-scatter.7
  536.3 22.5 reduce-scatter.5

commit v2 on v1

--- a/solution.py
+++ b/solution.py
@@ -576,10 +576,163 @@
     return lax.rsqrt(jnp.mean(values * values, axis=1, keepdims=True) + epsilon)
 
 
-def enter_kernel(tok_ref, dy_ref, gain_ref, normed_ref, dy_all_ref, mine, s0, r0, s1, r1, l0):
-    greet(partners())
+class Line:
+    def __init__(self, own, slot, send, recv, depth):
+        self.own, self.slot, self.send, self.recv, self.depth = own, slot, send, recv, depth
+        self.c, self.s, self.f = here()
+
+    def copy(self, i, distance, up):
+        owner = self.f - (distance - 1) if up else self.f + (distance - 1)
+        to = lax.rem(self.f + (1 if up else self.depth - 1), self.depth)
+        src = self.own[i] if distance == 1 else self.slot(i, owner)
+        k = 0 if up else 1
+        return REMOTE(
+            src,
+            self.slot(i, owner),
+            self.send.at[k, distance - 1, i],
+            self.recv.at[k, distance - 1, i],
+            (self.c, self.s, to),
+            MESH,
+        )
+
+    def may_send(self, distance, up):
+        if up:
+            return (self.f < self.depth - 1) & (self.f >= distance - 1)
+        return (self.f > 0) & (self.f + distance <= self.depth)
+
+    def gets(self, distance, up):
+        return self.f >= distance if up else self.f + distance < self.depth
+
+    def start(self):
+        for i in range(len(self.own)):
+            for up in (True, False):
+                pl.when(self.may_send(1, up))(self.copy(i, 1, up).start)
+
+    def pass_on(self, distance):
+        for i in range(len(self.own)):
+            for up in (True, False):
+                pl.when(self.gets(distance, up))(self.got(i, distance, up).wait_recv)
+                if distance < self.depth - 1:
+                    pl.when(self.may_send(distance + 1, up))(self.copy(i, distance + 1, up).start)
+
+    def got(self, i, distance, up):
+        owner = self.f - distance if up else self.f + distance
+        k = 0 if up else 1
+        place = self.slot(i, owner)
+        return REMOTE(
+            place,
+            place,
+            self.send.at[k, distance - 1, i],
+            self.recv.at[k, distance - 1, i],
+            (self.c, self.s, lax.rem(self.f + (self.depth - 1 if up else 1), self.depth)),
+            MESH,
+        )
+
+    def finish(self):
+        for distance in range(1, self.depth):
+            for i in range(len(self.own)):
+                for up in (True, False):
+                    pl.when(self.may_send(distance, up))(self.copy(i, distance, up).wait_send)
+
+
+class Spread:
+    def __init__(self, src, dst, origin, send, recv, depth, pieces):
+        self.c, self.s, self.f = here()
+        self.src, self.dst, self.origin, self.depth = src, dst, origin, depth
+        self.send, self.recv, self.pieces = send, recv, pieces
+        self.n = dst.shape[0] // pieces
+
+    def part(self, ref, i):
+        return ref.at[pl.ds(i * self.n, self.n)]
+
+    def copy(self, i, up, first):
+        k = 0 if up else 1
+        return REMOTE(
+            self.part(self.src if first else self.dst, i),
+            self.part(self.dst, i),
+            self.send.at[k, i],
+            self.recv.at[i],
+            (self.c, self.s, lax.rem(self.f + (1 if up else self.depth - 1), self.depth)),
+            MESH,
+        )
+
+    def above(self):
+        return (self.f > self.origin) & (self.f < self.depth - 1)
+
+    def below(self):
+        return (self.f < self.origin) & (self.f > 0)
+
+    def start(self, local):
+        first = self.f == self.origin
+
+        @pl.when(first)
+        def _():
+            pltpu.make_async_copy(self.src, self.dst, local).start()
+
+        for i in range(self.pieces):
+            pl.when(first & (self.f < self.depth - 1))(self.copy(i, True, True).start)
+            pl.when(first & (self.f > 0))(self.copy(i, False, True).start)
+
+    def pass_on(self):
+        for i in range(self.pieces):
+            pl.when(self.f != self.origin)(self.copy(i, True, False).wait_recv)
+            pl.when(self.above())(self.copy(i, True, False).start)
+            pl.when(self.below())(self.copy(i, False, False).start)
+
+    def finish(self, local):
+        first = self.f == self.origin
+
+        @pl.when(first)
+        def _():
+            pltpu.make_async_copy(self.src, self.dst, local).wait()
+
+        for i in range(self.pieces):
+            pl.when((first & (self.f < self.depth - 1)) | self.above())(
+                self.copy(i, True, False).wait_send
+            )
+            pl.when((first & (self.f > 0)) | self.below())(self.copy(i, False, False).wait_send)
+
+
+WEIGHT_PIECES = 4
+OUT_PIECES = 2
+
+
+def enter_kernel(
+    tok_ref, dy_ref, gain_ref, attn_ref, forget_ref, out_w_ref,
+    normed_ref, dy_all_ref, w_attn_ref, w_out_ref,
+    mine, forget_all, s0, r0, s1, r1, sz, rz, so, ro, l0, *, depth,
+):
     c, s, f = here()
+    lines = [(c, s, lax.rem(f + 1, depth)), (c, s, lax.rem(f + depth - 1, depth))]
+    greet(partners() + lines)
     n = tok_ref.shape[0]
+    shard, cols = attn_ref.shape
+    step = shard // WEIGHT_PIECES
+    own = [attn_ref.at[pl.ds(i * step, step)] for i in range(WEIGHT_PIECES)] + [forget_ref]
+
+    def slot(i, owner):
+        if i == WEIGHT_PIECES:
+            return forget_all.at[owner]
+        rows = pl.ds(pl.multiple_of(owner * shard + i * step, step), step)
+        return w_attn_ref.at[rows, pl.ds(0, cols)]
+
+    line = Line(own, slot, sz, rz, depth)
+    line.start()
+    heads_rows = w_out_ref.shape[0]
+    t = c * 4 + s
+    origin = (t * heads_rows) // shard
+    spread = Spread(
+        out_w_ref.at[pl.ds(pl.multiple_of(t * heads_rows - origin * shard, heads_rows), heads_rows)],
+        w_out_ref, origin, so, ro, depth, OUT_PIECES,
+    )
+    keep = [
+        pltpu.make_async_copy(
+            attn_ref,
+            w_attn_ref.at[pl.ds(pl.multiple_of(f * shard, shard), shard), pl.ds(0, cols)],
+            l0.at[2],
+        ),
+        pltpu.make_async_copy(forget_ref, forget_all.at[f], l0.at[3]),
+    ]
 
     def body(i, carry):
         r = rows_of(i, STEP)
@@ -590,40 +743,67 @@
     lax.fori_loop(0, n // STEP, body, 0)
     first = Gather(mine, normed_ref, s0, r0)
     second = Gather(dy_ref, dy_all_ref, s1, r1)
-    first.start()
-    second.start()
-    keep = [
+    keep += [
         pltpu.make_async_copy(mine, first.block(0), l0.at[0]),
         pltpu.make_async_copy(dy_ref, second.block(0), l0.at[1]),
     ]
+    first.start()
     for made in keep:
         made.start()
+    line.pass_on(1)
+    spread.start(l0.at[4])
     first.relay()
+    second.start()
+    line.pass_on(2)
     first.finish()
     second.relay()
+    spread.pass_on()
+    line.pass_on(3)
     second.finish()
+    line.finish()
     for made in keep:
         made.wait()
-
-
-def enter(tokens, cotangent, gain):
+    spread.finish(l0.at[4])
+    for owner in range(depth):
+        small = forget_all[owner].astype(F32)
+        tall = jnp.concatenate([small, jnp.zeros((128 - small.shape[0], shard), F32)], axis=0)
+        w_attn_ref[owner * shard : (owner + 1) * shard, cols:] = tall.T.astype(BF)
+
+
+def enter(tokens, cotangent, gain, own_attn, own_forget, output_weight, depth, heads_rows):
     n, w = tokens.shape
+    shard, cols = own_attn.shape
     whole = jax.ShapeDtypeStruct((8 * n, w), BF)
     dma = pltpu.SemaphoreType.DMA((Gather.sems,))
+    line = pltpu.SemaphoreType.DMA((2, depth - 1, WEIGHT_PIECES + 1))
+    vmem = pl.BlockSpec(memory_space=pltpu.VMEM)
+    anywhere = pl.BlockSpec(memory_space=pl.ANY)
     return pl.pallas_call(
-        enter_kernel,
+        functools.partial(enter_kernel, depth=depth),
         name="enter",
-        out_shape=(whole, whole),
-        in_specs=[pl.BlockSpec(memory_space=pltpu.VMEM)] * 3,
-        out_specs=[pl.BlockSpec(memory_space=pl.ANY)] * 2,
-        scratch_shapes=[pltpu.VMEM((n, w), BF), dma, dma, dma, dma, pltpu.SemaphoreType.DMA((2,))],
+        out_shape=(
+            whole,
+            whole,
+            jax.ShapeDtypeStruct((depth * shard, cols + 128), BF),
+            jax.ShapeDtypeStruct((heads_rows, w), BF),
+        ),
+        in_specs=[vmem] * 5 + [anywhere],
+        out_specs=[anywhere, anywhere, vmem, anywhere],
+        scratch_shapes=[
+            pltpu.VMEM((n, w), BF),
+            pltpu.VMEM((depth,) + own_forget.shape, BF),
+            dma, dma, dma, dma, line, line,
+            pltpu.SemaphoreType.DMA((2, OUT_PIECES)),
+            pltpu.SemaphoreType.DMA((OUT_PIECES,)),
+            pltpu.SemaphoreType.DMA((5,)),
+        ],
         compiler_params=pltpu.CompilerParams(
             collective_id=1, has_side_effects=True, vmem_limit_bytes=VMEM_BYTES
         ),
         cost_estimate=pl.CostEstimate(
             flops=50_000_000, bytes_accessed=4 * 8 * n * w * 2, transcendentals=0
         ),
-    )(tokens, cotangent, gain[None])
+    )(tokens, cotangent, gain[None], own_attn, own_forget, output_weight)
 
 
 def middle_kernel(
@@ -737,11 +917,20 @@
 
 
 def leave_kernel(
-    part_ref, down_ref, tok_ref, grad_mid_ref, mid_ref, gain_ref,
-    grad_ref, gain_term_ref, out_ref,
-    near, sums, far, last, near2, sums2, far2, last2, s0, r0, s1, r1,
+    part_ref, down_ref, tok_ref, grad_mid_ref, mid_ref, gain_ref, small_ref,
+    grad_ref, small_sum_ref, out_ref,
+    near, sums, far, last, near2, sums2, far2, last2, small, plane_small, line_small,
+    s0, r0, s1, r1, s2, r2, *, depth,
 ):
-    greet(partners())
+    c, s, f = here()
+    plane_peers = [
+        (core, flip(s, k) if k else s, f, k + 4 * i)
+        for i, core in enumerate((c, 1 - c))
+        for k in range(4)
+        if i or k
+    ]
+    line_peers = [(c, s, lax.rem(f + k, depth), k) for k in range(1, depth)]
+    greet([p[:3] for p in plane_peers + line_peers])
     reduce = Reduce(part_ref, (near, sums, far, last), s0, r0)
     other = Reduce(down_ref, (near2, sums2, far2, last2), s1, r1)
     reduce.start()
@@ -763,7 +952,17 @@
         return carry + jnp.sum(grad * tok * inverse, axis=0, keepdims=True)
 
     n, w = tok_ref.shape
-    gain_term_ref[...] = lax.fori_loop(0, n // STEP, body, jnp.zeros((1, w), F32))
+    small[...] = small_ref[...]
+    small[0:1, :] = lax.fori_loop(0, n // STEP, body, jnp.zeros((1, w), F32))
+    place = c * 4 + s
+    plane_small[pl.ds(place, 1)] = small[...][None]
+    sent = []
+    for core, other_s, other_f, k in plane_peers:
+        made = REMOTE(
+            small, plane_small.at[place], s2.at[k - 1], r2.at[k - 1], (core, other_s, other_f), MESH
+        )
+        made.start()
+        sent.append(made)
     other.arrive()
 
     def body2(i, carry):
@@ -772,32 +971,60 @@
         return carry
 
     lax.fori_loop(0, n // STEP, body2, 0)
+    for made in sent:
+        made.wait()
+    total = plane_small[0]
+    for i in range(1, 8):
+        total = total + plane_small[i]
+    small[...] = total
+    line_small[pl.ds(f, 1)] = total[None]
+    sent = []
+    for core, other_s, other_f, k in line_peers:
+        made = REMOTE(
+            small, line_small.at[f], s2.at[6 + k], r2.at[6 + k], (core, other_s, other_f), MESH
+        )
+        made.start()
+        sent.append(made)
     reduce.finish()
     other.finish()
-
-
-def leave(part, down_part, tokens, grad_mid, mid, gain):
+    for made in sent:
+        made.wait()
+    total = line_small[0]
+    for i in range(1, depth):
+        total = total + line_small[i]
+    small_sum_ref[...] = total
+
+
+def leave(part, down_part, tokens, grad_mid, mid, gain, small, depth):
     n, w = mid.shape
+    sems = pltpu.SemaphoreType.DMA((6 + depth,))
     dma = pltpu.SemaphoreType.DMA((16,))
     vmem = pl.BlockSpec(memory_space=pltpu.VMEM)
     return pl.pallas_call(
-        leave_kernel,
+        functools.partial(leave_kernel, depth=depth),
         name="leave",
         out_shape=(
             jax.ShapeDtypeStruct((n, w), F32),
-            jax.ShapeDtypeStruct((1, w), F32),
+            jax.ShapeDtypeStruct((8, w), F32),
             jax.ShapeDtypeStruct((n, w), BF),
         ),
-        in_specs=[vmem] * 6,
+        in_specs=[vmem] * 7,
         out_specs=[vmem] * 3,
-        scratch_shapes=Reduce.scratch(n, w) + Reduce.scratch(n, w) + [dma, dma, dma, dma],
+        scratch_shapes=Reduce.scratch(n, w)
+        + Reduce.scratch(n, w)
+        + [
+            pltpu.VMEM((8, w), F32),
+            pltpu.VMEM((8, 8, w), F32),
+            pltpu.VMEM((depth, 8, w), F32),
+            dma, dma, dma, dma, sems, sems,
+        ],
         compiler_params=pltpu.CompilerParams(
             collective_id=4, has_side_effects=True, vmem_limit_bytes=VMEM_BYTES
         ),
         cost_estimate=pl.CostEstimate(
             flops=50_000_000, bytes_accessed=4 * 8 * n * w * 2, transcendentals=0
         ),
-    )(part, down_part, tokens, grad_mid, mid, gain[None])
+    )(part, down_part, tokens, grad_mid, mid, gain[None], small)
 
 
 BQ = 256
@@ -1126,27 +1353,18 @@
     )
     ends = jnp.cumsum(seq_lengths[0])
 
-    forget_part = jnp.pad(columns(forget_weight, heads), ((0, 0), (0, 128 - heads)))
     own_attn = jnp.concatenate(
-        [
-            columns(query_weight, hw),
-            columns(key_weight, hw),
-            columns(value_weight, hw),
-            columns(outgate_weight, hw),
-            forget_part,
-        ],
-        axis=1,
-    )
-    own_out = columns(output_weight, hw)
+        [columns(w, hw) for w in (query_weight, key_weight, value_weight, outgate_weight)], axis=1
+    )
+    own_forget = jnp.pad(columns(forget_weight, heads).T, ((0, 16 - heads), (0, 0)))
     own_mlp = jnp.concatenate(
         [columns(gate_weight, fw), columns(up_weight, fw), columns(down_weight, fw)], axis=1
     )
-    w_attn = lax.all_gather(own_attn, "fsdp", axis=0, tiled=True)
-    w_out_cols = lax.all_gather(own_out, "fsdp", axis=0, tiled=True)
+    normed, cotangent_all, w_attn, w_out = enter(
+        inputs, cotangent, attn_gain, own_attn, own_forget, output_weight, depth, hw
+    )
+    own_mlp, w_attn = lax.optimization_barrier((own_mlp, w_attn))
     w_mlp = lax.all_gather(own_mlp, "fsdp", axis=0, tiled=True)
-    w_out = lax.all_to_all(w_out_cols, plane_axes, split_axis=0, concat_axis=1, tiled=True)
-
-    normed, cotangent_all = enter(inputs, cotangent, attn_gain)
     cat = dot(w_attn, normed, 0, 1)
     bias_own = lax.dynamic_slice_in_dim(forget_bias, place * heads, heads, 0)
     bias = jnp.broadcast_to(jnp.pad(bias_own, (0, 16 - heads))[:, None], (16, 128))
@@ -1177,10 +1395,11 @@
         ],
         axis=1,
     )
-    mlp_grad = lax.psum_scatter(
-        spread_rows(mlp_terms, plane, depth), "fsdp", scatter_dimension=0, tiled=True
+    mlp_part, mlp_spread = lax.optimization_barrier(
+        (mlp_part, spread_rows(mlp_terms, plane, depth))
     )
     grad_mid, mlp_gain_term, branch = turn(mlp_part, cotangent, mid, mlp_gain)
+    mlp_grad = lax.psum_scatter(mlp_spread, "fsdp", scatter_dimension=0, tiled=True)
 
     grad_gated = dot(w_out, branch, 1, 1)
     grad_cat, bias_grad = attention_back(
@@ -1188,14 +1407,24 @@
     )
     out_term = dot(gated, branch, 1, 0).astype(BF)
     attn_term = dot(normed, grad_cat, 0, 1).astype(BF)
+    grad_cat, attn_spread = lax.optimization_barrier(
+        (grad_cat, spread_rows(attn_term, plane, depth))
+    )
+    out_term, mlp_grad = lax.optimization_barrier((out_term, mlp_grad))
+    output_weight_grad = lax.psum_scatter(out_term, "fsdp", scatter_dimension=0, tiled=True)
+    attn_spread, output_weight_grad = lax.optimization_barrier((attn_spread, output_weight_grad))
+    attn_grad = lax.psum_scatter(attn_spread, "fsdp", scatter_dimension=0, tiled=True)
     attn_part = dot(grad_cat, w_attn, 0, 1).astype(BF)
-    attn_grad = lax.psum_scatter(
-        spread_rows(attn_term, plane, depth), "fsdp", scatter_dimension=0, tiled=True
-    )
-    output_weight_grad = lax.psum_scatter(out_term, "fsdp", scatter_dimension=0, tiled=True)
-    tokens_grad, attn_gain_term, block_out = leave(
-        attn_part, down_part, inputs, grad_mid, mid, attn_gain
-    )
+    bias_row = lax.dynamic_update_slice_in_dim(
+        jnp.zeros((width,), F32), bias_grad[:heads, 0], place * heads, 0
+    )
+    small = jnp.concatenate(
+        [jnp.zeros((1, width), F32), mlp_gain_term, bias_row[None], jnp.zeros((5, width), F32)]
+    )
+    tokens_grad, small_sum, block_out = leave(
+        attn_part, down_part, inputs, grad_mid, mid, attn_gain, small, depth
+    )
+    attn_grad, tokens_grad = lax.optimization_barrier((attn_grad, tokens_grad))
 
     def to_rows(grad):
         part = grad.shape[0] // plane
@@ -1216,12 +1445,8 @@
         pick(attn_rows, i * hw, hw) for i in range(4)
     )
     forget_grad = pick(attn_rows, 4 * hw, heads)
-    bias_term = lax.dynamic_update_slice_in_dim(
-        jnp.zeros((head_count,), F32), bias_grad[:heads, 0], place * heads, 0
-    )
-    attn_gain_grad, mlp_gain_grad, forget_bias_grad = lax.psum(
-        (attn_gain_term[0], mlp_gain_term[0], bias_term), ("cp", "sp", "fsdp")
-    )
+    attn_gain_grad, mlp_gain_grad = small_sum[0], small_sum[1]
+    forget_bias_grad = small_sum[2, :head_count]
     return (
         block_out[None],
         tokens_grad[None],

time: 683 us -> 530 us (0.78); the launches traced: 673 us -> 527 us
  waiting for transfers between devices: 91.9 us -> 20.7 us
  blocking collectives: 70.3 us -> 0 us
  matrix products: 110 us -> 94.6 us
  Pallas kernels: 325 us -> 332 us
    reduce_scatter x2, waiting for transfers between devices: 91.8 us -> 0.02 us  [the longest x1 0.02 us: local_plane(): lax.psum_scatter(attn_spread, 'fsdp', scatter_dimension=0, tiled=True)]
    psum x1 -> x0, blocking collectives: 40.3 us -> none  [local_plane(): lax.psum((attn_gain_term[0], mlp_gain_term[0], bias_term), ('cp', 'sp', '...]
    all_gather x1 -> x0, blocking collectives: 30 us -> none  [local_plane(): w_out_cols = lax.all_gather(own_out, 'fsdp', axis=0, tiled=True)]
    reduce_scatter x1, waiting for transfers between devices: 0.01 us -> 17.7 us  [local_plane(): lax.psum_scatter(out_term, 'fsdp', scatter_dimension=0, tiled=True)]
    pallas_call x2, Pallas kernels: 134 us -> 142 us  [the longest x1 76.7 us: leave(): pl.pallas_call(functools.partial(leave_kernel, depth=depth), name='leave'...]
    dot_general x3, matrix products: 17.3 us -> 10.4 us  [matmul_left_t(): lax.dot_general(left, right, (((0,), (0,)), ((), ())), preferred_element_...]
  transfers between devices with their start and end apart: 8 -> 6, of which waited for: 2 -> 2; matrix products, arithmetic and copies ran while one was open for 13% -> 13% of each run, Pallas kernels for 34% -> 51%
where the time goes in v2:
time: 530 us; the launch traced here: 527 us
  Pallas kernels  332 us (63%)
  matrix products  94.6 us (18%)
  local copies, waits for them, and re-layouts  46.5 us (9%)
  waiting for transfers between devices  20.7 us (4%)
  between operations  14.5 us (3%)
  other arithmetic  10.1 us (2%)
  starting transfers between devices  8.55 us (2%)
    pallas_call x1, Pallas kernels, leave(): pl.pallas_call(functools.partial(leave_kernel, depth=depth), name='leave'...  76.7 us
    pallas_call x1, Pallas kernels, middle(): pl.pallas_call(middle_kernel, name='middle', out_shape=(jax.ShapeDtypeStr...  69.8 us
    pallas_call x1, Pallas kernels, turn(): pl.pallas_call(turn_kernel, name='turn', out_shape=(jax.ShapeDtypeStruct(...  66.7 us
    pallas_call x1, Pallas kernels, enter(): pl.pallas_call(functools.partial(enter_kernel, depth=depth), name='enter'...  65.3 us
    dot_general x6, matrix products, dot(): lax.dot_general(a, b, (((ca,), (cb,)), ((), ())), preferred_element_type=...  45.9 us
    pallas_call x1, Pallas kernels, attention_back(): pl.pallas_call(functools.partial(attention_back_kernel, heads=heads, hd=h...  29.3 us
    pallas_call x1, Pallas kernels, attention(): pl.pallas_call(functools.partial(attention_kernel, heads=heads, hd=hd, sl...  24.1 us
    dot_general x3, matrix products, matmul_right_t(): lax.dot_general(left, right, (((1,), (1,)), ((), ())), preferred_element_...  20.2 us
  transfers between devices with their start and end apart: 6, of which 2 were waited for; matrix products, arithmetic and copies ran while one was open for 13% of the time, Pallas kernels for 51%

profile of v2, /device:TPU:0, one launch (start us, length us, event | category | flops | bytes accessed | tf_op | source)
XLA Modules:
  0.0 526.8 jit_solution(5216259698389698582)
XLA Ops:
  16.8 65.3 %enter.1 = (bf16[2048,1536]{1,0:T(8,128)(2,1)}, bf16[2048,1536]{1,0:T(8,128)(2,1)}, bf16[1536,896]{1,0:T(8,128)(2,1)}, bf16[192,1536]{1,0:T(8,128)(2,1)}) custom-call(bf16[256,1536]{1,0:T(8,128)(2,1)} %bitcast.73, bf16[256,1536]{1,0:T(8,128)(2,1)} %bitcast.76, f32[1,1536]{1,0:T(1,128)} %broadcast_in_dim.46.gain_ref, ...), custom_call_target="tpu_custom_call" | custom-call | flops 50000000 | bytes 25165824 | tf_op jit(solution)/shard_map/enter/pallas_call | solution.py:781
  84.4 10.7 %fusion.11.cat_ref = f32[896,2048]{1,0:T(8,128)} fusion(bf16[1536,896]{1,0:T(8,128)(2,1)} %get-tuple-element.46, bf16[2048,1536]{1,0:T(8,128)(2,1)} %get-tuple-element.47), kind=kOutput, calls=%fused_computation.50 | convolution fusion | flops 5637144576 | bytes 16384000 | tf_op jit(solution)/shard_map/dot_general | solution.py:1036
  95.7 24.1 %attention.1 = (bf16[192,2048]{1,0:T(8,128)(2,1)}, bf16[192,2048]{1,0:T(8,128)(2,1)}, f32[192,2048]{1,0:T(8,128)}, f32[8,2048]{1,0:T(8,128)}, f32[16,2048]{1,0:T(8,128)}) custom-call(s32[4]{0:T(128)} %select_reduce_fusion.place_ref, s32[8]{0:T(128)} %bitcast.92, f32[896,2048]{1,0:T(8,128)} %fusion.11.cat_ref, f32[16,128]{1,0:T(8,128)} %broadcast_in_dim.47.bias_ref), custom_call_target="tpu_custom_call" | custom-call | flops 6442450944 | bytes 7340032 | tf_op jit(solution)/shard_map/attention/pallas_call | solution.py:1176
  119.8 5.6 %convolution_convert_fusion.1.part_ref = bf16[2048,1536]{1,0:T(8,128)(2,1)} fusion(bf16[192,2048]{1,0:T(8,128)(2,1)} %get-tuple-element.51, bf16[192,1536]{1,0:T(8,128)(2,1)S(1)} %copy-done.4), kind=kOutput, calls=%fused_computation.2 | convolution fusion | flops 1211105280 | bytes 7667712 | tf_op jit(solution)/shard_map/dot_general | solution.py:1036
  125.4 69.8 %middle.1 = (f32[256,1536]{1,0:T(8,128)}, bf16[2048,1536]{1,0:T(8,128)(2,1)}) custom-call(bf16[2048,1536]{1,0:T(8,128)(2,1)} %convolution_convert_fusion.1.part_ref, bf16[256,1536]{1,0:T(8,128)(2,1)} %bitcast.74, f32[1,1536]{1,0:T(1,128)} %broadcast_in_dim.48.gain_ref), custom_call_target="tpu_custom_call" | custom-call | flops 50000000 | bytes 25165824 | tf_op jit(solution)/shard_map/middle/pallas_call | solution.py:841
  195.3 6.1 %fusion.3 = f32[2048,512]{1,0:T(8,128)S(1)} fusion(bf16[2048,1536]{1,0:T(8,128)(2,1)} %get-tuple-element.52, bf16[1536,1536]{1,0:T(8,128)(2,1)} %all-gather.2.cloned.1.call-done), kind=kOutput, calls=%fused_computation.17 | convolution fusion | flops 3221225472 | bytes 12058624 | tf_op jit(solution)/shard_map/dot_general | solution.py:20
  201.4 5.6 %fusion.9 = f32[2048,512]{1,0:T(8,128)S(1)} fusion(bf16[2048,1536]{1,0:T(8,128)(2,1)} %get-tuple-element.49, bf16[1536,1536]{1,0:T(8,128)(2,1)S(1)} %copy-done.11), kind=kOutput, calls=%fused_computation.23 | convolution fusion | flops 3221225472 | bytes 12058624 | tf_op jit(solution)/shard_map/dot_general | solution.py:20
  207.1 6.3 %multiply_convert_fusion = (bf16[2048,512]{1,0:T(8,128)(2,1)}, bf16[2048,512]{1,0:T(8,128)(2,1)S(1)}, bf16[2048,512]{1,0:T(8,128)(2,1)S(1)}) fusion(f32[2048,512]{1,0:T(8,128)S(1)} %fusion.3, f32[2048,512]{1,0:T(8,128)S(1)} %fusion.9, bf16[2048,1536]{1,0:T(8,128)(2,1)S(1)} %bitcast.89, bf16[1536,1536]{1,0:T(8,128)(2,1)S(1)} %copy-done.11), kind=kOutput, calls=%fused_computation.5 | convolution fusion | flops 3236954112 | bytes 22544384 | tf_op jit(solution)/shard_map/dot_general | solution.py:20
  216.9 3.5 convolution_convert_fusion.5
  220.4 3.5 convolution_convert_fusion.4
  226.3 7.1 %copy.49 = bf16[1536,1536]{1,0:T(8,128)(2,1)} copy(bf16[1536,1536]{0,1:T(8,128)(2,1)} %pad_maximum_fusion) | data formatting | bytes 9437184 | tf_op jit(solution)/shard_map/concatenate | solution.py:1390
  233.4 5.1 copy.50
  238.5 5.2 fusion.1
  243.7 6.9 %add_convert_fusion.part_ref = bf16[2048,1536]{1,0:T(8,128)(2,1)} fusion(f32[2048,1536]{1,0:T(8,128)S(1)} %fusion.1, bf16[2048,512]{1,0:T(8,128)(2,1)S(1)} %copy-done.18, bf16[1536,1536]{1,0:T(8,128)(2,1)} %all-gather.2.cloned.1.call-done), kind=kOutput, calls=%fused_computation | convolution fusion | flops 3227516928 | bytes 22544384 | tf_op jit(solution)/shard_map/dot_general | solution.py:24
  250.6 66.7 %turn.1 = (f32[256,1536]{1,0:T(8,128)}, f32[1,1536]{1,0:T(1,128)}, bf16[2048,1536]{1,0:T(8,128)(2,1)}) custom-call(bf16[2048,1536]{1,0:T(8,128)(2,1)} %add_convert_fusion.part_ref, bf16[256,1536]{1,0:T(8,128)(2,1)} %bitcast.77, f32[256,1536]{1,0:T(8,128)} %get-tuple-element.54.mid_ref, f32[1,1536]{1,0:T(1,128)} %broadcast_in_dim.48.gain_ref), custom_call_target="tpu_custom_call" | custom-call | flops 50000000 | bytes 25165824 | tf_op jit(solution)/shard_map/turn/pallas_call | solution.py:898
  317.3 6.3 %fusion.12.gg_ref = f32[192,2048]{1,0:T(8,128)} fusion(bf16[192,1536]{1,0:T(8,128)(2,1)S(1)} %copy-done.4, bf16[2048,1536]{1,0:T(8,128)(2,1)} %get-tuple-element.55), kind=kOutput, calls=%fused_computation.51 | convolution fusion | flops 1207959552 | bytes 8454144 | tf_op jit(solution)/shard_map/dot_general | solution.py:1036
  325.9 29.3 %attention_back.1 = (bf16[896,2048]{1,0:T(8,128)(2,1)}, f32[16,128]{1,0:T(8,128)}) custom-call(s32[4]{0:T(128)} %select_reduce_fusion.place_ref, s32[8]{0:T(128)} %bitcast.93, f32[896,2048]{1,0:T(8,128)} %fusion.11.cat_ref, f32[16,128]{1,0:T(8,128)} %broadcast_in_dim.47.bias_ref, f32[192,2048]{1,0:T(8,128)} %fusion.12.gg_ref, ...), custom_call_target="tpu_custom_call" | custom-call | flops 16106127360 | bytes 14680064 | tf_op jit(solution)/shard_map/attention_back/pallas_call | solution.py:1292
  355.3 10.1 %convolution_convert_fusion.3 = bf16[1536,896]{1,0:T(8,128)(2,1)S(1)} fusion(bf16[2048,1536]{1,0:T(8,128)(2,1)} %get-tuple-element.47, bf16[896,2048]{1,0:T(8,128)(2,1)} %get-tuple-element.61), kind=kOutput, calls=%fused_computation.10 | convolution fusion | flops 5638520832 | bytes 12713984 | tf_op jit(solution)/shard_map/dot_general | solution.py:1036
  367.2 17.7 %reduce-scatter.6.cloned.1.call-done = bf16[48,1536]{1,0:T(8,128)(2,1)} async-done(((bf16[192,1536]{1,0:T(8,128)(2,1)}), bf16[48,1536]{1,0:T(8,128)(2,1)}) %reduce-scatter.6.cloned.1.call-update) | async-done | bytes 147472 | tf_op jit(solution)/shard_map/reduce_scatter | solution.py:1414
  386.0 11.0 %convolution_convert_fusion.part_ref = bf16[2048,1536]{1,0:T(8,128)(2,1)} fusion(bf16[896,2048]{1,0:T(8,128)(2,1)} %get-tuple-element.61, bf16[1536,896]{1,0:T(8,128)(2,1)} %get-tuple-element.46), kind=kOutput, calls=%fused_computation.1 | convolution fusion | flops 5640290304 | bytes 12713984 | tf_op jit(solution)/shard_map/dot_general | solution.py:1036
  397.0 3.7 all-to-all-start.1
  401.4 8.2 %convolution_convert_fusion.2.down_ref = bf16[2048,1536]{1,0:T(8,128)(2,1)} fusion(bf16[2048,512]{1,0:T(8,128)(2,1)} %get-tuple-element.78, bf16[1536,1536]{1,0:T(8,128)(2,1)} %all-gather.2.cloned.1.call-done), kind=kOutput, calls=%fused_computation.3 | convolution fusion | flops 3224371200 | bytes 9961472 | tf_op jit(solution)/shard_map/dot_general | solution.py:24
  409.6 76.7 %leave.1 = (f32[256,1536]{1,0:T(8,128)}, f32[8,1536]{1,0:T(8,128)}, bf16[256,1536]{1,0:T(8,128)(2,1)}) custom-call(bf16[2048,1536]{1,0:T(8,128)(2,1)} %convolution_convert_fusion.part_ref, bf16[2048,1536]{1,0:T(8,128)(2,1)} %convolution_convert_fusion.2.down_ref, bf16[256,1536]{1,0:T(8,128)(2,1)} %bitcast.75, f32[256,1536]{1,0:T(8,128)} %get-tuple-element.62.grad_mid_ref, ...), custom_call_target="tpu_custom_call" | custom-call | flops 50000000 | bytes 25165824 | tf_op jit(solution)/shard_map/leave/pallas_call | solution.py:1003
  486.4 4.4 all-to-all-start
  (112 shorter events, 53.5 us)
Async XLA Ops:
  7.2 6.1 %copy-start = (bf16[384,4096]{1,0:T(8,128)(2,1)S(1)}, bf16[384,4096]{1,0:T(8,128)(2,1)}, u32[]{:S(2)}) copy-start(bf16[384,4096]{1,0:T(8,128)(2,1)} %param.29) | copy-start | bytes 9437188
  7.2 188.1 %all-gather.2.cloned.1.call-start = ((), (), s32[]{:S(2)}) async-start(), calls=%async_computation.5 | async-start | bytes 5898240 | tf_op jit(solution)/shard_map/all_gather | solution.py:1367
  14.5 67.8 %copy-start.12 = (f32[24]{0:T(128)S(1)}, f32[24]{0:T(128)}, u32[]{:S(2)}) copy-start(f32[24]{0:T(128)} %param.26) | copy-start | bytes 292
  14.5 67.9 %copy-start.13 = (s32[1,8]{1,0:T(1,128)S(1)}, s32[1,8]{1,0:T(1,128)}, u32[]{:S(2)}) copy-start(s32[1,8]{1,0:T(1,128)} %param.18) | copy-start | bytes 100
  14.5 68.6 %copy-start.9 = (f32[1536]{0:T(1024)S(1)}, f32[1536]{0:T(1024)}, u32[]{:S(2)}) copy-start(f32[1536]{0:T(1024)} %param.28) | copy-start | bytes 18436
  14.6 69.2 %copy-start.14 = (s32[1,4]{1,0:T(1,128)S(1)}, s32[1,4]{1,0:T(1,128)}, u32[]{:S(2)}) copy-start(s32[1,4]{1,0:T(1,128)} %param.19) | copy-start | bytes 52
  82.1 273.1 %reduce-scatter.4.cloned.1.call-start = ((), (), s32[]{:S(2)}) async-start(), calls=%async_computation.6 | async-start | bytes 5898240 | tf_op jit(solution)/shard_map/reduce_scatter | solution.py:1402
  95.7 24.1 %copy-start.4 = (bf16[192,1536]{1,0:T(8,128)(2,1)S(1)}, bf16[192,1536]{1,0:T(8,128)(2,1)}, u32[]{:S(2)}) copy-start(bf16[192,1536]{1,0:T(8,128)(2,1)} %get-tuple-element.48) | copy-start | bytes 1769476
  195.3 6.1 %copy-start.11 = (bf16[1536,1536]{1,0:T(8,128)(2,1)S(1)}, bf16[1536,1536]{1,0:T(8,128)(2,1)}, u32[]{:S(2)}) copy-start(bf16[1536,1536]{1,0:T(8,128)(2,1)} %all-gather.2.cloned.1.call-done) | copy-start | bytes 14155780
  195.3 11.8 %slice-start.2 = ((s8[6291456]{0:T(1024)(128)(4,1)}), s8[4194304]{0:T(1024)(128)(4,1)S(1)}, s32[]{:S(2)}) async-start(s8[6291456]{0:T(1024)(128)(4,1)} %bitcast.88), calls=%async_computation.11 | async-start | bytes 8388608
  201.4 5.7 %slice-start.3 = ((s8[6291456]{0:T(1024)(128)(4,1)}), s8[2097152]{0:T(1024)(128)(4,1)S(1)}, s32[]{:S(2)}) async-start(s8[6291456]{0:T(1024)(128)(4,1)} %bitcast.88), calls=%async_computation.12 | async-start | bytes 4194304
  213.4 7.0 %slice-start = ((s8[6291456]{0:T(1024)(128)(4,1)}), s8[4194304]{0:T(1024)(128)(4,1)S(1)}, s32[]{:S(2)}) async-start(s8[6291456]{0:T(1024)(128)(4,1)} %bitcast.86), calls=%async_computation.9 | async-start | bytes 8388608
  216.9 3.5 slice-start.1
  233.4 5.1 copy-start.16
  238.5 5.2 copy-start.18
  250.6 134.3 %reduce-scatter.6.cloned.1.call-start = ((), (), s32[]{:S(2)}) async-start(), calls=%async_computation.7 | async-start | bytes 737280 | tf_op jit(solution)/shard_map/reduce_scatter | solution.py:1414
  317.3 6.4 %copy-start.2 = (bf16[2048,1536]{1,0:T(8,128)(2,1)S(1)}, bf16[2048,1536]{1,0:T(8,128)(2,1)}, u32[]{:S(2)}) copy-start(bf16[2048,1536]{1,0:T(8,128)(2,1)} %get-tuple-element.55) | copy-start | bytes 18874372
  317.3 6.3 %copy-start.5 = (bf16[192,2048]{1,0:T(8,128)(2,1)S(1)}, bf16[192,2048]{1,0:T(8,128)(2,1)}, u32[]{:S(2)}) copy-start(bf16[192,2048]{1,0:T(8,128)(2,1)} %get-tuple-element.51) | copy-start | bytes 2359300
  355.3 131.1 %reduce-scatter.8.cloned.1.call-start = ((), (), s32[]{:S(2)}) async-start(), calls=%async_computation.8 | async-start | bytes 3440640 | tf_op jit(solution)/shard_map/reduce_scatter | solution.py:1416
  385.9 14.8 %copy-start.10 = (f32[1,1536]{1,0:T(1,128)S(1)}, f32[1,1536]{1,0:T(1,128)}, u32[]{:S(2)}) copy-start(f32[1,1536]{1,0:T(1,128)} %get-tuple-element.63) | copy-start | bytes 18436
  397.0 89.4 %all-to-all-start.1 = ((bf16[8,48,1536]{2,1,0:T(8,128)(2,1)}), bf16[8,48,1536]{2,1,0:T(8,128)(2,1)S(1)}, u32[]{:S(2)}, u32[]{:S(2)}) async-start(bf16[8,48,1536]{2,1,0:T(8,128)(2,1)} %bitcast.21), calls=%async_computation.4 | async-start | bytes 2359296 | tf_op jit(solution)/shard_map/all_to_all | solution.py:1431
  486.3 6.0 %copy-start.3 = (bf16[8,48,1536]{2,1,0:T(8,128)(2,1)}, bf16[8,48,1536]{2,1,0:T(8,128)(2,1)S(1)}, u32[]{:S(2)}) copy-start(bf16[8,48,1536]{2,1,0:T(8,128)(2,1)S(1)} %all-to-all-done.1) | copy-start | bytes 3538948
  486.4 15.4 %all-to-all-start = ((bf16[8,48,896]{2,1,0:T(8,128)(2,1)}), bf16[8,48,896]{2,1,0:T(8,128)(2,1)}, u32[]{:S(2)}, u32[]{:S(2)}) async-start(bf16[8,48,896]{2,1,0:T(8,128)(2,1)} %bitcast.84), calls=%async_computation.3 | async-start | bytes 1376256 | tf_op jit(solution)/shard_map/all_to_all | solution.py:1431
  506.8 13.2 %copy-start.1 = (bf16[384,4096]{1,0:T(8,128)(2,1)S(1)}, bf16[384,4096]{1,0:T(8,128)(2,1)}, u32[]{:S(2)}) copy-start(bf16[384,4096]{1,0:T(8,128)(2,1)} %param.29) | copy-start | bytes 9437188
  (6 other events, 18.4 us)
Sparse Core Ops, SparseCore 0:
  82.2 94.5 all-gather.1
  250.7 89.7 reduce-scatter.3
  355.4 29.4 reduce-scatter.5
  387.0 52.5 reduce-scatter.7

commit v3 on v2

--- a/solution.py
+++ b/solution.py
@@ -529,19 +529,29 @@
 
         lax.fori_loop(0, self.n // 32, body, 0)
 
+    def halves(self):
+        return pl.ds(0, self.w // 2), pl.ds(self.w // 2, self.w // 2)
+
     def run(self):
-        left, right = pl.ds(0, self.w // 2), pl.ds(self.w // 2, self.w // 2)
+        self.first()
+        self.second()
+
+    def first(self):
+        left, right = self.halves()
         self.chip_sum(3)
-        fx = self.copy(self.sums.at[3, :, left], self.far.at[1], 4, self.x)
-        fy = self.copy(self.sums.at[3, :, right], self.far.at[3], 5, self.y)
+        self.fx = self.copy(self.sums.at[3, :, left], self.far.at[1], 4, self.x)
+        self.fy = self.copy(self.sums.at[3, :, right], self.far.at[3], 5, self.y)
         self.chip_sum(1)
         self.nx = self.copy(self.sums.at[1, :, left], self.far.at[0], 6, self.x)
         self.chip_sum(2)
         self.ny = self.copy(self.sums.at[2, :, right], self.far.at[2], 7, self.y)
-        fx.wait_recv()
+
+    def second(self):
+        left, right = self.halves()
+        self.fx.wait_recv()
         self.add(2, left, 1)
         self.by = self.copy(self.sums.at[2, :, left], self.last.at[0], 8, self.y)
-        fy.wait_recv()
+        self.fy.wait_recv()
         self.add(1, right, 3)
         self.bx = self.copy(self.sums.at[1, :, right], self.last.at[1], 9, self.x)
         self.a[0].wait_recv()
@@ -855,19 +865,255 @@
     )(part, tokens, gain[None])
 
 
-def turn_kernel(
-    part_ref, dy_ref, mid_ref, gain_ref, grad_mid_ref, gain_term_ref, branch_ref,
-    near, sums, far, last, mine, s0, r0, s1, r1, l0,
+TERM_PIECES = 4
+
+
+class LineSum:
+    def __init__(self, term, got, send, recv, depth):
+        self.term, self.got, self.send, self.recv, self.depth = term, got, send, recv, depth
+        self.c, self.s, self.f = here()
+        self.n = term.shape[0] // TERM_PIECES
+
+    def source(self, i, g):
+        return self.term.at[pl.ds(i * self.n, self.n), g]
+
+    def copy(self, k, g, i, src):
+        to = lax.rem(self.f + (1 if k == 0 else self.depth - 1), self.depth)
+        return REMOTE(
+            src,
+            self.got.at[k, g, pl.ds(i * self.n, self.n)],
+            self.send.at[k, g, i],
+            self.recv.at[k, g, i],
+            (self.c, self.s, to),
+            MESH,
+        )
+
+    def targets(self, k):
+        return range(self.depth - 1, 0, -1) if k == 0 else range(self.depth - 1)
+
+    def is_end(self, k):
+        return self.f == (0 if k == 0 else self.depth - 1)
+
+    def start(self):
+        for i in range(TERM_PIECES):
+            self.start_piece(i)
+
+    def start_piece(self, i):
+        for n in range(self.depth - 1):
+            for k in (0, 1):
+                g = self.targets(k)[n]
+                pl.when(self.is_end(k))(self.copy(k, g, i, self.source(i, g)).start)
+
+    def add(self, k, g, i):
+        rows = pl.ds(i * self.n, self.n)
+        total = self.got[k, g, rows].astype(F32) + self.term[rows, g].astype(F32)
+        self.got[k, g, rows] = total.astype(BF)
+
+    def pass_on(self, i):
+        for n in range(self.depth - 2):
+            for k in (0, 1):
+                g = self.targets(k)[n]
+                beyond = self.f < g if k == 0 else self.f > g
+
+                @pl.when(beyond & jnp.logical_not(self.is_end(k)))
+                def _(k=k, g=g):
+                    made = self.copy(k, g, i, self.got.at[k, g, pl.ds(i * self.n, self.n)])
+                    made.wait_recv()
+                    self.add(k, g, i)
+                    made.start()
+
+    def collect(self, out):
+        for i in range(TERM_PIECES):
+            rows = pl.ds(i * self.n, self.n)
+            for g in range(self.depth):
+
+                @pl.when(self.f == g)
+                def _(g=g, i=i, rows=rows):
+                    total = self.term[rows, g].astype(F32)
+                    for k in (0, 1):
+                        if g != (0 if k == 0 else self.depth - 1):
+                            self.copy(k, g, i, self.source(i, g)).wait_recv()
+                            total = total + self.got[k, g, rows].astype(F32)
+                    out[rows] = total.astype(BF)
+
+    def finish(self):
+        for k in (0, 1):
+            for g in self.targets(k):
+                beyond = self.f < g if k == 0 else self.f > g
+                for i in range(TERM_PIECES):
+                    pl.when(beyond)(self.copy(k, g, i, self.source(i, g)).wait_send)
+
+
+class Exchange:
+    def __init__(self, rows, out, send, recv, peers):
+        c, s, f = here()
+        self.place = c * 4 + s
+        self.made = [
+            REMOTE(rows.at[core * 4 + other], out.at[self.place], send.at[k], recv.at[k], (core, other, f), MESH)
+            for core, other, f, k in peers
+        ]
+        self.keep = pltpu.make_async_copy(rows.at[self.place], out.at[self.place], send.at[0])
+
+    def start(self):
+        for made in self.made:
+            made.start()
+        self.keep.start()
+
+    def finish(self):
+        for made in self.made:
+            made.wait()
+        self.keep.wait()
+
+
+FFN_TILE = 256
+
+
+def ffn_kernel(
+    nm_ref, dy_all_ref, w_ref, dy_ref, mid_ref, gain_ref,
+    grad_mid_ref, gain_term_ref, branch_ref, down_part_ref, gu_rows_ref, low_term_ref,
+    nm, dy, w, grads, own, near, out, far, last, term, got, mine, stage,
+    l0, l1, s0, r0, s1, r1, s2, r2, *, depth,
 ):
-    greet(partners())
-    reduce = Reduce(part_ref, (near, sums, far, last), s0, r0)
-    reduce.start()
-    reduce.run()
-    reduce.arrive()
-
-    def body(i, carry):
-        r = rows_of(i, STEP)
-        grad = reduce.total(i, STEP)
+    c, s, f = here()
+    n, width = dy_ref.shape
+    fw = w.shape[1] // 3
+    x, y, sib = partners()
+    loads = []
+    w_load = pltpu.make_async_copy(w_ref, w, l0.at[8])
+    w_load.start()
+    for i, k in enumerate((3, 1, 2, 0)):
+        chip = flip(s, k) if k else s
+        pair = []
+        for half, core in enumerate((1 - c, c)):
+            src = pl.ds(pl.multiple_of((core * 4 + chip) * n, n), n)
+            dst = pl.ds((2 * i + half) * n, n)
+            pair.append(pltpu.make_async_copy(nm_ref.at[src], nm.at[dst], l0.at[2 * i + half]))
+            pair.append(pltpu.make_async_copy(dy_all_ref.at[src], dy.at[dst], l1.at[2 * i + half]))
+        for made in pair:
+            made.start()
+        loads.append(pair)
+    greet(partners() + [
+        (c, s, lax.rem(f + 1, depth)), (c, s, lax.rem(f + depth - 1, depth))
+    ])
+    left, right = pl.ds(0, width // 2), pl.ds(width // 2, width // 2)
+
+    def send(src, dst, k, device):
+        return REMOTE(src, dst, s0.at[k], r0.at[k], device, MESH)
+
+    def to_sibling(i):
+        return send(out.at[lax.rem(i, 2)], near.at[i], i, sib)
+
+    fx = send(own.at[0, :, left], far.at[1], 4, x)
+    fy = send(own.at[0, :, right], far.at[3], 5, y)
+    nx = send(own.at[1, :, left], far.at[0], 6, x)
+    ny = send(own.at[2, :, right], far.at[2], 7, y)
+    by = send(own.at[2, :, left], last.at[0], 8, y)
+    bx = send(own.at[1, :, right], last.at[1], 9, x)
+    w_load.wait()
+
+    def one_pair(i, unused):
+        rows = rows_of(i, 2 * n)
+        for at, pair in enumerate(loads):
+
+            @pl.when(i == at)
+            def _(pair=pair):
+                for made in pair:
+                    made.wait()
+
+        for t in range(fw // FFN_TILE):
+            cols = pl.ds(t * FFN_TILE, FFN_TILE)
+            ups = pl.ds(fw + t * FFN_TILE, FFN_TILE)
+            downs = pl.ds(2 * fw + t * FFN_TILE, FFN_TILE)
+            gate_lin = dot(nm[rows, :], w[:, cols], 1, 0)
+            up_lin = dot(nm[rows, :], w[:, ups], 1, 0)
+            grad_hidden = dot(dy[rows, :], w[:, downs], 1, 0)
+            sig = jax.nn.sigmoid(gate_lin)
+            active = gate_lin * sig
+            grads[rows, downs] = (active * up_lin).astype(BF)
+            grads[rows, cols] = (
+                grad_hidden * up_lin * sig * (1.0 + gate_lin * (1.0 - sig))
+            ).astype(BF)
+            grads[rows, ups] = (grad_hidden * active).astype(BF)
+
+        @pl.when(i >= 1)
+        def _():
+            to_sibling(i - 1).wait_recv()
+
+            def body(j, carry):
+                r = rows_of(j, 32)
+                total = own[i - 1, r, :].astype(F32) + near[i - 1, r, :].astype(F32)
+                own[i - 1, r, :] = total.astype(BF)
+                return carry
+
+            lax.fori_loop(0, n // 32, body, 0)
+
+        @pl.when(i == 1)
+        def _():
+            fx.start()
+            fy.start()
+
+        pl.when(i == 2)(nx.start)
+        pl.when(i == 3)(ny.start)
+
+        @pl.when(i >= 2)
+        def _():
+            to_sibling(i - 2).wait_send()
+
+        for t in range(width // FFN_TILE):
+            feats = pl.ds(t * FFN_TILE, FFN_TILE)
+            part = dot(grads[rows, 0 : 2 * fw], w[feats, 0 : 2 * fw], 1, 1).astype(BF)
+            out[lax.rem(i, 2), :, feats] = part[:n]
+            own[i, :, feats] = part[n:]
+        to_sibling(i).start()
+        return unused
+
+    lax.fori_loop(0, 4, one_pair, 0)
+    fx.wait_recv()
+
+    def add(at, cols, slot):
+        def body(j, carry):
+            r = rows_of(j, 32)
+            total = own[at, r, cols].astype(F32) + far[slot, r, :].astype(F32)
+            own[at, r, cols] = total.astype(BF)
+            return carry
+
+        lax.fori_loop(0, n // 32, body, 0)
+
+    add(2, left, 1)
+    by.start()
+    fy.wait_recv()
+    add(1, right, 3)
+    bx.start()
+
+    line = LineSum(term, got, s2, r2, depth)
+    deep = width // TERM_PIECES
+    per = term.shape[0] // TERM_PIECES
+    for i in range(TERM_PIECES):
+        feats = pl.ds(i * deep, deep)
+        tile = dot(nm[:, feats], grads[:, 0 : 2 * fw], 0, 0).astype(BF)
+        term[i * per : (i + 1) * per] = tile.reshape((per,) + term.shape[1:])
+        line.start_piece(i)
+    for i in range(TERM_PIECES):
+        feats = pl.ds(i * deep, deep)
+        tile = dot(dy[:, feats], grads[:, 2 * fw :], 0, 0).astype(BF)
+        tile = tile.reshape((per, depth, term.shape[2], fw))
+        for g in range(depth):
+            low_term_ref[g, i * per : (i + 1) * per] = tile[:, g]
+
+    to_sibling(3).wait_recv()
+    for made in (nx, ny, by, bx):
+        made.wait_recv()
+
+    def total_of(j, step):
+        r = rows_of(j, step)
+        total = own[3, r, :].astype(F32) + near[3, r, :].astype(F32)
+        a = jnp.concatenate([far[0, r, :], far[2, r, :]], axis=1).astype(F32)
+        b = jnp.concatenate([last[0, r, :], last[1, r, :]], axis=1).astype(F32)
+        return total + a + b
+
+    def body(j, carry):
+        r = rows_of(j, STEP)
+        grad = total_of(j, STEP)
         mid = mid_ref[r, :]
         inverse = mean_square_inverse(mid)
         weighted = grad * gain_ref[...]
@@ -879,48 +1125,103 @@
         mine[r, :] = grad_mid.astype(BF)
         return carry + jnp.sum(grad * mid * inverse, axis=0, keepdims=True)
 
-    n, w = mine.shape
-    gain_term_ref[...] = lax.fori_loop(0, n // STEP, body, jnp.zeros((1, w), F32))
+    gain_term_ref[...] = lax.fori_loop(0, n // STEP, body, jnp.zeros((1, width), F32))
     gather = Gather(mine, branch_ref, s1, r1)
     gather.start()
-    keep = pltpu.make_async_copy(mine, gather.block(0), l0.at[0])
+    keep = pltpu.make_async_copy(mine, gather.block(0), l1.at[8])
     keep.start()
-    reduce.finish()
+    line.pass_on(0)
+
+    def down_part(i):
+        chip = flip(s, (3, 1, 2, 0)[i]) if i < 3 else s
+        made = []
+        for half, core in enumerate((1 - c, c)):
+            rows = pl.ds((2 * i + half) * n, n)
+            for t in range(width // FFN_TILE):
+                feats = pl.ds(t * FFN_TILE, FFN_TILE)
+                part = dot(grads[rows, 2 * fw :], w[feats, 2 * fw :], 1, 1)
+                stage[half, :, feats] = part.astype(BF)
+            dst = pl.ds(pl.multiple_of((core * 4 + chip) * n, n), n)
+            made.append(
+                pltpu.make_async_copy(stage.at[half], down_part_ref.at[dst], l0.at[half])
+            )
+            made[-1].start()
+        return made
+
+    moved = []
+    for i in range(4):
+        for made in moved:
+            made.wait()
+        moved = down_part(i)
+        if i == 1:
+            line.pass_on(1)
     gather.relay()
+    line.pass_on(2)
     gather.finish()
+    for made in moved:
+        made.wait()
+    line.pass_on(3)
+    line.collect(gu_rows_ref)
     keep.wait()
-
-
-def turn(part, cotangent, mid, gain):
-    n, w = mid.shape
+    for made in (fx, fy, nx, ny, by, bx):
+        made.wait_send()
+    for i in (2, 3):
+        to_sibling(i).wait_send()
+    line.finish()
+
+
+def ffn(normed_all, cotangent_all, weights, cotangent, mid, gain, depth):
+    n, width = mid.shape
+    fw = weights.shape[1] // 3
+    r = width // (8 * depth)
     dma = pltpu.SemaphoreType.DMA((16,))
+    line = pltpu.SemaphoreType.DMA((2, depth, TERM_PIECES))
     vmem = pl.BlockSpec(memory_space=pltpu.VMEM)
+    anywhere = pl.BlockSpec(memory_space=pl.ANY)
     return pl.pallas_call(
-        turn_kernel,
-        name="turn",
+        functools.partial(ffn_kernel, depth=depth),
+        name="ffn",
         out_shape=(
-            jax.ShapeDtypeStruct((n, w), F32),
-            jax.ShapeDtypeStruct((1, w), F32),
-            jax.ShapeDtypeStruct((8 * n, w), BF),
-        ),
-        in_specs=[vmem] * 4,
-        out_specs=[vmem, vmem, pl.BlockSpec(memory_space=pl.ANY)],
-        scratch_shapes=Reduce.scratch(n, w)
-        + [pltpu.VMEM((n, w), BF), dma, dma, dma, dma, pltpu.SemaphoreType.DMA((2,))],
+            jax.ShapeDtypeStruct((n, width), F32),
+            jax.ShapeDtypeStruct((1, width), F32),
+            jax.ShapeDtypeStruct((8 * n, width), BF),
+            jax.ShapeDtypeStruct((8 * n, width), BF),
+            jax.ShapeDtypeStruct((8, r, 2 * fw), BF),
+            jax.ShapeDtypeStruct((depth, 8, r, fw), BF),
+        ),
+        in_specs=[anywhere] * 3 + [vmem] * 3,
+        out_specs=[vmem, vmem, anywhere, anywhere, vmem, vmem],
+        scratch_shapes=[
+            pltpu.VMEM((8 * n, width), BF),
+            pltpu.VMEM((8 * n, width), BF),
+            pltpu.VMEM((width, 3 * fw), BF),
+            pltpu.VMEM((8 * n, 3 * fw), BF),
+            pltpu.VMEM((4, n, width), BF),
+            pltpu.VMEM((4, n, width), BF),
+            pltpu.VMEM((2, n, width), BF),
+            pltpu.VMEM((4, n, width // 2), BF),
+            pltpu.VMEM((2, n, width // 2), BF),
+            pltpu.VMEM((8, depth, r, 2 * fw), BF),
+            pltpu.VMEM((2, depth, 8, r, 2 * fw), BF),
+            pltpu.VMEM((n, width), BF),
+            pltpu.VMEM((2, n, width), BF),
+            dma, dma, dma, dma, dma, dma, line, line,
+        ],
         compiler_params=pltpu.CompilerParams(
-            collective_id=3, has_side_effects=True, vmem_limit_bytes=VMEM_BYTES
+            collective_id=3, has_side_effects=True, vmem_limit_bytes=63 * 1024 * 1024
         ),
         cost_estimate=pl.CostEstimate(
-            flops=50_000_000, bytes_accessed=4 * 8 * n * w * 2, transcendentals=0
-        ),
-    )(part, cotangent, mid, gain[None])
+            flops=2 * 8 * n * width * fw * 9, bytes_accessed=4 * 8 * n * width * 2,
+            transcendentals=0,
+        ),
+    )(normed_all, cotangent_all, weights, cotangent, mid, gain[None])
 
 
 def leave_kernel(
-    part_ref, down_ref, tok_ref, grad_mid_ref, mid_ref, gain_ref, small_ref,
-    grad_ref, small_sum_ref, out_ref,
-    near, sums, far, last, near2, sums2, far2, last2, small, plane_small, line_small,
-    s0, r0, s1, r1, s2, r2, *, depth,
+    part_ref, down_ref, tok_ref, grad_mid_ref, mid_ref, gain_ref, small_ref, term_ref, mlp_ref, low_ref,
+    grad_ref, small_sum_ref, out_ref, attn_rows_ref, mlp_rows_ref, low_rows_ref,
+    near, sums, far, last, near2, sums2, far2, last2, small, plane_small, line_small, got, rows,
+    s0, r0, s1, r1, s2, r2, s3, r3, s4, r4, s5, r5, s6, r6, *, depth,
 ):
     c, s, f = here()
     plane_peers = [
@@ -931,12 +1232,21 @@
     ]
     line_peers = [(c, s, lax.rem(f + k, depth), k) for k in range(1, depth)]
     greet([p[:3] for p in plane_peers + line_peers])
+    line = LineSum(term_ref, got, s3, r3, depth)
+    line.start()
     reduce = Reduce(part_ref, (near, sums, far, last), s0, r0)
     other = Reduce(down_ref, (near2, sums2, far2, last2), s1, r1)
+    mlp_rows = Exchange(mlp_ref, mlp_rows_ref, s4, r4, plane_peers)
+    low_rows = Exchange(low_ref, low_rows_ref, s6, r6, plane_peers)
     reduce.start()
     other.start()
-    reduce.run()
-    other.run()
+    reduce.first()
+    mlp_rows.start()
+    low_rows.start()
+    reduce.second()
+    line.pass_on(0)
+    other.first()
+    line.pass_on(1)
     reduce.arrive()
 
     def body(i, carry):
@@ -963,14 +1273,9 @@
         )
         made.start()
         sent.append(made)
-    other.arrive()
-
-    def body2(i, carry):
-        r = rows_of(i, STEP)
-        out_ref[r, :] = (mid_ref[r, :] + other.total(i, STEP)).astype(BF)
-        return carry
-
-    lax.fori_loop(0, n // STEP, body2, 0)
+    line.pass_on(2)
+    other.second()
+    line.pass_on(3)
     for made in sent:
         made.wait()
     total = plane_small[0]
@@ -985,20 +1290,38 @@
         )
         made.start()
         sent.append(made)
-    reduce.finish()
-    other.finish()
+    other.arrive()
+
+    def body2(i, carry):
+        r = rows_of(i, STEP)
+        out_ref[r, :] = (mid_ref[r, :] + other.total(i, STEP)).astype(BF)
+        return carry
+
+    lax.fori_loop(0, n // STEP, body2, 0)
+    line.collect(rows)
+    attn_rows = Exchange(rows, attn_rows_ref, s5, r5, plane_peers)
+    attn_rows.start()
     for made in sent:
         made.wait()
     total = line_small[0]
     for i in range(1, depth):
         total = total + line_small[i]
     small_sum_ref[...] = total
-
-
-def leave(part, down_part, tokens, grad_mid, mid, gain, small, depth):
+    reduce.finish()
+    other.finish()
+    line.finish()
+    mlp_rows.finish()
+    low_rows.finish()
+    attn_rows.finish()
+
+
+def leave(part, down_part, tokens, grad_mid, mid, gain, small, term, mlp_rows, low_rows, depth):
     n, w = mid.shape
     sems = pltpu.SemaphoreType.DMA((6 + depth,))
+    plane, _, r, cols = term.shape
     dma = pltpu.SemaphoreType.DMA((16,))
+    eight = pltpu.SemaphoreType.DMA((8,))
+    line = pltpu.SemaphoreType.DMA((2, depth, TERM_PIECES))
     vmem = pl.BlockSpec(memory_space=pltpu.VMEM)
     return pl.pallas_call(
         functools.partial(leave_kernel, depth=depth),
@@ -1007,16 +1330,22 @@
             jax.ShapeDtypeStruct((n, w), F32),
             jax.ShapeDtypeStruct((8, w), F32),
             jax.ShapeDtypeStruct((n, w), BF),
-        ),
-        in_specs=[vmem] * 7,
-        out_specs=[vmem] * 3,
+            jax.ShapeDtypeStruct((plane, r, cols), BF),
+            jax.ShapeDtypeStruct(mlp_rows.shape, BF),
+            jax.ShapeDtypeStruct(low_rows.shape, BF),
+        ),
+        in_specs=[vmem] * 10,
+        out_specs=[vmem] * 6,
         scratch_shapes=Reduce.scratch(n, w)
         + Reduce.scratch(n, w)
         + [
             pltpu.VMEM((8, w), F32),
             pltpu.VMEM((8, 8, w), F32),
             pltpu.VMEM((depth, 8, w), F32),
-            dma, dma, dma, dma, sems, sems,
+            pltpu.VMEM((2, depth, plane, r, cols), BF),
+            pltpu.VMEM((plane, r, cols), BF),
+            dma, dma, dma, dma, sems, sems, line, line,
+            eight, eight, eight, eight, eight, eight,
         ],
         compiler_params=pltpu.CompilerParams(
             collective_id=4, has_side_effects=True, vmem_limit_bytes=VMEM_BYTES
@@ -1024,7 +1353,64 @@
         cost_estimate=pl.CostEstimate(
             flops=50_000_000, bytes_accessed=4 * 8 * n * w * 2, transcendentals=0
         ),
-    )(part, down_part, tokens, grad_mid, mid, gain[None], small)
+    )(part, down_part, tokens, grad_mid, mid, gain[None], small, term, mlp_rows, low_rows)
+
+
+def finish_kernel(
+    attn_ref, mlp_ref, low_ref, small_ref, out_w_ref, block_ref, tok_grad_ref,
+    q_ref, k_ref, v_ref, g_ref, f_ref, o_ref, gate_ref, up_ref, down_ref,
+    gain1_ref, gain2_ref, bias_ref, out_ref, tokens_ref, *, hw, heads,
+):
+    plane = attn_ref.shape[0]
+    fw = low_ref.shape[2]
+    for i, ref in enumerate((q_ref, k_ref, v_ref, g_ref)):
+        ref[...] = jnp.concatenate(
+            [attn_ref[t, :, i * hw : (i + 1) * hw].astype(F32) for t in range(plane)], axis=1
+        )
+    a = lax.broadcasted_iota(jnp.int32, (128, 128), 0)
+    b = lax.broadcasted_iota(jnp.int32, (128, 128), 1)
+    total = jnp.zeros((attn_ref.shape[1], 128), F32)
+    for t in range(plane):
+        pick = jnp.where((a + t * heads == b) & (a < heads), 1.0, 0.0).astype(BF)
+        total = total + dot(attn_ref[t, :, 4 * hw : 4 * hw + 128], pick, 1, 0)
+    f_ref[...] = total[:, : f_ref.shape[1]]
+    o_ref[...] = out_w_ref[...].astype(F32)
+    for i, ref in enumerate((gate_ref, up_ref)):
+        for t in range(plane):
+            ref[:, t * fw : (t + 1) * fw] = mlp_ref[t, :, i * fw : (i + 1) * fw].astype(F32)
+    for t in range(plane):
+        down_ref[:, t * fw : (t + 1) * fw] = low_ref[t].astype(F32)
+    gain1_ref[...] = small_ref[0:1, :]
+    gain2_ref[...] = small_ref[1:2, :]
+    bias_ref[...] = small_ref[2:3, 0 : bias_ref.shape[1]]
+    out_ref[...] = block_ref[...]
+    tokens_ref[...] = tok_grad_ref[...]
+
+
+def finish(attn_rows, mlp_rows, low_rows, small, out_w, block_out, tokens_grad, hw, heads):
+    plane, r, _ = attn_rows.shape
+    n, w = tokens_grad.shape
+    fw = low_rows.shape[2]
+    vmem = pl.BlockSpec(memory_space=pltpu.VMEM)
+    square = jax.ShapeDtypeStruct((r, plane * hw), F32)
+    wide = jax.ShapeDtypeStruct((r, plane * fw), F32)
+    row = jax.ShapeDtypeStruct((1, w), F32)
+    return pl.pallas_call(
+        functools.partial(finish_kernel, hw=hw, heads=heads),
+        name="finish",
+        out_shape=(
+            square, square, square, square,
+            jax.ShapeDtypeStruct((r, plane * heads), F32),
+            jax.ShapeDtypeStruct(out_w.shape, F32),
+            wide, wide, wide, row, row,
+            jax.ShapeDtypeStruct((1, plane * heads), F32),
+            jax.ShapeDtypeStruct((n, w), BF),
+            jax.ShapeDtypeStruct((n, w), F32),
+        ),
+        in_specs=[vmem] * 7,
+        out_specs=[vmem] * 14,
+        compiler_params=pltpu.CompilerParams(vmem_limit_bytes=VMEM_BYTES),
+    )(attn_rows, mlp_rows, low_rows, small, out_w, block_out, tokens_grad)
 
 
 BQ = 256
@@ -1317,12 +1703,6 @@
     )(place, ends, cat, bias, gg, att, exact, lse, prefix)
 
 
-def spread_rows(grad, plane, depth):
-    rows, cols = grad.shape
-    part = rows // (plane * depth)
-    return grad.reshape(plane, depth, part, cols).transpose(1, 0, 2, 3).reshape(rows, cols)
-
-
 def local_plane(
     tokens, out_cotangent, seq_lengths, slab_place, attn_gain, query_weight, key_weight,
     value_weight, outgate_weight, forget_weight, forget_bias, output_weight, mlp_gain,
@@ -1372,34 +1752,12 @@
     mid_part = dot(gated, w_out, 0, 0).astype(BF)
     mid, normed_mlp = middle(mid_part, inputs, mlp_gain)
 
-    w_gate, w_up, w_down = w_mlp[:, :fw], w_mlp[:, fw : 2 * fw], w_mlp[:, 2 * fw :]
-    gate_lin = matmul(normed_mlp, w_gate)
-    up_lin = matmul(normed_mlp, w_up)
-    gate_sig = jax.nn.sigmoid(gate_lin)
-    activated = gate_lin * gate_sig
-    hidden = (activated * up_lin).astype(BF)
-    grad_hidden = matmul(cotangent_all, w_down)
-    grad_gate_lin = (grad_hidden * up_lin * gate_sig * (1.0 + gate_lin * (1.0 - gate_sig))).astype(
-        BF
-    )
-    grad_up_lin = (grad_hidden * activated).astype(BF)
-    mlp_part = (
-        matmul_right_t(grad_gate_lin, w_gate) + matmul_right_t(grad_up_lin, w_up)
-    ).astype(BF)
-    down_part = matmul_right_t(hidden, w_down).astype(BF)
-    mlp_terms = jnp.concatenate(
-        [
-            matmul_left_t(normed_mlp, grad_gate_lin).astype(BF),
-            matmul_left_t(normed_mlp, grad_up_lin).astype(BF),
-            matmul_left_t(cotangent_all, hidden).astype(BF),
-        ],
-        axis=1,
-    )
-    mlp_part, mlp_spread = lax.optimization_barrier(
-        (mlp_part, spread_rows(mlp_terms, plane, depth))
-    )
-    grad_mid, mlp_gain_term, branch = turn(mlp_part, cotangent, mid, mlp_gain)
-    mlp_grad = lax.psum_scatter(mlp_spread, "fsdp", scatter_dimension=0, tiled=True)
+    grad_mid, mlp_gain_term, branch, down_part, mlp_rows, low_term = ffn(
+        normed_mlp, cotangent_all, w_mlp, cotangent, mid, mlp_gain, depth
+    )
+    low_grad = lax.psum_scatter(
+        low_term.reshape(width, fw), "fsdp", scatter_dimension=0, tiled=True
+    )
 
     grad_gated = dot(w_out, branch, 1, 1)
     grad_cat, bias_grad = attention_back(
@@ -1407,13 +1765,8 @@
     )
     out_term = dot(gated, branch, 1, 0).astype(BF)
     attn_term = dot(normed, grad_cat, 0, 1).astype(BF)
-    grad_cat, attn_spread = lax.optimization_barrier(
-        (grad_cat, spread_rows(attn_term, plane, depth))
-    )
-    out_term, mlp_grad = lax.optimization_barrier((out_term, mlp_grad))
+    out_term, low_grad = lax.optimization_barrier((out_term, low_grad))
     output_weight_grad = lax.psum_scatter(out_term, "fsdp", scatter_dimension=0, tiled=True)
-    attn_spread, output_weight_grad = lax.optimization_barrier((attn_spread, output_weight_grad))
-    attn_grad = lax.psum_scatter(attn_spread, "fsdp", scatter_dimension=0, tiled=True)
     attn_part = dot(grad_cat, w_attn, 0, 1).astype(BF)
     bias_row = lax.dynamic_update_slice_in_dim(
         jnp.zeros((width,), F32), bias_grad[:heads, 0], place * heads, 0
@@ -1421,44 +1774,30 @@
     small = jnp.concatenate(
         [jnp.zeros((1, width), F32), mlp_gain_term, bias_row[None], jnp.zeros((5, width), F32)]
     )
-    tokens_grad, small_sum, block_out = leave(
-        attn_part, down_part, inputs, grad_mid, mid, attn_gain, small, depth
-    )
-    attn_grad, tokens_grad = lax.optimization_barrier((attn_grad, tokens_grad))
-
-    def to_rows(grad):
-        part = grad.shape[0] // plane
-        got = lax.all_to_all(
-            grad.reshape(plane, part, -1), plane_axes, split_axis=0, concat_axis=0, tiled=True
-        )
-        return got.astype(F32)
-
-    mlp_rows = to_rows(mlp_grad)
-    attn_rows = to_rows(attn_grad)
-
-    def pick(rows, begin, count):
-        part = rows[:, :, begin : begin + count].transpose(1, 0, 2)
-        return part.reshape(part.shape[0], -1)
-
-    gate_grad, up_grad, down_grad = (pick(mlp_rows, i * fw, fw) for i in range(3))
-    query_grad, key_grad, value_grad, outgate_grad = (
-        pick(attn_rows, i * hw, hw) for i in range(4)
-    )
-    forget_grad = pick(attn_rows, 4 * hw, heads)
-    attn_gain_grad, mlp_gain_grad = small_sum[0], small_sum[1]
-    forget_bias_grad = small_sum[2, :head_count]
+    part = width // (plane * depth)
+    tokens_grad, small_sum, block_out, attn_rows, mlp_rows, low_rows = leave(
+        attn_part, down_part, inputs, grad_mid, mid, attn_gain, small,
+        attn_term.reshape(plane, depth, part, -1), mlp_rows, low_grad.reshape(plane, part, -1), depth,
+    )
+    (
+        query_grad, key_grad, value_grad, outgate_grad, forget_grad, out_grad, gate_grad, up_grad,
+        down_grad, attn_gain_grad, mlp_gain_grad, forget_bias_grad, block_out, tokens_grad,
+    ) = finish(
+        attn_rows, mlp_rows, low_rows, small_sum, output_weight_grad, block_out, tokens_grad,
+        hw, heads,
+    )
     return (
         block_out[None],
         tokens_grad[None],
-        attn_gain_grad,
+        attn_gain_grad[0],
         query_grad,
         key_grad,
         value_grad,
         outgate_grad,
         forget_grad,
-        forget_bias_grad,
-        output_weight_grad.astype(F32),
-        mlp_gain_grad,
+        forget_bias_grad[0],
+        out_grad,
+        mlp_gain_grad[0],
         gate_grad,
         up_grad,
         down_grad,

time: 530 us -> 483 us (0.911)
  Pallas kernels: 332 us -> 397 us
  matrix products: 94.6 us -> 49.9 us
  local copies, waits for them, and re-layouts: 46.5 us -> 10.4 us
  waiting for transfers between devices: 20.7 us -> 0.09 us
  starting transfers between devices: 8.55 us -> 0.47 us
    dot_general x9 -> x0, matrix products: 48.6 us -> none  [the longest x3 20.2 us: matmul_right_t(): lax.dot_general(left, right, (((1,), (1,)), ((), ())), preferred_element_...]
    pallas_call x1 -> x2, Pallas kernels: 66.7 us -> 108 us  [the longest x1 102 us: ffn(): pl.pallas_call(functools.partial(ffn_kernel, depth=depth), name='ffn', ou...]
    pallas_call x1, Pallas kernels: 76.7 us -> 94.5 us  [leave(): pl.pallas_call(functools.partial(leave_kernel, depth=depth), name='leave'...]
    reduce_scatter x1, waiting for transfers between devices: 17.7 us -> 0.02 us  [local_plane(): lax.psum_scatter(out_term, 'fsdp', scatter_dimension=0, tiled=True)]
    transpose x8 -> x0, local copies, waits for them, and re-layouts: 11.4 us -> none  [the longest x7 6.27 us: pick(): part = rows[:, :, begin:begin + count].transpose(1, 0, 2)]
    reshape x9 -> x0, local copies, waits for them, and re-layouts: 10.6 us -> none  [the longest x8 8.88 us: pick(): return part.reshape(part.shape[0], -1)]
    all_to_all x2 -> x0, starting transfers between devices: 8.17 us -> none  [to_rows(): lax.all_to_all(grad.reshape(plane, part, -1), plane_axes, split_axis=0, c...]
    concatenate x1 -> x0, local copies, waits for them, and re-layouts: 7.1 us -> none  [local_plane(): jnp.concatenate([matmul_left_t(normed_mlp, grad_gate_lin).astype(BF), mat...]
  transfers between devices with their start and end apart: 6 -> 3, of which waited for: 2 -> 0; matrix products, arithmetic and copies ran while one was open for 13% -> 9% of each run, Pallas kernels for 51% -> 47%
where the time goes in v3:
time: 483 us; the launch traced here: 479 us
  Pallas kernels  397 us (82%)
  matrix products  49.9 us (10%)
  between operations  14.2 us (3%)
  local copies, waits for them, and re-layouts  10.4 us (2%)
  other arithmetic  6.8 us (1%)
    pallas_call x1, Pallas kernels, ffn(): pl.pallas_call(functools.partial(ffn_kernel, depth=depth), name='ffn', ou...  102 us
    pallas_call x1, Pallas kernels, leave(): pl.pallas_call(functools.partial(leave_kernel, depth=depth), name='leave'...  94.5 us
    pallas_call x1, Pallas kernels, middle(): pl.pallas_call(middle_kernel, name='middle', out_shape=(jax.ShapeDtypeStr...  69.7 us
    pallas_call x1, Pallas kernels, enter(): pl.pallas_call(functools.partial(enter_kernel, depth=depth), name='enter'...  65.2 us
    dot_general x6, matrix products, dot(): lax.dot_general(a, b, (((ca,), (cb,)), ((), ())), preferred_element_type=...  49.9 us
    pallas_call x1, Pallas kernels, attention_back(): pl.pallas_call(functools.partial(attention_back_kernel, heads=heads, hd=h...  32.7 us
    pallas_call x1, Pallas kernels, attention(): pl.pallas_call(functools.partial(attention_kernel, heads=heads, hd=hd, sl...  27 us
  transfers between devices with their start and end apart: 3, of which 0 were waited for; matrix products, arithmetic and copies ran while one was open for 9% of the time, Pallas kernels for 47%

profile of v3, /device:TPU:0, one launch (start us, length us, event | category | flops | bytes accessed | tf_op | source)
XLA Modules:
  0.0 478.5 jit_solution(12712192618641090700)
XLA Ops:
  7.2 1.3 broadcast_in_dim.46.gain_ref
  8.5 1.2 constant_dynamic-slice_fusion
  9.8 1.2 constant_dynamic-slice_fusion.2
  11.7 1.0 constant_dynamic-slice_fusion.6
  12.7 1.2 constant_dynamic-slice_fusion.4
  13.9 1.1 pad_maximum_fusion
  15.0 1.1 pad_maximum_fusion.1.attn_ref
  16.1 65.2 %enter.1 = (bf16[2048,1536]{1,0:T(8,128)(2,1)}, bf16[2048,1536]{1,0:T(8,128)(2,1)}, bf16[1536,896]{1,0:T(8,128)(2,1)}, bf16[192,1536]{1,0:T(8,128)(2,1)}) custom-call(bf16[256,1536]{1,0:T(8,128)(2,1)} %bitcast.26, bf16[256,1536]{1,0:T(8,128)(2,1)} %bitcast.31, f32[1,1536]{1,0:T(1,128)} %broadcast_in_dim.46.gain_ref, ...), custom_call_target="tpu_custom_call" | custom-call | flops 50000000 | bytes 25165824 | tf_op jit(solution)/shard_map/enter/pallas_call | solution.py:791
  83.6 10.7 %fusion.cat_ref = f32[896,2048]{1,0:T(8,128)} fusion(bf16[1536,896]{1,0:T(8,128)(2,1)} %get-tuple-element.58, bf16[2048,1536]{1,0:T(8,128)(2,1)} %get-tuple-element.59), kind=kOutput, calls=%fused_computation.18 | convolution fusion | flops 5637144576 | bytes 16384000 | tf_op jit(solution)/shard_map/dot_general | solution.py:1422
  95.0 27.0 %attention.1 = (bf16[192,2048]{1,0:T(8,128)(2,1)}, bf16[192,2048]{1,0:T(8,128)(2,1)}, f32[192,2048]{1,0:T(8,128)}, f32[8,2048]{1,0:T(8,128)}, f32[16,2048]{1,0:T(8,128)}) custom-call(s32[4]{0:T(128)} %select_reduce_fusion.place_ref, s32[8]{0:T(128)} %bitcast.40, f32[896,2048]{1,0:T(8,128)} %fusion.cat_ref, f32[16,128]{1,0:T(8,128)} %broadcast_in_dim.47.bias_ref), custom_call_target="tpu_custom_call" | custom-call | flops 6442450944 | bytes 7340032 | tf_op jit(solution)/shard_map/attention/pallas_call | solution.py:1562
  121.9 5.7 %convolution_convert_fusion.1.part_ref = bf16[2048,1536]{1,0:T(8,128)(2,1)} fusion(bf16[192,2048]{1,0:T(8,128)(2,1)} %get-tuple-element.61, bf16[192,1536]{1,0:T(8,128)(2,1)S(1)} %copy-done.2), kind=kOutput, calls=%fused_computation.1 | convolution fusion | flops 1211105280 | bytes 7667712 | tf_op jit(solution)/shard_map/dot_general | solution.py:1422
  127.6 69.7 %middle.1 = (f32[256,1536]{1,0:T(8,128)}, bf16[2048,1536]{1,0:T(8,128)(2,1)}) custom-call(bf16[2048,1536]{1,0:T(8,128)(2,1)} %convolution_convert_fusion.1.part_ref, bf16[256,1536]{1,0:T(8,128)(2,1)} %bitcast.27, f32[1,1536]{1,0:T(1,128)} %broadcast_in_dim.48.gain_ref), custom_call_target="tpu_custom_call" | custom-call | flops 50000000 | bytes 25165824 | tf_op jit(solution)/shard_map/middle/pallas_call | solution.py:851
  197.4 102.4 %ffn.1 = (f32[256,1536]{1,0:T(8,128)}, f32[1,1536]{1,0:T(1,128)}, bf16[2048,1536]{1,0:T(8,128)(2,1)}, bf16[2048,1536]{1,0:T(8,128)(2,1)}, bf16[8,48,1024]{2,1,0:T(8,128)(2,1)}, /*index=5*/bf16[4,8,48,512]{3,2,1,0:T(8,128)(2,1)}) custom-call(bf16[2048,1536]{1,0:T(8,128)(2,1)} %get-tuple-element.62.nm_ref, bf16[2048,1536]{1,0:T(8,128)(2,1)} %get-tuple-element.63.dy_all_ref, ...), custom_call_target="tpu_custom_call" | custom-call | flops 28991029248 | bytes 25165824 | tf_op jit(solution)/shard_map/ffn/pallas_call | solution.py:1181
  299.9 5.3 %convolution_convert_fusion.3 = bf16[192,1536]{1,0:T(8,128)(2,1)} fusion(bf16[192,2048]{1,0:T(8,128)(2,1)} %get-tuple-element.61, bf16[2048,1536]{1,0:T(8,128)(2,1)} %get-tuple-element.66), kind=kOutput, calls=%fused_computation.3 | convolution fusion | flops 1208254464 | bytes 7667712 | tf_op jit(solution)/shard_map/dot_general | solution.py:1422
  305.1 6.1 %fusion.1.gg_ref = f32[192,2048]{1,0:T(8,128)} fusion(bf16[192,1536]{1,0:T(8,128)(2,1)S(1)} %copy-done.2, bf16[2048,1536]{1,0:T(8,128)(2,1)} %get-tuple-element.66), kind=kOutput, calls=%fused_computation.19 | convolution fusion | flops 1207959552 | bytes 8454144 | tf_op jit(solution)/shard_map/dot_general | solution.py:1422
  311.5 32.7 %attention_back.1 = (bf16[896,2048]{1,0:T(8,128)(2,1)}, f32[16,128]{1,0:T(8,128)}) custom-call(s32[4]{0:T(128)} %select_reduce_fusion.place_ref, s32[8]{0:T(128)} %bitcast.41, f32[896,2048]{1,0:T(8,128)} %fusion.cat_ref, f32[16,128]{1,0:T(8,128)} %broadcast_in_dim.47.bias_ref, f32[192,2048]{1,0:T(8,128)} %fusion.1.gg_ref, ...), custom_call_target="tpu_custom_call" | custom-call | flops 16106127360 | bytes 14680064 | tf_op jit(solution)/shard_map/attention_back/pallas_call | solution.py:1678
  344.1 11.3 %convolution_convert_fusion.2 = bf16[1536,896]{1,0:T(8,128)(2,1)} fusion(bf16[2048,1536]{1,0:T(8,128)(2,1)} %get-tuple-element.59, bf16[896,2048]{1,0:T(8,128)(2,1)} %get-tuple-element.71), kind=kOutput, calls=%fused_computation.2 | convolution fusion | flops 5638520832 | bytes 12713984 | tf_op jit(solution)/shard_map/dot_general | solution.py:1422
  355.5 11.0 %convolution_convert_fusion.part_ref = bf16[2048,1536]{1,0:T(8,128)(2,1)} fusion(bf16[896,2048]{1,0:T(8,128)(2,1)} %get-tuple-element.71, bf16[1536,896]{1,0:T(8,128)(2,1)S(1)} %copy-done.5), kind=kOutput, calls=%fused_computation | convolution fusion | flops 5640290304 | bytes 12713984 | tf_op jit(solution)/shard_map/dot_general | solution.py:1422
  366.4 0.8 slice_reduce_fusion
  368.1 94.5 %leave.1 = (f32[256,1536]{1,0:T(8,128)}, f32[8,1536]{1,0:T(8,128)}, bf16[256,1536]{1,0:T(8,128)(2,1)}, bf16[8,48,896]{2,1,0:T(8,128)(2,1)}, bf16[8,48,1024]{2,1,0:T(8,128)(2,1)}, /*index=5*/bf16[8,48,512]{2,1,0:T(8,128)(2,1)}) custom-call(bf16[2048,1536]{1,0:T(8,128)(2,1)} %convolution_convert_fusion.part_ref, ...), custom_call_target="tpu_custom_call" | custom-call | flops 50000000 | bytes 25165824 | tf_op jit(solution)/shard_map/leave/pallas_call | solution.py:1326
  462.7 5.1 %finish.1 = (f32[48,1536]{1,0:T(8,128)}, f32[48,1536]{1,0:T(8,128)}, f32[48,1536]{1,0:T(8,128)}, f32[48,1536]{1,0:T(8,128)}, f32[48,24]{1,0:T(8,128)}, /*index=5...) custom-call(bf16[8,48,896]{2,1,0:T(8,128)(2,1)} %get-tuple-element.7, ...), custom_call_target="tpu_custom_call" | custom-call | tf_op jit(solution)/shard_map/finish/pallas_call | solution.py:1398
  467.7 1.4 copy.32
  469.2 1.3 reduce.1
  470.5 1.3 reduce.2
  (41 shorter events, 4.8 us)
Async XLA Ops:
  7.2 3.9 copy-start
  7.2 190.2 %all-gather.2.cloned.1.call-start = ((), (), s32[]{:S(2)}) async-start(), calls=%async_computation.2 | async-start | bytes 5898240 | tf_op jit(solution)/shard_map/all_gather | solution.py:1747
  15.0 66.6 %copy-start.6 = (f32[24]{0:T(128)S(1)}, f32[24]{0:T(128)}, u32[]{:S(2)}) copy-start(f32[24]{0:T(128)} %param.26) | copy-start | bytes 292
  15.0 66.7 %copy-start.7 = (s32[1,8]{1,0:T(1,128)S(1)}, s32[1,8]{1,0:T(1,128)}, u32[]{:S(2)}) copy-start(s32[1,8]{1,0:T(1,128)} %param.18) | copy-start | bytes 100
  15.0 67.4 %copy-start.3 = (f32[1536]{0:T(1024)S(1)}, f32[1536]{0:T(1024)}, u32[]{:S(2)}) copy-start(f32[1536]{0:T(1024)} %param.28) | copy-start | bytes 18436
  15.0 68.0 %copy-start.8 = (s32[1,4]{1,0:T(1,128)S(1)}, s32[1,4]{1,0:T(1,128)}, u32[]{:S(2)}) copy-start(s32[1,4]{1,0:T(1,128)} %param.19) | copy-start | bytes 52
  81.3 274.1 %reduce-scatter.3.cloned.1.call-start = ((), (), s32[]{:S(2)}) async-start(), calls=%async_computation.3 | async-start | bytes 1966080 | tf_op jit(solution)/shard_map/reduce_scatter | solution.py:1758
  95.0 27.0 %copy-start.2 = (bf16[192,1536]{1,0:T(8,128)(2,1)S(1)}, bf16[192,1536]{1,0:T(8,128)(2,1)}, u32[]{:S(2)}) copy-start(bf16[192,1536]{1,0:T(8,128)(2,1)} %get-tuple-element.60) | copy-start | bytes 1769476
  311.3 151.4 %reduce-scatter.5.cloned.1.call-start = ((), (), s32[]{:S(2)}) async-start(), calls=%async_computation.4 | async-start | bytes 737280 | tf_op jit(solution)/shard_map/reduce_scatter | solution.py:1769
  344.1 11.3 %copy-start.5 = (bf16[1536,896]{1,0:T(8,128)(2,1)S(1)}, bf16[1536,896]{1,0:T(8,128)(2,1)}, u32[]{:S(2)}) copy-start(bf16[1536,896]{1,0:T(8,128)(2,1)} %get-tuple-element.58) | copy-start | bytes 8257540
  355.5 12.0 %copy-start.4 = (f32[1,1536]{1,0:T(1,128)S(1)}, f32[1,1536]{1,0:T(1,128)}, u32[]{:S(2)}) copy-start(f32[1,1536]{1,0:T(1,128)} %get-tuple-element.74) | copy-start | bytes 18436
  368.1 103.7 %copy-start.1 = (bf16[384,24]{0,1:T(8,128)(2,1)S(1)}, bf16[384,24]{0,1:T(8,128)(2,1)}, u32[]{:S(2)}) copy-start(bf16[384,24]{0,1:T(8,128)(2,1)} %param.25) | copy-start | bytes 55300
Sparse Core Ops, SparseCore 0:
  81.4 94.5 all-gather.1
  311.4 33.4 reduce-scatter.2
  355.6 20.0 reduce-scatter.4

commit v4 on v3

--- a/solution.py
+++ b/solution.py
@@ -471,107 +471,135 @@
             made.wait_send()
 
 
-class Reduce:
-    sems = 10
+class PairSum:
+    order = (3, 1, 2, 0)
 
     @staticmethod
     def scratch(n, w):
         return [
             pltpu.VMEM((4, n, w), BF),
             pltpu.VMEM((4, n, w), BF),
+            pltpu.VMEM((2, n, w), BF),
             pltpu.VMEM((4, n, w // 2), BF),
             pltpu.VMEM((2, n, w // 2), BF),
+            pltpu.SemaphoreType.DMA((10,)),
+            pltpu.SemaphoreType.DMA((10,)),
         ]
 
-    def __init__(self, part, refs, send, recv):
-        c, s, f = here()
-        self.part, self.send, self.recv = part, send, recv
-        self.near, self.sums, self.far, self.last = refs
-        self.c, self.s = c, s
-        self.n, self.w = self.sums.shape[1], self.sums.shape[2]
-        self.x, self.y, self.sib = (c, flip(s, 1), f), (c, flip(s, 2), f), (1 - c, s, f)
-        self.made = []
+    @staticmethod
+    def tail_scratch(n, w):
+        full = PairSum.scratch(n, w)
+        return full[:1] + full[3:]
+
+    def __init__(self, refs):
+        if len(refs) == 5:
+            refs = (refs[0], None, None) + tuple(refs[1:])
+        self.own, self.near, self.out, self.far, self.last, self.send, self.recv = refs
+        self.x, self.y, self.sib = partners()
+        self.n, w = self.own.shape[1], self.own.shape[2]
+        self.left, self.right = pl.ds(0, w // 2), pl.ds(w // 2, w // 2)
+        self.fx = self.copy(self.own.at[0, :, self.left], self.far.at[1], 4, self.x)
+        self.fy = self.copy(self.own.at[0, :, self.right], self.far.at[3], 5, self.y)
+        self.nx = self.copy(self.own.at[1, :, self.left], self.far.at[0], 6, self.x)
+        self.ny = self.copy(self.own.at[2, :, self.right], self.far.at[2], 7, self.y)
+        self.by = self.copy(self.own.at[2, :, self.left], self.last.at[0], 8, self.y)
+        self.bx = self.copy(self.own.at[1, :, self.right], self.last.at[1], 9, self.x)
+
+    @staticmethod
+    def blocks(c, s):
+        return [
+            core * 4 + (flip(s, k) if k else s) for k in PairSum.order for core in (1 - c, c)
+        ]
 
     def copy(self, src, dst, k, device):
-        made = REMOTE(src, dst, self.send.at[k], self.recv.at[k], device, MESH)
-        made.start()
-        self.made.append(made)
-        return made
-
-    def own(self, k, core):
-        index = core * 4 + (self.s if k == 0 else flip(self.s, k))
-        return index * self.n
+        return REMOTE(src, dst, self.send.at[k], self.recv.at[k], device, MESH)
+
+    def to_sibling(self, i):
+        return self.copy(self.out.at[lax.rem(i, 2)], self.near.at[i], i, self.sib)
+
+    def combine(self, i):
+        self.to_sibling(i).wait_recv()
+
+        def body(j, carry):
+            r = rows_of(j, 32)
+            total = self.own[i, r, :].astype(F32) + self.near[i, r, :].astype(F32)
+            self.own[i, r, :] = total.astype(BF)
+            return carry
+
+        lax.fori_loop(0, self.n // 32, body, 0)
+
+    def between(self, i):
+        @pl.when(i >= 1)
+        def _():
+            self.combine(i - 1)
+
+        @pl.when(i == 1)
+        def _():
+            self.fx.start()
+            self.fy.start()
+
+        pl.when(i == 2)(self.nx.start)
+        pl.when(i == 3)(self.ny.start)
+
+        @pl.when(i >= 2)
+        def _():
+            self.to_sibling(i - 2).wait_send()
+
+    def put(self, i, cols, part):
+        self.out[lax.rem(i, 2), :, cols] = part[: self.n]
+        self.own[i, :, cols] = part[self.n :]
+
+    def add(self, at, cols, slot):
+        def body(j, carry):
+            r = rows_of(j, 32)
+            total = self.own[at, r, cols].astype(F32) + self.far[slot, r, :].astype(F32)
+            self.own[at, r, cols] = total.astype(BF)
+            return carry
+
+        lax.fori_loop(0, self.n // 32, body, 0)
+
+    def relay(self):
+        self.fx.wait_recv()
+        self.add(2, self.left, 1)
+        self.by.start()
+        self.fy.wait_recv()
+        self.add(1, self.right, 3)
+        self.bx.start()
 
     def start(self):
-        self.a = {}
-        for sem, k in enumerate((3, 1, 2, 0)):
-            src = self.part.at[pl.ds(pl.multiple_of(self.own(k, 1 - self.c), self.n), self.n)]
-            self.a[k] = self.copy(src, self.near.at[k], sem, self.sib)
-
-    def chip_sum(self, k):
-        self.a[k].wait_recv()
-        base = self.own(k, self.c)
-
-        def body(i, carry):
-            r = rows_of(i, 32)
-            p = self.part[pl.ds(pl.multiple_of(base + i * 32, 32), 32), :].astype(F32)
-            self.sums[k, r, :] = (p + self.near[k, r, :].astype(F32)).astype(BF)
-            return carry
-
-        lax.fori_loop(0, self.n // 32, body, 0)
-
-    def add(self, k, cols, slot):
-        def body(i, carry):
-            r = rows_of(i, 32)
-            total = self.sums[k, r, cols].astype(F32) + self.far[slot, r, :].astype(F32)
-            self.sums[k, r, cols] = total.astype(BF)
-            return carry
-
-        lax.fori_loop(0, self.n // 32, body, 0)
-
-    def halves(self):
-        return pl.ds(0, self.w // 2), pl.ds(self.w // 2, self.w // 2)
-
-    def run(self):
-        self.first()
-        self.second()
-
-    def first(self):
-        left, right = self.halves()
-        self.chip_sum(3)
-        self.fx = self.copy(self.sums.at[3, :, left], self.far.at[1], 4, self.x)
-        self.fy = self.copy(self.sums.at[3, :, right], self.far.at[3], 5, self.y)
-        self.chip_sum(1)
-        self.nx = self.copy(self.sums.at[1, :, left], self.far.at[0], 6, self.x)
-        self.chip_sum(2)
-        self.ny = self.copy(self.sums.at[2, :, right], self.far.at[2], 7, self.y)
-
-    def second(self):
-        left, right = self.halves()
-        self.fx.wait_recv()
-        self.add(2, left, 1)
-        self.by = self.copy(self.sums.at[2, :, left], self.last.at[0], 8, self.y)
-        self.fy.wait_recv()
-        self.add(1, right, 3)
-        self.bx = self.copy(self.sums.at[1, :, right], self.last.at[1], 9, self.x)
-        self.a[0].wait_recv()
+        for made in (self.fx, self.fy, self.nx, self.ny):
+            made.start()
 
     def arrive(self):
+        if self.near is not None:
+            self.to_sibling(3).wait_recv()
         for made in (self.nx, self.ny, self.by, self.bx):
             made.wait_recv()
 
-    def total(self, i, step):
-        r = rows_of(i, step)
-        base = self.own(0, self.c)
-        p = self.part[pl.ds(pl.multiple_of(base + i * step, step), step), :].astype(F32)
-        p = p + self.near[0, r, :].astype(F32)
-        far = jnp.concatenate([self.far[0, r, :], self.far[2, r, :]], axis=1).astype(F32)
-        last = jnp.concatenate([self.last[0, r, :], self.last[1, r, :]], axis=1).astype(F32)
-        return p + far + last
+    def total(self, j, step):
+        r = rows_of(j, step)
+        total = self.own[3, r, :].astype(F32)
+        if self.near is not None:
+            total = total + self.near[3, r, :].astype(F32)
+        a = jnp.concatenate([self.far[0, r, :], self.far[2, r, :]], axis=1).astype(F32)
+        b = jnp.concatenate([self.last[0, r, :], self.last[1, r, :]], axis=1).astype(F32)
+        return total + a + b
 
     def finish(self):
-        for made in self.made:
+        for made in (self.fx, self.fy, self.nx, self.ny, self.by, self.bx):
             made.wait_send()
+        if self.near is not None:
+            for i in (2, 3):
+                self.to_sibling(i).wait_send()
+
+
+def wait_for(i, loads):
+    for at, pair in enumerate(loads):
+
+        @pl.when(i == at)
+        def _(pair=pair):
+            for made in pair:
+                made.wait()
 
 
 def partners():
@@ -709,8 +737,8 @@
 
 def enter_kernel(
     tok_ref, dy_ref, gain_ref, attn_ref, forget_ref, out_w_ref,
-    normed_ref, dy_all_ref, w_attn_ref, w_out_ref,
-    mine, forget_all, s0, r0, s1, r1, sz, rz, so, ro, l0, *, depth,
+    normed_ref, dy_all_ref, w_attn_ref, w_out_ref, cat_ref,
+    mine, forget_all, normed, turned, s0, r0, s1, r1, sz, rz, so, ro, l0, *, depth,
 ):
     c, s, f = here()
     lines = [(c, s, lax.rem(f + 1, depth)), (c, s, lax.rem(f + depth - 1, depth))]
@@ -766,18 +794,45 @@
     second.start()
     line.pass_on(2)
     first.finish()
+    for made in keep[2:3]:
+        made.wait()
+    load = pltpu.make_async_copy(normed_ref, normed, l0.at[5])
+    load.start()
+    keep[0].wait()
+    keep[1].wait()
+
+    def add_shard(owner, begin):
+        small = forget_all[owner].astype(F32)
+        tall = jnp.concatenate([small, jnp.zeros((128 - small.shape[0], shard), F32)], axis=0)
+        rows = rows_of(owner, shard)
+        w_attn_ref[rows, cols:] = tall.T.astype(BF)
+        turned[...] = w_attn_ref[rows, :].T
+
+        def tile(i, unused):
+            tokens = rows_of(i, 512)
+            part = dot(turned[...], normed[tokens, rows], 1, 1)
+            if begin:
+                cat_ref[:, tokens] = part
+            else:
+                cat_ref[:, tokens] += part
+            return unused
+
+        lax.fori_loop(0, normed.shape[0] // 512, tile, 0)
+
+    half = depth // 2
+    upper = lax.div(f, half)
+    load.wait()
+    for k in range(1, depth - 1):
+        add_shard(jnp.int32(k), k == 1)
+    add_shard(upper * (depth - 1), False)
     second.relay()
     spread.pass_on()
     line.pass_on(3)
+    add_shard((1 - upper) * (depth - 1), False)
     second.finish()
     line.finish()
-    for made in keep:
-        made.wait()
+    keep[3].wait()
     spread.finish(l0.at[4])
-    for owner in range(depth):
-        small = forget_all[owner].astype(F32)
-        tall = jnp.concatenate([small, jnp.zeros((128 - small.shape[0], shard), F32)], axis=0)
-        w_attn_ref[owner * shard : (owner + 1) * shard, cols:] = tall.T.astype(BF)
 
 
 def enter(tokens, cotangent, gain, own_attn, own_forget, output_weight, depth, heads_rows):
@@ -796,16 +851,19 @@
             whole,
             jax.ShapeDtypeStruct((depth * shard, cols + 128), BF),
             jax.ShapeDtypeStruct((heads_rows, w), BF),
+            jax.ShapeDtypeStruct((cols + 128, 8 * n), F32),
         ),
         in_specs=[vmem] * 5 + [anywhere],
-        out_specs=[anywhere, anywhere, vmem, anywhere],
+        out_specs=[anywhere, anywhere, vmem, anywhere, vmem],
         scratch_shapes=[
             pltpu.VMEM((n, w), BF),
             pltpu.VMEM((depth,) + own_forget.shape, BF),
+            pltpu.VMEM((8 * n, w), BF),
+            pltpu.VMEM((cols + 128, shard), BF),
             dma, dma, dma, dma, line, line,
             pltpu.SemaphoreType.DMA((2, OUT_PIECES)),
             pltpu.SemaphoreType.DMA((OUT_PIECES,)),
-            pltpu.SemaphoreType.DMA((5,)),
+            pltpu.SemaphoreType.DMA((6,)),
         ],
         compiler_params=pltpu.CompilerParams(
             collective_id=1, has_side_effects=True, vmem_limit_bytes=VMEM_BYTES
@@ -816,53 +874,87 @@
     )(tokens, cotangent, gain[None], own_attn, own_forget, output_weight)
 
 
+TILE = 256
+
+
 def middle_kernel(
-    part_ref, tok_ref, gain_ref, mid_ref, normed_ref,
-    near, sums, far, last, mine, s0, r0, s1, r1, l0,
+    gated_ref, w_ref, tok_ref, gain_ref, mid_ref, normed_ref,
+    gated, turned, mine, s1, r1, l0, *refs,
 ):
+    c, s, f = here()
+    pairs = PairSum(refs)
+    n, width = mine.shape
+    loads = [
+        pltpu.make_async_copy(
+            gated_ref.at[:, pl.ds(pl.multiple_of(block * n, n), n)],
+            gated.at[:, pl.ds(i * n, n)],
+            l0.at[i],
+        )
+        for i, block in enumerate(PairSum.blocks(c, s))
+    ]
+    for made in loads:
+        made.start()
     greet(partners())
-    reduce = Reduce(part_ref, (near, sums, far, last), s0, r0)
-    reduce.start()
-    reduce.run()
-    reduce.arrive()
+    for made in loads:
+        made.wait()
+
+    def one_pair(i, unused):
+        pairs.between(i)
+        turned[...] = gated[:, rows_of(i, 2 * n)].T
+        for t in range(width // TILE):
+            feats = pl.ds(t * TILE, TILE)
+            pairs.put(i, feats, dot(turned[...], w_ref[:, feats], 1, 0).astype(BF))
+        pairs.to_sibling(i).start()
+        return unused
+
+    lax.fori_loop(0, 4, one_pair, 0)
+    pairs.relay()
+    pairs.arrive()
 
     def body(i, carry):
         r = rows_of(i, STEP)
-        mid = tok_ref[r, :].astype(F32) + reduce.total(i, STEP)
+        mid = tok_ref[r, :].astype(F32) + pairs.total(i, STEP)
         mid_ref[r, :] = mid
         mine[r, :] = (mid * mean_square_inverse(mid) * gain_ref[...]).astype(BF)
         return carry
 
-    lax.fori_loop(0, mine.shape[0] // STEP, body, 0)
+    lax.fori_loop(0, n // STEP, body, 0)
     gather = Gather(mine, normed_ref, s1, r1)
     gather.start()
-    keep = pltpu.make_async_copy(mine, gather.block(0), l0.at[0])
+    keep = pltpu.make_async_copy(mine, gather.block(0), l0.at[8])
     keep.start()
-    reduce.finish()
     gather.relay()
     gather.finish()
+    pairs.finish()
     keep.wait()
 
 
-def middle(part, tokens, gain):
+def middle(gated, w_out, tokens, gain):
     n, w = tokens.shape
     dma = pltpu.SemaphoreType.DMA((16,))
     vmem = pl.BlockSpec(memory_space=pltpu.VMEM)
+    anywhere = pl.BlockSpec(memory_space=pl.ANY)
     return pl.pallas_call(
         middle_kernel,
         name="middle",
         out_shape=(jax.ShapeDtypeStruct((n, w), F32), jax.ShapeDtypeStruct((8 * n, w), BF)),
-        in_specs=[vmem] * 3,
-        out_specs=[vmem, pl.BlockSpec(memory_space=pl.ANY)],
-        scratch_shapes=Reduce.scratch(n, w)
-        + [pltpu.VMEM((n, w), BF), dma, dma, dma, dma, pltpu.SemaphoreType.DMA((2,))],
+        in_specs=[anywhere, vmem, vmem, vmem],
+        out_specs=[vmem, anywhere],
+        scratch_shapes=[
+            pltpu.VMEM(gated.shape, BF),
+            pltpu.VMEM((2 * n, gated.shape[0]), BF),
+            pltpu.VMEM((n, w), BF),
+            dma, dma, dma,
+        ]
+        + PairSum.scratch(n, w),
         compiler_params=pltpu.CompilerParams(
             collective_id=2, has_side_effects=True, vmem_limit_bytes=VMEM_BYTES
         ),
         cost_estimate=pl.CostEstimate(
-            flops=50_000_000, bytes_accessed=4 * 8 * n * w * 2, transcendentals=0
+            flops=2 * 8 * n * w * gated.shape[0], bytes_accessed=4 * 8 * n * w * 2,
+            transcendentals=0,
         ),
-    )(part, tokens, gain[None])
+    )(gated, w_out, tokens, gain[None])
 
 
 TERM_PIECES = 4
@@ -894,47 +986,49 @@
     def is_end(self, k):
         return self.f == (0 if k == 0 else self.depth - 1)
 
-    def start(self):
-        for i in range(TERM_PIECES):
-            self.start_piece(i)
-
-    def start_piece(self, i):
-        for n in range(self.depth - 1):
-            for k in (0, 1):
-                g = self.targets(k)[n]
-                pl.when(self.is_end(k))(self.copy(k, g, i, self.source(i, g)).start)
+    def start_piece(self, i, n):
+        for k in (0, 1):
+            g = self.targets(k)[n]
+            pl.when(self.is_end(k))(self.copy(k, g, i, self.source(i, g)).start)
 
     def add(self, k, g, i):
         rows = pl.ds(i * self.n, self.n)
         total = self.got[k, g, rows].astype(F32) + self.term[rows, g].astype(F32)
         self.got[k, g, rows] = total.astype(BF)
 
-    def pass_on(self, i):
-        for n in range(self.depth - 2):
-            for k in (0, 1):
-                g = self.targets(k)[n]
-                beyond = self.f < g if k == 0 else self.f > g
-
-                @pl.when(beyond & jnp.logical_not(self.is_end(k)))
-                def _(k=k, g=g):
-                    made = self.copy(k, g, i, self.got.at[k, g, pl.ds(i * self.n, self.n)])
-                    made.wait_recv()
-                    self.add(k, g, i)
-                    made.start()
-
-    def collect(self, out):
-        for i in range(TERM_PIECES):
-            rows = pl.ds(i * self.n, self.n)
-            for g in range(self.depth):
-
-                @pl.when(self.f == g)
-                def _(g=g, i=i, rows=rows):
-                    total = self.term[rows, g].astype(F32)
-                    for k in (0, 1):
-                        if g != (0 if k == 0 else self.depth - 1):
-                            self.copy(k, g, i, self.source(i, g)).wait_recv()
-                            total = total + self.got[k, g, rows].astype(F32)
-                    out[rows] = total.astype(BF)
+    def pass_on(self, i, n, hop):
+        for k in (0, 1):
+            g = self.targets(k)[n]
+            at = hop if k == 0 else self.depth - 1 - hop
+
+            @pl.when(self.f == at)
+            def _(k=k, g=g):
+                made = self.copy(k, g, i, self.got.at[k, g, pl.ds(i * self.n, self.n)])
+                made.wait_recv()
+                self.add(k, g, i)
+                made.start()
+
+    def steps(self):
+        todo = [
+            (n * TERM_PIECES + i + 2 * (hop - 1), -hop, i, n, hop)
+            for n in range(self.depth - 2)
+            for hop in range(1, self.depth - 1 - n)
+            for i in range(TERM_PIECES)
+        ]
+        return [step[2:] for step in sorted(todo)]
+
+    def collect(self, i, out):
+        rows = pl.ds(i * self.n, self.n)
+        for g in range(self.depth):
+
+            @pl.when(self.f == g)
+            def _(g=g):
+                total = self.term[rows, g].astype(F32)
+                for k in (0, 1):
+                    if g != (0 if k == 0 else self.depth - 1):
+                        self.copy(k, g, i, self.source(i, g)).wait_recv()
+                        total = total + self.got[k, g, rows].astype(F32)
+                out[rows] = total.astype(BF)
 
     def finish(self):
         for k in (0, 1):
@@ -945,85 +1039,86 @@
 
 
 class Exchange:
-    def __init__(self, rows, out, send, recv, peers):
-        c, s, f = here()
-        self.place = c * 4 + s
-        self.made = [
-            REMOTE(rows.at[core * 4 + other], out.at[self.place], send.at[k], recv.at[k], (core, other, f), MESH)
-            for core, other, f, k in peers
-        ]
-        self.keep = pltpu.make_async_copy(rows.at[self.place], out.at[self.place], send.at[0])
+    def __init__(self, rows, out, send, recv):
+        self.c, self.s, self.f = here()
+        self.place = self.c * 4 + self.s
+        self.rows, self.out, self.send, self.recv = rows, out, send, recv
+
+    def remote(self, j):
+        return REMOTE(
+            self.rows.at[j], self.out.at[self.place], self.send.at[j], self.recv.at[self.place],
+            (j // 4, j % 4, self.f), MESH,
+        )
+
+    def local(self, j):
+        return pltpu.make_async_copy(self.rows.at[j], self.out.at[j], self.send.at[j])
+
+    def push(self, j):
+        pl.when(self.place != j)(self.remote(j).start)
+        pl.when(self.place == j)(self.local(j).start)
 
     def start(self):
-        for made in self.made:
-            made.start()
-        self.keep.start()
+        for j in range(8):
+            self.push(j)
 
     def finish(self):
-        for made in self.made:
-            made.wait()
-        self.keep.wait()
-
-
-FFN_TILE = 256
+        for j in range(8):
+            got = REMOTE(
+                self.rows.at[j], self.out.at[j], self.send.at[j], self.recv.at[j],
+                (j // 4, j % 4, self.f), MESH,
+            )
+            pl.when(self.place != j)(got.wait_recv)
+            pl.when(self.place != j)(self.remote(j).wait_send)
+            pl.when(self.place == j)(self.local(j).wait)
+
+
+def plane_peers():
+    c, s, f = here()
+    return [
+        (core, flip(s, k) if k else s, f, k + 4 * i)
+        for i, core in enumerate((c, 1 - c))
+        for k in range(4)
+        if i or k
+    ]
 
 
 def ffn_kernel(
     nm_ref, dy_all_ref, w_ref, dy_ref, mid_ref, gain_ref,
-    grad_mid_ref, gain_term_ref, branch_ref, down_part_ref, gu_rows_ref, low_term_ref,
-    nm, dy, w, grads, own, near, out, far, last, term, got, mine, stage,
-    l0, l1, s0, r0, s1, r1, s2, r2, *, depth,
+    grad_mid_ref, gain_term_ref, branch_ref, down_ref, up_rows_ref, low_term_ref,
+    nm, dy, w, grads, term, got, rows_sum, mine, down_own, down_near, down_out,
+    l0, l1, l2, s1, r1, s2, r2, s3, r3, s4, r4, *refs, depth,
 ):
     c, s, f = here()
     n, width = dy_ref.shape
     fw = w.shape[1] // 3
-    x, y, sib = partners()
+    pairs = PairSum(refs)
     loads = []
-    w_load = pltpu.make_async_copy(w_ref, w, l0.at[8])
+    w_load = pltpu.make_async_copy(w_ref, w, l2.at[8])
     w_load.start()
-    for i, k in enumerate((3, 1, 2, 0)):
-        chip = flip(s, k) if k else s
-        pair = []
-        for half, core in enumerate((1 - c, c)):
-            src = pl.ds(pl.multiple_of((core * 4 + chip) * n, n), n)
-            dst = pl.ds((2 * i + half) * n, n)
-            pair.append(pltpu.make_async_copy(nm_ref.at[src], nm.at[dst], l0.at[2 * i + half]))
-            pair.append(pltpu.make_async_copy(dy_all_ref.at[src], dy.at[dst], l1.at[2 * i + half]))
-        for made in pair:
-            made.start()
-        loads.append(pair)
-    greet(partners() + [
+    for i, block in enumerate(PairSum.blocks(c, s)):
+        src, dst = pl.ds(pl.multiple_of(block * n, n), n), pl.ds(i * n, n)
+        made = [
+            pltpu.make_async_copy(nm_ref.at[src], nm.at[dst], l0.at[i]),
+            pltpu.make_async_copy(dy_all_ref.at[src], dy.at[dst], l1.at[i]),
+        ]
+        for one in made:
+            one.start()
+        if i % 2:
+            loads[-1] += made
+        else:
+            loads.append(made)
+    greet([p[:3] for p in plane_peers()] + [
         (c, s, lax.rem(f + 1, depth)), (c, s, lax.rem(f + depth - 1, depth))
     ])
-    left, right = pl.ds(0, width // 2), pl.ds(width // 2, width // 2)
-
-    def send(src, dst, k, device):
-        return REMOTE(src, dst, s0.at[k], r0.at[k], device, MESH)
-
-    def to_sibling(i):
-        return send(out.at[lax.rem(i, 2)], near.at[i], i, sib)
-
-    fx = send(own.at[0, :, left], far.at[1], 4, x)
-    fy = send(own.at[0, :, right], far.at[3], 5, y)
-    nx = send(own.at[1, :, left], far.at[0], 6, x)
-    ny = send(own.at[2, :, right], far.at[2], 7, y)
-    by = send(own.at[2, :, left], last.at[0], 8, y)
-    bx = send(own.at[1, :, right], last.at[1], 9, x)
     w_load.wait()
 
     def one_pair(i, unused):
         rows = rows_of(i, 2 * n)
-        for at, pair in enumerate(loads):
-
-            @pl.when(i == at)
-            def _(pair=pair):
-                for made in pair:
-                    made.wait()
-
-        for t in range(fw // FFN_TILE):
-            cols = pl.ds(t * FFN_TILE, FFN_TILE)
-            ups = pl.ds(fw + t * FFN_TILE, FFN_TILE)
-            downs = pl.ds(2 * fw + t * FFN_TILE, FFN_TILE)
+        wait_for(i, loads)
+        for t in range(fw // TILE):
+            cols = pl.ds(t * TILE, TILE)
+            ups = pl.ds(fw + t * TILE, TILE)
+            downs = pl.ds(2 * fw + t * TILE, TILE)
             gate_lin = dot(nm[rows, :], w[:, cols], 1, 0)
             up_lin = dot(nm[rows, :], w[:, ups], 1, 0)
             grad_hidden = dot(dy[rows, :], w[:, downs], 1, 0)
@@ -1034,56 +1129,16 @@
                 grad_hidden * up_lin * sig * (1.0 + gate_lin * (1.0 - sig))
             ).astype(BF)
             grads[rows, ups] = (grad_hidden * active).astype(BF)
-
-        @pl.when(i >= 1)
-        def _():
-            to_sibling(i - 1).wait_recv()
-
-            def body(j, carry):
-                r = rows_of(j, 32)
-                total = own[i - 1, r, :].astype(F32) + near[i - 1, r, :].astype(F32)
-                own[i - 1, r, :] = total.astype(BF)
-                return carry
-
-            lax.fori_loop(0, n // 32, body, 0)
-
-        @pl.when(i == 1)
-        def _():
-            fx.start()
-            fy.start()
-
-        pl.when(i == 2)(nx.start)
-        pl.when(i == 3)(ny.start)
-
-        @pl.when(i >= 2)
-        def _():
-            to_sibling(i - 2).wait_send()
-
-        for t in range(width // FFN_TILE):
-            feats = pl.ds(t * FFN_TILE, FFN_TILE)
+        pairs.between(i)
+        for t in range(width // TILE):
+            feats = pl.ds(t * TILE, TILE)
             part = dot(grads[rows, 0 : 2 * fw], w[feats, 0 : 2 * fw], 1, 1).astype(BF)
-            out[lax.rem(i, 2), :, feats] = part[:n]
-            own[i, :, feats] = part[n:]
-        to_sibling(i).start()
+            pairs.put(i, feats, part)
+        pairs.to_sibling(i).start()
         return unused
 
     lax.fori_loop(0, 4, one_pair, 0)
-    fx.wait_recv()
-
-    def add(at, cols, slot):
-        def body(j, carry):
-            r = rows_of(j, 32)
-            total = own[at, r, cols].astype(F32) + far[slot, r, :].astype(F32)
-            own[at, r, cols] = total.astype(BF)
-            return carry
-
-        lax.fori_loop(0, n // 32, body, 0)
-
-    add(2, left, 1)
-    by.start()
-    fy.wait_recv()
-    add(1, right, 3)
-    bx.start()
+    pairs.relay()
 
     line = LineSum(term, got, s2, r2, depth)
     deep = width // TERM_PIECES
@@ -1092,81 +1147,99 @@
         feats = pl.ds(i * deep, deep)
         tile = dot(nm[:, feats], grads[:, 0 : 2 * fw], 0, 0).astype(BF)
         term[i * per : (i + 1) * per] = tile.reshape((per,) + term.shape[1:])
-        line.start_piece(i)
+        line.start_piece(i, 0)
+    for k in range(1, depth - 1):
+        for i in range(TERM_PIECES):
+            line.start_piece(i, k)
+    todo = line.steps()
+    pairs.arrive()
+
+    def body(j, carry):
+        r = rows_of(j, STEP)
+        grad = pairs.total(j, STEP)
+        mid = mid_ref[r, :]
+        inverse = mean_square_inverse(mid)
+        weighted = grad * gain_ref[...]
+        back = inverse * weighted - mid * inverse**3 * jnp.mean(
+            weighted * mid, axis=1, keepdims=True
+        )
+        grad_mid = dy_ref[r, :].astype(F32) + back
+        grad_mid_ref[r, :] = grad_mid
+        mine[r, :] = grad_mid.astype(BF)
+        return carry + jnp.sum(grad * mid * inverse, axis=0, keepdims=True)
+
+    gain_term_ref[...] = lax.fori_loop(0, n // STEP, body, jnp.zeros((1, width), F32))
+    gather = Gather(mine, branch_ref, s1, r1)
+    gather.start()
+    keep = pltpu.make_async_copy(mine, gather.block(0), l0.at[8])
+    keep.start()
     for i in range(TERM_PIECES):
         feats = pl.ds(i * deep, deep)
         tile = dot(dy[:, feats], grads[:, 2 * fw :], 0, 0).astype(BF)
         tile = tile.reshape((per, depth, term.shape[2], fw))
         for g in range(depth):
             low_term_ref[g, i * per : (i + 1) * per] = tile[:, g]
-
-    to_sibling(3).wait_recv()
-    for made in (nx, ny, by, bx):
-        made.wait_recv()
-
-    def total_of(j, step):
-        r = rows_of(j, step)
-        total = own[3, r, :].astype(F32) + near[3, r, :].astype(F32)
-        a = jnp.concatenate([far[0, r, :], far[2, r, :]], axis=1).astype(F32)
-        b = jnp.concatenate([last[0, r, :], last[1, r, :]], axis=1).astype(F32)
-        return total + a + b
-
-    def body(j, carry):
-        r = rows_of(j, STEP)
-        grad = total_of(j, STEP)
-        mid = mid_ref[r, :]
-        inverse = mean_square_inverse(mid)
-        weighted = grad * gain_ref[...]
-        back = inverse * weighted - mid * inverse**3 * jnp.mean(
-            weighted * mid, axis=1, keepdims=True
-        )
-        grad_mid = dy_ref[r, :].astype(F32) + back
-        grad_mid_ref[r, :] = grad_mid
-        mine[r, :] = grad_mid.astype(BF)
-        return carry + jnp.sum(grad * mid * inverse, axis=0, keepdims=True)
-
-    gain_term_ref[...] = lax.fori_loop(0, n // STEP, body, jnp.zeros((1, width), F32))
-    gather = Gather(mine, branch_ref, s1, r1)
-    gather.start()
-    keep = pltpu.make_async_copy(mine, gather.block(0), l1.at[8])
-    keep.start()
-    line.pass_on(0)
-
-    def down_part(i):
-        chip = flip(s, (3, 1, 2, 0)[i]) if i < 3 else s
-        made = []
-        for half, core in enumerate((1 - c, c)):
-            rows = pl.ds((2 * i + half) * n, n)
-            for t in range(width // FFN_TILE):
-                feats = pl.ds(t * FFN_TILE, FFN_TILE)
-                part = dot(grads[rows, 2 * fw :], w[feats, 2 * fw :], 1, 1)
-                stage[half, :, feats] = part.astype(BF)
-            dst = pl.ds(pl.multiple_of((core * 4 + chip) * n, n), n)
-            made.append(
-                pltpu.make_async_copy(stage.at[half], down_part_ref.at[dst], l0.at[half])
-            )
-            made[-1].start()
-        return made
-
-    moved = []
-    for i in range(4):
-        for made in moved:
-            made.wait()
-        moved = down_part(i)
-        if i == 1:
-            line.pass_on(1)
+        for step in todo[i * 2 : i * 2 + 2]:
+            line.pass_on(*step)
+
+    def down_copy(i):
+        return REMOTE(
+            down_out.at[lax.rem(i, 2)], down_near.at[i], s3.at[i], r3.at[i], pairs.sib, MESH
+        )
+
+    def down_pair(i, unused):
+        rows = rows_of(i, 2 * n)
+
+        @pl.when(i >= 2)
+        def _():
+            down_copy(i - 2).wait_send()
+
+        for t in range(width // TILE):
+            feats = pl.ds(t * TILE, TILE)
+            part = dot(grads[rows, 2 * fw :], w[feats, 2 * fw :], 1, 1).astype(BF)
+            down_out[lax.rem(i, 2), :, feats] = part[:n]
+            down_own[i, :, feats] = part[n:]
+        down_copy(i).start()
+        return unused
+
+    lax.fori_loop(0, 4, down_pair, 0)
     gather.relay()
-    line.pass_on(2)
+    for step in todo[2 * TERM_PIECES :]:
+        line.pass_on(*step)
+
+    def down_sum(i, unused):
+        down_copy(i).wait_recv()
+
+        def body(j, carry):
+            r = rows_of(j, 32)
+            total = down_own[i, r, :].astype(F32) + down_near[i, r, :].astype(F32)
+            down_own[i, r, :] = total.astype(BF)
+            return carry
+
+        return lax.fori_loop(0, n // 32, body, unused)
+
+    lax.fori_loop(0, 4, down_sum, 0)
+    stores = [
+        pltpu.make_async_copy(
+            down_own.at[i], down_ref.at[flip(s, k) if k else s], l1.at[i]
+        )
+        for i, k in enumerate(PairSum.order)
+    ]
+    for made in stores:
+        made.start()
     gather.finish()
-    for made in moved:
+    exchange = Exchange(rows_sum, up_rows_ref, s4, r4)
+    for i in range(TERM_PIECES):
+        line.collect(i, rows_sum)
+        for j in range(i * per, (i + 1) * per):
+            exchange.push(j)
+    keep.wait()
+    exchange.finish()
+    for made in stores:
         made.wait()
-    line.pass_on(3)
-    line.collect(gu_rows_ref)
-    keep.wait()
-    for made in (fx, fy, nx, ny, by, bx):
-        made.wait_send()
+    pairs.finish()
     for i in (2, 3):
-        to_sibling(i).wait_send()
+        down_copy(i).wait_send()
     line.finish()
 
 
@@ -1175,6 +1248,8 @@
     fw = weights.shape[1] // 3
     r = width // (8 * depth)
     dma = pltpu.SemaphoreType.DMA((16,))
+    four = pltpu.SemaphoreType.DMA((4,))
+    eight = pltpu.SemaphoreType.DMA((8,))
     line = pltpu.SemaphoreType.DMA((2, depth, TERM_PIECES))
     vmem = pl.BlockSpec(memory_space=pltpu.VMEM)
     anywhere = pl.BlockSpec(memory_space=pl.ANY)
@@ -1185,7 +1260,7 @@
             jax.ShapeDtypeStruct((n, width), F32),
             jax.ShapeDtypeStruct((1, width), F32),
             jax.ShapeDtypeStruct((8 * n, width), BF),
-            jax.ShapeDtypeStruct((8 * n, width), BF),
+            jax.ShapeDtypeStruct((4, n, width), BF),
             jax.ShapeDtypeStruct((8, r, 2 * fw), BF),
             jax.ShapeDtypeStruct((depth, 8, r, fw), BF),
         ),
@@ -1196,17 +1271,16 @@
             pltpu.VMEM((8 * n, width), BF),
             pltpu.VMEM((width, 3 * fw), BF),
             pltpu.VMEM((8 * n, 3 * fw), BF),
+            pltpu.VMEM((8, depth, r, 2 * fw), BF),
+            pltpu.VMEM((2, depth, 8, r, 2 * fw), BF),
+            pltpu.VMEM((8, r, 2 * fw), BF),
+            pltpu.VMEM((n, width), BF),
             pltpu.VMEM((4, n, width), BF),
             pltpu.VMEM((4, n, width), BF),
             pltpu.VMEM((2, n, width), BF),
-            pltpu.VMEM((4, n, width // 2), BF),
-            pltpu.VMEM((2, n, width // 2), BF),
-            pltpu.VMEM((8, depth, r, 2 * fw), BF),
-            pltpu.VMEM((2, depth, 8, r, 2 * fw), BF),
-            pltpu.VMEM((n, width), BF),
-            pltpu.VMEM((2, n, width), BF),
-            dma, dma, dma, dma, dma, dma, line, line,
-        ],
+            dma, dma, dma, dma, dma, line, line, four, four, eight, eight,
+        ]
+        + PairSum.scratch(n, width),
         compiler_params=pltpu.CompilerParams(
             collective_id=3, has_side_effects=True, vmem_limit_bytes=63 * 1024 * 1024
         ),
@@ -1218,40 +1292,87 @@
 
 
 def leave_kernel(
-    part_ref, down_ref, tok_ref, grad_mid_ref, mid_ref, gain_ref, small_ref, term_ref, mlp_ref, low_ref,
-    grad_ref, small_sum_ref, out_ref, attn_rows_ref, mlp_rows_ref, low_rows_ref,
-    near, sums, far, last, near2, sums2, far2, last2, small, plane_small, line_small, got, rows,
-    s0, r0, s1, r1, s2, r2, s3, r3, s4, r4, s5, r5, s6, r6, *, depth,
+    normed_ref, cat_ref, w_ref, down_ref, tok_ref, grad_mid_ref, mid_ref, gain_ref, small_ref,
+    low_ref,
+    grad_ref, small_sum_ref, out_ref, attn_rows_ref, low_rows_ref,
+    normed, cat, turned, w, small, plane_small, line_small, term, got, rows,
+    l0, l1, s2, r2, s3, r3, s5, r5, s6, r6, *refs, depth,
 ):
     c, s, f = here()
-    plane_peers = [
-        (core, flip(s, k) if k else s, f, k + 4 * i)
-        for i, core in enumerate((c, 1 - c))
-        for k in range(4)
-        if i or k
+    n, width = tok_ref.shape
+    pairs = PairSum(refs[:7])
+    down = PairSum(refs[7:])
+    down_loads = [
+        pltpu.make_async_copy(down_ref.at[flip(s, k) if k else s], down.own.at[i], l0.at[9 + i])
+        for i, k in enumerate(PairSum.order)
     ]
+    loads = []
+    for i, block in enumerate(PairSum.blocks(c, s)):
+        src, dst = pl.ds(pl.multiple_of(block * n, n), n), pl.ds(i * n, n)
+        loads.append(pltpu.make_async_copy(cat_ref.at[:, src], cat.at[:, dst], l0.at[i]))
+        loads.append(pltpu.make_async_copy(normed_ref.at[src], normed.at[dst], l1.at[i]))
+    w_load = pltpu.make_async_copy(w_ref, w, l0.at[8])
+    for made in down_loads + loads:
+        made.start()
+    w_load.start()
+    peers = plane_peers()
     line_peers = [(c, s, lax.rem(f + k, depth), k) for k in range(1, depth)]
-    greet([p[:3] for p in plane_peers + line_peers])
-    line = LineSum(term_ref, got, s3, r3, depth)
-    line.start()
-    reduce = Reduce(part_ref, (near, sums, far, last), s0, r0)
-    other = Reduce(down_ref, (near2, sums2, far2, last2), s1, r1)
-    mlp_rows = Exchange(mlp_ref, mlp_rows_ref, s4, r4, plane_peers)
-    low_rows = Exchange(low_ref, low_rows_ref, s6, r6, plane_peers)
-    reduce.start()
-    other.start()
-    reduce.first()
-    mlp_rows.start()
+    greet([p[:3] for p in peers + line_peers])
+    line = LineSum(term, got, s3, r3, depth)
+    low_rows = Exchange(low_ref, low_rows_ref, s6, r6)
+    deep = width // TERM_PIECES
+    per = term.shape[0] // TERM_PIECES
+    for made in down_loads:
+        made.wait()
+    down.start()
     low_rows.start()
-    reduce.second()
-    line.pass_on(0)
-    other.first()
-    line.pass_on(1)
-    reduce.arrive()
+    for made in loads:
+        made.wait()
+    for i in range(TERM_PIECES):
+        tile = dot(cat[...], normed[:, pl.ds(i * deep, deep)], 1, 0).T.astype(BF)
+        term[i * per : (i + 1) * per] = tile.reshape((per,) + term.shape[1:])
+        line.start_piece(i, 0)
+    for k in range(1, depth - 1):
+        for i in range(TERM_PIECES):
+            line.start_piece(i, k)
+    w_load.wait()
+
+    def one_pair(i, unused):
+        pairs.between(i)
+        turned[...] = cat[:, rows_of(i, 2 * n)].T
+        for t in range(width // TILE):
+            feats = pl.ds(t * TILE, TILE)
+            pairs.put(i, feats, dot(turned[...], w[feats, :], 1, 1).astype(BF))
+        pairs.to_sibling(i).start()
+        for at in range(4):
+
+            @pl.when(i == at)
+            def _(at=at):
+                for step in todo[at : at + 1]:
+                    line.pass_on(*step)
+
+        return unused
+
+    todo = line.steps()
+    lax.fori_loop(0, 4, one_pair, 0)
+    for step in todo[4:6]:
+        line.pass_on(*step)
+    pairs.relay()
+    down.relay()
+    for step in todo[6:]:
+        line.pass_on(*step)
+    attn_rows = Exchange(rows, attn_rows_ref, s5, r5)
+
+    def collect(i):
+        line.collect(i, rows)
+        for j in range(i * per, (i + 1) * per):
+            attn_rows.push(j)
+
+    pairs.arrive()
 
     def body(i, carry):
         r = rows_of(i, STEP)
-        grad = reduce.total(i, STEP)
+        grad = pairs.total(i, STEP)
         tok = tok_ref[r, :].astype(F32)
         inverse = mean_square_inverse(tok)
         weighted = grad * gain_ref[...]
@@ -1261,21 +1382,22 @@
         grad_ref[r, :] = grad_mid_ref[r, :] + back
         return carry + jnp.sum(grad * tok * inverse, axis=0, keepdims=True)
 
-    n, w = tok_ref.shape
+    gain_term = lax.fori_loop(0, n // STEP, body, jnp.zeros((1, width), F32))
+    lane = small.shape[1]
     small[...] = small_ref[...]
-    small[0:1, :] = lax.fori_loop(0, n // STEP, body, jnp.zeros((1, w), F32))
+    for k in range(width // lane):
+        small[k : k + 1, :] = gain_term[:, k * lane : (k + 1) * lane]
     place = c * 4 + s
     plane_small[pl.ds(place, 1)] = small[...][None]
     sent = []
-    for core, other_s, other_f, k in plane_peers:
+    for core, other_s, other_f, k in peers:
         made = REMOTE(
             small, plane_small.at[place], s2.at[k - 1], r2.at[k - 1], (core, other_s, other_f), MESH
         )
         made.start()
         sent.append(made)
-    line.pass_on(2)
-    other.second()
-    line.pass_on(3)
+    collect(0)
+    collect(1)
     for made in sent:
         made.wait()
     total = plane_small[0]
@@ -1290,74 +1412,78 @@
         )
         made.start()
         sent.append(made)
-    other.arrive()
+    collect(2)
+    collect(3)
+    down.arrive()
 
     def body2(i, carry):
         r = rows_of(i, STEP)
-        out_ref[r, :] = (mid_ref[r, :] + other.total(i, STEP)).astype(BF)
+        out_ref[r, :] = (mid_ref[r, :] + down.total(i, STEP)).astype(BF)
         return carry
 
     lax.fori_loop(0, n // STEP, body2, 0)
-    line.collect(rows)
-    attn_rows = Exchange(rows, attn_rows_ref, s5, r5, plane_peers)
-    attn_rows.start()
     for made in sent:
         made.wait()
     total = line_small[0]
     for i in range(1, depth):
         total = total + line_small[i]
     small_sum_ref[...] = total
-    reduce.finish()
-    other.finish()
+    pairs.finish()
+    down.finish()
     line.finish()
-    mlp_rows.finish()
     low_rows.finish()
     attn_rows.finish()
 
 
-def leave(part, down_part, tokens, grad_mid, mid, gain, small, term, mlp_rows, low_rows, depth):
-    n, w = mid.shape
+def leave(normed, cat, w_attn, down_sum, tokens, grad_mid, mid, gain, small, low_rows, depth):
+    n, w = grad_mid.shape
+    plane = 8
+    cols = w_attn.shape[1]
+    r = w // (plane * depth)
     sems = pltpu.SemaphoreType.DMA((6 + depth,))
-    plane, _, r, cols = term.shape
     dma = pltpu.SemaphoreType.DMA((16,))
     eight = pltpu.SemaphoreType.DMA((8,))
     line = pltpu.SemaphoreType.DMA((2, depth, TERM_PIECES))
     vmem = pl.BlockSpec(memory_space=pltpu.VMEM)
+    anywhere = pl.BlockSpec(memory_space=pl.ANY)
     return pl.pallas_call(
         functools.partial(leave_kernel, depth=depth),
         name="leave",
         out_shape=(
             jax.ShapeDtypeStruct((n, w), F32),
-            jax.ShapeDtypeStruct((8, w), F32),
+            jax.ShapeDtypeStruct(small.shape, F32),
             jax.ShapeDtypeStruct((n, w), BF),
             jax.ShapeDtypeStruct((plane, r, cols), BF),
-            jax.ShapeDtypeStruct(mlp_rows.shape, BF),
             jax.ShapeDtypeStruct(low_rows.shape, BF),
         ),
-        in_specs=[vmem] * 10,
-        out_specs=[vmem] * 6,
-        scratch_shapes=Reduce.scratch(n, w)
-        + Reduce.scratch(n, w)
-        + [
-            pltpu.VMEM((8, w), F32),
-            pltpu.VMEM((8, 8, w), F32),
-            pltpu.VMEM((depth, 8, w), F32),
+        in_specs=[anywhere] * 4 + [vmem] * 6,
+        out_specs=[vmem] * 5,
+        scratch_shapes=[
+            pltpu.VMEM(normed.shape, BF),
+            pltpu.VMEM(cat.shape, BF),
+            pltpu.VMEM((2 * n, cols), BF),
+            pltpu.VMEM(w_attn.shape, BF),
+            pltpu.VMEM(small.shape, F32),
+            pltpu.VMEM((8,) + small.shape, F32),
+            pltpu.VMEM((depth,) + small.shape, F32),
+            pltpu.VMEM((plane, depth, r, cols), BF),
             pltpu.VMEM((2, depth, plane, r, cols), BF),
             pltpu.VMEM((plane, r, cols), BF),
-            dma, dma, dma, dma, sems, sems, line, line,
-            eight, eight, eight, eight, eight, eight,
-        ],
+            dma, dma, sems, sems, line, line, eight, eight, eight, eight,
+        ]
+        + PairSum.scratch(n, w)
+        + PairSum.tail_scratch(n, w),
         compiler_params=pltpu.CompilerParams(
             collective_id=4, has_side_effects=True, vmem_limit_bytes=VMEM_BYTES
         ),
         cost_estimate=pl.CostEstimate(
-            flops=50_000_000, bytes_accessed=4 * 8 * n * w * 2, transcendentals=0
+            flops=4 * 8 * n * w * cols, bytes_accessed=4 * 8 * n * w * 2, transcendentals=0
         ),
-    )(part, down_part, tokens, grad_mid, mid, gain[None], small, term, mlp_rows, low_rows)
+    )(normed, cat, w_attn, down_sum, tokens, grad_mid, mid, gain[None], small, low_rows)
 
 
 def finish_kernel(
-    attn_ref, mlp_ref, low_ref, small_ref, out_w_ref, block_ref, tok_grad_ref,
+    attn_ref, up_rows_ref, low_ref, small_ref, out_w_ref, block_ref, tok_grad_ref,
     q_ref, k_ref, v_ref, g_ref, f_ref, o_ref, gate_ref, up_ref, down_ref,
     gain1_ref, gain2_ref, bias_ref, out_ref, tokens_ref, *, hw, heads,
 ):
@@ -1375,19 +1501,22 @@
         total = total + dot(attn_ref[t, :, 4 * hw : 4 * hw + 128], pick, 1, 0)
     f_ref[...] = total[:, : f_ref.shape[1]]
     o_ref[...] = out_w_ref[...].astype(F32)
-    for i, ref in enumerate((gate_ref, up_ref)):
-        for t in range(plane):
-            ref[:, t * fw : (t + 1) * fw] = mlp_ref[t, :, i * fw : (i + 1) * fw].astype(F32)
     for t in range(plane):
-        down_ref[:, t * fw : (t + 1) * fw] = low_ref[t].astype(F32)
-    gain1_ref[...] = small_ref[0:1, :]
-    gain2_ref[...] = small_ref[1:2, :]
-    bias_ref[...] = small_ref[2:3, 0 : bias_ref.shape[1]]
+        cols = slice(t * fw, (t + 1) * fw)
+        gate_ref[:, cols] = up_rows_ref[t, :, 0:fw].astype(F32)
+        up_ref[:, cols] = up_rows_ref[t, :, fw:].astype(F32)
+        down_ref[:, cols] = low_ref[t].astype(F32)
+    lane = small_ref.shape[1]
+    count = gain1_ref.shape[1] // lane
+    for k in range(count):
+        gain1_ref[:, k * lane : (k + 1) * lane] = small_ref[k : k + 1, :]
+        gain2_ref[:, k * lane : (k + 1) * lane] = small_ref[count + k : count + k + 1, :]
+    bias_ref[...] = small_ref[2 * count : 2 * count + 1, 0 : bias_ref.shape[1]]
     out_ref[...] = block_ref[...]
     tokens_ref[...] = tok_grad_ref[...]
 
 
-def finish(attn_rows, mlp_rows, low_rows, small, out_w, block_out, tokens_grad, hw, heads):
+def finish(attn_rows, up_rows, low_rows, small, out_w, block_out, tokens_grad, hw, heads):
     plane, r, _ = attn_rows.shape
     n, w = tokens_grad.shape
     fw = low_rows.shape[2]
@@ -1410,7 +1539,7 @@
         in_specs=[vmem] * 7,
         out_specs=[vmem] * 14,
         compiler_params=pltpu.CompilerParams(vmem_limit_bytes=VMEM_BYTES),
-    )(attn_rows, mlp_rows, low_rows, small, out_w, block_out, tokens_grad)
+    )(attn_rows, up_rows, low_rows, small, out_w, block_out, tokens_grad)
 
 
 BQ = 256
@@ -1740,50 +1869,48 @@
     own_mlp = jnp.concatenate(
         [columns(gate_weight, fw), columns(up_weight, fw), columns(down_weight, fw)], axis=1
     )
-    normed, cotangent_all, w_attn, w_out = enter(
+    normed, cotangent_all, w_attn, w_out, cat = enter(
         inputs, cotangent, attn_gain, own_attn, own_forget, output_weight, depth, hw
     )
     own_mlp, w_attn = lax.optimization_barrier((own_mlp, w_attn))
     w_mlp = lax.all_gather(own_mlp, "fsdp", axis=0, tiled=True)
-    cat = dot(w_attn, normed, 0, 1)
     bias_own = lax.dynamic_slice_in_dim(forget_bias, place * heads, heads, 0)
     bias = jnp.broadcast_to(jnp.pad(bias_own, (0, 16 - heads))[:, None], (16, 128))
     gated, att, exact, lse, prefix = attention(storage, ends, cat, bias, heads, hd, slab)
-    mid_part = dot(gated, w_out, 0, 0).astype(BF)
-    mid, normed_mlp = middle(mid_part, inputs, mlp_gain)
-
-    grad_mid, mlp_gain_term, branch, down_part, mlp_rows, low_term = ffn(
+    mid, normed_mlp = middle(gated, w_out, inputs, mlp_gain)
+
+    grad_mid, mlp_gain_term, branch, down_sum, up_rows, low_term = ffn(
         normed_mlp, cotangent_all, w_mlp, cotangent, mid, mlp_gain, depth
     )
     low_grad = lax.psum_scatter(
         low_term.reshape(width, fw), "fsdp", scatter_dimension=0, tiled=True
     )
 
-    grad_gated = dot(w_out, branch, 1, 1)
+    grad_gated, out_term = lax.optimization_barrier(
+        (dot(w_out, branch, 1, 1), dot(gated, branch, 1, 0).astype(BF))
+    )
     grad_cat, bias_grad = attention_back(
         storage, ends, cat, bias, grad_gated, att, exact, lse, prefix, heads, hd, slab
     )
-    out_term = dot(gated, branch, 1, 0).astype(BF)
-    attn_term = dot(normed, grad_cat, 0, 1).astype(BF)
-    out_term, low_grad = lax.optimization_barrier((out_term, low_grad))
     output_weight_grad = lax.psum_scatter(out_term, "fsdp", scatter_dimension=0, tiled=True)
-    attn_part = dot(grad_cat, w_attn, 0, 1).astype(BF)
+    lane = width // 3
     bias_row = lax.dynamic_update_slice_in_dim(
-        jnp.zeros((width,), F32), bias_grad[:heads, 0], place * heads, 0
+        jnp.zeros((lane,), F32), bias_grad[:heads, 0], place * heads, 0
     )
     small = jnp.concatenate(
-        [jnp.zeros((1, width), F32), mlp_gain_term, bias_row[None], jnp.zeros((5, width), F32)]
+        [jnp.zeros((3, lane), F32), mlp_gain_term.reshape(3, lane), bias_row[None]]
+        + [jnp.zeros((1, lane), F32)]
     )
     part = width // (plane * depth)
-    tokens_grad, small_sum, block_out, attn_rows, mlp_rows, low_rows = leave(
-        attn_part, down_part, inputs, grad_mid, mid, attn_gain, small,
-        attn_term.reshape(plane, depth, part, -1), mlp_rows, low_grad.reshape(plane, part, -1), depth,
+    tokens_grad, small_sum, block_out, attn_rows, low_rows = leave(
+        normed, grad_cat, w_attn, down_sum, inputs, grad_mid, mid, attn_gain, small,
+        low_grad.reshape(plane, part, fw), depth,
     )
     (
         query_grad, key_grad, value_grad, outgate_grad, forget_grad, out_grad, gate_grad, up_grad,
         down_grad, attn_gain_grad, mlp_gain_grad, forget_bias_grad, block_out, tokens_grad,
     ) = finish(
-        attn_rows, mlp_rows, low_rows, small_sum, output_weight_grad, block_out, tokens_grad,
+        attn_rows, up_rows, low_rows, small_sum, output_weight_grad, block_out, tokens_grad,
         hw, heads,
     )
     return (
@@ -1820,7 +1947,7 @@
         and width // head_count == 64
         and slab % 256 == 0
         and group_rows <= 2048
-        and width % 256 == 0
+        and width % 768 == 0
         and gate_weight.shape[1] % (128 * plane) == 0
         and width % (16 * plane * sizes["fsdp"]) == 0
         and (group_rows // plane) % 64 == 0

time: 483 us -> 413 us (0.86)
  matrix products: 49.9 us -> 8.51 us
  Pallas kernels: 397 us -> 366 us
    dot_general x6 -> x2, matrix products: 49.9 us -> 8.51 us  [dot(): lax.dot_general(a, b, (((ca,), (cb,)), ((), ())), preferred_element_type=...]
    pallas_call x1, Pallas kernels: 94.5 us -> 73 us  [leave(): pl.pallas_call(functools.partial(leave_kernel, depth=depth), name='leave'...]
    pallas_call x1, Pallas kernels: 102 us -> 87.6 us  [ffn(): pl.pallas_call(functools.partial(ffn_kernel, depth=depth), name='ffn', ou...]
  transfers between devices with their start and end apart: 3 -> 3, of which waited for: 0 -> 0; matrix products, arithmetic and copies ran while one was open for 9% -> 3% of each run, Pallas kernels for 47% -> 50%
where the time goes in v4:
time: 413 us; the launch traced here: 408 us
  Pallas kernels  366 us (89%)
  between operations  14.4 us (3%)
  local copies, waits for them, and re-layouts  11.3 us (3%)
  matrix products  8.51 us (2%)
  other arithmetic  6.8 us (2%)
    pallas_call x1, Pallas kernels, ffn(): pl.pallas_call(functools.partial(ffn_kernel, depth=depth), name='ffn', ou...  87.6 us
    pallas_call x1, Pallas kernels, leave(): pl.pallas_call(functools.partial(leave_kernel, depth=depth), name='leave'...  73 us
    pallas_call x1, Pallas kernels, middle(): pl.pallas_call(middle_kernel, name='middle', out_shape=(jax.ShapeDtypeStr...  71.4 us
    pallas_call x1, Pallas kernels, enter(): pl.pallas_call(functools.partial(enter_kernel, depth=depth), name='enter'...  68.2 us
    pallas_call x1, Pallas kernels, attention_back(): pl.pallas_call(functools.partial(attention_back_kernel, heads=heads, hd=h...  33.6 us
    pallas_call x1, Pallas kernels, attention(): pl.pallas_call(functools.partial(attention_kernel, heads=heads, hd=hd, sl...  27.4 us
    dot_general x2, matrix products, dot(): lax.dot_general(a, b, (((ca,), (cb,)), ((), ())), preferred_element_type=...  8.51 us
  transfers between devices with their start and end apart: 3, of which 0 were waited for; matrix products, arithmetic and copies ran while one was open for 3% of the time, Pallas kernels for 50%

profile of v4, /device:TPU:0, one launch (start us, length us, event | category | flops | bytes accessed | tf_op | source)
XLA Modules:
  0.0 407.6 jit_solution(4767939686389754148)
XLA Ops:
  7.2 1.3 broadcast_in_dim.44.gain_ref
  8.5 1.2 constant_dynamic-slice_fusion.3
  9.8 1.2 constant_dynamic-slice_fusion.5
  11.7 1.0 constant_dynamic-slice_fusion.2
  12.7 1.2 constant_dynamic-slice_fusion
  13.9 1.1 pad_maximum_fusion
  15.0 1.1 pad_maximum_fusion.1.attn_ref
  16.1 68.2 %enter.1 = (bf16[2048,1536]{1,0:T(8,128)(2,1)}, bf16[2048,1536]{1,0:T(8,128)(2,1)}, bf16[1536,896]{1,0:T(8,128)(2,1)}, bf16[192,1536]{1,0:T(8,128)(2,1)}, f32[896,2048]{1,0:T(8,128)}) custom-call(bf16[256,1536]{1,0:T(8,128)(2,1)} %bitcast.20, bf16[256,1536]{1,0:T(8,128)(2,1)} %bitcast.18, f32[1,1536]{1,0:T(1,128)} %broadcast_in_dim.44.gain_ref, ...), custom_call_target="tpu_custom_call" | custom-call | flops 50000000 | bytes 25165824 | tf_op jit(solution)/shard_map/enter/pallas_call | solution.py:846
  84.5 0.7 reduce-window.9
  86.5 0.7 broadcast_in_dim.47.bias_ref
  87.2 27.4 %attention.1 = (bf16[192,2048]{1,0:T(8,128)(2,1)}, bf16[192,2048]{1,0:T(8,128)(2,1)}, f32[192,2048]{1,0:T(8,128)}, f32[8,2048]{1,0:T(8,128)}, f32[16,2048]{1,0:T(8,128)}) custom-call(s32[4]{0:T(128)} %select_reduce_fusion.place_ref, s32[8]{0:T(128)} %bitcast.30, f32[896,2048]{1,0:T(8,128)} %get-tuple-element.58.cat_ref, f32[16,128]{1,0:T(8,128)} %broadcast_in_dim.47.bias_ref), custom_call_target="tpu_custom_call" | custom-call | flops 6442450944 | bytes 7340032 | tf_op jit(solution)/shard_map/attention/pallas_call | solution.py:1691
  114.6 71.4 %middle.1 = (f32[256,1536]{1,0:T(8,128)}, bf16[2048,1536]{1,0:T(8,128)(2,1)}) custom-call(bf16[192,2048]{1,0:T(8,128)(2,1)} %get-tuple-element.60.gated_ref, bf16[192,1536]{1,0:T(8,128)(2,1)} %get-tuple-element.59.w_ref, bf16[256,1536]{1,0:T(8,128)(2,1)} %bitcast.21, f32[1,1536]{1,0:T(1,128)} %broadcast_in_dim.48.gain_ref), custom_call_target="tpu_custom_call" | custom-call | flops 1207959552 | bytes 25165824 | tf_op jit(solution)/shard_map/middle/pallas_call | solution.py:937
  186.0 87.6 %ffn.1 = (f32[256,1536]{1,0:T(8,128)}, f32[1,1536]{1,0:T(1,128)}, bf16[2048,1536]{1,0:T(8,128)(2,1)}, bf16[4,256,1536]{2,1,0:T(8,128)(2,1)}, bf16[8,48,1024]{2,1...) custom-call(bf16[2048,1536]{1,0:T(8,128)(2,1)} %get-tuple-element.61.nm_ref, bf16[2048,1536]{1,0:T(8,128)(2,1)} %get-tuple-element.62.dy_all_ref, ...), custom_call_target="tpu_custom_call" | custom-call | flops 28991029248 | bytes 25165824 | tf_op jit(solution)/shard_map/ffn/pallas_call | solution.py:1256
  273.7 1.0 copy-done.3
  274.6 6.3 %fusion.gg_ref = f32[192,2048]{1,0:T(8,128)} fusion(bf16[192,1536]{1,0:T(8,128)(2,1)S(1)} %copy-done.3, bf16[2048,1536]{1,0:T(8,128)(2,1)} %get-tuple-element.66), kind=kOutput, calls=%fused_computation.15 | convolution fusion | flops 1207959552 | bytes 8454144 | tf_op jit(solution)/shard_map/dot_general | solution.py:1551
  280.9 2.2 convolution_convert_fusion
  283.2 33.6 %attention_back.1 = (bf16[896,2048]{1,0:T(8,128)(2,1)}, f32[16,128]{1,0:T(8,128)}) custom-call(s32[4]{0:T(128)} %select_reduce_fusion.place_ref, s32[8]{0:T(128)} %bitcast.31, f32[896,2048]{1,0:T(8,128)} %get-tuple-element.58.cat_ref, f32[16,128]{1,0:T(8,128)} %broadcast_in_dim.47.bias_ref, f32[192,2048]{1,0:T(8,128)} %fusion.gg_ref, ...), custom_call_target="tpu_custom_call" | custom-call | flops 16106127360 | bytes 14680064 | tf_op jit(solution)/shard_map/attention_back/pallas_call | solution.py:1807
  316.8 0.8 slice_reduce_fusion
  317.8 0.7 pad_maximum_fusion.2.small_ref
  318.5 73.0 %leave.1 = (f32[256,1536]{1,0:T(8,128)}, f32[8,512]{1,0:T(8,128)}, bf16[256,1536]{1,0:T(8,128)(2,1)}, bf16[8,48,896]{2,1,0:T(8,128)(2,1)}, bf16[8,48,512]{2,1,0:T(8,128)(2,1)}) custom-call(bf16[2048,1536]{1,0:T(8,128)(2,1)} %get-tuple-element.57.normed_ref, bf16[896,2048]{1,0:T(8,128)(2,1)} %get-tuple-element.72.cat_ref, ...), custom_call_target="tpu_custom_call" | custom-call | flops 11274289152 | bytes 25165824 | tf_op jit(solution)/shard_map/leave/pallas_call | solution.py:1449
  391.6 5.1 %finish.1 = (f32[48,1536]{1,0:T(8,128)}, f32[48,1536]{1,0:T(8,128)}, f32[48,1536]{1,0:T(8,128)}, f32[48,1536]{1,0:T(8,128)}, f32[48,24]{1,0:T(8,128)}, /*index=5...) custom-call(bf16[8,48,896]{2,1,0:T(8,128)(2,1)} %get-tuple-element.7, ...), custom_call_target="tpu_custom_call" | custom-call | tf_op jit(solution)/shard_map/finish/pallas_call | solution.py:1527
  396.7 1.3 reduce.2
  398.0 1.4 copy.32
  399.4 1.3 reduce.3
  (41 shorter events, 2.6 us)
Async XLA Ops:
  7.2 3.8 copy-start
  7.2 178.8 %all-gather.2.cloned.1.call-start = ((), (), s32[]{:S(2)}) async-start(), calls=%async_computation.2 | async-start | bytes 5898240 | tf_op jit(solution)/shard_map/all_gather | solution.py:1876
  16.0 68.4 %copy-start.6 = (s32[1,8]{1,0:T(1,128)S(1)}, s32[1,8]{1,0:T(1,128)}, u32[]{:S(2)}) copy-start(s32[1,8]{1,0:T(1,128)} %param.18) | copy-start | bytes 100
  16.0 69.1 %copy-start.7 = (f32[24]{0:T(128)S(1)}, f32[24]{0:T(128)}, u32[]{:S(2)}) copy-start(f32[24]{0:T(128)} %param.26) | copy-start | bytes 292
  16.0 69.2 %copy-start.4 = (f32[1536]{0:T(1024)S(1)}, f32[1536]{0:T(1024)}, u32[]{:S(2)}) copy-start(f32[1536]{0:T(1024)} %param.28) | copy-start | bytes 18436
  16.0 69.8 %copy-start.8 = (s32[1,4]{1,0:T(1,128)S(1)}, s32[1,4]{1,0:T(1,128)}, u32[]{:S(2)}) copy-start(s32[1,4]{1,0:T(1,128)} %param.19) | copy-start | bytes 52
  84.3 234.3 %reduce-scatter.3.cloned.1.call-start = ((), (), s32[]{:S(2)}) async-start(), calls=%async_computation.3 | async-start | bytes 1966080 | tf_op jit(solution)/shard_map/reduce_scatter | solution.py:1885
  273.6 1.1 copy-start.3
  273.6 118.0 %reduce-scatter.5.cloned.1.call-start = ((), (), s32[]{:S(2)}) async-start(), calls=%async_computation.4 | async-start | bytes 737280 | tf_op jit(solution)/shard_map/reduce_scatter | solution.py:1895
  274.6 6.3 %copy-start.2 = (bf16[2048,1536]{1,0:T(8,128)(2,1)S(1)}, bf16[2048,1536]{1,0:T(8,128)(2,1)}, u32[]{:S(2)}) copy-start(bf16[2048,1536]{1,0:T(8,128)(2,1)} %get-tuple-element.66) | copy-start | bytes 18874372
  274.6 6.3 %copy-start.9 = (bf16[192,2048]{1,0:T(8,128)(2,1)S(1)}, bf16[192,2048]{1,0:T(8,128)(2,1)}, u32[]{:S(2)}) copy-start(bf16[192,2048]{1,0:T(8,128)(2,1)} %get-tuple-element.60.gated_ref) | copy-start | bytes 2359300
  280.9 2.2 copy-start.5
  391.6 9.1 %copy-start.1 = (bf16[384,24]{0,1:T(8,128)(2,1)S(1)}, bf16[384,24]{0,1:T(8,128)(2,1)}, u32[]{:S(2)}) copy-start(bf16[384,24]{0,1:T(8,128)(2,1)} %param.25) | copy-start | bytes 55300
Sparse Core Ops, SparseCore 0:
  84.4 95.5 all-gather.1
  273.7 35.7 reduce-scatter.2
  317.8 28.6 reduce-scatter.4

commit v5 on v4

--- a/solution.py
+++ b/solution.py
@@ -400,6 +400,26 @@
     pl.semaphore_wait(sem, len(devices))
 
 
+def signal_line(devices, depth):
+    c, s, f = here()
+    sem = pltpu.get_barrier_semaphore()
+    for device in devices:
+        pl.semaphore_signal(sem, inc=1, device_id=device, device_id_type=MESH)
+
+    @pl.when(f < depth - 1)
+    def _():
+        up = (c, s, lax.rem(f + 1, depth))
+        pl.semaphore_signal(sem, inc=1, device_id=up, device_id_type=MESH)
+
+    @pl.when(f > 0)
+    def _():
+        down = (c, s, lax.rem(f + depth - 1, depth))
+        pl.semaphore_signal(sem, inc=1, device_id=down, device_id_type=MESH)
+
+    neighbours = lax.div(f + depth - 1, depth) + lax.div(2 * depth - 2 - f, depth)
+    return len(devices) + neighbours
+
+
 def rows_of(index, count):
     return pl.ds(pl.multiple_of(index * count, count), count)
 
@@ -486,14 +506,7 @@
             pltpu.SemaphoreType.DMA((10,)),
         ]
 
-    @staticmethod
-    def tail_scratch(n, w):
-        full = PairSum.scratch(n, w)
-        return full[:1] + full[3:]
-
     def __init__(self, refs):
-        if len(refs) == 5:
-            refs = (refs[0], None, None) + tuple(refs[1:])
         self.own, self.near, self.out, self.far, self.last, self.send, self.recv = refs
         self.x, self.y, self.sib = partners()
         self.n, w = self.own.shape[1], self.own.shape[2]
@@ -566,31 +579,71 @@
         self.add(1, self.right, 3)
         self.bx.start()
 
-    def start(self):
-        for made in (self.fx, self.fy, self.nx, self.ny):
-            made.start()
-
     def arrive(self):
-        if self.near is not None:
-            self.to_sibling(3).wait_recv()
+        self.to_sibling(3).wait_recv()
         for made in (self.nx, self.ny, self.by, self.bx):
             made.wait_recv()
 
     def total(self, j, step):
         r = rows_of(j, step)
-        total = self.own[3, r, :].astype(F32)
-        if self.near is not None:
-            total = total + self.near[3, r, :].astype(F32)
+        total = self.own[3, r, :].astype(F32) + self.near[3, r, :].astype(F32)
         a = jnp.concatenate([self.far[0, r, :], self.far[2, r, :]], axis=1).astype(F32)
         b = jnp.concatenate([self.last[0, r, :], self.last[1, r, :]], axis=1).astype(F32)
         return total + a + b
 
-    def finish(self):
+    def finish_plane(self):
         for made in (self.fx, self.fy, self.nx, self.ny, self.by, self.bx):
             made.wait_send()
-        if self.near is not None:
-            for i in (2, 3):
-                self.to_sibling(i).wait_send()
+
+    def finish(self):
+        self.finish_plane()
+        for i in (2, 3):
+            self.to_sibling(i).wait_send()
+
+
+class PairTail:
+    @staticmethod
+    def scratch(n, w):
+        return [
+            pltpu.VMEM((3, n, w), BF),
+            pltpu.VMEM((4, n, w // 2), BF),
+            pltpu.SemaphoreType.DMA((4,)),
+            pltpu.SemaphoreType.DMA((4,)),
+        ]
+
+    def __init__(self, refs):
+        self.own, self.far, send, recv = refs
+        x, y, sib = partners()
+        w = self.own.shape[2]
+        left, right = pl.ds(0, w // 2), pl.ds(w // 2, w // 2)
+        self.made = [
+            REMOTE(src, self.far.at[i], send.at[i], recv.at[i], device, MESH)
+            for i, (src, device) in enumerate((
+                (self.own.at[0, :, left], x),
+                (self.own.at[0, :, right], x),
+                (self.own.at[1, :, left], y),
+                (self.own.at[1, :, right], y),
+            ))
+        ]
+
+    def start(self):
+        for made in self.made:
+            made.start()
+
+    def arrive(self):
+        for made in self.made:
+            made.wait_recv()
+
+    def total(self, j, step):
+        r = rows_of(j, step)
+        total = self.own[2, r, :].astype(F32)
+        a = jnp.concatenate([self.far[0, r, :], self.far[1, r, :]], axis=1).astype(F32)
+        b = jnp.concatenate([self.far[2, r, :], self.far[3, r, :]], axis=1).astype(F32)
+        return total + a + b
+
+    def finish(self):
+        for made in self.made:
+            made.wait_send()
 
 
 def wait_for(i, loads):
@@ -608,6 +661,10 @@
 
 
 STEP = 32
+
+
+def gain_row(ref):
+    return ref[...].reshape(1, ref.shape[0])
 
 
 def mean_square_inverse(values):
@@ -641,10 +698,9 @@
     def gets(self, distance, up):
         return self.f >= distance if up else self.f + distance < self.depth
 
-    def start(self):
-        for i in range(len(self.own)):
-            for up in (True, False):
-                pl.when(self.may_send(1, up))(self.copy(i, 1, up).start)
+    def start(self, i):
+        for up in (True, False):
+            pl.when(self.may_send(1, up))(self.copy(i, 1, up).start)
 
     def pass_on(self, distance):
         for i in range(len(self.own)):
@@ -736,17 +792,50 @@
 
 
 def enter_kernel(
-    tok_ref, dy_ref, gain_ref, attn_ref, forget_ref, out_w_ref,
-    normed_ref, dy_all_ref, w_attn_ref, w_out_ref, cat_ref,
-    mine, forget_all, normed, turned, s0, r0, s1, r1, sz, rz, so, ro, l0, *, depth,
+    tok_ref, dy_ref, gain_ref, bias_ref, forget_ref,
+    query_ref, key_ref, value_ref, outgate_ref, gate_ref, up_ref, down_ref, out_w_ref,
+    normed_ref, dy_all_ref, w_attn_ref, w_out_ref, cat_ref, mlp_ref,
+    mine, windows, attn, own_forget, forget_all, mlp, normed, turned, cat,
+    s0, r0, s1, r1, sz, rz, so, ro, l0, l1, l2, *, depth, heads,
 ):
     c, s, f = here()
-    lines = [(c, s, lax.rem(f + 1, depth)), (c, s, lax.rem(f + depth - 1, depth))]
-    greet(partners() + lines)
+    t = c * 4 + s
     n = tok_ref.shape[0]
-    shard, cols = attn_ref.shape
+    shard, cols = attn.shape
+    hw = cols // 4
+    fw = mlp.shape[1] // 3
+    base = ((t * hw) // 128) * 128
+    window = pl.ds(pl.multiple_of(base, 128), windows.shape[2])
+    slices = [
+        pltpu.make_async_copy(ref.at[:, window], windows.at[i], l2.at[i])
+        for i, ref in enumerate((query_ref, key_ref, value_ref, outgate_ref))
+    ]
+    hidden = pl.ds(pl.multiple_of(t * fw, fw), fw)
+    mlp_loads = [
+        pltpu.make_async_copy(ref.at[:, hidden], mlp.at[:, pl.ds(i * fw, fw)], l2.at[4 + i])
+        for i, ref in enumerate((gate_ref, up_ref, down_ref))
+    ]
+    for made in slices + mlp_loads:
+        made.start()
+    greeted = signal_line(partners(), depth)
+    gain = gain_ref[...].reshape(1, gain_ref.shape[0])
+
+    def body(i, carry):
+        r = rows_of(i, STEP)
+        v = tok_ref[r, :].astype(F32)
+        mine[r, :] = (v * mean_square_inverse(v) * gain).astype(BF)
+        return carry
+
+    lax.fori_loop(0, n // STEP, body, 0)
+    a = lax.broadcasted_iota(jnp.int32, (own_forget.shape[0], forget_ref.shape[1]), 0)
+    b = lax.broadcasted_iota(jnp.int32, (own_forget.shape[0], forget_ref.shape[1]), 1)
+    pick = jnp.where((b == a + t * heads) & (a < heads), 1.0, 0.0).astype(BF)
+    own_forget[...] = dot(pick, forget_ref[...], 1, 1).astype(BF)
+    for made in slices:
+        made.wait()
+
     step = shard // WEIGHT_PIECES
-    own = [attn_ref.at[pl.ds(i * step, step)] for i in range(WEIGHT_PIECES)] + [forget_ref]
+    own = [attn.at[pl.ds(i * step, step)] for i in range(WEIGHT_PIECES)] + [own_forget]
 
     def slot(i, owner):
         if i == WEIGHT_PIECES:
@@ -755,9 +844,23 @@
         return w_attn_ref.at[rows, pl.ds(0, cols)]
 
     line = Line(own, slot, sz, rz, depth)
-    line.start()
+    pl.semaphore_wait(pltpu.get_barrier_semaphore(), greeted)
+    first = Gather(mine, normed_ref, s0, r0)
+    second = Gather(dy_ref, dy_all_ref, s1, r1)
+    first.start()
+    for i in range(WEIGHT_PIECES):
+        rows = slice(i * step, (i + 1) * step)
+        for begin in (0, 64):
+
+            @pl.when(t * hw - base == begin)
+            def _(rows=rows, begin=begin):
+                attn[rows, :] = jnp.concatenate(
+                    [windows[k, rows, begin : begin + hw].astype(F32) for k in range(4)], axis=1
+                ).astype(BF)
+
+        line.start(i)
+    line.start(WEIGHT_PIECES)
     heads_rows = w_out_ref.shape[0]
-    t = c * 4 + s
     origin = (t * heads_rows) // shard
     spread = Spread(
         out_w_ref.at[pl.ds(pl.multiple_of(t * heads_rows - origin * shard, heads_rows), heads_rows)],
@@ -765,29 +868,20 @@
     )
     keep = [
         pltpu.make_async_copy(
-            attn_ref,
+            attn,
             w_attn_ref.at[pl.ds(pl.multiple_of(f * shard, shard), shard), pl.ds(0, cols)],
             l0.at[2],
         ),
-        pltpu.make_async_copy(forget_ref, forget_all.at[f], l0.at[3]),
-    ]
-
-    def body(i, carry):
-        r = rows_of(i, STEP)
-        v = tok_ref[r, :].astype(F32)
-        mine[r, :] = (v * mean_square_inverse(v) * gain_ref[...]).astype(BF)
-        return carry
-
-    lax.fori_loop(0, n // STEP, body, 0)
-    first = Gather(mine, normed_ref, s0, r0)
-    second = Gather(dy_ref, dy_all_ref, s1, r1)
-    keep += [
+        pltpu.make_async_copy(own_forget, forget_all.at[f], l0.at[3]),
         pltpu.make_async_copy(mine, first.block(0), l0.at[0]),
         pltpu.make_async_copy(dy_ref, second.block(0), l0.at[1]),
     ]
-    first.start()
     for made in keep:
         made.start()
+    for made in mlp_loads:
+        made.wait()
+    mlp_store = pltpu.make_async_copy(mlp, mlp_ref, l2.at[7])
+    mlp_store.start()
     line.pass_on(1)
     spread.start(l0.at[4])
     first.relay()
@@ -800,8 +894,16 @@
     load.start()
     keep[0].wait()
     keep[1].wait()
-
-    def add_shard(owner, begin):
+    r = lax.broadcasted_iota(jnp.int32, (16, 1), 0)
+    bias = jnp.zeros((16, 1), F32)
+    for h in range(heads):
+        bias = jnp.where(r == h, bias_ref[t * heads + h], bias)
+
+    def store(i):
+        tokens = rows_of(i, 512)
+        return pltpu.make_async_copy(cat.at[:, tokens], cat_ref.at[:, tokens], l1.at[i])
+
+    def add_shard(owner, begin, end):
         small = forget_all[owner].astype(F32)
         tall = jnp.concatenate([small, jnp.zeros((128 - small.shape[0], shard), F32)], axis=0)
         rows = rows_of(owner, shard)
@@ -812,9 +914,12 @@
             tokens = rows_of(i, 512)
             part = dot(turned[...], normed[tokens, rows], 1, 1)
             if begin:
-                cat_ref[:, tokens] = part
+                cat[:, tokens] = part
             else:
-                cat_ref[:, tokens] += part
+                cat[:, tokens] += part
+            if end:
+                cat[4 * hw : 4 * hw + 16, tokens] += bias
+                store(i).start()
             return unused
 
         lax.fori_loop(0, normed.shape[0] // 512, tile, 0)
@@ -823,55 +928,70 @@
     upper = lax.div(f, half)
     load.wait()
     for k in range(1, depth - 1):
-        add_shard(jnp.int32(k), k == 1)
-    add_shard(upper * (depth - 1), False)
+        add_shard(jnp.int32(k), k == 1, False)
+    add_shard(upper * (depth - 1), False, False)
     second.relay()
     spread.pass_on()
     line.pass_on(3)
-    add_shard((1 - upper) * (depth - 1), False)
+    add_shard((1 - upper) * (depth - 1), False, True)
     second.finish()
     line.finish()
     keep[3].wait()
     spread.finish(l0.at[4])
-
-
-def enter(tokens, cotangent, gain, own_attn, own_forget, output_weight, depth, heads_rows):
+    mlp_store.wait()
+    for i in range(normed.shape[0] // 512):
+        store(i).wait()
+
+
+def enter(tokens, cotangent, gain, bias, forget_weight, attn_weights, mlp_weights, out_weight, depth):
     n, w = tokens.shape
-    shard, cols = own_attn.shape
+    shard, head_count = forget_weight.shape
+    heads = head_count // 8
+    hw = w // 8
+    cols, fw = 4 * hw, mlp_weights[0].shape[1] // 8
     whole = jax.ShapeDtypeStruct((8 * n, w), BF)
     dma = pltpu.SemaphoreType.DMA((Gather.sems,))
     line = pltpu.SemaphoreType.DMA((2, depth - 1, WEIGHT_PIECES + 1))
     vmem = pl.BlockSpec(memory_space=pltpu.VMEM)
+    smem = pl.BlockSpec(memory_space=pltpu.SMEM)
     anywhere = pl.BlockSpec(memory_space=pl.ANY)
     return pl.pallas_call(
-        functools.partial(enter_kernel, depth=depth),
+        functools.partial(enter_kernel, depth=depth, heads=heads),
         name="enter",
         out_shape=(
             whole,
             whole,
             jax.ShapeDtypeStruct((depth * shard, cols + 128), BF),
-            jax.ShapeDtypeStruct((heads_rows, w), BF),
+            jax.ShapeDtypeStruct((hw, w), BF),
             jax.ShapeDtypeStruct((cols + 128, 8 * n), F32),
+            jax.ShapeDtypeStruct((shard, 3 * fw), BF),
         ),
-        in_specs=[vmem] * 5 + [anywhere],
-        out_specs=[anywhere, anywhere, vmem, anywhere, vmem],
+        in_specs=[vmem, vmem, vmem, smem, vmem] + [anywhere] * 8,
+        out_specs=[anywhere, anywhere, vmem, anywhere, anywhere, anywhere],
         scratch_shapes=[
             pltpu.VMEM((n, w), BF),
-            pltpu.VMEM((depth,) + own_forget.shape, BF),
+            pltpu.VMEM((4, shard, hw + 64), BF),
+            pltpu.VMEM((shard, cols), BF),
+            pltpu.VMEM((16, shard), BF),
+            pltpu.VMEM((depth, 16, shard), BF),
+            pltpu.VMEM((shard, 3 * fw), BF),
             pltpu.VMEM((8 * n, w), BF),
             pltpu.VMEM((cols + 128, shard), BF),
+            pltpu.VMEM((cols + 128, 8 * n), F32),
             dma, dma, dma, dma, line, line,
             pltpu.SemaphoreType.DMA((2, OUT_PIECES)),
             pltpu.SemaphoreType.DMA((OUT_PIECES,)),
             pltpu.SemaphoreType.DMA((6,)),
+            pltpu.SemaphoreType.DMA((8 * n // 512,)),
+            pltpu.SemaphoreType.DMA((8,)),
         ],
         compiler_params=pltpu.CompilerParams(
             collective_id=1, has_side_effects=True, vmem_limit_bytes=VMEM_BYTES
         ),
         cost_estimate=pl.CostEstimate(
-            flops=50_000_000, bytes_accessed=4 * 8 * n * w * 2, transcendentals=0
+            flops=2 * 8 * n * w * cols, bytes_accessed=4 * 8 * n * w * 2, transcendentals=0
         ),
-    )(tokens, cotangent, gain[None], own_attn, own_forget, output_weight)
+    )(tokens, cotangent, gain, bias, forget_weight, *attn_weights, *mlp_weights, out_weight)
 
 
 TILE = 256
@@ -915,7 +1035,7 @@
         r = rows_of(i, STEP)
         mid = tok_ref[r, :].astype(F32) + pairs.total(i, STEP)
         mid_ref[r, :] = mid
-        mine[r, :] = (mid * mean_square_inverse(mid) * gain_ref[...]).astype(BF)
+        mine[r, :] = (mid * mean_square_inverse(mid) * gain_row(gain_ref)).astype(BF)
         return carry
 
     lax.fori_loop(0, n // STEP, body, 0)
@@ -954,17 +1074,18 @@
             flops=2 * 8 * n * w * gated.shape[0], bytes_accessed=4 * 8 * n * w * 2,
             transcendentals=0,
         ),
-    )(gated, w_out, tokens, gain[None])
+    )(gated, w_out, tokens, gain)
 
 
 TERM_PIECES = 4
 
 
 class LineSum:
-    def __init__(self, term, got, send, recv, depth):
+    def __init__(self, term, got, send, recv, depth, pieces=TERM_PIECES):
         self.term, self.got, self.send, self.recv, self.depth = term, got, send, recv, depth
         self.c, self.s, self.f = here()
-        self.n = term.shape[0] // TERM_PIECES
+        self.pieces = pieces
+        self.n = term.shape[0] // pieces
 
     def source(self, i, g):
         return self.term.at[pl.ds(i * self.n, self.n), g]
@@ -973,7 +1094,7 @@
         to = lax.rem(self.f + (1 if k == 0 else self.depth - 1), self.depth)
         return REMOTE(
             src,
-            self.got.at[k, g, pl.ds(i * self.n, self.n)],
+            self.got.at[k, g + k - 1, pl.ds(i * self.n, self.n)],
             self.send.at[k, g, i],
             self.recv.at[k, g, i],
             (self.c, self.s, to),
@@ -993,8 +1114,8 @@
 
     def add(self, k, g, i):
         rows = pl.ds(i * self.n, self.n)
-        total = self.got[k, g, rows].astype(F32) + self.term[rows, g].astype(F32)
-        self.got[k, g, rows] = total.astype(BF)
+        total = self.got[k, g + k - 1, rows].astype(F32) + self.term[rows, g].astype(F32)
+        self.got[k, g + k - 1, rows] = total.astype(BF)
 
     def pass_on(self, i, n, hop):
         for k in (0, 1):
@@ -1003,17 +1124,17 @@
 
             @pl.when(self.f == at)
             def _(k=k, g=g):
-                made = self.copy(k, g, i, self.got.at[k, g, pl.ds(i * self.n, self.n)])
+                made = self.copy(k, g, i, self.got.at[k, g + k - 1, pl.ds(i * self.n, self.n)])
                 made.wait_recv()
                 self.add(k, g, i)
                 made.start()
 
     def steps(self):
         todo = [
-            (n * TERM_PIECES + i + 2 * (hop - 1), -hop, i, n, hop)
+            (n * self.pieces + i + 2 * (hop - 1), -hop, i, n, hop)
             for n in range(self.depth - 2)
             for hop in range(1, self.depth - 1 - n)
-            for i in range(TERM_PIECES)
+            for i in range(self.pieces)
         ]
         return [step[2:] for step in sorted(todo)]
 
@@ -1027,14 +1148,14 @@
                 for k in (0, 1):
                     if g != (0 if k == 0 else self.depth - 1):
                         self.copy(k, g, i, self.source(i, g)).wait_recv()
-                        total = total + self.got[k, g, rows].astype(F32)
+                        total = total + self.got[k, g + k - 1, rows].astype(F32)
                 out[rows] = total.astype(BF)
 
     def finish(self):
         for k in (0, 1):
             for g in self.targets(k):
                 beyond = self.f < g if k == 0 else self.f > g
-                for i in range(TERM_PIECES):
+                for i in range(self.pieces):
                     pl.when(beyond)(self.copy(k, g, i, self.source(i, g)).wait_send)
 
 
@@ -1083,13 +1204,13 @@
 
 
 def ffn_kernel(
-    nm_ref, dy_all_ref, w_ref, dy_ref, mid_ref, gain_ref,
-    grad_mid_ref, gain_term_ref, branch_ref, down_ref, up_rows_ref, low_term_ref,
-    nm, dy, w, grads, term, got, rows_sum, mine, down_own, down_near, down_out,
+    nm_ref, dy_all_ref, w_ref, mid_ref, gain_ref, gated_ref, w_out_ref,
+    grad_mid_ref, gain_term_ref, gg_ref, out_term_ref, down_ref, up_rows_ref, low_term_ref,
+    nm, dy, w, grads, term, got, rows_sum, mine, branch, stage, down_own, down_near, down_far,
     l0, l1, l2, s1, r1, s2, r2, s3, r3, s4, r4, *refs, depth,
 ):
     c, s, f = here()
-    n, width = dy_ref.shape
+    n, width = mid_ref.shape
     fw = w.shape[1] // 3
     pairs = PairSum(refs)
     loads = []
@@ -1107,9 +1228,8 @@
             loads[-1] += made
         else:
             loads.append(made)
-    greet([p[:3] for p in plane_peers()] + [
-        (c, s, lax.rem(f + 1, depth)), (c, s, lax.rem(f + depth - 1, depth))
-    ])
+    greeted = signal_line([p[:3] for p in plane_peers()], depth)
+    pl.semaphore_wait(pltpu.get_barrier_semaphore(), greeted)
     w_load.wait()
 
     def one_pair(i, unused):
@@ -1151,6 +1271,10 @@
     for k in range(1, depth - 1):
         for i in range(TERM_PIECES):
             line.start_piece(i, k)
+    hw = gated_ref.shape[0]
+    w_out, out_term = nm.at[pl.ds(0, hw)], nm.at[pl.ds(hw, hw)]
+    w_out_load = pltpu.make_async_copy(w_out_ref, w_out, l2.at[9])
+    w_out_load.start()
     todo = line.steps()
     pairs.arrive()
 
@@ -1159,17 +1283,18 @@
         grad = pairs.total(j, STEP)
         mid = mid_ref[r, :]
         inverse = mean_square_inverse(mid)
-        weighted = grad * gain_ref[...]
+        weighted = grad * gain_row(gain_ref)
         back = inverse * weighted - mid * inverse**3 * jnp.mean(
             weighted * mid, axis=1, keepdims=True
         )
-        grad_mid = dy_ref[r, :].astype(F32) + back
+        own_dy = dy[pl.ds(pl.multiple_of(7 * n + j * STEP, STEP), STEP), :]
+        grad_mid = own_dy.astype(F32) + back
         grad_mid_ref[r, :] = grad_mid
         mine[r, :] = grad_mid.astype(BF)
         return carry + jnp.sum(grad * mid * inverse, axis=0, keepdims=True)
 
     gain_term_ref[...] = lax.fori_loop(0, n // STEP, body, jnp.zeros((1, width), F32))
-    gather = Gather(mine, branch_ref, s1, r1)
+    gather = Gather(mine, branch, s1, r1)
     gather.start()
     keep = pltpu.make_async_copy(mine, gather.block(0), l0.at[8])
     keep.start()
@@ -1184,8 +1309,11 @@
 
     def down_copy(i):
         return REMOTE(
-            down_out.at[lax.rem(i, 2)], down_near.at[i], s3.at[i], r3.at[i], pairs.sib, MESH
-        )
+            pairs.out.at[lax.rem(i, 2)], down_near.at[i], s3.at[i], r3.at[i], pairs.sib, MESH
+        )
+
+    for i in (2, 3):
+        pairs.to_sibling(i).wait_send()
 
     def down_pair(i, unused):
         rows = rows_of(i, 2 * n)
@@ -1197,7 +1325,7 @@
         for t in range(width // TILE):
             feats = pl.ds(t * TILE, TILE)
             part = dot(grads[rows, 2 * fw :], w[feats, 2 * fw :], 1, 1).astype(BF)
-            down_out[lax.rem(i, 2), :, feats] = part[:n]
+            pairs.out[lax.rem(i, 2), :, feats] = part[:n]
             down_own[i, :, feats] = part[n:]
         down_copy(i).start()
         return unused
@@ -1219,36 +1347,82 @@
         return lax.fori_loop(0, n // 32, body, unused)
 
     lax.fori_loop(0, 4, down_sum, 0)
+    down_fx = REMOTE(
+        down_own.at[0, :, pairs.left], down_far.at[0], s3.at[4], r3.at[4], pairs.x, MESH
+    )
+    down_fy = REMOTE(
+        down_own.at[0, :, pairs.right], down_far.at[1], s3.at[5], r3.at[5], pairs.y, MESH
+    )
+    down_fx.start()
+    down_fy.start()
+    gather.finish()
+    keep.wait()
+
+    def gg_copy(i):
+        return pltpu.make_async_copy(
+            stage.at[lax.rem(i, 2)], gg_ref.at[:, rows_of(i, stage.shape[2])], l2.at[lax.rem(i, 2)]
+        )
+
+    def gg_tile(i, unused):
+        @pl.when(i >= 2)
+        def _():
+            gg_copy(i - 2).wait()
+
+        stage[lax.rem(i, 2)] = dot(w_out[...], branch[rows_of(i, stage.shape[2]), :], 1, 1)
+        gg_copy(i).start()
+        return unused
+
+    tiles = branch.shape[0] // stage.shape[2]
+    w_out_load.wait()
+    lax.fori_loop(0, tiles, gg_tile, 0)
+    out_term[...] = dot(gated_ref[...], branch[...], 1, 0).astype(BF)
+    out_store = pltpu.make_async_copy(out_term, out_term_ref, l2.at[10])
+    out_store.start()
+    exchange = Exchange(rows_sum, up_rows_ref, s4, r4)
+    down_fx.wait_recv()
+    down_fy.wait_recv()
+
+    def down_add(at, cols, slot):
+        def body(j, carry):
+            r = rows_of(j, 32)
+            total = down_own[at, r, cols].astype(F32) + down_far[slot, r, :].astype(F32)
+            down_own[at, r, cols] = total.astype(BF)
+            return carry
+
+        lax.fori_loop(0, n // 32, body, 0)
+
+    down_add(2, pairs.left, 0)
+    down_add(1, pairs.right, 1)
     stores = [
-        pltpu.make_async_copy(
-            down_own.at[i], down_ref.at[flip(s, k) if k else s], l1.at[i]
-        )
-        for i, k in enumerate(PairSum.order)
+        pltpu.make_async_copy(down_own.at[i], down_ref.at[i - 1], l1.at[i]) for i in (1, 2, 3)
     ]
     for made in stores:
         made.start()
-    gather.finish()
-    exchange = Exchange(rows_sum, up_rows_ref, s4, r4)
     for i in range(TERM_PIECES):
         line.collect(i, rows_sum)
         for j in range(i * per, (i + 1) * per):
             exchange.push(j)
-    keep.wait()
     exchange.finish()
     for made in stores:
         made.wait()
-    pairs.finish()
+    for i in (2, 3):
+        gg_copy(jnp.int32(tiles - 4 + i)).wait()
+    out_store.wait()
+    down_fx.wait_send()
+    down_fy.wait_send()
+    pairs.finish_plane()
     for i in (2, 3):
         down_copy(i).wait_send()
     line.finish()
 
 
-def ffn(normed_all, cotangent_all, weights, cotangent, mid, gain, depth):
+def ffn(normed_all, cotangent_all, weights, mid, gain, gated, w_out, depth):
     n, width = mid.shape
     fw = weights.shape[1] // 3
     r = width // (8 * depth)
+    hw = gated.shape[0]
     dma = pltpu.SemaphoreType.DMA((16,))
-    four = pltpu.SemaphoreType.DMA((4,))
+    six = pltpu.SemaphoreType.DMA((6,))
     eight = pltpu.SemaphoreType.DMA((8,))
     line = pltpu.SemaphoreType.DMA((2, depth, TERM_PIECES))
     vmem = pl.BlockSpec(memory_space=pltpu.VMEM)
@@ -1259,53 +1433,53 @@
         out_shape=(
             jax.ShapeDtypeStruct((n, width), F32),
             jax.ShapeDtypeStruct((1, width), F32),
-            jax.ShapeDtypeStruct((8 * n, width), BF),
-            jax.ShapeDtypeStruct((4, n, width), BF),
+            jax.ShapeDtypeStruct((hw, 8 * n), F32),
+            jax.ShapeDtypeStruct((hw, width), BF),
+            jax.ShapeDtypeStruct((3, n, width), BF),
             jax.ShapeDtypeStruct((8, r, 2 * fw), BF),
             jax.ShapeDtypeStruct((depth, 8, r, fw), BF),
         ),
-        in_specs=[anywhere] * 3 + [vmem] * 3,
-        out_specs=[vmem, vmem, anywhere, anywhere, vmem, vmem],
+        in_specs=[anywhere] * 3 + [vmem] * 3 + [anywhere],
+        out_specs=[vmem, vmem, anywhere, anywhere, anywhere, vmem, vmem],
         scratch_shapes=[
             pltpu.VMEM((8 * n, width), BF),
             pltpu.VMEM((8 * n, width), BF),
             pltpu.VMEM((width, 3 * fw), BF),
             pltpu.VMEM((8 * n, 3 * fw), BF),
             pltpu.VMEM((8, depth, r, 2 * fw), BF),
-            pltpu.VMEM((2, depth, 8, r, 2 * fw), BF),
+            pltpu.VMEM((2, depth - 1, 8, r, 2 * fw), BF),
             pltpu.VMEM((8, r, 2 * fw), BF),
             pltpu.VMEM((n, width), BF),
+            pltpu.VMEM((8 * n, width), BF),
+            pltpu.VMEM((2, hw, 256), F32),
             pltpu.VMEM((4, n, width), BF),
             pltpu.VMEM((4, n, width), BF),
-            pltpu.VMEM((2, n, width), BF),
-            dma, dma, dma, dma, dma, line, line, four, four, eight, eight,
+            pltpu.VMEM((2, n, width // 2), BF),
+            dma, dma, dma, dma, dma, line, line, six, six, eight, eight,
         ]
         + PairSum.scratch(n, width),
         compiler_params=pltpu.CompilerParams(
-            collective_id=3, has_side_effects=True, vmem_limit_bytes=63 * 1024 * 1024
+            collective_id=3, has_side_effects=True, vmem_limit_bytes=67_043_328
         ),
         cost_estimate=pl.CostEstimate(
             flops=2 * 8 * n * width * fw * 9, bytes_accessed=4 * 8 * n * width * 2,
             transcendentals=0,
         ),
-    )(normed_all, cotangent_all, weights, cotangent, mid, gain[None])
+    )(normed_all, cotangent_all, weights, mid, gain, gated, w_out)
 
 
 def leave_kernel(
-    normed_ref, cat_ref, w_ref, down_ref, tok_ref, grad_mid_ref, mid_ref, gain_ref, small_ref,
-    low_ref,
-    grad_ref, small_sum_ref, out_ref, attn_rows_ref, low_rows_ref,
-    normed, cat, turned, w, small, plane_small, line_small, term, got, rows,
-    l0, l1, s2, r2, s3, r3, s5, r5, s6, r6, *refs, depth,
+    normed_ref, cat_ref, w_ref, down_ref, tok_ref, grad_mid_ref, mid_ref, gain_ref,
+    mlp_term_ref, bias_grad_ref, low_ref, wide_ref,
+    grad_ref, small_sum_ref, out_ref, attn_rows_ref, low_rows_ref, wide_rows_ref,
+    normed, cat, turned, w, small, plane_small, line_small, term, got, rows, wide_got,
+    l0, l1, s2, r2, s3, r3, s5, r5, s6, r6, s7, r7, *refs, depth, heads,
 ):
     c, s, f = here()
     n, width = tok_ref.shape
     pairs = PairSum(refs[:7])
-    down = PairSum(refs[7:])
-    down_loads = [
-        pltpu.make_async_copy(down_ref.at[flip(s, k) if k else s], down.own.at[i], l0.at[9 + i])
-        for i, k in enumerate(PairSum.order)
-    ]
+    down = PairTail(refs[7:])
+    down_loads = [pltpu.make_async_copy(down_ref, down.own, l0.at[9])]
     loads = []
     for i, block in enumerate(PairSum.blocks(c, s)):
         src, dst = pl.ds(pl.multiple_of(block * n, n), n), pl.ds(i * n, n)
@@ -1318,6 +1492,9 @@
     peers = plane_peers()
     line_peers = [(c, s, lax.rem(f + k, depth), k) for k in range(1, depth)]
     greet([p[:3] for p in peers + line_peers])
+    wide = LineSum(wide_ref, wide_got, s7, r7, depth, 1)
+    for k in range(depth - 1):
+        wide.start_piece(0, k)
     line = LineSum(term, got, s3, r3, depth)
     low_rows = Exchange(low_ref, low_rows_ref, s6, r6)
     deep = width // TERM_PIECES
@@ -1354,11 +1531,12 @@
         return unused
 
     todo = line.steps()
+    for step in wide.steps():
+        wide.pass_on(*step)
     lax.fori_loop(0, 4, one_pair, 0)
     for step in todo[4:6]:
         line.pass_on(*step)
     pairs.relay()
-    down.relay()
     for step in todo[6:]:
         line.pass_on(*step)
     attn_rows = Exchange(rows, attn_rows_ref, s5, r5)
@@ -1375,7 +1553,7 @@
         grad = pairs.total(i, STEP)
         tok = tok_ref[r, :].astype(F32)
         inverse = mean_square_inverse(tok)
-        weighted = grad * gain_ref[...]
+        weighted = grad * gain_row(gain_ref)
         back = inverse * weighted - tok * inverse**3 * jnp.mean(
             weighted * tok, axis=1, keepdims=True
         )
@@ -1384,10 +1562,16 @@
 
     gain_term = lax.fori_loop(0, n // STEP, body, jnp.zeros((1, width), F32))
     lane = small.shape[1]
-    small[...] = small_ref[...]
-    for k in range(width // lane):
+    place = c * 4 + s
+    for k in range(3):
         small[k : k + 1, :] = gain_term[:, k * lane : (k + 1) * lane]
-    place = c * 4 + s
+        small[3 + k : 4 + k, :] = mlp_term_ref[:, k * lane : (k + 1) * lane]
+    at = lax.broadcasted_iota(jnp.int32, (1, lane), 1)
+    bias_row = jnp.zeros((1, lane), F32)
+    for h in range(heads):
+        bias_row = jnp.where(at == place * heads + h, bias_grad_ref[h : h + 1, 0:1], bias_row)
+    small[6:7, :] = bias_row
+    small[7:8, :] = jnp.zeros((1, lane), F32)
     plane_small[pl.ds(place, 1)] = small[...][None]
     sent = []
     for core, other_s, other_f, k in peers:
@@ -1396,6 +1580,7 @@
         )
         made.start()
         sent.append(made)
+    wide.collect(0, wide_rows_ref)
     collect(0)
     collect(1)
     for made in sent:
@@ -1431,11 +1616,15 @@
     pairs.finish()
     down.finish()
     line.finish()
+    wide.finish()
     low_rows.finish()
     attn_rows.finish()
 
 
-def leave(normed, cat, w_attn, down_sum, tokens, grad_mid, mid, gain, small, low_rows, depth):
+def leave(
+    normed, cat, w_attn, down_sum, tokens, grad_mid, mid, gain, mlp_term, bias_grad, low_rows, wide,
+    depth, heads,
+):
     n, w = grad_mid.shape
     plane = 8
     cols = w_attn.shape[1]
@@ -1444,42 +1633,48 @@
     dma = pltpu.SemaphoreType.DMA((16,))
     eight = pltpu.SemaphoreType.DMA((8,))
     line = pltpu.SemaphoreType.DMA((2, depth, TERM_PIECES))
+    one = pltpu.SemaphoreType.DMA((2, depth, 1))
     vmem = pl.BlockSpec(memory_space=pltpu.VMEM)
     anywhere = pl.BlockSpec(memory_space=pl.ANY)
     return pl.pallas_call(
-        functools.partial(leave_kernel, depth=depth),
+        functools.partial(leave_kernel, depth=depth, heads=heads),
         name="leave",
         out_shape=(
             jax.ShapeDtypeStruct((n, w), F32),
-            jax.ShapeDtypeStruct(small.shape, F32),
+            jax.ShapeDtypeStruct((8, w // 3), F32),
             jax.ShapeDtypeStruct((n, w), BF),
             jax.ShapeDtypeStruct((plane, r, cols), BF),
             jax.ShapeDtypeStruct(low_rows.shape, BF),
+            jax.ShapeDtypeStruct((1,) + wide.shape[2:], BF),
         ),
-        in_specs=[anywhere] * 4 + [vmem] * 6,
-        out_specs=[vmem] * 5,
+        in_specs=[anywhere] * 4 + [vmem] * 8,
+        out_specs=[vmem] * 6,
         scratch_shapes=[
             pltpu.VMEM(normed.shape, BF),
             pltpu.VMEM(cat.shape, BF),
             pltpu.VMEM((2 * n, cols), BF),
             pltpu.VMEM(w_attn.shape, BF),
-            pltpu.VMEM(small.shape, F32),
-            pltpu.VMEM((8,) + small.shape, F32),
-            pltpu.VMEM((depth,) + small.shape, F32),
+            pltpu.VMEM((8, w // 3), F32),
+            pltpu.VMEM((8, 8, w // 3), F32),
+            pltpu.VMEM((depth, 8, w // 3), F32),
             pltpu.VMEM((plane, depth, r, cols), BF),
-            pltpu.VMEM((2, depth, plane, r, cols), BF),
+            pltpu.VMEM((2, depth - 1, plane, r, cols), BF),
             pltpu.VMEM((plane, r, cols), BF),
-            dma, dma, sems, sems, line, line, eight, eight, eight, eight,
+            pltpu.VMEM((2, depth - 1, 1) + wide.shape[2:], BF),
+            dma, dma, sems, sems, line, line, eight, eight, eight, eight, one, one,
         ]
         + PairSum.scratch(n, w)
-        + PairSum.tail_scratch(n, w),
+        + PairTail.scratch(n, w),
         compiler_params=pltpu.CompilerParams(
             collective_id=4, has_side_effects=True, vmem_limit_bytes=VMEM_BYTES
         ),
         cost_estimate=pl.CostEstimate(
             flops=4 * 8 * n * w * cols, bytes_accessed=4 * 8 * n * w * 2, transcendentals=0
         ),
-    )(normed, cat, w_attn, down_sum, tokens, grad_mid, mid, gain[None], small, low_rows)
+    )(
+        normed, cat, w_attn, down_sum, tokens, grad_mid, mid, gain, mlp_term, bias_grad, low_rows,
+        wide,
+    )
 
 
 def finish_kernel(
@@ -1499,18 +1694,18 @@
     for t in range(plane):
         pick = jnp.where((a + t * heads == b) & (a < heads), 1.0, 0.0).astype(BF)
         total = total + dot(attn_ref[t, :, 4 * hw : 4 * hw + 128], pick, 1, 0)
-    f_ref[...] = total[:, : f_ref.shape[1]]
-    o_ref[...] = out_w_ref[...].astype(F32)
+    f_ref[...] = total.T[: f_ref.shape[0]]
+    o_ref[...] = out_w_ref[0].astype(F32)
     for t in range(plane):
         cols = slice(t * fw, (t + 1) * fw)
         gate_ref[:, cols] = up_rows_ref[t, :, 0:fw].astype(F32)
         up_ref[:, cols] = up_rows_ref[t, :, fw:].astype(F32)
         down_ref[:, cols] = low_ref[t].astype(F32)
     lane = small_ref.shape[1]
-    count = gain1_ref.shape[1] // lane
+    count = gain1_ref.shape[0] // lane
     for k in range(count):
-        gain1_ref[:, k * lane : (k + 1) * lane] = small_ref[k : k + 1, :]
-        gain2_ref[:, k * lane : (k + 1) * lane] = small_ref[count + k : count + k + 1, :]
+        gain1_ref[k * lane : (k + 1) * lane] = small_ref[k, :]
+        gain2_ref[k * lane : (k + 1) * lane] = small_ref[count + k, :]
     bias_ref[...] = small_ref[2 * count : 2 * count + 1, 0 : bias_ref.shape[1]]
     out_ref[...] = block_ref[...]
     tokens_ref[...] = tok_grad_ref[...]
@@ -1523,14 +1718,14 @@
     vmem = pl.BlockSpec(memory_space=pltpu.VMEM)
     square = jax.ShapeDtypeStruct((r, plane * hw), F32)
     wide = jax.ShapeDtypeStruct((r, plane * fw), F32)
-    row = jax.ShapeDtypeStruct((1, w), F32)
+    row = jax.ShapeDtypeStruct((w,), F32)
     return pl.pallas_call(
         functools.partial(finish_kernel, hw=hw, heads=heads),
         name="finish",
         out_shape=(
             square, square, square, square,
-            jax.ShapeDtypeStruct((r, plane * heads), F32),
-            jax.ShapeDtypeStruct(out_w.shape, F32),
+            jax.ShapeDtypeStruct((plane * heads, r), F32),
+            jax.ShapeDtypeStruct(out_w.shape[1:], F32),
             wide, wide, wide, row, row,
             jax.ShapeDtypeStruct((1, plane * heads), F32),
             jax.ShapeDtypeStruct((n, w), BF),
@@ -1542,8 +1737,8 @@
     )(attn_rows, up_rows, low_rows, small, out_w, block_out, tokens_grad)
 
 
-BQ = 256
-BK = 256
+BQ = 512
+BK = 512
 AUG = 128
 
 
@@ -1568,20 +1763,19 @@
     return jnp.minimum(v, 0.0) - jnp.log1p(jnp.exp(-jnp.abs(v)))
 
 
-def doc_starts(ends_ref, pos):
-    start = jnp.zeros_like(pos)
-    for n in range(ends_ref.shape[0]):
-        end = ends_ref[n]
-        start = jnp.where(pos >= end, jnp.maximum(start, end), start)
+def doc_starts(lens_ref, pos):
+    start, end = jnp.zeros_like(pos), jnp.int32(0)
+    for n in range(lens_ref.shape[1]):
+        end = end + lens_ref[0, n]
+        start = jnp.where(pos >= end, end, start)
     return start
 
 
-def first_block(ends_ref, pos):
-    start = jnp.int32(0)
-    for n in range(ends_ref.shape[0]):
-        end = ends_ref[n]
-        start = jnp.where(pos >= end, jnp.maximum(start, end), start)
-    return start // BK
+def storage_of(place_ref, p):
+    found = jnp.int32(0)
+    for n in range(place_ref.shape[1]):
+        found = jnp.where(place_ref[0, n] == p, n, found)
+    return found
 
 
 def extend(prefix_row, sign_first):
@@ -1600,7 +1794,7 @@
     hw = heads * hd
     slabs = cat_ref.shape[1] // slab
     for p in range(slabs):
-        src = pl.ds(pl.multiple_of(place_ref[p] * slab, slab), slab)
+        src = pl.ds(pl.multiple_of(storage_of(place_ref, p) * slab, slab), slab)
         dst = pl.ds(p * slab, slab)
         for h in range(heads):
             q = cat_ref[h * hd : (h + 1) * hd, src].astype(BF).astype(F32)
@@ -1616,7 +1810,7 @@
 
 
 def attention_kernel(
-    place_ref, ends_ref, cat_ref, bias_ref,
+    place_ref, lens_ref, cat_ref,
     gated_ref, att_ref, exact_ref, lse_ref, prefix_ref,
     qa, ka, va, *, heads, hd, slab,
 ):
@@ -1626,8 +1820,8 @@
     tri = triangle(slab, False)
     carry = jnp.zeros((16, 1), F32)
     for p in range(slabs):
-        src = pl.ds(pl.multiple_of(place_ref[p] * slab, slab), slab)
-        pre = cat_ref[4 * hw : 4 * hw + 16, src] + bias_ref[:, 0:1]
+        src = pl.ds(pl.multiple_of(storage_of(place_ref, p) * slab, slab), slab)
+        pre = cat_ref[4 * hw : 4 * hw + 16, src]
         steps = log_sigmoid(pre).astype(BF)
         part = dot(steps, tri, 1, 0) + carry
         prefix_ref[:, p * slab : (p + 1) * slab] = part
@@ -1642,8 +1836,8 @@
     def one_query_block(qb, unused):
         q0 = pl.multiple_of(qb * BQ, BQ)
         pos = q0 + lax.broadcasted_iota(jnp.int32, (1, BQ), 1)
-        start = doc_starts(ends_ref, pos)
-        low = first_block(ends_ref, q0)
+        start = doc_starts(lens_ref, pos)
+        low = doc_starts(lens_ref, q0) // BK
         inside = lax.broadcasted_iota(jnp.int32, (BK, BQ), 0)
 
         def one_key_block(kb, held):
@@ -1666,8 +1860,8 @@
             (jnp.full((1, BQ), very_low, F32), jnp.zeros((1, BQ), F32), jnp.zeros((hd, BQ), F32))
             for _ in range(heads)
         )
-        done = lax.fori_loop(low, qb + 1, one_key_block, begin)
-        dst = pl.ds(pl.multiple_of(place_ref[qb // per] * slab + lax.rem(qb, per) * BQ, BQ), BQ)
+        done = lax.fori_loop(low, (q0 + BQ + BK - 1) // BK, one_key_block, begin)
+        dst = pl.ds(pl.multiple_of(storage_of(place_ref, qb // per) * slab + lax.rem(qb, per) * BQ, BQ), BQ)
         for h in range(heads):
             m, l, acc = done[h]
             lse_ref[h : h + 1, pl.ds(q0, BQ)] = m + jnp.log(l)
@@ -1683,7 +1877,7 @@
     lax.fori_loop(0, tokens // BQ, one_query_block, 0)
 
 
-def attention(place, ends, cat, bias, heads, hd, slab):
+def attention(place, lens, cat, heads, hd, slab):
     tokens = cat.shape[1]
     hw = heads * hd
     vmem = pl.BlockSpec(memory_space=pltpu.VMEM)
@@ -1698,7 +1892,7 @@
             jax.ShapeDtypeStruct((8, tokens), F32),
             jax.ShapeDtypeStruct((16, tokens), F32),
         ),
-        in_specs=[smem, smem, vmem, vmem],
+        in_specs=[smem, smem, vmem],
         out_specs=[vmem] * 5,
         scratch_shapes=[
             pltpu.VMEM((heads, AUG, tokens), BF),
@@ -1710,11 +1904,11 @@
             flops=8 * heads * tokens * tokens * hd, bytes_accessed=cat.size * 4,
             transcendentals=heads * tokens * tokens // 2,
         ),
-    )(place, ends, cat, bias)
+    )(place, lens, cat)
 
 
 def attention_back_kernel(
-    place_ref, ends_ref, cat_ref, bias_ref, gg_ref, att_ref, exact_ref, lse_ref, prefix_ref,
+    place_ref, lens_ref, cat_ref, gg_ref, att_ref, exact_ref, lse_ref, prefix_ref,
     out_ref, bias_grad_ref,
     qa, ka, kta, va, do, delta_ref, dk, dv, gp, *, heads, hd, slab,
 ):
@@ -1729,7 +1923,7 @@
     dv[...] = jnp.zeros_like(dv)
     out_ref[4 * hw :, :] = jnp.zeros((out_ref.shape[0] - 4 * hw, tokens), BF)
     for p in range(slabs):
-        src = pl.ds(pl.multiple_of(place_ref[p] * slab, slab), slab)
+        src = pl.ds(pl.multiple_of(storage_of(place_ref, p) * slab, slab), slab)
         dst = pl.ds(p * slab, slab)
         for h in range(heads):
             rows = slice(h * hd, (h + 1) * hd)
@@ -1748,8 +1942,8 @@
     def one_query_block(qb, unused):
         q0 = pl.multiple_of(qb * BQ, BQ)
         pos = q0 + lax.broadcasted_iota(jnp.int32, (1, BQ), 1)
-        start = doc_starts(ends_ref, pos)
-        low = first_block(ends_ref, q0)
+        start = doc_starts(lens_ref, pos)
+        low = doc_starts(lens_ref, q0) // BK
         inside = lax.broadcasted_iota(jnp.int32, (BK, BQ), 0)
 
         def one_key_block(kb, held):
@@ -1770,8 +1964,8 @@
             return tuple(out)
 
         begin = tuple(jnp.zeros((AUG, BQ), F32) for _ in range(heads))
-        done = lax.fori_loop(low, qb + 1, one_key_block, begin)
-        dst = pl.ds(pl.multiple_of(place_ref[qb // per] * slab + lax.rem(qb, per) * BQ, BQ), BQ)
+        done = lax.fori_loop(low, (q0 + BQ + BK - 1) // BK, one_key_block, begin)
+        dst = pl.ds(pl.multiple_of(storage_of(place_ref, qb // per) * slab + lax.rem(qb, per) * BQ, BQ), BQ)
         for h in range(heads):
             out_ref[h * hd : (h + 1) * hd, dst] = (done[h][0:hd, :] * hd**-0.5).astype(BF)
             gp[h : h + 1, pl.ds(q0, BQ)] = done[h][hd : hd + 1, :]
@@ -1782,7 +1976,7 @@
     carry = jnp.zeros((16, 1), F32)
     bias_grad = jnp.zeros((16, 1), F32)
     for p in reversed(range(slabs)):
-        src = pl.ds(pl.multiple_of(place_ref[p] * slab, slab), slab)
+        src = pl.ds(pl.multiple_of(storage_of(place_ref, p) * slab, slab), slab)
         dst = pl.ds(p * slab, slab)
         for h in range(heads):
             out_ref[hw + h * hd : hw + (h + 1) * hd, src] = dk[h, 0:hd, dst].astype(BF)
@@ -1793,14 +1987,14 @@
         for piece in three_parts(grad):
             total = total + dot(piece.astype(BF), tri, 1, 0)
         carry = total[:, 0:1]
-        pre = cat_ref[4 * hw : 4 * hw + 16, src] + bias_ref[:, 0:1]
+        pre = cat_ref[4 * hw : 4 * hw + 16, src]
         low = (total.astype(BF).astype(F32) * jax.nn.sigmoid(-pre)).astype(BF)
         out_ref[4 * hw : 4 * hw + 16, src] = low
         bias_grad = bias_grad + jnp.sum(low.astype(F32), axis=1, keepdims=True)
     bias_grad_ref[...] = jnp.broadcast_to(bias_grad, bias_grad_ref.shape)
 
 
-def attention_back(place, ends, cat, bias, gg, att, exact, lse, prefix, heads, hd, slab):
+def attention_back(place, lens, cat, gg, att, exact, lse, prefix, heads, hd, slab):
     tokens = cat.shape[1]
     vmem = pl.BlockSpec(memory_space=pltpu.VMEM)
     smem = pl.BlockSpec(memory_space=pltpu.SMEM)
@@ -1811,7 +2005,7 @@
             jax.ShapeDtypeStruct(cat.shape, BF),
             jax.ShapeDtypeStruct((16, 128), F32),
         ),
-        in_specs=[smem, smem] + [vmem] * 7,
+        in_specs=[smem, smem] + [vmem] * 6,
         out_specs=[vmem] * 2,
         scratch_shapes=[
             pltpu.VMEM((heads, AUG, tokens), BF),
@@ -1829,7 +2023,7 @@
             flops=20 * heads * tokens * tokens * hd, bytes_accessed=cat.size * 8,
             transcendentals=heads * tokens * tokens // 2,
         ),
-    )(place, ends, cat, bias, gg, att, exact, lse, prefix)
+    )(place, lens, cat, gg, att, exact, lse, prefix)
 
 
 def local_plane(
@@ -1851,80 +2045,51 @@
     group_rows = tokens.shape[1] * plane
     slab = group_rows // slab_place.shape[1]
 
-    def columns(weight, count):
-        return lax.dynamic_slice_in_dim(weight, place * count, count, 1)
-
     inputs, cotangent = tokens[0], out_cotangent[0]
-    slabs = slab_place.shape[1]
-    order = jnp.arange(slabs, dtype=jnp.int32)
-    storage = jnp.sum(
-        jnp.where(slab_place[0][None, :] == order[:, None], order[None, :], 0), axis=1
-    )
-    ends = jnp.cumsum(seq_lengths[0])
-
-    own_attn = jnp.concatenate(
-        [columns(w, hw) for w in (query_weight, key_weight, value_weight, outgate_weight)], axis=1
-    )
-    own_forget = jnp.pad(columns(forget_weight, heads).T, ((0, 16 - heads), (0, 0)))
-    own_mlp = jnp.concatenate(
-        [columns(gate_weight, fw), columns(up_weight, fw), columns(down_weight, fw)], axis=1
-    )
-    normed, cotangent_all, w_attn, w_out, cat = enter(
-        inputs, cotangent, attn_gain, own_attn, own_forget, output_weight, depth, hw
-    )
-    own_mlp, w_attn = lax.optimization_barrier((own_mlp, w_attn))
+    normed, cotangent_all, w_attn, w_out, cat, own_mlp = enter(
+        inputs, cotangent, attn_gain, forget_bias, forget_weight,
+        (query_weight, key_weight, value_weight, outgate_weight),
+        (gate_weight, up_weight, down_weight), output_weight, depth,
+    )
     w_mlp = lax.all_gather(own_mlp, "fsdp", axis=0, tiled=True)
-    bias_own = lax.dynamic_slice_in_dim(forget_bias, place * heads, heads, 0)
-    bias = jnp.broadcast_to(jnp.pad(bias_own, (0, 16 - heads))[:, None], (16, 128))
-    gated, att, exact, lse, prefix = attention(storage, ends, cat, bias, heads, hd, slab)
+    gated, att, exact, lse, prefix = attention(slab_place, seq_lengths, cat, heads, hd, slab)
     mid, normed_mlp = middle(gated, w_out, inputs, mlp_gain)
 
-    grad_mid, mlp_gain_term, branch, down_sum, up_rows, low_term = ffn(
-        normed_mlp, cotangent_all, w_mlp, cotangent, mid, mlp_gain, depth
+    grad_mid, mlp_gain_term, grad_gated, out_term, down_sum, up_rows, low_term = ffn(
+        normed_mlp, cotangent_all, w_mlp, mid, mlp_gain, gated, w_out, depth
     )
     low_grad = lax.psum_scatter(
         low_term.reshape(width, fw), "fsdp", scatter_dimension=0, tiled=True
     )
 
-    grad_gated, out_term = lax.optimization_barrier(
-        (dot(w_out, branch, 1, 1), dot(gated, branch, 1, 0).astype(BF))
-    )
     grad_cat, bias_grad = attention_back(
-        storage, ends, cat, bias, grad_gated, att, exact, lse, prefix, heads, hd, slab
-    )
-    output_weight_grad = lax.psum_scatter(out_term, "fsdp", scatter_dimension=0, tiled=True)
-    lane = width // 3
-    bias_row = lax.dynamic_update_slice_in_dim(
-        jnp.zeros((lane,), F32), bias_grad[:heads, 0], place * heads, 0
-    )
-    small = jnp.concatenate(
-        [jnp.zeros((3, lane), F32), mlp_gain_term.reshape(3, lane), bias_row[None]]
-        + [jnp.zeros((1, lane), F32)]
+        slab_place, seq_lengths, cat, grad_gated, att, exact, lse, prefix, heads, hd, slab
     )
     part = width // (plane * depth)
-    tokens_grad, small_sum, block_out, attn_rows, low_rows = leave(
-        normed, grad_cat, w_attn, down_sum, inputs, grad_mid, mid, attn_gain, small,
-        low_grad.reshape(plane, part, fw), depth,
+    tokens_grad, small_sum, block_out, attn_rows, low_rows, wide_rows = leave(
+        normed, grad_cat, w_attn, down_sum, inputs, grad_mid, mid, attn_gain, mlp_gain_term,
+        bias_grad, low_grad.reshape(plane, part, fw), out_term.reshape(1, depth, part, width),
+        depth, heads,
     )
     (
         query_grad, key_grad, value_grad, outgate_grad, forget_grad, out_grad, gate_grad, up_grad,
         down_grad, attn_gain_grad, mlp_gain_grad, forget_bias_grad, block_out, tokens_grad,
     ) = finish(
-        attn_rows, up_rows, low_rows, small_sum, output_weight_grad, block_out, tokens_grad,
+        attn_rows, up_rows, low_rows, small_sum, wide_rows, block_out, tokens_grad,
         hw, heads,
     )
     return (
         block_out[None],
         tokens_grad[None],
-        attn_gain_grad[0],
+        attn_gain_grad,
         query_grad,
         key_grad,
         value_grad,
         outgate_grad,
-        forget_grad,
+        forget_grad.T,
         forget_bias_grad[0],
         out_grad,
-        mlp_gain_grad[0],
+        mlp_gain_grad,
         gate_grad,
         up_grad,
         down_grad,
@@ -1945,7 +2110,9 @@
         head_count % plane == 0
         and heads <= 8
         and width // head_count == 64
-        and slab % 256 == 0
+        and heads % 2 == 1
+        and width == 8 * heads * 64
+        and slab % 512 == 0
         and group_rows <= 2048
         and width % 768 == 0
         and gate_weight.shape[1] % (128 * plane) == 0

time: 413 us -> 388 us (0.939)
  Pallas kernels: 366 us -> 356 us
  local copies, waits for them, and re-layouts: 11.3 us -> 1.47 us
  matrix products: 8.51 us -> 0 us
  waiting for transfers between devices: 0.1 us -> 7.98 us
  other arithmetic: 6.8 us -> 0 us
    pallas_call x2, Pallas kernels: 141 us -> 132 us  [the longest x1 66.7 us: leave(): pl.pallas_call(functools.partial(leave_kernel, depth=depth, heads=heads),...]
    dot_general x2 -> x0, matrix products: 8.51 us -> none  [dot(): lax.dot_general(a, b, (((ca,), (cb,)), ((), ())), preferred_element_type=...]
    reduce_scatter x1, waiting for transfers between devices: 0.01 us -> 5.84 us  [local_plane(): lax.psum_scatter(low_term.reshape(width, fw), 'fsdp', scatter_dimension=0...]
    pallas_call x1, Pallas kernels: 87.6 us -> 93.4 us  [ffn(): pl.pallas_call(functools.partial(ffn_kernel, depth=depth), name='ffn', ou...]
    pallas_call x1, Pallas kernels: 27.4 us -> 22.1 us  [attention(): pl.pallas_call(functools.partial(attention_kernel, heads=heads, hd=hd, sl...]
    dynamic_slice x5 -> x0, local copies, waits for them, and re-layouts: 4.74 us -> none  [the longest x4 4.67 us: columns(): return lax.dynamic_slice_in_dim(weight, place * count, count, 1)]
  transfers between devices with their start and end apart: 3 -> 2, of which waited for: 0 -> 2; matrix products, arithmetic and copies ran while one was open for 3% -> 0% of each run, Pallas kernels for 50% -> 33%
where the time goes in v5:
time: 388 us; the launch traced here: 380 us
  Pallas kernels  356 us (92%)
  between operations  14.5 us (4%)
  waiting for transfers between devices  7.98 us (2%)
    pallas_call x1, Pallas kernels, ffn(): pl.pallas_call(functools.partial(ffn_kernel, depth=depth), name='ffn', ou...  93.4 us
    pallas_call x1, Pallas kernels, middle(): pl.pallas_call(middle_kernel, name='middle', out_shape=(jax.ShapeDtypeStr...  71.3 us
    pallas_call x1, Pallas kernels, leave(): pl.pallas_call(functools.partial(leave_kernel, depth=depth, heads=heads),...  66.7 us
    pallas_call x1, Pallas kernels, enter(): pl.pallas_call(functools.partial(enter_kernel, depth=depth, heads=heads),...  65.1 us
    pallas_call x1, Pallas kernels, attention_back(): pl.pallas_call(functools.partial(attention_back_kernel, heads=heads, hd=h...  32.2 us
    pallas_call x1, Pallas kernels, attention(): pl.pallas_call(functools.partial(attention_kernel, heads=heads, hd=hd, sl...  22.1 us
  transfers between devices with their start and end apart: 2, of which 2 were waited for; matrix products, arithmetic and copies ran while one was open for 0% of the time, Pallas kernels for 33%

profile of v5, /device:TPU:0, one launch (start us, length us, event | category | flops | bytes accessed | tf_op | source)
XLA Modules:
  0.0 380.0 jit_solution(10136162990911702840)
XLA Ops:
  7.2 0.0 all-gather.2.cloned.1.call-start
  7.2 1.5 copy.30.forget_ref
  8.7 65.1 %enter.1 = (bf16[2048,1536]{1,0:T(8,128)(2,1)}, bf16[2048,1536]{1,0:T(8,128)(2,1)}, bf16[1536,896]{1,0:T(8,128)(2,1)}, bf16[192,1536]{1,0:T(8,128)(2,1)}, f32[89...) custom-call(bf16[256,1536]{1,0:T(8,128)(2,1)} %bitcast.12, bf16[256,1536]{1,0:T(8,128)(2,1)} %bitcast.11, f32[1536]{0:T(1024)} %gain_ref.7, ...), custom_call_target="tpu_custom_call" | custom-call | flops 4831838208 | bytes 25165824 | tf_op jit(solution)/shard_map/enter/pallas_call | solution.py:958
  73.8 0.0 all-gather.2.cloned.1.call-update
  73.9 0.0 reduce-scatter.2.cloned.1.call-start
  73.9 22.1 %attention.1 = (bf16[192,2048]{1,0:T(8,128)(2,1)}, bf16[192,2048]{1,0:T(8,128)(2,1)}, f32[192,2048]{1,0:T(8,128)}, f32[8,2048]{1,0:T(8,128)}, f32[16,2048]{1,0:T(8,128)}) custom-call(s32[1,4]{1,0:T(1,128)} %place_ref.3, s32[1,8]{1,0:T(1,128)} %lens_ref.3, f32[896,2048]{1,0:T(8,128)} %get-tuple-element.57.cat_ref), custom_call_target="tpu_custom_call" | custom-call | flops 6442450944 | bytes 7340032 | tf_op jit(solution)/shard_map/attention/pallas_call | solution.py:1885
  96.0 71.3 %middle.1 = (f32[256,1536]{1,0:T(8,128)}, bf16[2048,1536]{1,0:T(8,128)(2,1)}) custom-call(bf16[192,2048]{1,0:T(8,128)(2,1)} %get-tuple-element.58.gated_ref, bf16[192,1536]{1,0:T(8,128)(2,1)} %get-tuple-element.59.w_ref.w_out_ref, bf16[256,1536]{1,0:T(8,128)(2,1)} %bitcast.13, f32[1536]{0:T(1024)} %gain_ref.6), custom_call_target="tpu_custom_call" | custom-call | flops 1207959552 | bytes 25165824 | tf_op jit(solution)/shard_map/middle/pallas_call | solution.py:1057
  167.3 2.1 all-gather.2.cloned.1.call-done.w_ref
  169.4 93.4 %ffn.1 = (f32[256,1536]{1,0:T(8,128)}, f32[1,1536]{1,0:T(1,128)}, f32[192,2048]{1,0:T(8,128)}, bf16[192,1536]{1,0:T(8,128)(2,1)}, bf16[3,256,1536]{2,1,0:T(8,128...) custom-call(bf16[2048,1536]{1,0:T(8,128)(2,1)} %get-tuple-element.60.nm_ref, ...), custom_call_target="tpu_custom_call" | custom-call | flops 28991029248 | bytes 25165824 | tf_op jit(solution)/shard_map/ffn/pallas_call | solution.py:1430
  262.8 0.0 reduce-scatter.2.cloned.1.call-update
  262.8 32.2 %attention_back.1 = (bf16[896,2048]{1,0:T(8,128)(2,1)}, f32[16,128]{1,0:T(8,128)}) custom-call(s32[1,4]{1,0:T(1,128)} %place_ref.3, s32[1,8]{1,0:T(1,128)} %lens_ref.3, f32[896,2048]{1,0:T(8,128)} %get-tuple-element.57.cat_ref, f32[192,2048]{1,0:T(8,128)} %get-tuple-element.64.gg_ref, bf16[192,2048]{1,0:T(8,128)(2,1)} %get-tuple-element.65.att_ref, ...), custom_call_target="tpu_custom_call" | custom-call | flops 16106127360 | bytes 14680064 | tf_op jit(solution)/shard_map/attention_back/pallas_call | solution.py:2001
  295.1 5.8 %reduce-scatter.2.cloned.1.call-done = bf16[384,512]{1,0:T(8,128)(2,1)} async-done(((bf16[1536,512]{1,0:T(8,128)(2,1)}), bf16[384,512]{1,0:T(8,128)(2,1)}) %reduce-scatter.2.cloned.1.call-update) | async-done | bytes 393232 | tf_op jit(solution)/shard_map/reduce_scatter | solution.py:2061
  300.9 66.7 %leave.1 = (f32[256,1536]{1,0:T(8,128)}, f32[8,512]{1,0:T(8,128)}, bf16[256,1536]{1,0:T(8,128)(2,1)}, bf16[8,48,896]{2,1,0:T(8,128)(2,1)}, bf16[8,48,512]{2,1,0:T(8,128)(2,1)}, /*index=5*/bf16[1,48,1536]{2,1,0:T(8,128)(2,1)}) custom-call(bf16[2048,1536]{1,0:T(8,128)(2,1)} %get-tuple-element.56.normed_ref, bf16[896,2048]{1,0:T(8,128)(2,1)} %get-tuple-element.69.cat_ref, ...), custom_call_target="tpu_custom_call" | custom-call | flops 11274289152 | bytes 25165824 | tf_op jit(solution)/shard_map/leave/pallas_call | solution.py:1639
  367.6 5.1 %finish.1 = (f32[48,1536]{1,0:T(8,128)}, f32[48,1536]{1,0:T(8,128)}, f32[48,1536]{1,0:T(8,128)}, f32[48,1536]{1,0:T(8,128)}, f32[24,48]{1,0:T(8,128)}, /*index=5...) custom-call(bf16[8,48,896]{2,1,0:T(8,128)(2,1)} %get-tuple-element.7, ...), custom_call_target="tpu_custom_call" | custom-call | tf_op jit(solution)/shard_map/finish/pallas_call | solution.py:1722
Async XLA Ops:
  7.2 162.2 %all-gather.2.cloned.1.call-start = ((), (), s32[]{:S(2)}) async-start(), calls=%async_computation.1 | async-start | bytes 5898240 | tf_op jit(solution)/shard_map/all_gather | solution.py:2054
  73.9 227.0 %reduce-scatter.2.cloned.1.call-start = ((), (), s32[]{:S(2)}) async-start(), calls=%async_computation.2 | async-start | bytes 1966080 | tf_op jit(solution)/shard_map/reduce_scatter | solution.py:2061
Sparse Core Ops, SparseCore 0:
  74.0 95.3 all-gather.1
  262.9 37.9 reduce-scatter.1

commit v6 on v5

--- a/solution.py
+++ b/solution.py
@@ -434,19 +434,21 @@
 class Gather:
     sems = 13
 
-    def __init__(self, src, out, send, recv):
+    def __init__(self, src, out, send, recv, stride=None, offset=0):
         c, s, f = here()
         self.src, self.out, self.send, self.recv = src, out, send, recv
         self.c, self.s, self.rows = c, s, src.shape[0]
+        self.stride, self.offset = stride or self.rows, offset
         self.x, self.y, self.sib = (c, flip(s, 1), f), (c, flip(s, 2), f), (1 - c, s, f)
         self.made = []
 
     def block(self, k, half=None):
         index = self.c * 4 + (self.s if k == 0 else flip(self.s, k))
         n = self.rows
+        begin = index * self.stride + self.offset
         if half is None:
-            return self.out.at[pl.ds(pl.multiple_of(index * n, n), n)]
-        return self.out.at[pl.ds(pl.multiple_of(index * n + half * (n // 2), n // 2), n // 2)]
+            return self.out.at[pl.ds(pl.multiple_of(begin, n), n)]
+        return self.out.at[pl.ds(pl.multiple_of(begin + half * (n // 2), n // 2), n // 2)]
 
     def copy(self, src, dst, k, device):
         made = REMOTE(src, dst, self.send.at[k], self.recv.at[k], device, MESH)
@@ -626,8 +628,8 @@
             ))
         ]
 
-    def start(self):
-        for made in self.made:
+    def start(self, part):
+        for made in self.made[part::2]:
             made.start()
 
     def arrive(self):
@@ -789,14 +791,15 @@
 
 WEIGHT_PIECES = 4
 OUT_PIECES = 2
+EARLY = 128
 
 
 def enter_kernel(
     tok_ref, dy_ref, gain_ref, bias_ref, forget_ref,
     query_ref, key_ref, value_ref, outgate_ref, gate_ref, up_ref, down_ref, out_w_ref,
-    normed_ref, dy_all_ref, w_attn_ref, w_out_ref, cat_ref, mlp_ref,
+    normed_ref, dy_all_ref, w_attn_ref, w_out_ref, cat_ref, mlp_ref, early_ref,
     mine, windows, attn, own_forget, forget_all, mlp, normed, turned, cat,
-    s0, r0, s1, r1, sz, rz, so, ro, l0, l1, l2, *, depth, heads,
+    s0, r0, s1, r1, sz, rz, se, re, so, ro, l0, l1, l2, *, depth, heads,
 ):
     c, s, f = here()
     t = c * 4 + s
@@ -827,10 +830,10 @@
         return carry
 
     lax.fori_loop(0, n // STEP, body, 0)
-    a = lax.broadcasted_iota(jnp.int32, (own_forget.shape[0], forget_ref.shape[1]), 0)
-    b = lax.broadcasted_iota(jnp.int32, (own_forget.shape[0], forget_ref.shape[1]), 1)
+    a = lax.broadcasted_iota(jnp.int32, (own_forget.shape[0], forget_ref.shape[0]), 0)
+    b = lax.broadcasted_iota(jnp.int32, (own_forget.shape[0], forget_ref.shape[0]), 1)
     pick = jnp.where((b == a + t * heads) & (a < heads), 1.0, 0.0).astype(BF)
-    own_forget[...] = dot(pick, forget_ref[...], 1, 1).astype(BF)
+    own_forget[...] = dot(pick, forget_ref[...], 1, 0).astype(BF)
     for made in slices:
         made.wait()
 
@@ -880,10 +883,19 @@
         made.start()
     for made in mlp_loads:
         made.wait()
-    mlp_store = pltpu.make_async_copy(mlp, mlp_ref, l2.at[7])
+    mlp_store = pltpu.make_async_copy(mlp.at[:, pl.ds(EARLY, 3 * fw - EARLY)], mlp_ref, l2.at[7])
     mlp_store.start()
+    first_columns = mlp.at[:, pl.ds(0, EARLY)]
+
+    def early_slot(i, owner):
+        return early_ref.at[pl.ds(pl.multiple_of(owner * shard, shard), shard)]
+
+    early = Line([first_columns], early_slot, se, re, depth)
+    early_keep = pltpu.make_async_copy(first_columns, early_slot(0, f), l2.at[8])
+    early_keep.start()
     line.pass_on(1)
     spread.start(l0.at[4])
+    early.start(0)
     first.relay()
     second.start()
     line.pass_on(2)
@@ -930,12 +942,17 @@
     for k in range(1, depth - 1):
         add_shard(jnp.int32(k), k == 1, False)
     add_shard(upper * (depth - 1), False, False)
+    early.pass_on(1)
     second.relay()
     spread.pass_on()
+    early.pass_on(2)
     line.pass_on(3)
     add_shard((1 - upper) * (depth - 1), False, True)
+    early.pass_on(3)
     second.finish()
     line.finish()
+    early.finish()
+    early_keep.wait()
     keep[3].wait()
     spread.finish(l0.at[4])
     mlp_store.wait()
@@ -952,6 +969,7 @@
     whole = jax.ShapeDtypeStruct((8 * n, w), BF)
     dma = pltpu.SemaphoreType.DMA((Gather.sems,))
     line = pltpu.SemaphoreType.DMA((2, depth - 1, WEIGHT_PIECES + 1))
+    early = pltpu.SemaphoreType.DMA((2, depth - 1, 1))
     vmem = pl.BlockSpec(memory_space=pltpu.VMEM)
     smem = pl.BlockSpec(memory_space=pltpu.SMEM)
     anywhere = pl.BlockSpec(memory_space=pl.ANY)
@@ -964,10 +982,11 @@
             jax.ShapeDtypeStruct((depth * shard, cols + 128), BF),
             jax.ShapeDtypeStruct((hw, w), BF),
             jax.ShapeDtypeStruct((cols + 128, 8 * n), F32),
-            jax.ShapeDtypeStruct((shard, 3 * fw), BF),
+            jax.ShapeDtypeStruct((shard, 3 * fw - EARLY), BF),
+            jax.ShapeDtypeStruct((depth * shard, EARLY), BF),
         ),
         in_specs=[vmem, vmem, vmem, smem, vmem] + [anywhere] * 8,
-        out_specs=[anywhere, anywhere, vmem, anywhere, anywhere, anywhere],
+        out_specs=[anywhere, anywhere, vmem, anywhere, anywhere, anywhere, anywhere],
         scratch_shapes=[
             pltpu.VMEM((n, w), BF),
             pltpu.VMEM((4, shard, hw + 64), BF),
@@ -978,12 +997,12 @@
             pltpu.VMEM((8 * n, w), BF),
             pltpu.VMEM((cols + 128, shard), BF),
             pltpu.VMEM((cols + 128, 8 * n), F32),
-            dma, dma, dma, dma, line, line,
+            dma, dma, dma, dma, line, line, early, early,
             pltpu.SemaphoreType.DMA((2, OUT_PIECES)),
             pltpu.SemaphoreType.DMA((OUT_PIECES,)),
             pltpu.SemaphoreType.DMA((6,)),
             pltpu.SemaphoreType.DMA((8 * n // 512,)),
-            pltpu.SemaphoreType.DMA((8,)),
+            pltpu.SemaphoreType.DMA((9,)),
         ],
         compiler_params=pltpu.CompilerParams(
             collective_id=1, has_side_effects=True, vmem_limit_bytes=VMEM_BYTES
@@ -991,7 +1010,7 @@
         cost_estimate=pl.CostEstimate(
             flops=2 * 8 * n * w * cols, bytes_accessed=4 * 8 * n * w * 2, transcendentals=0
         ),
-    )(tokens, cotangent, gain, bias, forget_weight, *attn_weights, *mlp_weights, out_weight)
+    )(tokens, cotangent, gain, bias, forget_weight.T, *attn_weights, *mlp_weights, out_weight)
 
 
 TILE = 256
@@ -999,11 +1018,13 @@
 
 def middle_kernel(
     gated_ref, w_ref, tok_ref, gain_ref, mid_ref, normed_ref,
-    gated, turned, mine, s1, r1, l0, *refs,
+    gated, turned, mine, s0, r0, s1, r1, l0, *refs,
 ):
     c, s, f = here()
-    pairs = PairSum(refs)
     n, width = mine.shape
+    h = n // 2
+    count = len(refs) // 2
+    halves = [PairSum(refs[:count]), PairSum(refs[count:])]
     loads = [
         pltpu.make_async_copy(
             gated_ref.at[:, pl.ds(pl.multiple_of(block * n, n), n)],
@@ -1017,36 +1038,48 @@
     greet(partners())
     for made in loads:
         made.wait()
-
-    def one_pair(i, unused):
-        pairs.between(i)
-        turned[...] = gated[:, rows_of(i, 2 * n)].T
-        for t in range(width // TILE):
-            feats = pl.ds(t * TILE, TILE)
-            pairs.put(i, feats, dot(turned[...], w_ref[:, feats], 1, 0).astype(BF))
-        pairs.to_sibling(i).start()
-        return unused
-
-    lax.fori_loop(0, 4, one_pair, 0)
-    pairs.relay()
-    pairs.arrive()
-
-    def body(i, carry):
-        r = rows_of(i, STEP)
-        mid = tok_ref[r, :].astype(F32) + pairs.total(i, STEP)
-        mid_ref[r, :] = mid
-        mine[r, :] = (mid * mean_square_inverse(mid) * gain_row(gain_ref)).astype(BF)
-        return carry
-
-    lax.fori_loop(0, n // STEP, body, 0)
-    gather = Gather(mine, normed_ref, s1, r1)
-    gather.start()
-    keep = pltpu.make_async_copy(mine, gather.block(0), l0.at[8])
-    keep.start()
-    gather.relay()
-    gather.finish()
-    pairs.finish()
-    keep.wait()
+    for q, pairs in enumerate(halves):
+
+        def one_pair(i, unused, q=q, pairs=pairs):
+            pairs.between(i)
+            for core in (0, 1):
+                tokens = pl.ds(pl.multiple_of((2 * i + core) * n + q * h, h), h)
+                turned[core * h : (core + 1) * h, :] = gated[:, tokens].T
+            for t in range(width // TILE):
+                feats = pl.ds(t * TILE, TILE)
+                pairs.put(i, feats, dot(turned[...], w_ref[:, feats], 1, 0).astype(BF))
+            pairs.to_sibling(i).start()
+            return unused
+
+        lax.fori_loop(0, 4, one_pair, 0)
+    for pairs in halves:
+        pairs.relay()
+    gathers = [
+        Gather(mine.at[pl.ds(q * h, h)], normed_ref, send, recv, n, q * h)
+        for q, (send, recv) in enumerate(((s0, r0), (s1, r1)))
+    ]
+    keep = []
+    for q, pairs in enumerate(halves):
+        pairs.arrive()
+
+        def body(i, carry, q=q, pairs=pairs):
+            r = pl.ds(pl.multiple_of(q * h + i * STEP, STEP), STEP)
+            mid = tok_ref[r, :].astype(F32) + pairs.total(i, STEP)
+            mid_ref[r, :] = mid
+            mine[r, :] = (mid * mean_square_inverse(mid) * gain_row(gain_ref)).astype(BF)
+            return carry
+
+        lax.fori_loop(0, h // STEP, body, 0)
+        gathers[q].start()
+        keep.append(pltpu.make_async_copy(gathers[q].src, gathers[q].block(0), l0.at[8 + q]))
+        keep[q].start()
+    for gather in gathers:
+        gather.relay()
+        gather.finish()
+    for pairs in halves:
+        pairs.finish()
+    for made in keep:
+        made.wait()
 
 
 def middle(gated, w_out, tokens, gain):
@@ -1062,11 +1095,12 @@
         out_specs=[vmem, anywhere],
         scratch_shapes=[
             pltpu.VMEM(gated.shape, BF),
-            pltpu.VMEM((2 * n, gated.shape[0]), BF),
+            pltpu.VMEM((n, gated.shape[0]), BF),
             pltpu.VMEM((n, w), BF),
-            dma, dma, dma,
+            dma, dma, dma, dma, dma,
         ]
-        + PairSum.scratch(n, w),
+        + PairSum.scratch(n // 2, w)
+        + PairSum.scratch(n // 2, w),
         compiler_params=pltpu.CompilerParams(
             collective_id=2, has_side_effects=True, vmem_limit_bytes=VMEM_BYTES
         ),
@@ -1160,19 +1194,22 @@
 
 
 class Exchange:
-    def __init__(self, rows, out, send, recv):
+    def __init__(self, rows, out, send, recv, cols=None):
         self.c, self.s, self.f = here()
         self.place = self.c * 4 + self.s
-        self.rows, self.out, self.send, self.recv = rows, out, send, recv
+        self.rows, self.out, self.send, self.recv, self.cols = rows, out, send, recv, cols
+
+    def mine(self, j):
+        return self.rows.at[j] if self.cols is None else self.rows.at[j, :, self.cols]
 
     def remote(self, j):
         return REMOTE(
-            self.rows.at[j], self.out.at[self.place], self.send.at[j], self.recv.at[self.place],
+            self.mine(j), self.out.at[self.place], self.send.at[j], self.recv.at[self.place],
             (j // 4, j % 4, self.f), MESH,
         )
 
     def local(self, j):
-        return pltpu.make_async_copy(self.rows.at[j], self.out.at[j], self.send.at[j])
+        return pltpu.make_async_copy(self.mine(j), self.out.at[j], self.send.at[j])
 
     def push(self, j):
         pl.when(self.place != j)(self.remote(j).start)
@@ -1185,7 +1222,7 @@
     def finish(self):
         for j in range(8):
             got = REMOTE(
-                self.rows.at[j], self.out.at[j], self.send.at[j], self.recv.at[j],
+                self.mine(j), self.out.at[j], self.send.at[j], self.recv.at[j],
                 (j // 4, j % 4, self.f), MESH,
             )
             pl.when(self.place != j)(got.wait_recv)
@@ -1204,18 +1241,33 @@
 
 
 def ffn_kernel(
-    nm_ref, dy_all_ref, w_ref, mid_ref, gain_ref, gated_ref, w_out_ref,
-    grad_mid_ref, gain_term_ref, gg_ref, out_term_ref, down_ref, up_rows_ref, low_term_ref,
-    nm, dy, w, grads, term, got, rows_sum, mine, branch, stage, down_own, down_near, down_far,
-    l0, l1, l2, s1, r1, s2, r2, s3, r3, s4, r4, *refs, depth,
+    nm_ref, dy_all_ref, early_ref, mid_ref, gain_ref, gated_ref, w_out_ref, *more, depth,
 ):
+    w_refs, more = more[:depth], more[depth:]
+    (
+        grad_mid_ref, gain_term_ref, gg_ref, out_term_ref, down_ref, gate_rows_ref, up_own_ref,
+    ) = more[:7]
+    low_refs, more = more[7 : 7 + depth], more[7 + depth :]
+    (
+        nm, dy, w, grads, term, got, rows_sum, mine, branch, stage, down_own, down_near, down_far,
+        l0, l1, l2, s1, r1, s2, r2, s3, r3, s4, r4, *refs,
+    ) = more
     c, s, f = here()
     n, width = mid_ref.shape
     fw = w.shape[1] // 3
     pairs = PairSum(refs)
     loads = []
-    w_load = pltpu.make_async_copy(w_ref, w, l2.at[8])
-    w_load.start()
+    w_loads = [
+        pltpu.make_async_copy(early_ref, w.at[:, pl.ds(0, EARLY)], l2.at[11]),
+    ]
+    shard = w_refs[0].shape[0]
+    for k, ref in enumerate(w_refs):
+        rows = pl.ds(pl.multiple_of(lax.rem(f + depth - k, depth) * shard, shard), shard)
+        w_loads.append(
+            pltpu.make_async_copy(ref, w.at[rows, pl.ds(EARLY, 3 * fw - EARLY)], l2.at[12 + k])
+        )
+    for made in w_loads:
+        made.start()
     for i, block in enumerate(PairSum.blocks(c, s)):
         src, dst = pl.ds(pl.multiple_of(block * n, n), n), pl.ds(i * n, n)
         made = [
@@ -1230,7 +1282,8 @@
             loads.append(made)
     greeted = signal_line([p[:3] for p in plane_peers()], depth)
     pl.semaphore_wait(pltpu.get_barrier_semaphore(), greeted)
-    w_load.wait()
+    for made in w_loads:
+        made.wait()
 
     def one_pair(i, unused):
         rows = rows_of(i, 2 * n)
@@ -1303,7 +1356,12 @@
         tile = dot(dy[:, feats], grads[:, 2 * fw :], 0, 0).astype(BF)
         tile = tile.reshape((per, depth, term.shape[2], fw))
         for g in range(depth):
-            low_term_ref[g, i * per : (i + 1) * per] = tile[:, g]
+            for k in range(depth):
+
+                @pl.when(lax.rem(g + depth - f, depth) == k)
+                def _(g=g, k=k, tile=tile):
+                    low_refs[k][i * per : (i + 1) * per] = tile[:, g]
+
         for step in todo[i * 2 : i * 2 + 2]:
             line.pass_on(*step)
 
@@ -1372,15 +1430,22 @@
         gg_copy(i).start()
         return unused
 
+    exchange = Exchange(rows_sum, gate_rows_ref, s4, r4, pl.ds(0, fw))
+
+    def collect(i):
+        line.collect(i, rows_sum)
+        for j in range(i * per, (i + 1) * per):
+            exchange.push(j)
+
+    collect(0)
+    collect(1)
     tiles = branch.shape[0] // stage.shape[2]
     w_out_load.wait()
     lax.fori_loop(0, tiles, gg_tile, 0)
+    collect(2)
     out_term[...] = dot(gated_ref[...], branch[...], 1, 0).astype(BF)
     out_store = pltpu.make_async_copy(out_term, out_term_ref, l2.at[10])
     out_store.start()
-    exchange = Exchange(rows_sum, up_rows_ref, s4, r4)
-    down_fx.wait_recv()
-    down_fy.wait_recv()
 
     def down_add(at, cols, slot):
         def body(j, carry):
@@ -1391,6 +1456,9 @@
 
         lax.fori_loop(0, n // 32, body, 0)
 
+    collect(3)
+    down_fx.wait_recv()
+    down_fy.wait_recv()
     down_add(2, pairs.left, 0)
     down_add(1, pairs.right, 1)
     stores = [
@@ -1398,10 +1466,7 @@
     ]
     for made in stores:
         made.start()
-    for i in range(TERM_PIECES):
-        line.collect(i, rows_sum)
-        for j in range(i * per, (i + 1) * per):
-            exchange.push(j)
+    up_own_ref[...] = rows_sum[:, :, fw:]
     exchange.finish()
     for made in stores:
         made.wait()
@@ -1416,9 +1481,9 @@
     line.finish()
 
 
-def ffn(normed_all, cotangent_all, weights, mid, gain, gated, w_out, depth):
+def ffn(normed_all, cotangent_all, weights, early, mid, gain, gated, w_out, depth):
     n, width = mid.shape
-    fw = weights.shape[1] // 3
+    fw = (weights[0].shape[1] + EARLY) // 3
     r = width // (8 * depth)
     hw = gated.shape[0]
     dma = pltpu.SemaphoreType.DMA((16,))
@@ -1436,11 +1501,12 @@
             jax.ShapeDtypeStruct((hw, 8 * n), F32),
             jax.ShapeDtypeStruct((hw, width), BF),
             jax.ShapeDtypeStruct((3, n, width), BF),
-            jax.ShapeDtypeStruct((8, r, 2 * fw), BF),
-            jax.ShapeDtypeStruct((depth, 8, r, fw), BF),
-        ),
-        in_specs=[anywhere] * 3 + [vmem] * 3 + [anywhere],
-        out_specs=[vmem, vmem, anywhere, anywhere, anywhere, vmem, vmem],
+            jax.ShapeDtypeStruct((8, r, fw), BF),
+            jax.ShapeDtypeStruct((8, r, fw), BF),
+        )
+        + (jax.ShapeDtypeStruct((8, r, fw), BF),) * depth,
+        in_specs=[anywhere] * 3 + [vmem] * 3 + [anywhere] * (1 + depth),
+        out_specs=[vmem, vmem, anywhere, anywhere, anywhere, vmem, vmem] + [vmem] * depth,
         scratch_shapes=[
             pltpu.VMEM((8 * n, width), BF),
             pltpu.VMEM((8 * n, width), BF),
@@ -1465,16 +1531,19 @@
             flops=2 * 8 * n * width * fw * 9, bytes_accessed=4 * 8 * n * width * 2,
             transcendentals=0,
         ),
-    )(normed_all, cotangent_all, weights, mid, gain, gated, w_out)
+    )(normed_all, cotangent_all, early, mid, gain, gated, w_out, *weights)
 
 
 def leave_kernel(
     normed_ref, cat_ref, w_ref, down_ref, tok_ref, grad_mid_ref, mid_ref, gain_ref,
-    mlp_term_ref, bias_grad_ref, low_ref, wide_ref,
-    grad_ref, small_sum_ref, out_ref, attn_rows_ref, low_rows_ref, wide_rows_ref,
-    normed, cat, turned, w, small, plane_small, line_small, term, got, rows, wide_got,
-    l0, l1, s2, r2, s3, r3, s5, r5, s6, r6, s7, r7, *refs, depth, heads,
+    mlp_term_ref, bias_grad_ref, up_ref, wide_ref, *more, depth, heads,
 ):
+    low_refs, more = more[:depth], more[depth:]
+    (
+        grad_ref, small_sum_ref, out_ref, attn_rows_ref, low_rows_ref, up_rows_ref, wide_rows_ref,
+        normed, cat, turned, w, small, plane_small, line_small, term, got, rows, wide_got, low_sum,
+        l0, l1, s2, r2, s3, r3, s5, r5, s6, r6, s7, r7, s8, r8, *refs,
+    ) = more
     c, s, f = here()
     n, width = tok_ref.shape
     pairs = PairSum(refs[:7])
@@ -1496,13 +1565,19 @@
     for k in range(depth - 1):
         wide.start_piece(0, k)
     line = LineSum(term, got, s3, r3, depth)
-    low_rows = Exchange(low_ref, low_rows_ref, s6, r6)
+    low_total = low_refs[0][...].astype(F32)
+    for ref in low_refs[1:]:
+        low_total = low_total + ref[...].astype(F32)
+    low_sum[...] = low_total.astype(BF)
+    low_rows = Exchange(low_sum, low_rows_ref, s6, r6)
     deep = width // TERM_PIECES
     per = term.shape[0] // TERM_PIECES
+    low_rows.start()
+    up_rows = Exchange(up_ref, up_rows_ref, s8, r8)
+    up_rows.start()
     for made in down_loads:
         made.wait()
-    down.start()
-    low_rows.start()
+    down.start(0)
     for made in loads:
         made.wait()
     for i in range(TERM_PIECES):
@@ -1537,6 +1612,7 @@
     for step in todo[4:6]:
         line.pass_on(*step)
     pairs.relay()
+    down.start(1)
     for step in todo[6:]:
         line.pass_on(*step)
     attn_rows = Exchange(rows, attn_rows_ref, s5, r5)
@@ -1618,12 +1694,13 @@
     line.finish()
     wide.finish()
     low_rows.finish()
+    up_rows.finish()
     attn_rows.finish()
 
 
 def leave(
-    normed, cat, w_attn, down_sum, tokens, grad_mid, mid, gain, mlp_term, bias_grad, low_rows, wide,
-    depth, heads,
+    normed, cat, w_attn, down_sum, tokens, grad_mid, mid, gain, mlp_term, bias_grad, low, up_own,
+    wide, depth, heads,
 ):
     n, w = grad_mid.shape
     plane = 8
@@ -1644,11 +1721,12 @@
             jax.ShapeDtypeStruct((8, w // 3), F32),
             jax.ShapeDtypeStruct((n, w), BF),
             jax.ShapeDtypeStruct((plane, r, cols), BF),
-            jax.ShapeDtypeStruct(low_rows.shape, BF),
+            jax.ShapeDtypeStruct(low[0].shape, BF),
+            jax.ShapeDtypeStruct(up_own.shape, BF),
             jax.ShapeDtypeStruct((1,) + wide.shape[2:], BF),
         ),
-        in_specs=[anywhere] * 4 + [vmem] * 8,
-        out_specs=[vmem] * 6,
+        in_specs=[anywhere] * 4 + [vmem] * (8 + depth),
+        out_specs=[vmem] * 7,
         scratch_shapes=[
             pltpu.VMEM(normed.shape, BF),
             pltpu.VMEM(cat.shape, BF),
@@ -1661,7 +1739,8 @@
             pltpu.VMEM((2, depth - 1, plane, r, cols), BF),
             pltpu.VMEM((plane, r, cols), BF),
             pltpu.VMEM((2, depth - 1, 1) + wide.shape[2:], BF),
-            dma, dma, sems, sems, line, line, eight, eight, eight, eight, one, one,
+            pltpu.VMEM(low[0].shape, BF),
+            dma, dma, sems, sems, line, line, eight, eight, eight, eight, one, one, eight, eight,
         ]
         + PairSum.scratch(n, w)
         + PairTail.scratch(n, w),
@@ -1672,13 +1751,13 @@
             flops=4 * 8 * n * w * cols, bytes_accessed=4 * 8 * n * w * 2, transcendentals=0
         ),
     )(
-        normed, cat, w_attn, down_sum, tokens, grad_mid, mid, gain, mlp_term, bias_grad, low_rows,
-        wide,
+        normed, cat, w_attn, down_sum, tokens, grad_mid, mid, gain, mlp_term, bias_grad, up_own,
+        wide, *low,
     )
 
 
 def finish_kernel(
-    attn_ref, up_rows_ref, low_ref, small_ref, out_w_ref, block_ref, tok_grad_ref,
+    attn_ref, gate_rows_ref, up_rows_ref, low_ref, small_ref, out_w_ref, block_ref, tok_grad_ref,
     q_ref, k_ref, v_ref, g_ref, f_ref, o_ref, gate_ref, up_ref, down_ref,
     gain1_ref, gain2_ref, bias_ref, out_ref, tokens_ref, *, hw, heads,
 ):
@@ -1698,8 +1777,8 @@
     o_ref[...] = out_w_ref[0].astype(F32)
     for t in range(plane):
         cols = slice(t * fw, (t + 1) * fw)
-        gate_ref[:, cols] = up_rows_ref[t, :, 0:fw].astype(F32)
-        up_ref[:, cols] = up_rows_ref[t, :, fw:].astype(F32)
+        gate_ref[:, cols] = gate_rows_ref[t].astype(F32)
+        up_ref[:, cols] = up_rows_ref[t].astype(F32)
         down_ref[:, cols] = low_ref[t].astype(F32)
     lane = small_ref.shape[1]
     count = gain1_ref.shape[0] // lane
@@ -1711,7 +1790,9 @@
     tokens_ref[...] = tok_grad_ref[...]
 
 
-def finish(attn_rows, up_rows, low_rows, small, out_w, block_out, tokens_grad, hw, heads):
+def finish(
+    attn_rows, gate_rows, up_rows, low_rows, small, out_w, block_out, tokens_grad, hw, heads
+):
     plane, r, _ = attn_rows.shape
     n, w = tokens_grad.shape
     fw = low_rows.shape[2]
@@ -1731,10 +1812,10 @@
             jax.ShapeDtypeStruct((n, w), BF),
             jax.ShapeDtypeStruct((n, w), F32),
         ),
-        in_specs=[vmem] * 7,
+        in_specs=[vmem] * 8,
         out_specs=[vmem] * 14,
         compiler_params=pltpu.CompilerParams(vmem_limit_bytes=VMEM_BYTES),
-    )(attn_rows, up_rows, low_rows, small, out_w, block_out, tokens_grad)
+    )(attn_rows, gate_rows, up_rows, low_rows, small, out_w, block_out, tokens_grad)
 
 
 BQ = 512
@@ -2045,37 +2126,38 @@
     group_rows = tokens.shape[1] * plane
     slab = group_rows // slab_place.shape[1]
 
+    def shift(value, k):
+        return lax.ppermute(value, "fsdp", [(j, (j + k) % depth) for j in range(depth)])
+
     inputs, cotangent = tokens[0], out_cotangent[0]
-    normed, cotangent_all, w_attn, w_out, cat, own_mlp = enter(
+    normed, cotangent_all, w_attn, w_out, cat, own_mlp, early = enter(
         inputs, cotangent, attn_gain, forget_bias, forget_weight,
         (query_weight, key_weight, value_weight, outgate_weight),
         (gate_weight, up_weight, down_weight), output_weight, depth,
     )
-    w_mlp = lax.all_gather(own_mlp, "fsdp", axis=0, tiled=True)
+    w_mlp = [own_mlp] + [shift(own_mlp, k) for k in range(1, depth)]
     gated, att, exact, lse, prefix = attention(slab_place, seq_lengths, cat, heads, hd, slab)
     mid, normed_mlp = middle(gated, w_out, inputs, mlp_gain)
 
-    grad_mid, mlp_gain_term, grad_gated, out_term, down_sum, up_rows, low_term = ffn(
-        normed_mlp, cotangent_all, w_mlp, mid, mlp_gain, gated, w_out, depth
-    )
-    low_grad = lax.psum_scatter(
-        low_term.reshape(width, fw), "fsdp", scatter_dimension=0, tiled=True
-    )
+    grad_mid, mlp_gain_term, grad_gated, out_term, down_sum, gate_rows, up_own, *low_terms = ffn(
+        normed_mlp, cotangent_all, w_mlp, early, mid, mlp_gain, gated, w_out, depth
+    )
+    low = [low_terms[0]] + [shift(low_terms[k], k) for k in range(1, depth)]
 
     grad_cat, bias_grad = attention_back(
         slab_place, seq_lengths, cat, grad_gated, att, exact, lse, prefix, heads, hd, slab
     )
     part = width // (plane * depth)
-    tokens_grad, small_sum, block_out, attn_rows, low_rows, wide_rows = leave(
+    tokens_grad, small_sum, block_out, attn_rows, low_rows, up_rows, wide_rows = leave(
         normed, grad_cat, w_attn, down_sum, inputs, grad_mid, mid, attn_gain, mlp_gain_term,
-        bias_grad, low_grad.reshape(plane, part, fw), out_term.reshape(1, depth, part, width),
-        depth, heads,
+        bias_grad, low, up_own,
+        out_term.reshape(1, depth, part, width), depth, heads,
     )
     (
         query_grad, key_grad, value_grad, outgate_grad, forget_grad, out_grad, gate_grad, up_grad,
         down_grad, attn_gain_grad, mlp_gain_grad, forget_bias_grad, block_out, tokens_grad,
     ) = finish(
-        attn_rows, up_rows, low_rows, small_sum, wide_rows, block_out, tokens_grad,
+        attn_rows, gate_rows, up_rows, low_rows, small_sum, wide_rows, block_out, tokens_grad,
         hw, heads,
     )
     return (

time: 388 us -> 380 us (0.979)
  starting transfers between devices: 0.08 us -> 21.5 us
  between operations: 14.5 us -> 1.17 us
  Pallas kernels: 356 us -> 346 us
  waiting for transfers between devices: 7.98 us -> 3.51 us
    ppermute x0 -> x6, starting transfers between devices: none -> 21.5 us  [shift(): lax.ppermute(value, 'fsdp', [(j, (j + k) % depth) for j in range(depth)])]
    pallas_call x1, Pallas kernels: 66.7 us -> 76 us  [leave(): pl.pallas_call(functools.partial(leave_kernel, depth=depth, heads=heads),...]
    pallas_call x1, Pallas kernels: 93.4 us -> 86.3 us  [ffn(): pl.pallas_call(functools.partial(ffn_kernel, depth=depth), name='ffn', ou...]
    reduce_scatter x1 -> x0, waiting for transfers between devices: 5.84 us -> none  [local_plane(): lax.psum_scatter(low_term.reshape(width, fw), 'fsdp', scatter_dimension=0...]
    pallas_call x1, Pallas kernels: 71.3 us -> 65.5 us  [middle(): pl.pallas_call(middle_kernel, name='middle', out_shape=(jax.ShapeDtypeStr...]
    pallas_call x1, Pallas kernels: 32.2 us -> 26.6 us  [attention_back(): pl.pallas_call(functools.partial(attention_back_kernel, heads=heads, hd=h...]
    pallas_call x1, Pallas kernels: 22.1 us -> 18.2 us  [attention(): pl.pallas_call(functools.partial(attention_kernel, heads=heads, hd=hd, sl...]
  transfers between devices with their start and end apart: 2 -> 6, of which waited for: 2 -> 1; matrix products, arithmetic and copies ran while one was open for 0% -> 0% of each run, Pallas kernels for 33% -> 30%
where the time goes in v6:
time: 380 us; the launch traced here: 373 us
  Pallas kernels  346 us (91%)
  starting transfers between devices  21.5 us (6%)
    pallas_call x1, Pallas kernels, ffn(): pl.pallas_call(functools.partial(ffn_kernel, depth=depth), name='ffn', ou...  86.3 us
    pallas_call x1, Pallas kernels, leave(): pl.pallas_call(functools.partial(leave_kernel, depth=depth, heads=heads),...  76 us
    pallas_call x1, Pallas kernels, enter(): pl.pallas_call(functools.partial(enter_kernel, depth=depth, heads=heads),...  68.1 us
    pallas_call x1, Pallas kernels, middle(): pl.pallas_call(middle_kernel, name='middle', out_shape=(jax.ShapeDtypeStr...  65.5 us
    pallas_call x1, Pallas kernels, attention_back(): pl.pallas_call(functools.partial(attention_back_kernel, heads=heads, hd=h...  26.6 us
    ppermute x6, starting transfers between devices, shift(): lax.ppermute(value, 'fsdp', [(j, (j + k) % depth) for j in range(depth)])  21.5 us
    pallas_call x1, Pallas kernels, attention(): pl.pallas_call(functools.partial(attention_kernel, heads=heads, hd=hd, sl...  18.2 us
  transfers between devices with their start and end apart: 6, of which 1 were waited for; matrix products, arithmetic and copies ran while one was open for 0% of the time, Pallas kernels for 30%

profile of v6, /device:TPU:0, one launch (start us, length us, event | category | flops | bytes accessed | tf_op | source)
XLA Modules:
  0.0 373.0 jit_solution(11440081881273963059)
XLA Ops:
  0.6 68.1 %enter.1 = (bf16[2048,1536]{1,0:T(8,128)(2,1)}, bf16[2048,1536]{1,0:T(8,128)(2,1)}, bf16[1536,896]{1,0:T(8,128)(2,1)}, bf16[192,1536]{1,0:T(8,128)(2,1)}, f32[89...) custom-call(bf16[256,1536]{1,0:T(8,128)(2,1)} %bitcast.10, bf16[256,1536]{1,0:T(8,128)(2,1)} %bitcast.9, ...), custom_call_target="tpu_custom_call" | custom-call | flops 4831838208 | bytes 25165824 | tf_op jit(solution)/shard_map/enter/pallas_call | solution.py:976
  68.7 7.2 %collective-permute-start.2 = (bf16[384,1408]{1,0:T(8,128)(2,1)}, bf16[384,1408]{1,0:T(8,128)(2,1)}, u32[]{:S(2)}, u32[]{:S(2)}) collective-permute-start(bf16[384,1408]{1,0:T(8,128)(2,1)} %get-tuple-element.70.more_0_), channel_id=1, source_target_pairs={{0,3},{1,0},{2,1},{3,2},{4,7},{5,4},{6,5},{7,6},{8,11},{9,8},{10,9... | collective-permute-start | bytes 3244040 | tf_op jit(solution)/shard_map/ppermute | solution.py:2130
  75.9 0.0 collective-permute-start.1
  75.9 0.6 collective-permute-start
  76.6 18.2 %attention.1 = (bf16[192,2048]{1,0:T(8,128)(2,1)}, bf16[192,2048]{1,0:T(8,128)(2,1)}, f32[192,2048]{1,0:T(8,128)}, f32[8,2048]{1,0:T(8,128)}, f32[16,2048]{1,0:T(8,128)}) custom-call(s32[1,4]{1,0:T(1,128)} %place_ref.3, s32[1,8]{1,0:T(1,128)} %lens_ref.3, f32[896,2048]{1,0:T(8,128)} %get-tuple-element.63.cat_ref), custom_call_target="tpu_custom_call" | custom-call | flops 6442450944 | bytes 7340032 | tf_op jit(solution)/shard_map/attention/pallas_call | solution.py:1966
  94.8 65.5 %middle.1 = (f32[256,1536]{1,0:T(8,128)}, bf16[2048,1536]{1,0:T(8,128)(2,1)}) custom-call(bf16[192,2048]{1,0:T(8,128)(2,1)} %get-tuple-element.64.gated_ref, bf16[192,1536]{1,0:T(8,128)(2,1)} %get-tuple-element.65.w_ref.w_out_ref, bf16[256,1536]{1,0:T(8,128)(2,1)} %bitcast.11, f32[1536]{0:T(1024)} %gain_ref.6), custom_call_target="tpu_custom_call" | custom-call | flops 1207959552 | bytes 25165824 | tf_op jit(solution)/shard_map/middle/pallas_call | solution.py:1090
  160.3 0.0 collective-permute-done.2.more_3_
  160.3 3.5 collective-permute-done.1.more_2_
  163.8 0.0 collective-permute-done.more_1_
  163.8 86.3 %ffn.1 = (f32[256,1536]{1,0:T(8,128)}, f32[1,1536]{1,0:T(1,128)}, f32[192,2048]{1,0:T(8,128)}, bf16[192,1536]{1,0:T(8,128)(2,1)}, bf16[3,256,1536]{2,1,0:T(8,128...) custom-call(bf16[2048,1536]{1,0:T(8,128)(2,1)} %get-tuple-element.66, ...), custom_call_target="tpu_custom_call" | custom-call | flops 28991029248 | bytes 25165824 | tf_op jit(solution)/shard_map/ffn/pallas_call | solution.py:1495
  250.1 11.2 %collective-permute-start.3 = (bf16[8,48,512]{2,1,0:T(8,128)(2,1)}, bf16[8,48,512]{2,1,0:T(8,128)(2,1)S(1)}, u32[]{:S(2)}, u32[]{:S(2)}) collective-permute-start(bf16[8,48,512]{2,1,0:T(8,128)(2,1)} %get-tuple-element.85), channel_id=1, source_target_pairs={{0,1},{1,2},{2,3},{3,0},{4,5},{5,6},{6,7},{7,4},{8,9},{9,10},{10,1... | collective-permute-start | bytes 1179656 | tf_op jit(solution)/shard_map/ppermute | solution.py:2130
  261.3 0.0 collective-permute-start.4
  261.3 2.5 collective-permute-start.5
  263.7 26.6 %attention_back.1 = (bf16[896,2048]{1,0:T(8,128)(2,1)}, f32[16,128]{1,0:T(8,128)}) custom-call(s32[1,4]{1,0:T(1,128)} %place_ref.3, s32[1,8]{1,0:T(1,128)} %lens_ref.3, f32[896,2048]{1,0:T(8,128)} %get-tuple-element.63.cat_ref, f32[192,2048]{1,0:T(8,128)} %get-tuple-element.71.gg_ref, bf16[192,2048]{1,0:T(8,128)(2,1)} %get-tuple-element.72.att_ref, ...), custom_call_target="tpu_custom_call" | custom-call | flops 16106127360 | bytes 14680064 | tf_op jit(solution)/shard_map/attention_back/pallas_call | solution.py:2082
  290.4 0.0 collective-permute-done.3.more_1_
  290.4 0.0 collective-permute-done.4.more_2_
  290.4 0.0 copy-start.1
  290.4 0.0 collective-permute-done.5.more_3_
  290.4 0.0 copy-start.2
  290.4 0.7 copy-done
  291.1 0.1 copy-done.1
  291.2 0.1 copy-done.2
  291.4 76.0 %leave.1 = (f32[256,1536]{1,0:T(8,128)}, f32[8,512]{1,0:T(8,128)}, bf16[256,1536]{1,0:T(8,128)(2,1)}, bf16[8,48,896]{2,1,0:T(8,128)(2,1)}, bf16[8,48,512]{2,1,0:...) custom-call(bf16[2048,1536]{1,0:T(8,128)(2,1)} %get-tuple-element.62.normed_ref, ...), custom_call_target="tpu_custom_call" | custom-call | flops 11274289152 | bytes 25165824 | tf_op jit(solution)/shard_map/leave/pallas_call | solution.py:1716
  367.4 5.1 %finish.1 = (f32[48,1536]{1,0:T(8,128)}, f32[48,1536]{1,0:T(8,128)}, f32[48,1536]{1,0:T(8,128)}, f32[48,1536]{1,0:T(8,128)}, f32[24,48]{1,0:T(8,128)}, /*index=5...) custom-call(bf16[8,48,896]{2,1,0:T(8,128)(2,1)} %get-tuple-element.8, ...), custom_call_target="tpu_custom_call" | custom-call | tf_op jit(solution)/shard_map/finish/pallas_call | solution.py:1803
  (1 shorter events, 0.0 us)
Async XLA Ops:
  68.7 91.5 %collective-permute-start.2 = (bf16[384,1408]{1,0:T(8,128)(2,1)}, bf16[384,1408]{1,0:T(8,128)(2,1)}, u32[]{:S(2)}, u32[]{:S(2)}) collective-permute-start(bf16[384,1408]{1,0:T(8,128)(2,1)} %get-tuple-element.70.more_0_), channel_id=1, source_target_pairs={{0,3},{1,0},{2,1},{3,2},{4,7},{5,4},{6,5},{7,6},{8,11},{9,8},{10,9... | collective-permute-start | bytes 3244040 | tf_op jit(solution)/shard_map/ppermute | solution.py:2130
  75.9 87.9 %collective-permute-start.1 = (bf16[384,1408]{1,0:T(8,128)(2,1)}, bf16[384,1408]{1,0:T(8,128)(2,1)}, u32[]{:S(2)}, u32[]{:S(2)}) collective-permute-start(bf16[384,1408]{1,0:T(8,128)(2,1)} %get-tuple-element.70.more_0_), channel_id=1, source_target_pairs={{0,2},{1,3},{2,0},{3,1},{4,6},{5,7},{6,4},{7,5},{8,10},{9,11},{10,... | collective-permute-start | bytes 3244040 | tf_op jit(solution)/shard_map/ppermute | solution.py:2130
  75.9 87.9 %collective-permute-start = (bf16[384,1408]{1,0:T(8,128)(2,1)}, bf16[384,1408]{1,0:T(8,128)(2,1)}, u32[]{:S(2)}, u32[]{:S(2)}) collective-permute-start(bf16[384,1408]{1,0:T(8,128)(2,1)} %get-tuple-element.70.more_0_), channel_id=1, source_target_pairs={{0,1},{1,2},{2,3},{3,0},{4,5},{5,6},{6,7},{7,4},{8,9},{9,10},{10,1... | collective-permute-start | bytes 3244040 | tf_op jit(solution)/shard_map/ppermute | solution.py:2130
  250.1 40.3 %collective-permute-start.3 = (bf16[8,48,512]{2,1,0:T(8,128)(2,1)}, bf16[8,48,512]{2,1,0:T(8,128)(2,1)S(1)}, u32[]{:S(2)}, u32[]{:S(2)}) collective-permute-start(bf16[8,48,512]{2,1,0:T(8,128)(2,1)} %get-tuple-element.85), channel_id=1, source_target_pairs={{0,1},{1,2},{2,3},{3,0},{4,5},{5,6},{6,7},{7,4},{8,9},{9,10},{10,1... | collective-permute-start | bytes 1179656 | tf_op jit(solution)/shard_map/ppermute | solution.py:2130
  261.3 29.1 %collective-permute-start.4 = (bf16[8,48,512]{2,1,0:T(8,128)(2,1)}, bf16[8,48,512]{2,1,0:T(8,128)(2,1)S(1)}, u32[]{:S(2)}, u32[]{:S(2)}) collective-permute-start(bf16[8,48,512]{2,1,0:T(8,128)(2,1)} %get-tuple-element.86), channel_id=1, source_target_pairs={{0,2},{1,3},{2,0},{3,1},{4,6},{5,7},{6,4},{7,5},{8,10},{9,11},{10,... | collective-permute-start | bytes 1179656 | tf_op jit(solution)/shard_map/ppermute | solution.py:2130
  261.3 29.1 %collective-permute-start.5 = (bf16[8,48,512]{2,1,0:T(8,128)(2,1)}, bf16[8,48,512]{2,1,0:T(8,128)(2,1)S(1)}, u32[]{:S(2)}, u32[]{:S(2)}) collective-permute-start(bf16[8,48,512]{2,1,0:T(8,128)(2,1)} %get-tuple-element.87), channel_id=1, source_target_pairs={{0,3},{1,0},{2,1},{3,2},{4,7},{5,4},{6,5},{7,6},{8,11},{9,8},{10,9... | collective-permute-start | bytes 1179656 | tf_op jit(solution)/shard_map/ppermute | solution.py:2130
  290.4 0.7 copy-start
  290.4 0.9 copy-start.1
  290.4 1.0 copy-start.2

commit v7 on v6

--- a/solution.py
+++ b/solution.py
@@ -1316,11 +1316,14 @@
     line = LineSum(term, got, s2, r2, depth)
     deep = width // TERM_PIECES
     per = term.shape[0] // TERM_PIECES
-    for i in range(TERM_PIECES):
-        feats = pl.ds(i * deep, deep)
-        tile = dot(nm[:, feats], grads[:, 0 : 2 * fw], 0, 0).astype(BF)
-        term[i * per : (i + 1) * per] = tile.reshape((per,) + term.shape[1:])
+
+    def weight_tile(i, unused):
+        tile = dot(nm[:, rows_of(i, deep)], grads[:, 0 : 2 * fw], 0, 0).astype(BF)
+        term[pl.ds(i * per, per)] = tile.reshape((per,) + term.shape[1:])
         line.start_piece(i, 0)
+        return unused
+
+    lax.fori_loop(0, TERM_PIECES, weight_tile, 0)
     for k in range(1, depth - 1):
         for i in range(TERM_PIECES):
             line.start_piece(i, k)
@@ -1351,19 +1354,27 @@
     gather.start()
     keep = pltpu.make_async_copy(mine, gather.block(0), l0.at[8])
     keep.start()
-    for i in range(TERM_PIECES):
-        feats = pl.ds(i * deep, deep)
-        tile = dot(dy[:, feats], grads[:, 2 * fw :], 0, 0).astype(BF)
+
+    def low_tile(i, unused):
+        tile = dot(dy[:, rows_of(i, deep)], grads[:, 2 * fw :], 0, 0).astype(BF)
         tile = tile.reshape((per, depth, term.shape[2], fw))
         for g in range(depth):
             for k in range(depth):
 
                 @pl.when(lax.rem(g + depth - f, depth) == k)
-                def _(g=g, k=k, tile=tile):
-                    low_refs[k][i * per : (i + 1) * per] = tile[:, g]
-
-        for step in todo[i * 2 : i * 2 + 2]:
-            line.pass_on(*step)
+                def _(g=g, k=k):
+                    low_refs[k][pl.ds(i * per, per)] = tile[:, g]
+
+        for at in range(TERM_PIECES):
+
+            @pl.when(i == at)
+            def _(at=at):
+                for step in todo[at * 2 : at * 2 + 2]:
+                    line.pass_on(*step)
+
+        return unused
+
+    lax.fori_loop(0, TERM_PIECES, low_tile, 0)
 
     def down_copy(i):
         return REMOTE(
@@ -1535,14 +1546,14 @@
 
 
 def leave_kernel(
-    normed_ref, cat_ref, w_ref, down_ref, tok_ref, grad_mid_ref, mid_ref, gain_ref,
+    normed_ref, cat_ref, w_ref, down_ref, tok_in, grad_mid_in, mid_in, gain_ref,
     mlp_term_ref, bias_grad_ref, up_ref, wide_ref, *more, depth, heads,
 ):
     low_refs, more = more[:depth], more[depth:]
     (
         grad_ref, small_sum_ref, out_ref, attn_rows_ref, low_rows_ref, up_rows_ref, wide_rows_ref,
         normed, cat, turned, w, small, plane_small, line_small, term, got, rows, wide_got, low_sum,
-        l0, l1, s2, r2, s3, r3, s5, r5, s6, r6, s7, r7, s8, r8, *refs,
+        tok_ref, grad_mid_ref, mid_ref, l0, l1, s2, r2, s3, r3, s5, r5, s6, r6, s7, r7, s8, r8, *refs,
     ) = more
     c, s, f = here()
     n, width = tok_ref.shape
@@ -1555,9 +1566,17 @@
         loads.append(pltpu.make_async_copy(cat_ref.at[:, src], cat.at[:, dst], l0.at[i]))
         loads.append(pltpu.make_async_copy(normed_ref.at[src], normed.at[dst], l1.at[i]))
     w_load = pltpu.make_async_copy(w_ref, w, l0.at[8])
+    late = [
+        pltpu.make_async_copy(src, dst, l0.at[10 + i])
+        for i, (src, dst) in enumerate(
+            ((tok_in, tok_ref), (grad_mid_in, grad_mid_ref), (mid_in, mid_ref))
+        )
+    ]
     for made in down_loads + loads:
         made.start()
     w_load.start()
+    for made in late:
+        made.start()
     peers = plane_peers()
     line_peers = [(c, s, lax.rem(f + k, depth), k) for k in range(1, depth)]
     greet([p[:3] for p in peers + line_peers])
@@ -1580,10 +1599,14 @@
     down.start(0)
     for made in loads:
         made.wait()
-    for i in range(TERM_PIECES):
-        tile = dot(cat[...], normed[:, pl.ds(i * deep, deep)], 1, 0).T.astype(BF)
-        term[i * per : (i + 1) * per] = tile.reshape((per,) + term.shape[1:])
+
+    def weight_tile(i, unused):
+        tile = dot(cat[...], normed[:, rows_of(i, deep)], 1, 0).T.astype(BF)
+        term[pl.ds(i * per, per)] = tile.reshape((per,) + term.shape[1:])
         line.start_piece(i, 0)
+        return unused
+
+    lax.fori_loop(0, TERM_PIECES, weight_tile, 0)
     for k in range(1, depth - 1):
         for i in range(TERM_PIECES):
             line.start_piece(i, k)
@@ -1636,6 +1659,8 @@
         grad_ref[r, :] = grad_mid_ref[r, :] + back
         return carry + jnp.sum(grad * tok * inverse, axis=0, keepdims=True)
 
+    for made in late:
+        made.wait()
     gain_term = lax.fori_loop(0, n // STEP, body, jnp.zeros((1, width), F32))
     lane = small.shape[1]
     place = c * 4 + s
@@ -1725,7 +1750,7 @@
             jax.ShapeDtypeStruct(up_own.shape, BF),
             jax.ShapeDtypeStruct((1,) + wide.shape[2:], BF),
         ),
-        in_specs=[anywhere] * 4 + [vmem] * (8 + depth),
+        in_specs=[anywhere] * 7 + [vmem] * (5 + depth),
         out_specs=[vmem] * 7,
         scratch_shapes=[
             pltpu.VMEM(normed.shape, BF),
@@ -1740,6 +1765,9 @@
             pltpu.VMEM((plane, r, cols), BF),
             pltpu.VMEM((2, depth - 1, 1) + wide.shape[2:], BF),
             pltpu.VMEM(low[0].shape, BF),
+            pltpu.VMEM((n, w), BF),
+            pltpu.VMEM((n, w), F32),
+            pltpu.VMEM((n, w), F32),
             dma, dma, sems, sems, line, line, eight, eight, eight, eight, one, one, eight, eight,
         ]
         + PairSum.scratch(n, w)

time: 380 us -> 373 us (0.982); the launches traced: 373 us -> 372 us
  no operation moved by 1% of the time
where the time goes in v7:
time: 373 us; the launch traced here: 372 us
  Pallas kernels  346 us (93%)
  starting transfers between devices  21.3 us (6%)
    pallas_call x1, Pallas kernels, ffn(): pl.pallas_call(functools.partial(ffn_kernel, depth=depth), name='ffn', ou...  86.3 us
    pallas_call x1, Pallas kernels, leave(): pl.pallas_call(functools.partial(leave_kernel, depth=depth, heads=heads),...  75.9 us
    pallas_call x1, Pallas kernels, enter(): pl.pallas_call(functools.partial(enter_kernel, depth=depth, heads=heads),...  68.1 us
    pallas_call x1, Pallas kernels, middle(): pl.pallas_call(middle_kernel, name='middle', out_shape=(jax.ShapeDtypeStr...  65.5 us
    pallas_call x1, Pallas kernels, attention_back(): pl.pallas_call(functools.partial(attention_back_kernel, heads=heads, hd=h...  26.6 us
    ppermute x6, starting transfers between devices, shift(): lax.ppermute(value, 'fsdp', [(j, (j + k) % depth) for j in range(depth)])  21.3 us
    pallas_call x1, Pallas kernels, attention(): pl.pallas_call(functools.partial(attention_kernel, heads=heads, hd=hd, sl...  18.2 us
  transfers between devices with their start and end apart: 6, of which 1 were waited for; matrix products, arithmetic and copies ran while one was open for 0% of the time, Pallas kernels for 30%

profile of v7, /device:TPU:0, one launch (start us, length us, event | category | flops | bytes accessed | tf_op | source)
XLA Modules:
  0.0 372.2 jit_solution(11824102977545821386)
XLA Ops:
  0.6 68.1 %enter.1 = (bf16[2048,1536]{1,0:T(8,128)(2,1)}, bf16[2048,1536]{1,0:T(8,128)(2,1)}, bf16[1536,896]{1,0:T(8,128)(2,1)}, bf16[192,1536]{1,0:T(8,128)(2,1)}, f32[89...) custom-call(bf16[256,1536]{1,0:T(8,128)(2,1)} %bitcast.10, bf16[256,1536]{1,0:T(8,128)(2,1)} %bitcast.9, ...), custom_call_target="tpu_custom_call" | custom-call | flops 4831838208 | bytes 25165824 | tf_op jit(solution)/shard_map/enter/pallas_call | solution.py:976
  68.7 7.2 %collective-permute-start.2 = (bf16[384,1408]{1,0:T(8,128)(2,1)}, bf16[384,1408]{1,0:T(8,128)(2,1)}, u32[]{:S(2)}, u32[]{:S(2)}) collective-permute-start(bf16[384,1408]{1,0:T(8,128)(2,1)} %get-tuple-element.70.more_0_), channel_id=1, source_target_pairs={{0,3},{1,0},{2,1},{3,2},{4,7},{5,4},{6,5},{7,6},{8,11},{9,8},{10,9... | collective-permute-start | bytes 3244040 | tf_op jit(solution)/shard_map/ppermute | solution.py:2158
  75.9 0.0 collective-permute-start.1
  75.9 0.6 collective-permute-start
  76.6 18.2 %attention.1 = (bf16[192,2048]{1,0:T(8,128)(2,1)}, bf16[192,2048]{1,0:T(8,128)(2,1)}, f32[192,2048]{1,0:T(8,128)}, f32[8,2048]{1,0:T(8,128)}, f32[16,2048]{1,0:T(8,128)}) custom-call(s32[1,4]{1,0:T(1,128)} %place_ref.3, s32[1,8]{1,0:T(1,128)} %lens_ref.3, f32[896,2048]{1,0:T(8,128)} %get-tuple-element.63.cat_ref), custom_call_target="tpu_custom_call" | custom-call | flops 6442450944 | bytes 7340032 | tf_op jit(solution)/shard_map/attention/pallas_call | solution.py:1994
  94.8 65.5 %middle.1 = (f32[256,1536]{1,0:T(8,128)}, bf16[2048,1536]{1,0:T(8,128)(2,1)}) custom-call(bf16[192,2048]{1,0:T(8,128)(2,1)} %get-tuple-element.64.gated_ref, bf16[192,1536]{1,0:T(8,128)(2,1)} %get-tuple-element.65.w_ref.w_out_ref, bf16[256,1536]{1,0:T(8,128)(2,1)} %bitcast.11, f32[1536]{0:T(1024)} %gain_ref.6), custom_call_target="tpu_custom_call" | custom-call | flops 1207959552 | bytes 25165824 | tf_op jit(solution)/shard_map/middle/pallas_call | solution.py:1090
  160.3 0.0 collective-permute-done.2.more_3_
  160.3 3.5 collective-permute-done.1.more_2_
  163.8 0.0 collective-permute-done.more_1_
  163.8 86.3 %ffn.1 = (f32[256,1536]{1,0:T(8,128)}, f32[1,1536]{1,0:T(1,128)}, f32[192,2048]{1,0:T(8,128)}, bf16[192,1536]{1,0:T(8,128)(2,1)}, bf16[3,256,1536]{2,1,0:T(8,128...) custom-call(bf16[2048,1536]{1,0:T(8,128)(2,1)} %get-tuple-element.66, ...), custom_call_target="tpu_custom_call" | custom-call | flops 28991029248 | bytes 25165824 | tf_op jit(solution)/shard_map/ffn/pallas_call | solution.py:1506
  250.1 11.0 %collective-permute-start.3 = (bf16[8,48,512]{2,1,0:T(8,128)(2,1)}, bf16[8,48,512]{2,1,0:T(8,128)(2,1)S(1)}, u32[]{:S(2)}, u32[]{:S(2)}) collective-permute-start(bf16[8,48,512]{2,1,0:T(8,128)(2,1)} %get-tuple-element.85), channel_id=1, source_target_pairs={{0,1},{1,2},{2,3},{3,0},{4,5},{5,6},{6,7},{7,4},{8,9},{9,10},{10,1... | collective-permute-start | bytes 1179656 | tf_op jit(solution)/shard_map/ppermute | solution.py:2158
  261.1 0.0 collective-permute-start.4
  261.1 2.4 collective-permute-start.5
  263.5 26.6 %attention_back.1 = (bf16[896,2048]{1,0:T(8,128)(2,1)}, f32[16,128]{1,0:T(8,128)}) custom-call(s32[1,4]{1,0:T(1,128)} %place_ref.3, s32[1,8]{1,0:T(1,128)} %lens_ref.3, f32[896,2048]{1,0:T(8,128)} %get-tuple-element.63.cat_ref, f32[192,2048]{1,0:T(8,128)} %get-tuple-element.71.gg_ref, bf16[192,2048]{1,0:T(8,128)(2,1)} %get-tuple-element.72.att_ref, ...), custom_call_target="tpu_custom_call" | custom-call | flops 16106127360 | bytes 14680064 | tf_op jit(solution)/shard_map/attention_back/pallas_call | solution.py:2110
  290.1 0.0 collective-permute-done.3.more_1_
  290.1 0.0 collective-permute-done.4.more_2_
  290.2 0.0 copy-start.1
  290.2 0.0 collective-permute-done.5.more_3_
  290.2 0.0 copy-start.2
  290.2 0.7 copy-done
  290.9 0.1 copy-done.1
  291.0 0.1 copy-done.2
  291.1 75.9 %leave.1 = (f32[256,1536]{1,0:T(8,128)}, f32[8,512]{1,0:T(8,128)}, bf16[256,1536]{1,0:T(8,128)(2,1)}, bf16[8,48,896]{2,1,0:T(8,128)(2,1)}, bf16[8,48,512]{2,1,0:...) custom-call(bf16[2048,1536]{1,0:T(8,128)(2,1)} %get-tuple-element.62.normed_ref, ...), custom_call_target="tpu_custom_call" | custom-call | flops 11274289152 | bytes 25165824 | tf_op jit(solution)/shard_map/leave/pallas_call | solution.py:1741
  367.1 5.1 %finish.1 = (f32[48,1536]{1,0:T(8,128)}, f32[48,1536]{1,0:T(8,128)}, f32[48,1536]{1,0:T(8,128)}, f32[48,1536]{1,0:T(8,128)}, f32[24,48]{1,0:T(8,128)}, /*index=5...) custom-call(bf16[8,48,896]{2,1,0:T(8,128)(2,1)} %get-tuple-element.8, ...), custom_call_target="tpu_custom_call" | custom-call | tf_op jit(solution)/shard_map/finish/pallas_call | solution.py:1831
  (1 shorter events, 0.0 us)
Async XLA Ops:
  68.7 91.5 %collective-permute-start.2 = (bf16[384,1408]{1,0:T(8,128)(2,1)}, bf16[384,1408]{1,0:T(8,128)(2,1)}, u32[]{:S(2)}, u32[]{:S(2)}) collective-permute-start(bf16[384,1408]{1,0:T(8,128)(2,1)} %get-tuple-element.70.more_0_), channel_id=1, source_target_pairs={{0,3},{1,0},{2,1},{3,2},{4,7},{5,4},{6,5},{7,6},{8,11},{9,8},{10,9... | collective-permute-start | bytes 3244040 | tf_op jit(solution)/shard_map/ppermute | solution.py:2158
  75.9 87.9 %collective-permute-start.1 = (bf16[384,1408]{1,0:T(8,128)(2,1)}, bf16[384,1408]{1,0:T(8,128)(2,1)}, u32[]{:S(2)}, u32[]{:S(2)}) collective-permute-start(bf16[384,1408]{1,0:T(8,128)(2,1)} %get-tuple-element.70.more_0_), channel_id=1, source_target_pairs={{0,2},{1,3},{2,0},{3,1},{4,6},{5,7},{6,4},{7,5},{8,10},{9,11},{10,... | collective-permute-start | bytes 3244040 | tf_op jit(solution)/shard_map/ppermute | solution.py:2158
  75.9 87.9 %collective-permute-start = (bf16[384,1408]{1,0:T(8,128)(2,1)}, bf16[384,1408]{1,0:T(8,128)(2,1)}, u32[]{:S(2)}, u32[]{:S(2)}) collective-permute-start(bf16[384,1408]{1,0:T(8,128)(2,1)} %get-tuple-element.70.more_0_), channel_id=1, source_target_pairs={{0,1},{1,2},{2,3},{3,0},{4,5},{5,6},{6,7},{7,4},{8,9},{9,10},{10,1... | collective-permute-start | bytes 3244040 | tf_op jit(solution)/shard_map/ppermute | solution.py:2158
  250.1 40.1 %collective-permute-start.3 = (bf16[8,48,512]{2,1,0:T(8,128)(2,1)}, bf16[8,48,512]{2,1,0:T(8,128)(2,1)S(1)}, u32[]{:S(2)}, u32[]{:S(2)}) collective-permute-start(bf16[8,48,512]{2,1,0:T(8,128)(2,1)} %get-tuple-element.85), channel_id=1, source_target_pairs={{0,1},{1,2},{2,3},{3,0},{4,5},{5,6},{6,7},{7,4},{8,9},{9,10},{10,1... | collective-permute-start | bytes 1179656 | tf_op jit(solution)/shard_map/ppermute | solution.py:2158
  261.1 29.1 %collective-permute-start.4 = (bf16[8,48,512]{2,1,0:T(8,128)(2,1)}, bf16[8,48,512]{2,1,0:T(8,128)(2,1)S(1)}, u32[]{:S(2)}, u32[]{:S(2)}) collective-permute-start(bf16[8,48,512]{2,1,0:T(8,128)(2,1)} %get-tuple-element.86), channel_id=1, source_target_pairs={{0,2},{1,3},{2,0},{3,1},{4,6},{5,7},{6,4},{7,5},{8,10},{9,11},{10,... | collective-permute-start | bytes 1179656 | tf_op jit(solution)/shard_map/ppermute | solution.py:2158
  261.1 29.1 %collective-permute-start.5 = (bf16[8,48,512]{2,1,0:T(8,128)(2,1)}, bf16[8,48,512]{2,1,0:T(8,128)(2,1)S(1)}, u32[]{:S(2)}, u32[]{:S(2)}) collective-permute-start(bf16[8,48,512]{2,1,0:T(8,128)(2,1)} %get-tuple-element.87), channel_id=1, source_target_pairs={{0,3},{1,0},{2,1},{3,2},{4,7},{5,4},{6,5},{7,6},{8,11},{9,8},{10,9... | collective-permute-start | bytes 1179656 | tf_op jit(solution)/shard_map/ppermute | solution.py:2158
  290.1 0.7 copy-start
  290.2 0.9 copy-start.1
  290.2 1.0 copy-start.2

commit v8 on v7

--- a/solution.py
+++ b/solution.py
@@ -679,7 +679,7 @@
         self.c, self.s, self.f = here()
 
     def copy(self, i, distance, up):
-        owner = self.f - (distance - 1) if up else self.f + (distance - 1)
+        owner = self.owner(distance - 1, up)
         to = lax.rem(self.f + (1 if up else self.depth - 1), self.depth)
         src = self.own[i] if distance == 1 else self.slot(i, owner)
         k = 0 if up else 1
@@ -692,6 +692,9 @@
             MESH,
         )
 
+    def owner(self, distance, up):
+        return lax.rem(self.f + (self.depth - distance if up else distance), self.depth)
+
     def may_send(self, distance, up):
         if up:
             return (self.f < self.depth - 1) & (self.f >= distance - 1)
@@ -712,7 +715,7 @@
                     pl.when(self.may_send(distance + 1, up))(self.copy(i, distance + 1, up).start)
 
     def got(self, i, distance, up):
-        owner = self.f - distance if up else self.f + distance
+        owner = self.owner(distance, up)
         k = 0 if up else 1
         place = self.slot(i, owner)
         return REMOTE(

time: 373 us -> 373 us (level)
  Pallas kernels: 346 us -> 351 us
    pallas_call x1, Pallas kernels: 75.9 us -> 70.3 us  [leave(): pl.pallas_call(functools.partial(leave_kernel, depth=depth, heads=heads),...]
    pallas_call x1, Pallas kernels: 26.6 us -> 32.2 us  [attention_back(): pl.pallas_call(functools.partial(attention_back_kernel, heads=heads, hd=h...]
    pallas_call x1, Pallas kernels: 18.2 us -> 22.1 us  [attention(): pl.pallas_call(functools.partial(attention_kernel, heads=heads, hd=hd, sl...]
  transfers between devices with their start and end apart: 6 -> 6, of which waited for: 1 -> 0; matrix products, arithmetic and copies ran while one was open for 0% -> 0% of each run, Pallas kernels for 30% -> 32%
where the time goes in v8:
time: 373 us; the launch traced here: 372 us
  Pallas kernels  351 us (94%)
  starting transfers between devices  19.9 us (5%)
    pallas_call x1, Pallas kernels, ffn(): pl.pallas_call(functools.partial(ffn_kernel, depth=depth), name='ffn', ou...  87.2 us
    pallas_call x1, Pallas kernels, leave(): pl.pallas_call(functools.partial(leave_kernel, depth=depth, heads=heads),...  70.3 us
    pallas_call x1, Pallas kernels, enter(): pl.pallas_call(functools.partial(enter_kernel, depth=depth, heads=heads),...  68.1 us
    pallas_call x1, Pallas kernels, middle(): pl.pallas_call(middle_kernel, name='middle', out_shape=(jax.ShapeDtypeStr...  65.5 us
    pallas_call x1, Pallas kernels, attention_back(): pl.pallas_call(functools.partial(attention_back_kernel, heads=heads, hd=h...  32.2 us
    pallas_call x1, Pallas kernels, attention(): pl.pallas_call(functools.partial(attention_kernel, heads=heads, hd=hd, sl...  22.1 us
    ppermute x6, starting transfers between devices, shift(): lax.ppermute(value, 'fsdp', [(j, (j + k) % depth) for j in range(depth)])  19.9 us
  transfers between devices with their start and end apart: 6, of which 0 were waited for; matrix products, arithmetic and copies ran while one was open for 0% of the time, Pallas kernels for 32%

profile of v8, /device:TPU:0, one launch (start us, length us, event | category | flops | bytes accessed | tf_op | source)
XLA Modules:
  0.0 372.2 jit_solution(11405442776238157579)
XLA Ops:
  0.6 68.1 %enter.1 = (bf16[2048,1536]{1,0:T(8,128)(2,1)}, bf16[2048,1536]{1,0:T(8,128)(2,1)}, bf16[1536,896]{1,0:T(8,128)(2,1)}, bf16[192,1536]{1,0:T(8,128)(2,1)}, f32[89...) custom-call(bf16[256,1536]{1,0:T(8,128)(2,1)} %bitcast.10, bf16[256,1536]{1,0:T(8,128)(2,1)} %bitcast.9, ...), custom_call_target="tpu_custom_call" | custom-call | flops 4831838208 | bytes 25165824 | tf_op jit(solution)/shard_map/enter/pallas_call | solution.py:979
  68.7 7.2 %collective-permute-start.2 = (bf16[384,1408]{1,0:T(8,128)(2,1)}, bf16[384,1408]{1,0:T(8,128)(2,1)}, u32[]{:S(2)}, u32[]{:S(2)}) collective-permute-start(bf16[384,1408]{1,0:T(8,128)(2,1)} %get-tuple-element.70.more_0_), channel_id=1, source_target_pairs={{0,3},{1,0},{2,1},{3,2},{4,7},{5,4},{6,5},{7,6},{8,11},{9,8},{10,9... | collective-permute-start | bytes 3244040 | tf_op jit(solution)/shard_map/ppermute | solution.py:2161
  75.9 0.0 collective-permute-start.1
  75.9 0.6 collective-permute-start
  76.6 22.1 %attention.1 = (bf16[192,2048]{1,0:T(8,128)(2,1)}, bf16[192,2048]{1,0:T(8,128)(2,1)}, f32[192,2048]{1,0:T(8,128)}, f32[8,2048]{1,0:T(8,128)}, f32[16,2048]{1,0:T(8,128)}) custom-call(s32[1,4]{1,0:T(1,128)} %place_ref.3, s32[1,8]{1,0:T(1,128)} %lens_ref.3, f32[896,2048]{1,0:T(8,128)} %get-tuple-element.63.cat_ref), custom_call_target="tpu_custom_call" | custom-call | flops 6442450944 | bytes 7340032 | tf_op jit(solution)/shard_map/attention/pallas_call | solution.py:1997
  98.7 65.5 %middle.1 = (f32[256,1536]{1,0:T(8,128)}, bf16[2048,1536]{1,0:T(8,128)(2,1)}) custom-call(bf16[192,2048]{1,0:T(8,128)(2,1)} %get-tuple-element.64.gated_ref, bf16[192,1536]{1,0:T(8,128)(2,1)} %get-tuple-element.65.w_ref.w_out_ref, bf16[256,1536]{1,0:T(8,128)(2,1)} %bitcast.11, f32[1536]{0:T(1024)} %gain_ref.6), custom_call_target="tpu_custom_call" | custom-call | flops 1207959552 | bytes 25165824 | tf_op jit(solution)/shard_map/middle/pallas_call | solution.py:1093
  164.2 0.0 collective-permute-done.2.more_3_
  164.2 0.0 collective-permute-done.1.more_2_
  164.2 0.0 collective-permute-done.more_1_
  164.2 87.2 %ffn.1 = (f32[256,1536]{1,0:T(8,128)}, f32[1,1536]{1,0:T(1,128)}, f32[192,2048]{1,0:T(8,128)}, bf16[192,1536]{1,0:T(8,128)(2,1)}, bf16[3,256,1536]{2,1,0:T(8,128...) custom-call(bf16[2048,1536]{1,0:T(8,128)(2,1)} %get-tuple-element.66, ...), custom_call_target="tpu_custom_call" | custom-call | flops 28991029248 | bytes 25165824 | tf_op jit(solution)/shard_map/ffn/pallas_call | solution.py:1509
  251.5 9.6 %collective-permute-start.3 = (bf16[8,48,512]{2,1,0:T(8,128)(2,1)}, bf16[8,48,512]{2,1,0:T(8,128)(2,1)S(1)}, u32[]{:S(2)}, u32[]{:S(2)}) collective-permute-start(bf16[8,48,512]{2,1,0:T(8,128)(2,1)} %get-tuple-element.85), channel_id=1, source_target_pairs={{0,1},{1,2},{2,3},{3,0},{4,5},{5,6},{6,7},{7,4},{8,9},{9,10},{10,1... | collective-permute-start | bytes 1179656 | tf_op jit(solution)/shard_map/ppermute | solution.py:2161
  261.1 0.0 collective-permute-start.4
  261.1 2.4 collective-permute-start.5
  263.5 32.2 %attention_back.1 = (bf16[896,2048]{1,0:T(8,128)(2,1)}, f32[16,128]{1,0:T(8,128)}) custom-call(s32[1,4]{1,0:T(1,128)} %place_ref.3, s32[1,8]{1,0:T(1,128)} %lens_ref.3, f32[896,2048]{1,0:T(8,128)} %get-tuple-element.63.cat_ref, f32[192,2048]{1,0:T(8,128)} %get-tuple-element.71.gg_ref, bf16[192,2048]{1,0:T(8,128)(2,1)} %get-tuple-element.72.att_ref, ...), custom_call_target="tpu_custom_call" | custom-call | flops 16106127360 | bytes 14680064 | tf_op jit(solution)/shard_map/attention_back/pallas_call | solution.py:2113
  295.7 0.0 collective-permute-done.3.more_1_
  295.8 0.0 collective-permute-done.4.more_2_
  295.8 0.0 copy-start.1
  295.8 0.0 collective-permute-done.5.more_3_
  295.8 0.0 copy-start.2
  295.8 0.7 copy-done
  296.5 0.1 copy-done.1
  296.6 0.1 copy-done.2
  296.8 70.3 %leave.1 = (f32[256,1536]{1,0:T(8,128)}, f32[8,512]{1,0:T(8,128)}, bf16[256,1536]{1,0:T(8,128)(2,1)}, bf16[8,48,896]{2,1,0:T(8,128)(2,1)}, bf16[8,48,512]{2,1,0:...) custom-call(bf16[2048,1536]{1,0:T(8,128)(2,1)} %get-tuple-element.62.normed_ref, ...), custom_call_target="tpu_custom_call" | custom-call | flops 11274289152 | bytes 25165824 | tf_op jit(solution)/shard_map/leave/pallas_call | solution.py:1744
  367.0 5.1 %finish.1 = (f32[48,1536]{1,0:T(8,128)}, f32[48,1536]{1,0:T(8,128)}, f32[48,1536]{1,0:T(8,128)}, f32[48,1536]{1,0:T(8,128)}, f32[24,48]{1,0:T(8,128)}, /*index=5...) custom-call(bf16[8,48,896]{2,1,0:T(8,128)(2,1)} %get-tuple-element.8, ...), custom_call_target="tpu_custom_call" | custom-call | tf_op jit(solution)/shard_map/finish/pallas_call | solution.py:1834
  (1 shorter events, 0.0 us)
Async XLA Ops:
  68.7 95.4 %collective-permute-start.2 = (bf16[384,1408]{1,0:T(8,128)(2,1)}, bf16[384,1408]{1,0:T(8,128)(2,1)}, u32[]{:S(2)}, u32[]{:S(2)}) collective-permute-start(bf16[384,1408]{1,0:T(8,128)(2,1)} %get-tuple-element.70.more_0_), channel_id=1, source_target_pairs={{0,3},{1,0},{2,1},{3,2},{4,7},{5,4},{6,5},{7,6},{8,11},{9,8},{10,9... | collective-permute-start | bytes 3244040 | tf_op jit(solution)/shard_map/ppermute | solution.py:2161
  75.9 88.3 %collective-permute-start.1 = (bf16[384,1408]{1,0:T(8,128)(2,1)}, bf16[384,1408]{1,0:T(8,128)(2,1)}, u32[]{:S(2)}, u32[]{:S(2)}) collective-permute-start(bf16[384,1408]{1,0:T(8,128)(2,1)} %get-tuple-element.70.more_0_), channel_id=1, source_target_pairs={{0,2},{1,3},{2,0},{3,1},{4,6},{5,7},{6,4},{7,5},{8,10},{9,11},{10,... | collective-permute-start | bytes 3244040 | tf_op jit(solution)/shard_map/ppermute | solution.py:2161
  75.9 88.3 %collective-permute-start = (bf16[384,1408]{1,0:T(8,128)(2,1)}, bf16[384,1408]{1,0:T(8,128)(2,1)}, u32[]{:S(2)}, u32[]{:S(2)}) collective-permute-start(bf16[384,1408]{1,0:T(8,128)(2,1)} %get-tuple-element.70.more_0_), channel_id=1, source_target_pairs={{0,1},{1,2},{2,3},{3,0},{4,5},{5,6},{6,7},{7,4},{8,9},{9,10},{10,1... | collective-permute-start | bytes 3244040 | tf_op jit(solution)/shard_map/ppermute | solution.py:2161
  251.5 44.3 %collective-permute-start.3 = (bf16[8,48,512]{2,1,0:T(8,128)(2,1)}, bf16[8,48,512]{2,1,0:T(8,128)(2,1)S(1)}, u32[]{:S(2)}, u32[]{:S(2)}) collective-permute-start(bf16[8,48,512]{2,1,0:T(8,128)(2,1)} %get-tuple-element.85), channel_id=1, source_target_pairs={{0,1},{1,2},{2,3},{3,0},{4,5},{5,6},{6,7},{7,4},{8,9},{9,10},{10,1... | collective-permute-start | bytes 1179656 | tf_op jit(solution)/shard_map/ppermute | solution.py:2161
  261.1 34.7 %collective-permute-start.4 = (bf16[8,48,512]{2,1,0:T(8,128)(2,1)}, bf16[8,48,512]{2,1,0:T(8,128)(2,1)S(1)}, u32[]{:S(2)}, u32[]{:S(2)}) collective-permute-start(bf16[8,48,512]{2,1,0:T(8,128)(2,1)} %get-tuple-element.86), channel_id=1, source_target_pairs={{0,2},{1,3},{2,0},{3,1},{4,6},{5,7},{6,4},{7,5},{8,10},{9,11},{10,... | collective-permute-start | bytes 1179656 | tf_op jit(solution)/shard_map/ppermute | solution.py:2161
  261.1 34.7 %collective-permute-start.5 = (bf16[8,48,512]{2,1,0:T(8,128)(2,1)}, bf16[8,48,512]{2,1,0:T(8,128)(2,1)S(1)}, u32[]{:S(2)}, u32[]{:S(2)}) collective-permute-start(bf16[8,48,512]{2,1,0:T(8,128)(2,1)} %get-tuple-element.87), channel_id=1, source_target_pairs={{0,3},{1,0},{2,1},{3,2},{4,7},{5,4},{6,5},{7,6},{8,11},{9,8},{10,9... | collective-permute-start | bytes 1179656 | tf_op jit(solution)/shard_map/ppermute | solution.py:2161
  295.8 0.7 copy-start
  295.8 0.9 copy-start.1
  295.8 1.0 copy-start.2
